TPU v7x, 32 devices: a whole 2x2x4 slice. The times are simulated.
32 devices in a mesh: row: 4 (over y, x), col: 8 (over z, core).
Axes of the slice: x: 2, y: 2, z: 4, core: 2. Of those that a mesh axis runs over, the one named last changes fastest.
Arguments:
- stream_in: bfloat16 [12288, 2048], P('row', 'col'), may hold values from -50 to 50
- w_qkv: bfloat16 [3, 2048, 2048], P(None, 'col', 'row'), may hold values from -0.125 to 0.125
- w_out: bfloat16 [2048, 2048], P('row', 'col'), may hold values from -0.5 to 0.5
- w_gate_up: bfloat16 [2, 2048, 8192], P(None, 'col', 'row'), may hold values from -0.125 to 0.125
- w_down: bfloat16 [8192, 2048], P('row', 'col'), may hold values from -0.125 to 0.125
- gain_attn: float32 [2048], P('col'), may hold values from 0.5 to 1.5
- gain_ffn: float32 [2048], P('col'), may hold values from 0.5 to 1.5
- gate_logit: float32 [16], P('row'), may hold values from -2 to 2
- memory: float32 [8, 16, 128, 128], P('col', 'row'), may hold values from -1.2 to 1.2
- memory_norm: float32 [8, 16, 128], P('col', 'row'), may hold values from 0.05 to 0.2
- offsets: int32 [8, 4], P('col'), may hold values from 512 to 1024, as said below
- lengths: int32 [8, 4], P('col'), may hold values from 64 to 128, as said below
- cotangent: bfloat16 [12288, 2048], P('row', 'col'), may hold values from -6 to 6
Outputs:
- stream_out: bfloat16 [12288, 2048], P('row', 'col')
- stream_grad: float32 [12288, 2048], P('row', 'col')
- grad_qkv: float32 [3, 2048, 2048], P(None, 'col', 'row')
- grad_out: float32 [2048, 2048], P('row', 'col')
- grad_gate_up: float32 [2, 2048, 8192], P(None, 'col', 'row')
- grad_down: float32 [8192, 2048], P('row', 'col')
- grad_gain_attn: float32 [2048], P('col')
- grad_gain_ffn: float32 [2048], P('col')
- grad_gate_logit: float32 [16], P('row')
- memory_new: float32 [8, 16, 128, 128], P('col', 'row')
- memory_norm_new: float32 [8, 16, 128], P('col', 'row')
- rms_table: float32 [4, 12288], P(None, 'row')
Inputs may be any that keep to these rules, and one draw needn't show every extreme that they name: `offsets`: every group has a continuation that sees all 1024 prompt tokens. `lengths`: positions of a continuation at or after its length are padding: no query attends to their keys. Every group has a full continuation.
All inputs are finite; a program needn't handle non-finite values.
Results may differ from a plain program's by a relative error of at most 0.019.
Values may be sent and summed in bfloat16 or wider, within the bound.
A program may use at most 320 MiB of HBM per device.

v0:
```python
import jax
import jax.numpy as jnp
from jax import lax
from jax.sharding import PartitionSpec as P

D = 2048
HD = 128
PROMPT = 1024
CONT = 4
CLEN = 128
GLEN = 1536


EPSILON = 1e-06
MASKED_LOGIT = -1e30
TOP_PRECISION = lax.Precision.HIGHEST


def shortened(value):

    def short(part):
        return part.astype(jnp.bfloat16) if part.dtype == jnp.float32 else part

    return jax.tree.map(short, value)


def feature_map(values):
    return jnp.where(values > 0, values + 1.0, jnp.exp(jnp.minimum(values, 0.0)))


def feature_slope(values):
    return jnp.where(values > 0, 1.0, jnp.exp(jnp.minimum(values, 0.0)))


def row_collect(values):
    return jax.tree.map(
        lambda part, own: part.astype(own.dtype),
        lax.all_gather(shortened(values), "row", axis=0, tiled=True),
        values,
    )


def row_reduce(addend, row_count):
    return lax.psum_scatter(
        addend(jnp.int32(0), row_count * lax.axis_size("row")),
        "row",
        scatter_dimension=0,
        tiled=True,
    )


def to_local(gathered):
    return jax.tree.map(
        lambda part, own: part.astype(own.dtype),
        lax.all_to_all(shortened(gathered), "col", split_axis=0, concat_axis=1, tiled=True),
        gathered,
    )


def from_local(partial_rows):
    return lax.all_to_all(partial_rows, "col", split_axis=1, concat_axis=0, tiled=True)


def tokens_contract(left, right):
    return lax.dot_general(
        left, right, (((0,), (0,)), ((), ())), preferred_element_type=jnp.float32
    )


def against_rows(left, right):
    return lax.dot_general(
        left, right, (((1,), (1,)), ((), ())), preferred_element_type=jnp.float32
    )


def rows_of(whole):

    def addend(begin_row, row_count):
        return whole

    return addend


def land_rows(partial_rows, rows_here):
    return row_reduce(rows_of(from_local(partial_rows)), rows_here)


def score_blocks(queries, keys_in, offsets, lengths):
    head_count = queries.shape[0]
    logit_scale_factor = HD ** (-0.5)
    query_prompt = queries[:, :PROMPT]
    prompt_key_rows = keys_in[:, :PROMPT]
    continuation_query = queries[:, PROMPT:].reshape(head_count, CONT, CLEN, HD)
    key_cont = keys_in[:, PROMPT:].reshape(head_count, CONT, CLEN, HD)
    pos_prompt = jnp.arange(PROMPT)
    pos_cont = jnp.arange(CLEN)
    keep_prompt = pos_prompt[:, None] >= pos_prompt[None, :]
    cross_keep_mask = pos_prompt[None, None, :] < offsets[:, None, None]
    keep_self = (pos_cont[None, :, None] >= pos_cont[None, None, :]) & (
        pos_cont[None, None, :] < lengths[:, None, None]
    )
    scores_prompt = (
        jnp.einsum(
            "hqd,hkd->hqk", query_prompt, prompt_key_rows, preferred_element_type=jnp.float32
        )
        * logit_scale_factor
    )
    cross_logit_table = (
        jnp.einsum(
            "hcld,hkd->hclk",
            continuation_query,
            prompt_key_rows,
            preferred_element_type=jnp.float32,
        )
        * logit_scale_factor
    )
    scores_self = (
        jnp.einsum(
            "hcld,hcmd->hclm", continuation_query, key_cont, preferred_element_type=jnp.float32
        )
        * logit_scale_factor
    )
    return (
        jnp.where(keep_prompt[None], scores_prompt, MASKED_LOGIT),
        jnp.where(cross_keep_mask[None], cross_logit_table, MASKED_LOGIT),
        jnp.where(keep_self[None], scores_self, MASKED_LOGIT),
    )


def attend_group(queries, keys_in, values_in, memory_one, norm_one, offsets, lengths, gate_value):
    head_count = queries.shape[0]
    scores_prompt, cross_logit_table, scores_self = score_blocks(queries, keys_in, offsets, lengths)
    peak_prompt = jnp.max(scores_prompt, axis=2)
    logsum_prompt = peak_prompt + jnp.log(
        jnp.sum(jnp.exp(scores_prompt - peak_prompt[..., None]), axis=2)
    )
    peak_cont = jnp.maximum(jnp.max(cross_logit_table, axis=3), jnp.max(scores_self, axis=3))
    logsum_cont = peak_cont + jnp.log(
        jnp.sum(jnp.exp(cross_logit_table - peak_cont[..., None]), axis=3)
        + jnp.sum(jnp.exp(scores_self - peak_cont[..., None]), axis=3)
    )
    probs_prompt = jnp.exp(scores_prompt - logsum_prompt[..., None]).astype(jnp.bfloat16)
    cross_probability = jnp.exp(cross_logit_table - logsum_cont[..., None]).astype(jnp.bfloat16)
    self_probability = jnp.exp(scores_self - logsum_cont[..., None]).astype(jnp.bfloat16)
    prompt_value_rows = values_in[:, :PROMPT]
    continuation_value = values_in[:, PROMPT:].reshape(head_count, CONT, CLEN, HD)
    dot_prompt = jnp.einsum(
        "hqk,hkd->hqd", probs_prompt, prompt_value_rows, preferred_element_type=jnp.float32
    )
    continuation_product = jnp.einsum(
        "hclk,hkd->hcld", cross_probability, prompt_value_rows, preferred_element_type=jnp.float32
    ) + jnp.einsum(
        "hclm,hcmd->hcld", self_probability, continuation_value, preferred_element_type=jnp.float32
    )
    dot_part = jnp.concatenate(
        [dot_prompt, continuation_product.reshape(head_count, CONT * CLEN, HD)], axis=1
    )
    lifted = feature_map(queries.astype(jnp.float32))
    numerator = jnp.einsum("htd,hde->hte", lifted, memory_one, precision=TOP_PRECISION)
    denominator = jnp.einsum("htd,hd->ht", lifted, norm_one, precision=TOP_PRECISION)
    memory_part = numerator / denominator[..., None]
    mixing = gate_value[:, None, None]
    attended = mixing * memory_part + (1.0 - mixing) * dot_part
    lifted_keys = feature_map(keys_in[:, :PROMPT].astype(jnp.float32))
    memory_new = (
        memory_one
        + jnp.einsum(
            "hkd,hke->hde",
            lifted_keys,
            prompt_value_rows.astype(jnp.float32),
            precision=TOP_PRECISION,
        )
        / PROMPT
    )
    norm_new = norm_one + jnp.mean(lifted_keys, axis=1)
    return (attended, logsum_prompt, logsum_cont, memory_part, dot_part, memory_new, norm_new)


def attend_back(
    queries,
    keys_in,
    values_in,
    grad_attn,
    logsum_prompt,
    logsum_cont,
    memory_part,
    dot_part,
    memory_one,
    norm_one,
    offsets,
    lengths,
    gate_value,
):
    head_count = queries.shape[0]
    logit_scale_factor = HD ** (-0.5)
    scores_prompt, cross_logit_table, scores_self = score_blocks(queries, keys_in, offsets, lengths)
    probs_prompt = jnp.exp(scores_prompt - logsum_prompt[..., None])
    cross_probability = jnp.exp(cross_logit_table - logsum_cont[..., None])
    self_probability = jnp.exp(scores_self - logsum_cont[..., None])
    keep_dot = (1.0 - gate_value)[:, None, None]
    keep_four = keep_dot[..., None]
    grad_float = grad_attn.astype(jnp.float32)
    grad_gate = jnp.sum(grad_float * (memory_part - dot_part), axis=(1, 2))
    query_prompt = queries[:, :PROMPT]
    prompt_key_rows = keys_in[:, :PROMPT]
    prompt_value_rows = values_in[:, :PROMPT]
    continuation_query = queries[:, PROMPT:].reshape(head_count, CONT, CLEN, HD)
    key_cont = keys_in[:, PROMPT:].reshape(head_count, CONT, CLEN, HD)
    continuation_value = values_in[:, PROMPT:].reshape(head_count, CONT, CLEN, HD)
    grad_prompt = grad_attn[:, :PROMPT]
    grad_cont = grad_attn[:, PROMPT:].reshape(head_count, CONT, CLEN, HD)
    dprob_prompt = (
        jnp.einsum(
            "hqd,hkd->hqk", grad_prompt, prompt_value_rows, preferred_element_type=jnp.float32
        )
        * keep_dot
    )
    dscore_prompt = probs_prompt * (
        dprob_prompt - jnp.sum(probs_prompt * dprob_prompt, axis=2, keepdims=True)
    )
    dprob_cross = (
        jnp.einsum(
            "hcld,hkd->hclk", grad_cont, prompt_value_rows, preferred_element_type=jnp.float32
        )
        * keep_four
    )
    dprob_self = (
        jnp.einsum(
            "hcld,hcmd->hclm", grad_cont, continuation_value, preferred_element_type=jnp.float32
        )
        * keep_four
    )
    centre = jnp.sum(cross_probability * dprob_cross, axis=3, keepdims=True) + jnp.sum(
        self_probability * dprob_self, axis=3, keepdims=True
    )
    low_prompt = dscore_prompt.astype(jnp.bfloat16)
    low_cross = (cross_probability * (dprob_cross - centre)).astype(jnp.bfloat16)
    low_self = (self_probability * (dprob_self - centre)).astype(jnp.bfloat16)
    query_grad_prompt = (
        jnp.einsum("hqk,hkd->hqd", low_prompt, prompt_key_rows, preferred_element_type=jnp.float32)
        * logit_scale_factor
    )
    query_grad_cont = (
        jnp.einsum("hclk,hkd->hcld", low_cross, prompt_key_rows, preferred_element_type=jnp.float32)
        + jnp.einsum("hclm,hcmd->hcld", low_self, key_cont, preferred_element_type=jnp.float32)
    ) * logit_scale_factor
    key_grad_prompt = (
        jnp.einsum("hqk,hqd->hkd", low_prompt, query_prompt, preferred_element_type=jnp.float32)
        + jnp.einsum(
            "hclk,hcld->hkd", low_cross, continuation_query, preferred_element_type=jnp.float32
        )
    ) * logit_scale_factor
    key_grad_cont = (
        jnp.einsum(
            "hclm,hcld->hcmd", low_self, continuation_query, preferred_element_type=jnp.float32
        )
        * logit_scale_factor
    )
    prob_low_prompt = probs_prompt.astype(jnp.bfloat16)
    prob_low_cross = cross_probability.astype(jnp.bfloat16)
    prob_low_self = self_probability.astype(jnp.bfloat16)
    value_grad_prompt = (
        jnp.einsum("hqk,hqd->hkd", prob_low_prompt, grad_prompt, preferred_element_type=jnp.float32)
        + jnp.einsum(
            "hclk,hcld->hkd", prob_low_cross, grad_cont, preferred_element_type=jnp.float32
        )
    ) * keep_dot
    value_grad_cont = (
        jnp.einsum("hclm,hcld->hcmd", prob_low_self, grad_cont, preferred_element_type=jnp.float32)
        * keep_four
    )
    query_float = queries.astype(jnp.float32)
    lifted = feature_map(query_float)
    denominator = jnp.einsum("htd,hd->ht", lifted, norm_one, precision=TOP_PRECISION)
    grad_memory = gate_value[:, None, None] * grad_float
    grad_numerator = grad_memory / denominator[..., None]
    grad_denominator = -jnp.sum(grad_memory * memory_part, axis=2) / denominator
    grad_lifted = (
        jnp.einsum("hte,hde->htd", grad_numerator, memory_one, precision=TOP_PRECISION)
        + grad_denominator[..., None] * norm_one[:, None, :]
    )
    grad_queries = jnp.concatenate(
        [query_grad_prompt, query_grad_cont.reshape(head_count, CONT * CLEN, HD)], axis=1
    ) + grad_lifted * feature_slope(query_float)
    grad_keys = jnp.concatenate(
        [key_grad_prompt, key_grad_cont.reshape(head_count, CONT * CLEN, HD)], axis=1
    )
    grad_values = jnp.concatenate(
        [value_grad_prompt, value_grad_cont.reshape(head_count, CONT * CLEN, HD)], axis=1
    )
    return (grad_queries, grad_keys, grad_values, grad_gate)


def local(
    stream_in,
    w_qkv,
    w_out,
    w_gate_up,
    w_down,
    gain_attn,
    gain_ffn,
    gate_logit,
    memory,
    memory_norm,
    offsets,
    lengths,
    cotangent,
):
    rows_here = stream_in.shape[0]
    group_count = memory.shape[0]
    head_here = memory.shape[1]
    rows_col = group_count * GLEN
    stream = stream_in.astype(jnp.float32)
    square_in = lax.psum(jnp.sum(stream * stream, axis=1), "col")
    inv_in = lax.rsqrt(square_in / D + EPSILON)[:, None]
    gain_in = gain_attn[None, :]
    normed_in = (stream * inv_in * gain_in).astype(jnp.bfloat16)
    gathered_in, gathered_cot = row_collect((normed_in, cotangent))
    whole_qkv, whole_out, whole_gu, whole_down = (
        lax.all_gather(w_qkv, "col", axis=1, tiled=True),
        lax.all_gather(w_out, "col", axis=1, tiled=True),
        lax.all_gather(w_gate_up, "col", axis=1, tiled=True),
        lax.all_gather(w_down, "col", axis=1, tiled=True),
    )
    local_in, local_cot = to_local((gathered_in, gathered_cot))
    packed = jnp.einsum("td,kdo->tko", local_in, whole_qkv, preferred_element_type=jnp.float32)
    heads_all = (
        packed.astype(jnp.bfloat16)
        .reshape(group_count, GLEN, 3, head_here, HD)
        .transpose(0, 2, 3, 1, 4)
    )
    gate_value = jax.nn.sigmoid(gate_logit)

    def forward_group(items):
        heads_one, memory_one, norm_one, offset_one, length_one = items
        return attend_group(
            heads_one[0],
            heads_one[1],
            heads_one[2],
            memory_one,
            norm_one,
            offset_one,
            length_one,
            gate_value,
        )

    attended, logsum_prompt, logsum_cont, memory_part, dot_part, memory_new, norm_new = lax.map(
        forward_group, (heads_all, memory, memory_norm, offsets, lengths)
    )
    attn_low = attended.astype(jnp.bfloat16).transpose(0, 2, 1, 3).reshape(rows_col, head_here * HD)
    branch = land_rows(jnp.dot(attn_low, whole_out, preferred_element_type=jnp.float32), rows_here)
    middle = stream + branch
    branch_square, middle_square = lax.psum(
        (jnp.sum(branch * branch, axis=1), jnp.sum(middle * middle, axis=1)), "col"
    )
    inv_mid = lax.rsqrt(middle_square / D + EPSILON)[:, None]
    gain_mid = gain_ffn[None, :]
    normed_ffn = (middle * inv_mid * gain_mid).astype(jnp.bfloat16)
    gathered_ffn = row_collect(normed_ffn)
    local_ffn = to_local(gathered_ffn)
    gate_up = jnp.einsum("td,kdo->tko", local_ffn, whole_gu, preferred_element_type=jnp.float32)
    gate_pre = gate_up[:, 0]
    up_pre = gate_up[:, 1]
    sigmoid_gate = jax.nn.sigmoid(gate_pre)
    hidden_low = (gate_pre * sigmoid_gate * up_pre).astype(jnp.bfloat16)
    ffn = land_rows(jnp.dot(hidden_low, whole_down, preferred_element_type=jnp.float32), rows_here)
    result = middle + ffn
    stream_out = result.astype(jnp.bfloat16)
    grad_hidden = against_rows(local_cot, whole_down)
    part_down = tokens_contract(hidden_low, local_cot)
    grad_up = grad_hidden * gate_pre * sigmoid_gate
    grad_gate = grad_hidden * up_pre * sigmoid_gate * (1.0 + gate_pre * (1.0 - sigmoid_gate))
    grad_gu_low = jnp.stack([grad_gate, grad_up], axis=1).astype(jnp.bfloat16)
    grad_normed_ffn = land_rows(
        jnp.einsum("tko,kdo->td", grad_gu_low, whole_gu, preferred_element_type=jnp.float32),
        rows_here,
    )
    part_gu = jnp.einsum("td,tko->kdo", local_ffn, grad_gu_low, preferred_element_type=jnp.float32)
    scaled_mid = grad_normed_ffn * gain_mid
    ffn_square, out_square, inner_mid = (
        lax.psum(jnp.sum(ffn * ffn, axis=1).astype(jnp.bfloat16), "col").astype(jnp.float32),
        lax.psum(jnp.sum(result * result, axis=1).astype(jnp.bfloat16), "col").astype(jnp.float32),
        lax.psum(jnp.sum(scaled_mid * middle, axis=1).astype(jnp.bfloat16), "col").astype(
            jnp.float32
        ),
    )
    grad_middle = (
        cotangent.astype(jnp.float32)
        + inv_mid * scaled_mid
        - middle * inv_mid**3 * (inner_mid / D)[:, None]
    )
    part_gain_ffn = jnp.sum(grad_normed_ffn * middle * inv_mid, axis=0)
    branch_low = grad_middle.astype(jnp.bfloat16)
    gathered_branch = row_collect(branch_low)
    local_branch = to_local(gathered_branch)
    grad_attn_rows = against_rows(local_branch, whole_out)
    part_out = tokens_contract(attn_low, local_branch)
    grad_heads = (
        grad_attn_rows.astype(jnp.bfloat16)
        .reshape(group_count, GLEN, head_here, HD)
        .transpose(0, 2, 1, 3)
    )

    def backward_group(items):
        (
            heads_one,
            grad_one,
            prompt_logsum,
            cont_logsum,
            part_memory,
            part_dot,
            memory_one,
            norm_one,
            offset_one,
            length_one,
        ) = items
        return attend_back(
            heads_one[0],
            heads_one[1],
            heads_one[2],
            grad_one,
            prompt_logsum,
            cont_logsum,
            part_memory,
            part_dot,
            memory_one,
            norm_one,
            offset_one,
            length_one,
            gate_value,
        )

    grad_queries, grad_keys, grad_values, grad_gates = lax.map(
        backward_group,
        (
            heads_all,
            grad_heads,
            logsum_prompt,
            logsum_cont,
            memory_part,
            dot_part,
            memory,
            memory_norm,
            offsets,
            lengths,
        ),
    )
    logit_part = gate_value * (1.0 - gate_value) * jnp.sum(grad_gates, axis=0)
    grad_packed = (
        jnp.stack([grad_queries, grad_keys, grad_values], axis=1)
        .transpose(0, 3, 1, 2, 4)
        .reshape(rows_col, 3, head_here * HD)
        .astype(jnp.bfloat16)
    )
    grad_normed_in = land_rows(
        jnp.einsum("tko,kdo->td", grad_packed, whole_qkv, preferred_element_type=jnp.float32),
        rows_here,
    )
    part_qkv = jnp.einsum("td,tko->kdo", local_in, grad_packed, preferred_element_type=jnp.float32)
    grad_qkv, grad_out, grad_gate_up, grad_down = (
        lax.psum_scatter(
            part_qkv.astype(jnp.bfloat16), "col", scatter_dimension=1, tiled=True
        ).astype(jnp.float32),
        lax.psum_scatter(
            part_out.astype(jnp.bfloat16), "col", scatter_dimension=1, tiled=True
        ).astype(jnp.float32),
        lax.psum_scatter(
            part_gu.astype(jnp.bfloat16), "col", scatter_dimension=1, tiled=True
        ).astype(jnp.float32),
        lax.psum_scatter(
            part_down.astype(jnp.bfloat16), "col", scatter_dimension=1, tiled=True
        ).astype(jnp.float32),
    )
    scaled_in = grad_normed_in * gain_in
    inner_in, grad_gate_logit = lax.psum((jnp.sum(scaled_in * stream, axis=1), logit_part), "col")
    stream_grad = grad_middle + inv_in * scaled_in - stream * inv_in**3 * (inner_in / D)[:, None]
    part_gain_attn = jnp.sum(grad_normed_in * stream * inv_in, axis=0)
    grad_gain_attn, grad_gain_ffn = lax.psum((part_gain_attn, part_gain_ffn), "row")
    rms_table = jnp.sqrt(jnp.stack([branch_square, middle_square, ffn_square, out_square]) / D)
    return (
        stream_out,
        stream_grad,
        grad_qkv,
        grad_out,
        grad_gate_up,
        grad_down,
        grad_gain_attn,
        grad_gain_ffn,
        grad_gate_logit,
        memory_new,
        norm_new,
        rms_table,
    )


def solution(mesh):
    return jax.shard_map(
        local,
        mesh=mesh,
        in_specs=(
            P("row", "col"),
            P(None, "col", "row"),
            P("row", "col"),
            P(None, "col", "row"),
            P("row", "col"),
            P("col"),
            P("col"),
            P("row"),
            P("col", "row", None, None),
            P("col", "row", None),
            P("col", None),
            P("col", None),
            P("row", "col"),
        ),
        out_specs=(
            P("row", "col"),
            P("row", "col"),
            P(None, "col", "row"),
            P("row", "col"),
            P(None, "col", "row"),
            P("row", "col"),
            P("col"),
            P("col"),
            P("row"),
            P("col", "row", None, None),
            P("col", "row", None),
            P(None, "row"),
        ),
        check_vma=False,
    )
```

profile of v0, /device:TPU:27, one launch (start us, length us, event | category | flops | bytes accessed | tf_op | source)
XLA Modules:
  0.0 3204.0 jit_solution(17999240340777596172)
XLA Ops:
  9.1 25.2 psum.70
  39.4 71.0 %all-gather.9.cloned.1.call-done = bf16[12288,256]{1,0:T(8,128)(2,1)} async-done(((bf16[3072,256]{1,0:T(8,128)(2,1)}), bf16[12288,256]{1,0:T(8,128)(2,1)}) %all-gather.9.cloned.1.call-update) | async-done | bytes 6291472 | tf_op jit(solution)/shard_map/all_gather | solution.py:38
  118.0 52.0 %all-gather.13.cloned.1.call-done = bf16[512,2048]{1,0:T(8,128)(2,1)} async-done(((bf16[512,256]{1,0:T(8,128)(2,1)}), bf16[512,2048]{1,0:T(8,128)(2,1)}) %all-gather.13.cloned.1.call-update) | async-done | bytes 2097168 | tf_op jit(solution)/shard_map/all_gather | solution.py:321
  173.9 146.0 %all-to-all-done = bf16[8,1536,256]{2,1,0:T(8,128)(2,1)} async-done(((bf16[8,1536,256]{2,1,0:T(8,128)(2,1)}), bf16[8,1536,256]{2,1,0:T(8,128)(2,1)}, u32[]{:S(2)}, u32[]{:S(2)}) %all-to-all-start) | async-done | bytes 6291488 | tf_op jit(solution)/shard_map/all_to_all | solution.py:55
  319.8 8.2 copy.143
  328.0 10.4 reshape.282
  338.5 15.3 convolution_convert_fusion.1
  390.5 9.5 fusion.99
  400.0 8.3 add_convert_fusion
  411.8 277.4 %all_to_all.143 = f32[1536,8,256]{2,0,1:T(8,128)} all-to-all(f32[1536,8,256]{2,0,1:T(8,128)S(1)} %fusion.129), channel_id=1, replica_groups=mesh['row'=4,'col'=8] {'col'}, dimensions={1} | all-to-all | bytes 25165824 | tf_op jit(solution)/shard_map/all_to_all | solution.py:61
  690.1 119.7 %reduce-scatter.9.cloned.1.call-done = f32[3072,256]{1,0:T(8,128)} async-done(((f32[12288,256]{1,0:T(8,128)}), f32[3072,256]{1,0:T(8,128)}) %reduce-scatter.9.cloned.1.call-update) | async-done | bytes 3145744 | tf_op jit(solution)/shard_map/reduce_scatter | solution.py:44
  813.6 25.2 psum.71
  842.5 39.3 %all-gather.21.cloned.1.call-done = bf16[12288,256]{1,0:T(8,128)(2,1)} async-done(((bf16[3072,256]{1,0:T(8,128)(2,1)}), bf16[12288,256]{1,0:T(8,128)(2,1)}) %all-gather.21.cloned.1.call-update) | async-done | bytes 6291472 | tf_op jit(solution)/shard_map/all_gather | solution.py:38
  881.8 245.2 %all_to_all.144 = bf16[8,1536,256]{2,1,0:T(8,128)(2,1)} all-to-all(bf16[8,1536,256]{2,1,0:T(8,128)(2,1)} %bitcast.270), channel_id=1, replica_groups=mesh['row'=4,'col'=8] {'col'}, dimensions={0} | all-to-all | bytes 12582912 | tf_op jit(solution)/shard_map/all_to_all | solution.py:55
  1134.5 8.7 copy.155
  1143.2 217.5 %all-to-all-done.2 = bf16[8,1536,256]{2,1,0:T(8,128)(2,1)} async-done(((bf16[8,1536,256]{2,1,0:T(8,128)(2,1)}), bf16[8,1536,256]{2,1,0:T(8,128)(2,1)}, u32[]{:S(2)}, u32[]{:S(2)}) %all-to-all-start.2) | async-done | bytes 6291488 | tf_op jit(solution)/shard_map/all_to_all | solution.py:55
  1360.7 8.1 copy.153
  1368.8 10.4 reshape.288
  1379.2 33.6 %fusion.130 = f32[1536,2,2048]{2,0,1:T(8,128)} fusion(bf16[1536,2048,1]{1,0,2:T(8,128)(2,1)} %reshape.288, bf16[2,2048,2048]{2,1,0:T(8,128)(2,1)} %all-gather.17.cloned.1.call-done), kind=kOutput, calls=%fused_computation.200 | convolution fusion | flops 25769803776 | bytes 48234496 | tf_op jit(solution)/shard_map/td,kdo->tko/dot_general | solution.py:361
  1412.9 27.3 fusion.19
  1440.1 34.6 %fusion.11 = f32[1536,2048,1]{1,0,2:T(8,128)} fusion(bf16[2,2048,2048]{2,1,0:T(8,128)(2,1)} %all-gather.17.cloned.1.call-done, bf16[1536,1,2048]{2,0,1:T(8,128)(2,1)} %get-tuple-element.175, bf16[1536,1,2048]{2,0,1:T(8,128)(2,1)} %get-tuple-element.174), kind=kOutput, calls=%fused_computation.29 | convolution fusion | flops 25776095232 | bytes 41943040 | tf_op jit(solution)/shard_map/tko,kdo->td/dot_general | solution.py:375
  1474.7 10.3 copy.225
  1485.0 7.7 all-to-all-start.5
  1492.7 12.4 copy.154
  1505.0 258.8 %all-to-all-done.5 = f32[1536,8,256]{2,0,1:T(8,128)} async-done(((f32[1536,8,256]{2,0,1:T(8,128)}), f32[1536,8,256]{2,0,1:T(8,128)}, u32[]{:S(2)}, u32[]{:S(2)}) %all-to-all-start.5) | async-done | bytes 12582944 | tf_op jit(solution)/shard_map/all_to_all | solution.py:61
  1763.9 11.4 multiply_convert_fusion.1
  1775.6 13.6 fusion.15
  1789.2 277.6 %all_to_all.145 = f32[1536,8,256]{2,0,1:T(8,128)} all-to-all(f32[1536,8,256]{2,0,1:T(8,128)S(1)} %fusion.15), channel_id=1, replica_groups=mesh['row'=4,'col'=8] {'col'}, dimensions={1} | all-to-all | bytes 25165824 | tf_op jit(solution)/shard_map/all_to_all | solution.py:61
  2066.9 120.4 %reduce-scatter.11.cloned.1.call-done = f32[3072,256]{1,0:T(8,128)} async-done(((f32[12288,256]{1,0:T(8,128)}), f32[3072,256]{1,0:T(8,128)}) %reduce-scatter.11.cloned.1.call-update) | async-done | bytes 3145744 | tf_op jit(solution)/shard_map/reduce_scatter | solution.py:44
  2193.4 25.8 all-reduce.2
  2225.3 19.4 convolution_convert_fusion
  2244.8 32.9 %convert_bitcast_fusion = bf16[2,2048,2048]{1,2,0:T(8,128)(2,1)} fusion(bf16[1536,2048,1]{1,0,2:T(8,128)(2,1)} %reshape.288, bf16[1536,1,2048]{2,0,1:T(8,128)(2,1)} %get-tuple-element.175, bf16[1536,1,2048]{2,0,1:T(8,128)(2,1)} %get-tuple-element.174), kind=kOutput, calls=%fused_computation | convolution fusion | flops 25784483840 | bytes 35651584 | tf_op jit(solution)/shard_map/td,tko->kdo/dot_general | solution.py:378
  2277.8 18.5 all-gather.23.cloned.1.call-done
  2296.2 215.7 %all_to_all.146 = bf16[8,1536,256]{2,1,0:T(8,128)(2,1)} all-to-all(bf16[8,1536,256]{2,1,0:T(8,128)(2,1)} %bitcast.272), channel_id=1, replica_groups=mesh['row'=4,'col'=8] {'col'}, dimensions={0} | all-to-all | bytes 12582912 | tf_op jit(solution)/shard_map/all_to_all | solution.py:55
  2511.9 8.8 copy.157
  2535.3 7.4 multiply_reduce_fusion.1
  2544.6 7.4 multiply_convert_fusion.2
  2559.5 12.8 multiply_reduce_fusion
  2572.3 12.8 multiply_convert_fusion
  2593.0 11.4 fusion.86
  2620.5 8.7 fusion.45
  2638.2 16.4 convolution_bitcast_fusion
  2654.6 7.9 all-to-all-start.7
  2662.5 7.7 convolution_convert_fusion.3
  2670.3 15.2 convert_bitcast_fusion.1
  2685.6 347.6 %all-to-all-done.7 = f32[1536,8,256]{2,0,1:T(8,128)} async-done(((f32[1536,8,256]{2,0,1:T(8,128)}), f32[1536,8,256]{2,0,1:T(8,128)}, u32[]{:S(2)}, u32[]{:S(2)}) %all-to-all-start.7) | async-done | bytes 12582944 | tf_op jit(solution)/shard_map/all_to_all | solution.py:61
  3049.2 105.5 %reduce-scatter.15.cloned.1.call-done = f32[3072,256]{1,0:T(8,128)} async-done(((f32[12288,256]{1,0:T(8,128)}), f32[3072,256]{1,0:T(8,128)}) %reduce-scatter.15.cloned.1.call-update) | async-done | bytes 3145744 | tf_op jit(solution)/shard_map/reduce_scatter | solution.py:44
  3158.3 25.2 all-reduce
  (286 shorter events, 176.2 us)
Async XLA Ops:
  7.2 103.2 %all-gather.9.cloned.1.call-start = ((), (), s32[]{:S(2)}) async-start(), calls=%async_computation.16 | async-start | bytes 7864320 | tf_op jit(solution)/shard_map/all_gather | solution.py:38
  38.6 131.3 %all-gather.13.cloned.1.call-start = ((), (), s32[]{:S(2)}) async-start(), calls=%async_computation.18 | async-start | bytes 2359296 | tf_op jit(solution)/shard_map/all_gather | solution.py:321
  110.4 209.4 %all-to-all-start = ((bf16[8,1536,256]{2,1,0:T(8,128)(2,1)}), bf16[8,1536,256]{2,1,0:T(8,128)(2,1)}, u32[]{:S(2)}, u32[]{:S(2)}) async-start(bf16[8,1536,256]{2,1,0:T(8,128)(2,1)} %bitcast.269), calls=%async_computation | async-start | bytes 12582912 | tf_op jit(solution)/shard_map/all_to_all | solution.py:55
  116.0 222.4 %all-gather.11.cloned.1.call-start = ((), (), s32[]{:S(2)}) async-start(), calls=%async_computation.17 | async-start | bytes 7077888 | tf_op jit(solution)/shard_map/all_gather | solution.py:320
  117.2 692.5 %reduce-scatter.9.cloned.1.call-start = ((), (), s32[]{:S(2)}) async-start(), calls=%async_computation.19 | async-start | bytes 15728640 | tf_op jit(solution)/shard_map/reduce_scatter | solution.py:44
  117.6 272.8 %copy-start.11 = (pred[1024,1024]{0,1:T(8,128)(4,1)}, pred[1024,1024]{0,1:T(8,128)(4,1)S(1)}, u32[]{:S(2)}) copy-start(pred[1024,1024]{0,1:T(8,128)(4,1)S(1)} %iota_compare_fusion) | copy-start | bytes 3145732
  117.7 282.3 %copy-start.60 = (f32[4]{0:T(128)}, f32[4]{0:T(128)S(1)}, u32[]{:S(2)}) copy-start(f32[4]{0:T(128)S(1)} %get-tuple-element.172) | copy-start | bytes 52
  117.7 282.3 %copy-start.72 = (f32[4]{0:T(128)}, f32[4]{0:T(128)S(1)}, u32[]{:S(2)}) copy-start(f32[4]{0:T(128)S(1)} %get-tuple-element.173) | copy-start | bytes 52
  117.8 256.0 %copy-start.45 = (pred[4,1024]{1,0:T(4,128)(4,1)}, pred[4,1024]{1,0:T(4,128)(4,1)S(1)}, u32[]{:S(2)}) copy-start(pred[4,1024]{1,0:T(4,128)(4,1)S(1)} %iota_compare_fusion.2) | copy-start | bytes 12292
  363.3 10.5 copy-start.15
  363.3 16.7 copy-start.9
  369.3 30.6 copy-start.62
  689.2 192.5 %all-gather.21.cloned.1.call-start = ((), (), s32[]{:S(2)}) async-start(), calls=%async_computation.24 | async-start | bytes 7864320 | tf_op jit(solution)/shard_map/all_gather | solution.py:38
  689.8 150.2 %copy-start.66 = (f32[256]{0:T(256)S(1)}, f32[256]{0:T(256)}, u32[]{:S(2)}) copy-start(f32[256]{0:T(256)} %param.19) | copy-start | bytes 3076
  689.9 437.1 %all-gather.15.cloned.1.call-start = ((), (), s32[]{:S(2)}) async-start(), calls=%async_computation.20 | async-start | bytes 7864320 | tf_op jit(solution)/shard_map/all_gather | solution.py:38
  813.6 28.8 copy-start.4
  838.8 288.2 %copy-start.53 = (f32[3072]{0:T(1024)}, f32[3072]{0:T(1024)S(1)}, u32[]{:S(2)}) copy-start(f32[3072]{0:T(1024)S(1)} %psum.71) | copy-start | bytes 36868
  841.7 537.5 %all-gather.17.cloned.1.call-start = ((), (), s32[]{:S(2)}) async-start(), calls=%async_computation.21 | async-start | bytes 18874368 | tf_op jit(solution)/shard_map/all_gather | solution.py:322
  1127.0 233.7 %all-to-all-start.2 = ((bf16[8,1536,256]{2,1,0:T(8,128)(2,1)}), bf16[8,1536,256]{2,1,0:T(8,128)(2,1)}, u32[]{:S(2)}, u32[]{:S(2)}) async-start(bf16[8,1536,256]{2,1,0:T(8,128)(2,1)} %bitcast.271), calls=%async_computation.3 | async-start | bytes 12582912 | tf_op jit(solution)/shard_map/all_to_all | solution.py:55
  1133.8 279.1 %all-gather.19.cloned.1.call-start = ((), (), s32[]{:S(2)}) async-start(), calls=%async_computation.22 | async-start | bytes 9437184 | tf_op jit(solution)/shard_map/all_gather | solution.py:323
  1485.0 278.9 %all-to-all-start.5 = ((f32[1536,8,256]{2,0,1:T(8,128)}), f32[1536,8,256]{2,0,1:T(8,128)}, u32[]{:S(2)}, u32[]{:S(2)}) async-start(f32[1536,8,256]{2,0,1:T(8,128)} %bitcast.240), calls=%async_computation.7 | async-start | bytes 25165824 | tf_op jit(solution)/shard_map/all_to_all | solution.py:61
  1492.7 574.2 %reduce-scatter.13.cloned.1.call-start = ((), (), s32[]{:S(2)}) async-start(), calls=%async_computation.25 | async-start | bytes 15728640 | tf_op jit(solution)/shard_map/reduce_scatter | solution.py:44
  1763.9 423.4 %reduce-scatter.11.cloned.1.call-start = ((), (), s32[]{:S(2)}) async-start(), calls=%async_computation.23 | async-start | bytes 15728640 | tf_op jit(solution)/shard_map/reduce_scatter | solution.py:44
  1763.9 11.6 copy-start.24
  1775.4 13.8 copy-start.26
  2066.8 120.5 %copy-start.5 = (f32[3072,256]{1,0:T(8,128)S(1)}, f32[3072,256]{1,0:T(8,128)}, u32[]{:S(2)}) copy-start(f32[3072,256]{1,0:T(8,128)} %copy-done.4) | copy-start | bytes 9437188
  2066.8 120.5 %copy-start.50 = (f32[3072]{0:T(1024)S(1)}, f32[3072]{0:T(1024)}, u32[]{:S(2)}) copy-start(f32[3072]{0:T(1024)} %copy-done.49) | copy-start | bytes 36868
  2066.8 120.5 %copy-start.67 = (f32[256]{0:T(256)S(1)}, f32[256]{0:T(256)}, u32[]{:S(2)}) copy-start(f32[256]{0:T(256)} %param.19) | copy-start | bytes 3076
  2066.8 152.5 %copy-start.58 = (f32[3072]{0:T(1024)S(1)}, f32[3072]{0:T(1024)}, u32[]{:S(2)}) copy-start(f32[3072]{0:T(1024)} %get-tuple-element.183) | copy-start | bytes 36868
  2066.8 229.4 %all-gather.23.cloned.1.call-start = ((), (), s32[]{:S(2)}) async-start(), calls=%async_computation.26 | async-start | bytes 7864320 | tf_op jit(solution)/shard_map/all_gather | solution.py:38
  2225.2 812.2 %reduce-scatter.23.cloned.1.call-start = ((), (), s32[]{:S(2)}) async-start(), calls=%async_computation.31 | async-start | bytes 9437184 | tf_op jit(solution)/shard_map/reduce_scatter | solution.py:470
  2244.8 795.4 %reduce-scatter.21.cloned.1.call-start = ((), (), s32[]{:S(2)}) async-start(), calls=%async_computation.30 | async-start | bytes 18874368 | tf_op jit(solution)/shard_map/reduce_scatter | solution.py:467
  2520.7 9.6 copy-start.44
  2520.7 9.6 copy-start.61
  2572.3 12.8 copy-start.35
  2593.0 11.4 copy-start.22
  2604.5 11.3 slice-start
  2654.6 378.6 %all-to-all-start.7 = ((f32[1536,8,256]{2,0,1:T(8,128)}), f32[1536,8,256]{2,0,1:T(8,128)}, u32[]{:S(2)}, u32[]{:S(2)}) async-start(f32[1536,8,256]{2,0,1:T(8,128)} %convolution_bitcast_fusion), calls=%async_computation.10 | async-start | bytes 25165824 | tf_op jit(solution)/shard_map/all_to_all | solution.py:61
  2662.5 382.3 %reduce-scatter.19.cloned.1.call-start = ((), (), s32[]{:S(2)}) async-start(), calls=%async_computation.29 | async-start | bytes 2359296 | tf_op jit(solution)/shard_map/reduce_scatter | solution.py:464
  2670.2 376.4 %reduce-scatter.17.cloned.1.call-start = ((), (), s32[]{:S(2)}) async-start(), calls=%async_computation.28 | async-start | bytes 7077888 | tf_op jit(solution)/shard_map/reduce_scatter | solution.py:461
  2685.6 469.1 %reduce-scatter.15.cloned.1.call-start = ((), (), s32[]{:S(2)}) async-start(), calls=%async_computation.27 | async-start | bytes 15728640 | tf_op jit(solution)/shard_map/reduce_scatter | solution.py:44
  3040.2 114.5 %copy-start.6 = (bf16[3072,256]{1,0:T(8,128)(2,1)S(1)}, bf16[3072,256]{1,0:T(8,128)(2,1)}, u32[]{:S(2)}) copy-start(bf16[3072,256]{1,0:T(8,128)(2,1)} %param.13) | copy-start | bytes 4718596
  3040.2 114.5 %copy-start.48 = (f32[3072]{0:T(1024)S(1)}, f32[3072]{0:T(1024)}, u32[]{:S(2)}) copy-start(f32[3072]{0:T(1024)} %copy-done.47) | copy-start | bytes 36868
  3040.2 114.5 %copy-start.68 = (f32[256]{0:T(256)S(1)}, f32[256]{0:T(256)}, u32[]{:S(2)}) copy-start(f32[256]{0:T(256)} %param.18) | copy-start | bytes 3076
  3044.7 113.5 %copy-start.57 = (f32[3072]{0:T(1024)S(1)}, f32[3072]{0:T(1024)}, u32[]{:S(2)}) copy-start(f32[3072]{0:T(1024)} %get-tuple-element.180) | copy-start | bytes 36868
  3044.7 138.8 %copy-start.69 = (f32[256]{0:T(256)S(1)}, f32[256]{0:T(256)}, u32[]{:S(2)}) copy-start(f32[256]{0:T(256)} %get-tuple-element.157) | copy-start | bytes 3076
  3044.7 145.7 %copy-start.54 = (f32[3072]{0:T(1024)S(1)}, f32[3072]{0:T(1024)}, u32[]{:S(2)}) copy-start(f32[3072]{0:T(1024)} %copy-done.53) | copy-start | bytes 36868
  3044.7 146.4 %copy-start.59 = (f32[3072]{0:T(1024)S(1)}, f32[3072]{0:T(1024)}, u32[]{:S(2)}) copy-start(f32[3072]{0:T(1024)} %get-tuple-element.181) | copy-start | bytes 36868
  (55 other events, 269.2 us)
Sparse Core Ops, SparseCore 0:
  38.7 71.6 all-gather.8
  112.0 57.9 all-gather.12
  172.1 124.6 all-gather.10
  689.4 120.3 reduce-scatter.8
  811.5 70.2 all-gather.20
  884.1 70.1 all-gather.14
  955.8 273.2 all-gather.16
  1230.7 132.8 all-gather.18
  1764.0 120.3 reduce-scatter.12
  2066.9 120.3 reduce-scatter.10
  2225.4 70.8 all-gather.22
  2298.4 186.1 reduce-scatter.22
  2487.0 219.7 reduce-scatter.20
  2709.5 122.7 reduce-scatter.18
  2834.5 161.5 reduce-scatter.16
  3033.4 121.2 reduce-scatter.14
where the time goes:
time: 3220 us; the launch traced here: 3200 us
  waiting for transfers between devices  1500 us (47%)
  blocking collectives  1120 us (35%)
  matrix products  325 us (10%)
  local copies, waits for them, and re-layouts  129 us (4%)
  other arithmetic  82.4 us (3%)
    all_to_all x2, waiting for transfers between devices, from_local(): lax.all_to_all(partial_rows, 'col', split_axis=1, concat_axis=0, tiled=True)  606 us
    all_to_all x2, blocking collectives, from_local(): lax.all_to_all(partial_rows, 'col', split_axis=1, concat_axis=0, tiled=True)  555 us
    all_to_all x2, blocking collectives, to_local(): lax.all_to_all(shortened(gathered), 'col', split_axis=0, concat_axis=1, t...  461 us
    all_to_all x2, waiting for transfers between devices, to_local(): lax.all_to_all(shortened(gathered), 'col', split_axis=0, concat_axis=1, t...  363 us
    reduce_scatter x4, waiting for transfers between devices, row_reduce(): lax.psum_scatter(addend(jnp.int32(0), row_count * lax.axis_size('row')),...  346 us
    all_gather x4, waiting for transfers between devices, row_collect(): lax.all_gather(shortened(values), 'row', axis=0, tiled=True)  129 us
  transfers between devices with their start and end apart: 20, of which 11 were waited for; matrix products, arithmetic and copies ran while one was open for 11% of the time, Pallas kernels for 0%

commit v1 on v0

--- a/solution.py
+++ b/solution.py
@@ -32,35 +32,6 @@
     return jnp.where(values > 0, 1.0, jnp.exp(jnp.minimum(values, 0.0)))
 
 
-def row_collect(values):
-    return jax.tree.map(
-        lambda part, own: part.astype(own.dtype),
-        lax.all_gather(shortened(values), "row", axis=0, tiled=True),
-        values,
-    )
-
-
-def row_reduce(addend, row_count):
-    return lax.psum_scatter(
-        addend(jnp.int32(0), row_count * lax.axis_size("row")),
-        "row",
-        scatter_dimension=0,
-        tiled=True,
-    )
-
-
-def to_local(gathered):
-    return jax.tree.map(
-        lambda part, own: part.astype(own.dtype),
-        lax.all_to_all(shortened(gathered), "col", split_axis=0, concat_axis=1, tiled=True),
-        gathered,
-    )
-
-
-def from_local(partial_rows):
-    return lax.all_to_all(partial_rows, "col", split_axis=1, concat_axis=0, tiled=True)
-
-
 def tokens_contract(left, right):
     return lax.dot_general(
         left, right, (((0,), (0,)), ((), ())), preferred_element_type=jnp.float32
@@ -73,16 +44,37 @@
     )
 
 
-def rows_of(whole):
-
-    def addend(begin_row, row_count):
-        return whole
-
-    return addend
-
-
-def land_rows(partial_rows, rows_here):
-    return row_reduce(rows_of(from_local(partial_rows)), rows_here)
+def to_tokens(block):
+    row_size = lax.axis_size("row")
+    features = block.shape[1]
+    groups = block.shape[0] // GLEN
+    piece = GLEN // row_size
+    split = block.reshape(groups, row_size, piece, features)
+    split = lax.all_to_all(split, "row", split_axis=1, concat_axis=0, tiled=True)
+    split = split.reshape(row_size * groups, piece, features)
+    whole = lax.all_to_all(split, "col", split_axis=0, concat_axis=2, tiled=True)
+    return whole.reshape(piece, -1)
+
+
+def from_tokens(whole):
+    row_size = lax.axis_size("row")
+    col_size = lax.axis_size("col")
+    piece = whole.shape[0]
+    split = lax.all_to_all(whole[None], "col", split_axis=2, concat_axis=0, tiled=True)
+    groups = col_size // row_size
+    split = split.reshape(row_size, groups, piece, -1)
+    split = lax.all_to_all(split, "row", split_axis=0, concat_axis=2, tiled=True)
+    return split.reshape(groups * GLEN, -1)
+
+
+def collect(values):
+    return lax.all_gather(values, "row", axis=0, tiled=True)
+
+
+def land(partial):
+    return lax.psum_scatter(
+        partial.astype(jnp.bfloat16), "row", scatter_dimension=0, tiled=True
+    ).astype(jnp.float32)
 
 
 def score_blocks(queries, keys_in, offsets, lengths):
@@ -306,155 +298,100 @@
     lengths,
     cotangent,
 ):
-    rows_here = stream_in.shape[0]
-    group_count = memory.shape[0]
     head_here = memory.shape[1]
-    rows_col = group_count * GLEN
-    stream = stream_in.astype(jnp.float32)
-    square_in = lax.psum(jnp.sum(stream * stream, axis=1), "col")
-    inv_in = lax.rsqrt(square_in / D + EPSILON)[:, None]
-    gain_in = gain_attn[None, :]
-    normed_in = (stream * inv_in * gain_in).astype(jnp.bfloat16)
-    gathered_in, gathered_cot = row_collect((normed_in, cotangent))
+    row_size = lax.axis_size("row")
+    col_size = lax.axis_size("col")
+    row_index = lax.axis_index("row")
+    col_index = lax.axis_index("col")
+    gains = lax.all_gather(jnp.stack([gain_attn, gain_ffn]), "col", axis=1, tiled=True)
+    gain_in, gain_mid = gains[0:1], gains[1:2]
     whole_qkv, whole_out, whole_gu, whole_down = (
         lax.all_gather(w_qkv, "col", axis=1, tiled=True),
         lax.all_gather(w_out, "col", axis=1, tiled=True),
         lax.all_gather(w_gate_up, "col", axis=1, tiled=True),
         lax.all_gather(w_down, "col", axis=1, tiled=True),
     )
-    local_in, local_cot = to_local((gathered_in, gathered_cot))
+    stream = to_tokens(stream_in).astype(jnp.float32)
+    inv_in = lax.rsqrt(jnp.mean(stream * stream, axis=1, keepdims=True) + EPSILON)
+    normed_in = (stream * inv_in * gain_in).astype(jnp.bfloat16)
+    local_in = collect(normed_in)
+    cot_tokens = to_tokens(cotangent)
+    local_cot = collect(cot_tokens)
     packed = jnp.einsum("td,kdo->tko", local_in, whole_qkv, preferred_element_type=jnp.float32)
     heads_all = (
-        packed.astype(jnp.bfloat16)
-        .reshape(group_count, GLEN, 3, head_here, HD)
-        .transpose(0, 2, 3, 1, 4)
+        packed.astype(jnp.bfloat16).reshape(GLEN, 3, head_here, HD).transpose(1, 2, 0, 3)
     )
     gate_value = jax.nn.sigmoid(gate_logit)
-
-    def forward_group(items):
-        heads_one, memory_one, norm_one, offset_one, length_one = items
-        return attend_group(
-            heads_one[0],
-            heads_one[1],
-            heads_one[2],
-            memory_one,
-            norm_one,
-            offset_one,
-            length_one,
-            gate_value,
-        )
-
-    attended, logsum_prompt, logsum_cont, memory_part, dot_part, memory_new, norm_new = lax.map(
-        forward_group, (heads_all, memory, memory_norm, offsets, lengths)
-    )
-    attn_low = attended.astype(jnp.bfloat16).transpose(0, 2, 1, 3).reshape(rows_col, head_here * HD)
-    branch = land_rows(jnp.dot(attn_low, whole_out, preferred_element_type=jnp.float32), rows_here)
+    attended, logsum_prompt, logsum_cont, memory_part, dot_part, memory_new, norm_new = attend_group(
+        heads_all[0],
+        heads_all[1],
+        heads_all[2],
+        memory[0],
+        memory_norm[0],
+        offsets[0],
+        lengths[0],
+        gate_value,
+    )
+    attn_low = attended.astype(jnp.bfloat16).transpose(1, 0, 2).reshape(GLEN, head_here * HD)
+    branch = land(jnp.dot(attn_low, whole_out, preferred_element_type=jnp.float32))
     middle = stream + branch
-    branch_square, middle_square = lax.psum(
-        (jnp.sum(branch * branch, axis=1), jnp.sum(middle * middle, axis=1)), "col"
-    )
-    inv_mid = lax.rsqrt(middle_square / D + EPSILON)[:, None]
-    gain_mid = gain_ffn[None, :]
+    inv_mid = lax.rsqrt(jnp.mean(middle * middle, axis=1, keepdims=True) + EPSILON)
     normed_ffn = (middle * inv_mid * gain_mid).astype(jnp.bfloat16)
-    gathered_ffn = row_collect(normed_ffn)
-    local_ffn = to_local(gathered_ffn)
+    local_ffn = collect(normed_ffn)
     gate_up = jnp.einsum("td,kdo->tko", local_ffn, whole_gu, preferred_element_type=jnp.float32)
     gate_pre = gate_up[:, 0]
     up_pre = gate_up[:, 1]
     sigmoid_gate = jax.nn.sigmoid(gate_pre)
     hidden_low = (gate_pre * sigmoid_gate * up_pre).astype(jnp.bfloat16)
-    ffn = land_rows(jnp.dot(hidden_low, whole_down, preferred_element_type=jnp.float32), rows_here)
+    ffn = land(jnp.dot(hidden_low, whole_down, preferred_element_type=jnp.float32))
     result = middle + ffn
-    stream_out = result.astype(jnp.bfloat16)
+    stream_out = from_tokens(result.astype(jnp.bfloat16))
     grad_hidden = against_rows(local_cot, whole_down)
     part_down = tokens_contract(hidden_low, local_cot)
     grad_up = grad_hidden * gate_pre * sigmoid_gate
     grad_gate = grad_hidden * up_pre * sigmoid_gate * (1.0 + gate_pre * (1.0 - sigmoid_gate))
     grad_gu_low = jnp.stack([grad_gate, grad_up], axis=1).astype(jnp.bfloat16)
-    grad_normed_ffn = land_rows(
-        jnp.einsum("tko,kdo->td", grad_gu_low, whole_gu, preferred_element_type=jnp.float32),
-        rows_here,
+    grad_normed_ffn = land(
+        jnp.einsum("tko,kdo->td", grad_gu_low, whole_gu, preferred_element_type=jnp.float32)
     )
     part_gu = jnp.einsum("td,tko->kdo", local_ffn, grad_gu_low, preferred_element_type=jnp.float32)
     scaled_mid = grad_normed_ffn * gain_mid
-    ffn_square, out_square, inner_mid = (
-        lax.psum(jnp.sum(ffn * ffn, axis=1).astype(jnp.bfloat16), "col").astype(jnp.float32),
-        lax.psum(jnp.sum(result * result, axis=1).astype(jnp.bfloat16), "col").astype(jnp.float32),
-        lax.psum(jnp.sum(scaled_mid * middle, axis=1).astype(jnp.bfloat16), "col").astype(
-            jnp.float32
-        ),
-    )
+    inner_mid = jnp.mean(scaled_mid * middle, axis=1, keepdims=True)
     grad_middle = (
-        cotangent.astype(jnp.float32)
-        + inv_mid * scaled_mid
-        - middle * inv_mid**3 * (inner_mid / D)[:, None]
+        cot_tokens.astype(jnp.float32) + inv_mid * scaled_mid - middle * inv_mid**3 * inner_mid
     )
     part_gain_ffn = jnp.sum(grad_normed_ffn * middle * inv_mid, axis=0)
     branch_low = grad_middle.astype(jnp.bfloat16)
-    gathered_branch = row_collect(branch_low)
-    local_branch = to_local(gathered_branch)
+    local_branch = collect(branch_low)
     grad_attn_rows = against_rows(local_branch, whole_out)
     part_out = tokens_contract(attn_low, local_branch)
     grad_heads = (
-        grad_attn_rows.astype(jnp.bfloat16)
-        .reshape(group_count, GLEN, head_here, HD)
-        .transpose(0, 2, 1, 3)
-    )
-
-    def backward_group(items):
-        (
-            heads_one,
-            grad_one,
-            prompt_logsum,
-            cont_logsum,
-            part_memory,
-            part_dot,
-            memory_one,
-            norm_one,
-            offset_one,
-            length_one,
-        ) = items
-        return attend_back(
-            heads_one[0],
-            heads_one[1],
-            heads_one[2],
-            grad_one,
-            prompt_logsum,
-            cont_logsum,
-            part_memory,
-            part_dot,
-            memory_one,
-            norm_one,
-            offset_one,
-            length_one,
-            gate_value,
-        )
-
-    grad_queries, grad_keys, grad_values, grad_gates = lax.map(
-        backward_group,
-        (
-            heads_all,
-            grad_heads,
-            logsum_prompt,
-            logsum_cont,
-            memory_part,
-            dot_part,
-            memory,
-            memory_norm,
-            offsets,
-            lengths,
-        ),
-    )
-    logit_part = gate_value * (1.0 - gate_value) * jnp.sum(grad_gates, axis=0)
+        grad_attn_rows.astype(jnp.bfloat16).reshape(GLEN, head_here, HD).transpose(1, 0, 2)
+    )
+    grad_queries, grad_keys, grad_values, grad_gates = attend_back(
+        heads_all[0],
+        heads_all[1],
+        heads_all[2],
+        grad_heads,
+        logsum_prompt,
+        logsum_cont,
+        memory_part,
+        dot_part,
+        memory[0],
+        memory_norm[0],
+        offsets[0],
+        lengths[0],
+        gate_value,
+    )
+    logit_part = gate_value * (1.0 - gate_value) * grad_gates
     grad_packed = (
-        jnp.stack([grad_queries, grad_keys, grad_values], axis=1)
-        .transpose(0, 3, 1, 2, 4)
-        .reshape(rows_col, 3, head_here * HD)
+        jnp.stack([grad_queries, grad_keys, grad_values], axis=0)
+        .transpose(2, 0, 1, 3)
+        .reshape(GLEN, 3, head_here * HD)
         .astype(jnp.bfloat16)
     )
-    grad_normed_in = land_rows(
-        jnp.einsum("tko,kdo->td", grad_packed, whole_qkv, preferred_element_type=jnp.float32),
-        rows_here,
+    grad_normed_in = land(
+        jnp.einsum("tko,kdo->td", grad_packed, whole_qkv, preferred_element_type=jnp.float32)
     )
     part_qkv = jnp.einsum("td,tko->kdo", local_in, grad_packed, preferred_element_type=jnp.float32)
     grad_qkv, grad_out, grad_gate_up, grad_down = (
@@ -472,11 +409,26 @@
         ).astype(jnp.float32),
     )
     scaled_in = grad_normed_in * gain_in
-    inner_in, grad_gate_logit = lax.psum((jnp.sum(scaled_in * stream, axis=1), logit_part), "col")
-    stream_grad = grad_middle + inv_in * scaled_in - stream * inv_in**3 * (inner_in / D)[:, None]
+    inner_in = jnp.mean(scaled_in * stream, axis=1, keepdims=True)
+    grad_stream = grad_middle + inv_in * scaled_in - stream * inv_in**3 * inner_in
+    stream_grad = from_tokens(grad_stream.astype(jnp.bfloat16)).astype(jnp.float32)
     part_gain_attn = jnp.sum(grad_normed_in * stream * inv_in, axis=0)
-    grad_gain_attn, grad_gain_ffn = lax.psum((part_gain_attn, part_gain_ffn), "row")
-    rms_table = jnp.sqrt(jnp.stack([branch_square, middle_square, ffn_square, out_square]) / D)
+    logit_slots = lax.dynamic_update_slice(
+        jnp.zeros((row_size * head_here,), jnp.float32), logit_part, (row_index * head_here,)
+    )
+    small = lax.psum(
+        jnp.concatenate([part_gain_attn, part_gain_ffn, logit_slots]), ("row", "col")
+    )
+    features_here = gain_attn.shape[0]
+    grad_gain_attn = lax.dynamic_slice(small, (col_index * features_here,), (features_here,))
+    grad_gain_ffn = lax.dynamic_slice(small, (D + col_index * features_here,), (features_here,))
+    grad_gate_logit = lax.dynamic_slice(small, (2 * D + row_index * head_here,), (head_here,))
+    rms_here = jnp.sqrt(
+        jnp.stack([jnp.mean(part * part, axis=1) for part in (branch, middle, ffn, result)])
+    )
+    rms_all = lax.all_gather(rms_here, ("col", "row"), axis=1, tiled=True)
+    rows_here = stream_in.shape[0]
+    rms_table = lax.dynamic_slice(rms_all, (0, row_index * rows_here), (4, rows_here))
     return (
         stream_out,
         stream_grad,
@@ -487,8 +439,8 @@
         grad_gain_attn,
         grad_gain_ffn,
         grad_gate_logit,
-        memory_new,
-        norm_new,
+        memory_new[None],
+        norm_new[None],
         rms_table,
     )
 

time: 3220 us -> 1670 us (0.52)
  blocking collectives: 1120 us -> 319 us
  waiting for transfers between devices: 1500 us -> 721 us
  other arithmetic: 82.4 us -> 131 us
  local copies, waits for them, and re-layouts: 129 us -> 90.1 us
    all_to_all x4 -> x5, waiting for transfers between devices: 970 us -> 50.3 us  [the longest x2 44.5 us: from_tokens(): lax.all_to_all(whole[None], 'col', split_axis=2, concat_axis=0, tiled=True)]
    all_to_all x4 -> x3, blocking collectives: 1020 us -> 129 us  [the longest x1 86.4 us: to_tokens(): lax.all_to_all(split, 'col', split_axis=0, concat_axis=2, tiled=True)]
    reduce_scatter x4, waiting for transfers between devices: 346 us -> 179 us  [land(): lax.psum_scatter(partial.astype(jnp.bfloat16), 'row', scatter_dimension=0...]
    all_gather x0 -> x2, blocking collectives: none -> 149 us  [the longest x1 75.5 us: local(): rms_all = lax.all_gather(rms_here, ('col', 'row'), axis=1, tiled=True)]
    all_gather x4, waiting for transfers between devices: 129 us -> 249 us  [collect(): return lax.all_gather(values, 'row', axis=0, tiled=True)]
    all_gather x1, waiting for transfers between devices: 0.01 us -> 81.7 us  [local(): lax.all_gather(w_down, 'col', axis=1, tiled=True)]
    unnamed x1 -> x5, other arithmetic: 0.01 us -> 69.1 us
    all_gather x1, waiting for transfers between devices: 0.01 us -> 67.8 us  [local(): lax.all_gather(w_gate_up, 'col', axis=1, tiled=True)]
  transfers between devices with their start and end apart: 20 -> 21, of which waited for: 11 -> 14; matrix products, arithmetic and copies ran while one was open for 11% -> 22% of each run, Pallas kernels for 0% -> 0%
where the time goes in v1:
time: 1670 us; the launch traced here: 1660 us
  waiting for transfers between devices  721 us (43%)
  matrix products  349 us (21%)
  blocking collectives  319 us (19%)
  other arithmetic  131 us (8%)
  local copies, waits for them, and re-layouts  90.1 us (5%)
  starting transfers between devices  28.6 us (2%)
    all_gather x4, waiting for transfers between devices, collect(): return lax.all_gather(values, 'row', axis=0, tiled=True)  249 us
    reduce_scatter x4, waiting for transfers between devices, land(): lax.psum_scatter(partial.astype(jnp.bfloat16), 'row', scatter_dimension=0...  179 us
    all_to_all x1, blocking collectives, to_tokens(): lax.all_to_all(split, 'col', split_axis=0, concat_axis=2, tiled=True)  86.4 us
    all_gather x1, waiting for transfers between devices, local(): lax.all_gather(w_down, 'col', axis=1, tiled=True)  81.7 us
    all_gather x1, blocking collectives, local(): rms_all = lax.all_gather(rms_here, ('col', 'row'), axis=1, tiled=True)  75.5 us
    all_gather x1, blocking collectives, local(): lax.all_gather(jnp.stack([gain_attn, gain_ffn]), 'col', axis=1, tiled=True)  73.5 us
    unnamed x5, other arithmetic  69.1 us
    all_gather x1, waiting for transfers between devices, local(): lax.all_gather(w_gate_up, 'col', axis=1, tiled=True)  67.8 us
  transfers between devices with their start and end apart: 21, of which 14 were waited for; matrix products, arithmetic and copies ran while one was open for 22% of the time, Pallas kernels for 0%

profile of v1, /device:TPU:27, one launch (start us, length us, event | category | flops | bytes accessed | tf_op | source)
XLA Modules:
  0.0 1655.2 jit_solution(4007418091041222623)
XLA Ops:
  9.8 21.6 %all_to_all.108 = bf16[2,4,384,256]{3,2,0,1:T(8,128)(2,1)} all-to-all(bf16[2,4,384,256]{3,2,0,1:T(8,128)(2,1)S(1)} %copy.137), channel_id=1, replica_groups=mesh['row'=4,'col'=8] {'row'}, dimensions={1} | all-to-all | bytes 3145728 | tf_op jit(solution)/shard_map/all_to_all | solution.py:53
  31.4 6.6 all-to-all-start.1
  38.0 73.5 %all_gather.30 = f32[2,2048]{1,0:T(2,128)S(1)} all-gather(f32[2,256]{1,0:T(2,128)S(1)} %pad_maximum_fusion.5), channel_id=1, replica_groups=mesh['row'=4,'col'=8] {'col'}, dimensions={1}, use_global_device_ids=true | all-gather | bytes 18432 | tf_op jit(solution)/shard_map/all_gather | solution.py:306
  119.7 68.1 %all-gather.9.cloned.1.call-done = bf16[1536,2048]{1,0:T(8,128)(2,1)} async-done(((bf16[384,2048]{1,0:T(8,128)(2,1)}), bf16[1536,2048]{1,0:T(8,128)(2,1)}) %all-gather.9.cloned.1.call-update) | async-done | bytes 6291472 | tf_op jit(solution)/shard_map/all_gather | solution.py:71
  187.8 15.3 fusion.12
  203.1 6.7 copy.140
  239.9 12.1 fusion.109
  252.0 8.7 add_convert_fusion
  260.7 8.2 convolution_convert_fusion.2
  269.7 69.4 %reduce-scatter.9.cloned.1.call-done = bf16[384,2048]{1,0:T(8,128)(2,1)} async-done(((bf16[1536,2048]{1,0:T(8,128)(2,1)}), bf16[384,2048]{1,0:T(8,128)(2,1)}) %reduce-scatter.9.cloned.1.call-update) | async-done | bytes 1572880 | tf_op jit(solution)/shard_map/reduce_scatter | solution.py:75
  345.4 21.2 %all_to_all.109 = bf16[2,4,384,256]{3,2,0,1:T(8,128)(2,1)S(1)} all-to-all(bf16[2,4,384,256]{3,2,0,1:T(8,128)(2,1)S(1)} %copy.149), channel_id=1, replica_groups=mesh['row'=4,'col'=8] {'row'}, dimensions={1} | all-to-all | bytes 3145728 | tf_op jit(solution)/shard_map/all_to_all | solution.py:53
  366.6 86.4 %all_to_all.110 = bf16[8,384,256]{2,1,0:T(8,128)(2,1)S(1)} all-to-all(bf16[8,384,256]{2,1,0:T(8,128)(2,1)S(1)} %bitcast.280), channel_id=1, replica_groups=mesh['row'=4,'col'=8] {'col'}, dimensions={0} | all-to-all | bytes 3145728 | tf_op jit(solution)/shard_map/all_to_all | solution.py:55
  455.1 67.8 %all-gather.17.cloned.1.call-done = bf16[2,2048,2048]{2,1,0:T(8,128)(2,1)} async-done(((bf16[2,256,2048]{2,1,0:T(8,128)(2,1)}), bf16[2,2048,2048]{2,1,0:T(8,128)(2,1)}) %all-gather.17.cloned.1.call-update) | async-done | bytes 16777232 | tf_op jit(solution)/shard_map/all_gather | solution.py:311
  523.0 72.5 %all-gather.15.cloned.1.call-done = bf16[1536,2048]{1,0:T(8,128)(2,1)} async-done(((bf16[384,2048]{1,0:T(8,128)(2,1)}), bf16[1536,2048]{1,0:T(8,128)(2,1)}) %all-gather.15.cloned.1.call-update) | async-done | bytes 6291472 | tf_op jit(solution)/shard_map/all_gather | solution.py:71
  595.5 33.6 %fusion.4 = f32[1536,2,2048]{2,0,1:T(8,128)} fusion(bf16[2,2048,2048]{2,1,0:T(8,128)(2,1)} %all-gather.17.cloned.1.call-done, bf16[1536,2048]{1,0:T(8,128)(2,1)} %all-gather.15.cloned.1.call-done), kind=kOutput, calls=%fused_computation.27 | convolution fusion | flops 25769803776 | bytes 48234496 | tf_op jit(solution)/shard_map/td,kdo->tko/dot_general | solution.py:341
  629.1 38.4 %all-gather.21.cloned.1.call-done = bf16[1536,2048]{1,0:T(8,128)(2,1)} async-done(((bf16[384,2048]{1,0:T(8,128)(2,1)}), bf16[1536,2048]{1,0:T(8,128)(2,1)}) %all-gather.21.cloned.1.call-update) | async-done | bytes 6291472 | tf_op jit(solution)/shard_map/all_gather | solution.py:71
  667.5 81.7 %all-gather.19.cloned.1.call-done = bf16[2048,2048]{1,0:T(8,128)(2,1)} async-done(((bf16[2048,256]{1,0:T(8,128)(2,1)}), bf16[2048,2048]{1,0:T(8,128)(2,1)}) %all-gather.19.cloned.1.call-update) | async-done | bytes 8388624 | tf_op jit(solution)/shard_map/all_gather | solution.py:312
  749.2 28.5 %fusion.11 = (bf16[1536,1,2048]{2,0,1:T(8,128)(2,1)}, bf16[1536,1,2048]{2,0,1:T(8,128)(2,1)}, bf16[1536,2048]{1,0:T(8,128)(2,1)}) fusion(f32[1536,2,2048]{2,0,1:T(8,128)} %fusion.4, bf16[1536,2048]{1,0:T(8,128)(2,1)} %all-gather.21.cloned.1.call-done, bf16[2048,2048]{1,0:T(8,128)(2,1)} %all-gather.19.cloned.1.call-done), kind=kOutput, calls=%fused_computation.35 | convolution fusion | flops 12935233536 | bytes 58720256 | tf_op jit(solution)/shard_map/dot_general | solution.py:42
  777.7 16.8 %convolution_convert_fusion.1 = bf16[1536,2048]{1,0:T(8,128)(2,1)} fusion(bf16[1536,2048]{1,0:T(8,128)(2,1)} %get-tuple-element.73, bf16[2048,2048]{1,0:T(8,128)(2,1)S(1)} %copy-done.81), kind=kOutput, calls=%fused_computation.23 | convolution fusion | flops 12888047616 | bytes 20971520 | tf_op jit(solution)/shard_map/dot_general | solution.py:346
  794.6 34.1 %bitcast_convert_fusion.1 = bf16[1536,2048]{1,0:T(8,128)(2,1)} fusion(bf16[2,2048,2048]{2,1,0:T(8,128)(2,1)} %all-gather.17.cloned.1.call-done, bf16[1536,1,2048]{2,0,1:T(8,128)(2,1)} %get-tuple-element.72, bf16[1536,1,2048]{2,0,1:T(8,128)(2,1)} %get-tuple-element.71), kind=kOutput, calls=%fused_computation.11 | convolution fusion | flops 25779240960 | bytes 35651584 | tf_op jit(solution)/shard_map/tko,kdo->td/dot_general | solution.py:355
  828.8 36.6 %reduce-scatter.11.cloned.1.call-done = bf16[384,2048]{1,0:T(8,128)(2,1)} async-done(((bf16[1536,2048]{1,0:T(8,128)(2,1)}), bf16[384,2048]{1,0:T(8,128)(2,1)}) %reduce-scatter.11.cloned.1.call-update) | async-done | bytes 1572880 | tf_op jit(solution)/shard_map/reduce_scatter | solution.py:75
  865.3 73.1 %reduce-scatter.13.cloned.1.call-done = bf16[384,2048]{1,0:T(8,128)(2,1)} async-done(((bf16[1536,2048]{1,0:T(8,128)(2,1)}), bf16[384,2048]{1,0:T(8,128)(2,1)}) %reduce-scatter.13.cloned.1.call-update) | async-done | bytes 1572880 | tf_op jit(solution)/shard_map/reduce_scatter | solution.py:75
  946.5 70.4 %all-gather.23.cloned.1.call-done = bf16[1536,2048]{1,0:T(8,128)(2,1)} async-done(((bf16[384,2048]{1,0:T(8,128)(2,1)}), bf16[1536,2048]{1,0:T(8,128)(2,1)}) %all-gather.23.cloned.1.call-update) | async-done | bytes 6291472 | tf_op jit(solution)/shard_map/all_gather | solution.py:71
  1016.9 6.9 convolution_convert_fusion.4
  1023.8 13.0 multiply_reduce_fusion
  1037.2 7.5 multiply_reduce_fusion.1
  1046.1 11.2 fusion.96
  1058.7 15.4 multiply_convert_fusion
  1074.1 7.9 convolution_multiply_fusion
  1082.1 7.5 fusion.100
  1101.9 7.5 fusion.59
  1116.9 8.7 fusion.52
  1128.5 6.6 copy.170
  1135.1 15.4 bitcast_convert_fusion
  1150.6 19.4 %convolution_convert_fusion = bf16[2048,2048]{1,0:T(8,128)(2,1)} fusion(bf16[1536,2048]{1,0:T(8,128)(2,1)} %get-tuple-element.73, bf16[1536,2048]{1,0:T(8,128)(2,1)} %all-gather.21.cloned.1.call-done), kind=kOutput, calls=%fused_computation.22 | convolution fusion | flops 12889096192 | bytes 20971520 | tf_op jit(solution)/shard_map/dot_general | solution.py:36
  1171.5 8.0 convolution_convert_fusion.3
  1179.5 33.1 %convert_bitcast_fusion = bf16[2,2048,2048]{1,2,0:T(8,128)(2,1)} fusion(bf16[1536,1,2048]{2,0,1:T(8,128)(2,1)} %get-tuple-element.72, bf16[1536,1,2048]{2,0,1:T(8,128)(2,1)} %get-tuple-element.71, bf16[1536,2048]{1,0:T(8,128)(2,1)} %all-gather.15.cloned.1.call-done), kind=kOutput, calls=%fused_computation | convolution fusion | flops 25784483840 | bytes 35651584 | tf_op jit(solution)/shard_map/td,tko->kdo/dot_general | solution.py:357
  1212.7 15.5 convert_bitcast_fusion.1
  1228.2 8.0 copy.146
  1236.7 34.4 %reduce.3 = bf16[2048,384]{1,0:T(8,128)(2,1)} reduce(bf16[2048,1,384]{2,1,0:T(2,128)(2,1)S(1)} %bitcast.272, bf16[]{:T(256)} %broadcast.276), dimensions={1}, to_apply=%bitcast.191.reduce_sub_computation | reduce | bytes 3145730
  1289.2 7.9 copy.173
  1297.2 34.4 %reduce.4 = bf16[2048,384]{1,0:T(8,128)(2,1)} reduce(bf16[2048,1,384]{2,1,0:T(2,128)(2,1)S(1)} %bitcast.273, bf16[]{:T(256)} %broadcast.276), dimensions={1}, to_apply=%bitcast.193.reduce_sub_computation | reduce | bytes 3145730
  1338.1 7.0 all-to-all-start.6
  1353.9 41.7 %all-to-all-done.6 = bf16[8,2,49152]{2,1,0:T(2,128)(2,1)} async-done(((bf16[8,2,49152]{2,1,0:T(2,128)(2,1)}), bf16[8,2,49152]{2,1,0:T(2,128)(2,1)}, u32[]{:S(2)}, u32[]{:S(2)}) %all-to-all-start.6) | async-done | bytes 1572896 | tf_op jit(solution)/shard_map/all_to_all | solution.py:63
  1422.9 75.5 %all_gather.39 = f32[4,12288]{1,0:T(4,128)S(1)} all-gather(f32[4,384]{1,0:T(4,128)S(1)} %maximum_sqrt_fusion), channel_id=1, replica_groups=mesh['row'=4,'col'=8] {'col','row'}, dimensions={1}, use_global_device_ids=true | all-gather | bytes 202752 | tf_op jit(solution)/shard_map/all_gather | solution.py:429
  1506.3 64.6 %reduce-scatter.21.cloned.1.call-done = bf16[2,256,2048]{1,2,0:T(8,128)(2,1)} async-done(((bf16[2,2048,2048]{1,2,0:T(8,128)(2,1)}), bf16[2,256,2048]{1,2,0:T(8,128)(2,1)}) %reduce-scatter.21.cloned.1.call-update) | async-done | bytes 2097168 | tf_op jit(solution)/shard_map/reduce_scatter | solution.py:404
  1574.9 41.3 %psum.7 = f32[4112]{0:T(1024)S(1)} all-reduce(f32[4112]{0:T(1024)S(1)} %pad_maximum_fusion.4), channel_id=1, replica_groups=mesh['row'=4,'col'=8] {'row','col'}, use_global_device_ids=true, to_apply=%region_25.26 | all-reduce | flops 4112 | bytes 32896 | tf_op jit(solution)/shard_map/psum | solution.py:419
  1616.9 26.4 %reduce-scatter.17.cloned.1.call-done = bf16[3,256,512]{1,2,0:T(8,128)(2,1)} async-done(((bf16[3,2048,512]{1,2,0:T(8,128)(2,1)}), bf16[3,256,512]{1,2,0:T(8,128)(2,1)}) %reduce-scatter.17.cloned.1.call-update) | async-done | bytes 786448 | tf_op jit(solution)/shard_map/reduce_scatter | solution.py:398
  (321 shorter events, 163.8 us)
Async XLA Ops:
  7.2 112.5 %all-gather.11.cloned.1.call-start = ((), (), s32[]{:S(2)}) async-start(), calls=%async_computation.17 | async-start | bytes 7077888 | tf_op jit(solution)/shard_map/all_gather | solution.py:309
  9.8 28.2 %copy-start.78 = (f32[256]{0:T(256)S(1)}, f32[256]{0:T(256)}, u32[]{:S(2)}) copy-start(f32[256]{0:T(256)} %param.19) | copy-start | bytes 3076
  9.8 28.2 %copy-start.79 = (f32[256]{0:T(256)S(1)}, f32[256]{0:T(256)}, u32[]{:S(2)}) copy-start(f32[256]{0:T(256)} %param.18) | copy-start | bytes 3076
  31.4 80.2 %all-to-all-start.1 = ((bf16[8,384,256]{2,1,0:T(8,128)(2,1)}), bf16[8,384,256]{2,1,0:T(8,128)(2,1)S(1)}, u32[]{:S(2)}, u32[]{:S(2)}) async-start(bf16[8,384,256]{2,1,0:T(8,128)(2,1)} %bitcast.3), calls=%async_computation.1 | async-start | bytes 3145728 | tf_op jit(solution)/shard_map/all_to_all | solution.py:55
  38.0 149.8 %all-gather.9.cloned.1.call-start = ((), (), s32[]{:S(2)}) async-start(), calls=%async_computation.16 | async-start | bytes 7864320 | tf_op jit(solution)/shard_map/all_gather | solution.py:71
  111.6 230.9 %copy-start.44 = (f32[1,2048]{1,0:T(1,128)}, f32[1,2048]{1,0:T(1,128)S(1)}, u32[]{:S(2)}) copy-start(f32[1,2048]{1,0:T(1,128)S(1)} %get-tuple-element.82) | copy-start | bytes 24580
  114.5 224.7 %copy-start.5 = (f32[48,8,8,256]{3,1,2,0:T(8,128)}, f32[48,8,8,256]{3,1,2,0:T(8,128)S(1)}, u32[]{:S(2)}) copy-start(f32[48,8,8,256]{3,1,2,0:T(8,128)S(1)} %copy.210) | copy-start | bytes 9437188
  117.3 143.4 %all-gather.13.cloned.1.call-start = ((), (), s32[]{:S(2)}) async-start(), calls=%async_computation.18 | async-start | bytes 2359296 | tf_op jit(solution)/shard_map/all_gather | solution.py:310
  118.0 221.1 %reduce-scatter.9.cloned.1.call-start = ((), (), s32[]{:S(2)}) async-start(), calls=%async_computation.19 | async-start | bytes 7864320 | tf_op jit(solution)/shard_map/reduce_scatter | solution.py:75
  119.4 98.8 %copy-start.47 = (pred[4,1024]{1,0:T(4,128)(4,1)}, pred[4,1024]{1,0:T(4,128)(4,1)S(1)}, u32[]{:S(2)}) copy-start(pred[4,1024]{1,0:T(4,128)(4,1)S(1)} %iota_compare_fusion.2) | copy-start | bytes 12292
  119.5 132.5 %copy-start.58 = (f32[4]{0:T(128)}, f32[4]{0:T(128)S(1)}, u32[]{:S(2)}) copy-start(f32[4]{0:T(128)S(1)} %get-tuple-element.69) | copy-start | bytes 52
  119.5 132.5 %copy-start.74 = (f32[4]{0:T(128)}, f32[4]{0:T(128)S(1)}, u32[]{:S(2)}) copy-start(f32[4]{0:T(128)S(1)} %get-tuple-element.70) | copy-start | bytes 52
  235.1 16.9 %copy-start.63 = (f32[4,1,1536]{2,0,1:T(4,128)}, f32[4,1,1536]{2,0,1:T(4,128)S(1)}, u32[]{:S(2)}) copy-start(f32[4,1,1536]{2,0,1:T(4,128)S(1)} %copy.218) | copy-start | bytes 73732
  268.9 254.1 %all-gather.17.cloned.1.call-start = ((), (), s32[]{:S(2)}) async-start(), calls=%async_computation.21 | async-start | bytes 18874368 | tf_op jit(solution)/shard_map/all_gather | solution.py:311
  269.5 326.0 %all-gather.15.cloned.1.call-start = ((), (), s32[]{:S(2)}) async-start(), calls=%async_computation.20 | async-start | bytes 7864320 | tf_op jit(solution)/shard_map/all_gather | solution.py:71
  345.1 322.4 %all-gather.21.cloned.1.call-start = ((), (), s32[]{:S(2)}) async-start(), calls=%async_computation.24 | async-start | bytes 7864320 | tf_op jit(solution)/shard_map/all_gather | solution.py:71
  454.3 294.9 %all-gather.19.cloned.1.call-start = ((), (), s32[]{:S(2)}) async-start(), calls=%async_computation.22 | async-start | bytes 9437184 | tf_op jit(solution)/shard_map/all_gather | solution.py:312
  455.1 410.2 %reduce-scatter.11.cloned.1.call-start = ((), (), s32[]{:S(2)}) async-start(), calls=%async_computation.23 | async-start | bytes 7864320 | tf_op jit(solution)/shard_map/reduce_scatter | solution.py:75
  749.2 28.5 %copy-start.81 = (bf16[2048,2048]{1,0:T(8,128)(2,1)S(1)}, bf16[2048,2048]{1,0:T(8,128)(2,1)}, u32[]{:S(2)}) copy-start(bf16[2048,2048]{1,0:T(8,128)(2,1)} %all-gather.19.cloned.1.call-done) | copy-start | bytes 25165828
  794.5 143.9 %reduce-scatter.13.cloned.1.call-start = ((), (), s32[]{:S(2)}) async-start(), calls=%async_computation.25 | async-start | bytes 7864320 | tf_op jit(solution)/shard_map/reduce_scatter | solution.py:75
  828.7 109.7 %copy-start.3 = (f32[384,2048]{1,0:T(8,128)S(1)}, f32[384,2048]{1,0:T(8,128)}, u32[]{:S(2)}) copy-start(f32[384,2048]{1,0:T(8,128)} %copy-done.2) | copy-start | bytes 9437188
  828.7 109.7 %copy-start.45 = (f32[1,2048]{1,0:T(1,128)S(1)}, f32[1,2048]{1,0:T(1,128)}, u32[]{:S(2)}) copy-start(f32[1,2048]{1,0:T(1,128)} %copy-done.44) | copy-start | bytes 24580
  828.7 109.7 %copy-start.56 = (f32[384]{0:T(512)S(1)}, f32[384]{0:T(512)}, u32[]{:S(2)}) copy-start(f32[384]{0:T(512)} %copy-done.55) | copy-start | bytes 4612
  828.7 115.5 %copy-start.67 = (f32[384]{0:T(512)S(1)}, f32[384]{0:T(512)}, u32[]{:S(2)}) copy-start(f32[384]{0:T(512)} %get-tuple-element.85) | copy-start | bytes 4612
  828.7 188.1 %all-gather.23.cloned.1.call-start = ((), (), s32[]{:S(2)}) async-start(), calls=%async_computation.26 | async-start | bytes 7864320 | tf_op jit(solution)/shard_map/all_gather | solution.py:71
  946.4 77.3 %copy-start.15 = (pred[1024,1024]{0,1:T(8,128)(4,1)S(1)}, pred[1024,1024]{0,1:T(8,128)(4,1)}, u32[]{:S(2)}) copy-start(pred[1024,1024]{0,1:T(8,128)(4,1)} %iota_compare_fusion) | copy-start | bytes 3145732
  946.4 77.3 %copy-start.50 = (f32[4,1024]{1,0:T(4,128)S(1)}, f32[4,1024]{1,0:T(4,128)}, u32[]{:S(2)}) copy-start(f32[4,1024]{1,0:T(4,128)} %copy-done.49) | copy-start | bytes 49156
  946.4 77.3 %copy-start.59 = (f32[4]{0:T(128)S(1)}, f32[4]{0:T(128)}, u32[]{:S(2)}) copy-start(f32[4]{0:T(128)} %copy-done.58) | copy-start | bytes 52
  946.4 334.1 %reduce-scatter.15.cloned.1.call-start = ((), (), s32[]{:S(2)}) async-start(), calls=%async_computation.27 | async-start | bytes 7864320 | tf_op jit(solution)/shard_map/reduce_scatter | solution.py:75
  1023.7 13.1 copy-start.23
  1023.8 13.4 copy-start.43
  1023.8 13.4 copy-start.48
  1037.1 20.3 %copy-start.25 = (bf16[4,512,128]{2,1,0:T(8,128)(2,1)}, bf16[4,512,128]{2,1,0:T(8,128)(2,1)S(1)}, u32[]{:S(2)}) copy-start(bf16[4,512,128]{2,1,0:T(8,128)(2,1)S(1)} %copy.207) | copy-start | bytes 1572868
  1058.7 15.4 copy-start.12
  1074.1 16.9 %slice-start = ((s8[8388608]{0:T(1024)(128)(4,1)}), s8[4194304]{0:T(1024)(128)(4,1)S(1)}, s32[]{:S(2)}) async-start(s8[8388608]{0:T(1024)(128)(4,1)} %bitcast.248), calls=%async_computation.32 | async-start | bytes 8388608
  1074.1 16.9 %slice-start.2 = ((s8[8388608]{0:T(1024)(128)(4,1)}), s8[4194304]{0:T(1024)(128)(4,1)S(1)}, s32[]{:S(2)}) async-start(s8[8388608]{0:T(1024)(128)(4,1)} %bitcast.254), calls=%async_computation.34 | async-start | bytes 8388608
  1150.6 351.1 %reduce-scatter.23.cloned.1.call-start = ((), (), s32[]{:S(2)}) async-start(), calls=%async_computation.31 | async-start | bytes 9437184 | tf_op jit(solution)/shard_map/reduce_scatter | solution.py:407
  1170.1 334.4 %reduce-scatter.19.cloned.1.call-start = ((), (), s32[]{:S(2)}) async-start(), calls=%async_computation.29 | async-start | bytes 2359296 | tf_op jit(solution)/shard_map/reduce_scatter | solution.py:401
  1179.5 391.4 %reduce-scatter.21.cloned.1.call-start = ((), (), s32[]{:S(2)}) async-start(), calls=%async_computation.30 | async-start | bytes 18874368 | tf_op jit(solution)/shard_map/reduce_scatter | solution.py:404
  1212.6 430.7 %reduce-scatter.17.cloned.1.call-start = ((), (), s32[]{:S(2)}) async-start(), calls=%async_computation.28 | async-start | bytes 7077888 | tf_op jit(solution)/shard_map/reduce_scatter | solution.py:398
  1274.9 63.2 %all-to-all-start.2 = ((bf16[8,2,49152]{2,1,0:T(2,128)(2,1)}), bf16[8,2,49152]{2,1,0:T(2,128)(2,1)}, u32[]{:S(2)}, u32[]{:S(2)}) async-start(bf16[8,2,49152]{2,1,0:T(2,128)(2,1)} %reshape.340), calls=%async_computation.4 | async-start | bytes 3145728 | tf_op jit(solution)/shard_map/all_to_all | solution.py:63
  1338.1 57.5 %all-to-all-start.6 = ((bf16[8,2,49152]{2,1,0:T(2,128)(2,1)}), bf16[8,2,49152]{2,1,0:T(2,128)(2,1)}, u32[]{:S(2)}, u32[]{:S(2)}) async-start(bf16[8,2,49152]{2,1,0:T(2,128)(2,1)} %reshape.342), calls=%async_computation.10 | async-start | bytes 3145728 | tf_op jit(solution)/shard_map/all_to_all | solution.py:63
  1351.1 49.3 %copy-start.13 = (bf16[4,1536,128]{2,1,0:T(8,128)(2,1)S(1)}, bf16[4,1536,128]{2,1,0:T(8,128)(2,1)}, u32[]{:S(2)}) copy-start(bf16[4,1536,128]{2,1,0:T(8,128)(2,1)} %copy-done.11) | copy-start | bytes 4718596
  1351.1 50.4 %copy-start.19 = (bf16[4,1536,128]{2,1,0:T(8,128)(2,1)S(1)}, bf16[4,1536,128]{2,1,0:T(8,128)(2,1)}, u32[]{:S(2)}) copy-start(bf16[4,1536,128]{2,1,0:T(8,128)(2,1)} %copy-done.18) | copy-start | bytes 4718596
  1395.6 23.4 %all-to-all-start.3 = ((bf16[4,2,384,256]{3,2,1,0:T(8,128)(2,1)}), bf16[4,2,384,256]{3,2,1,0:T(8,128)(2,1)}, u32[]{:S(2)}, u32[]{:S(2)}) async-start(bf16[4,2,384,256]{3,2,1,0:T(8,128)(2,1)} %copy.147), calls=%async_computation.5 | async-start | bytes 3145728 | tf_op jit(solution)/shard_map/all_to_all | solution.py:66
  1410.5 12.4 copy-start.72
  1419.0 227.5 %all-to-all-start.7 = ((bf16[4,2,384,256]{3,2,1,0:T(8,128)(2,1)}), bf16[4,2,384,256]{3,2,1,0:T(8,128)(2,1)S(1)}, u32[]{:S(2)}, u32[]{:S(2)}) async-start(bf16[4,2,384,256]{3,2,1,0:T(8,128)(2,1)} %copy.174), calls=%async_computation.11 | async-start | bytes 3145728 | tf_op jit(solution)/shard_map/all_to_all | solution.py:66
  1506.3 68.7 %copy-start.62 = (f32[2048]{0:T(1024)S(1)}, f32[2048]{0:T(1024)}, u32[]{:S(2)}) copy-start(f32[2048]{0:T(1024)} %get-tuple-element.62) | copy-start | bytes 24580
  (64 other events, 316.7 us)
Sparse Core Ops, SparseCore 0:
  10.2 97.3 all-gather.10
  117.4 70.3 all-gather.8
  189.4 28.9 all-gather.12
  269.0 70.0 reduce-scatter.8
  340.6 182.3 all-gather.16
  524.7 70.7 all-gather.14
  597.3 70.1 all-gather.20
  669.1 80.0 all-gather.18
  794.6 70.6 reduce-scatter.10
  868.2 70.1 reduce-scatter.12
  946.5 70.2 all-gather.22
  1150.7 70.0 reduce-scatter.14
  1223.1 112.3 reduce-scatter.22
  1338.2 62.1 reduce-scatter.18
  1402.7 168.1 reduce-scatter.20
  1573.0 70.2 reduce-scatter.16

commit v2 on v1

v2 whole, which is shorter than its diff:
```python
import jax
import jax.numpy as jnp
from jax import lax
from jax.experimental import pallas as pl
from jax.experimental.pallas import tpu as pltpu
from jax.sharding import PartitionSpec as P

D = 2048
HD = 128
PROMPT = 1024
CONT = 4
CLEN = 128
GLEN = 1536


EPSILON = 1e-06
MASKED_LOGIT = -1e30
BIG_VMEM = 60 * 1024 * 1024


def feature_map(values):
    return jnp.where(values > 0, values + 1.0, jnp.exp(jnp.minimum(values, 0.0)))


def feature_slope(values):
    return jnp.where(values > 0, 1.0, jnp.exp(jnp.minimum(values, 0.0)))


def split_two(value):
    high = value.astype(jnp.bfloat16)
    return high, (value - high.astype(jnp.float32)).astype(jnp.bfloat16)


def wide_dot(left, right, dims):
    left_high, left_low = split_two(left)
    right_high, right_low = split_two(right)

    def one(a, b):
        return lax.dot_general(a, b, (dims, ((), ())), preferred_element_type=jnp.float32)

    return one(left_high, right_high) + one(left_high, right_low) + one(left_low, right_high)


def narrow_dot(left, right, dims):
    right_high, right_low = split_two(right)

    def one(b):
        return lax.dot_general(left, b, (dims, ((), ())), preferred_element_type=jnp.float32)

    return one(right_high) + one(right_low)


def plain_dot(left, right, dims):
    return lax.dot_general(left, right, (dims, ((), ())), preferred_element_type=jnp.float32)


NN = ((1,), (0,))
NT = ((1,), (1,))
TN = ((0,), (0,))
QT = 256
PROMPT_TILES = PROMPT // QT
TILES = GLEN // QT


def tile_scores(tile, q, k_ref, offsets_ref, lengths_ref):
    scale = HD ** (-0.5)
    row = lax.broadcasted_iota(jnp.int32, (QT, QT), 0)
    column = lax.broadcasted_iota(jnp.int32, (QT, QT), 1)
    seen = min(tile * QT, PROMPT)
    own = plain_dot(q, k_ref[tile * QT : (tile + 1) * QT], NT) * scale
    if tile < PROMPT_TILES:
        own = jnp.where(row >= column, own, MASKED_LOGIT)
        ahead = plain_dot(q, k_ref[:seen], NT) * scale if seen else None
        return ahead, own, seen
    first = (tile - PROMPT_TILES) * (QT // CLEN)
    upper = lax.broadcasted_iota(jnp.int32, (QT, 1), 0) >= CLEN
    limit = jnp.where(upper, offsets_ref[first + 1], offsets_ref[first])
    live = jnp.where(upper, lengths_ref[first + 1] + CLEN, lengths_ref[first])
    same = (row >= CLEN) == (column >= CLEN)
    own = jnp.where((row >= column) & same & (column < live), own, MASKED_LOGIT)
    ahead = plain_dot(q, k_ref[:seen], NT) * scale
    position = lax.broadcasted_iota(jnp.int32, (QT, PROMPT), 1)
    return jnp.where(position < limit, ahead, MASKED_LOGIT), own, seen


def attend_kernel(
    offsets_ref, lengths_ref, gate_ref, qkv_ref, memory_ref, norm_ref,
    attn_ref, dot_ref, part_ref, logsum_ref, memory_new_ref, norm_new_ref,
):
    head = pl.program_id(0)
    gate = gate_ref[head]
    q_ref, k_ref, v_ref = qkv_ref.at[0, 0], qkv_ref.at[1, 0], qkv_ref.at[2, 0]
    memory_one = memory_ref[0]
    norm_one = norm_ref[0]
    for tile in range(TILES):
        rows = slice(tile * QT, (tile + 1) * QT)
        q = q_ref[rows]
        ahead, own, seen = tile_scores(tile, q, k_ref, offsets_ref, lengths_ref)
        peak = jnp.max(own, axis=1, keepdims=True)
        if ahead is not None:
            peak = jnp.maximum(peak, jnp.max(ahead, axis=1, keepdims=True))
        own = jnp.exp(own - peak)
        total = jnp.sum(own, axis=1, keepdims=True)
        dot_part = plain_dot(own.astype(jnp.bfloat16), v_ref[rows], NN)
        if ahead is not None:
            ahead = jnp.exp(ahead - peak)
            total += jnp.sum(ahead, axis=1, keepdims=True)
            dot_part += plain_dot(ahead.astype(jnp.bfloat16), v_ref[:seen], NN)
        dot_part = dot_part / total
        lifted = feature_map(q.astype(jnp.float32))
        memory_part = wide_dot(lifted, memory_one, NN) / jnp.sum(
            lifted * norm_one, axis=1, keepdims=True
        )
        attn_ref[rows, :] = (gate * memory_part + (1.0 - gate) * dot_part).astype(jnp.bfloat16)
        dot_ref[0, rows, :] = dot_part
        part_ref[0, rows, :] = memory_part
        logsum_ref[0, rows, :] = peak + jnp.log(total)
    lifted_keys = feature_map(k_ref[:PROMPT].astype(jnp.float32))
    high, low = split_two(lifted_keys)
    v = v_ref[:PROMPT]
    memory_new_ref[0] = memory_one + (plain_dot(high, v, TN) + plain_dot(low, v, TN)) / PROMPT
    norm_new_ref[0] = norm_one + jnp.mean(lifted_keys, axis=0, keepdims=True)


def head_block(shape, lead=0):
    zeros = (0,) * (len(shape) - 1 - lead)
    return pl.BlockSpec(shape, lambda h: (0,) * lead + (h,) + zeros)


SMEM_SPEC = pl.BlockSpec(memory_space=pltpu.SMEM)


def attend(heads_all, memory_one, norm_one, offsets, lengths, gate_value):
    heads = heads_all.shape[1]
    f32 = jnp.float32
    row_block = head_block((1, GLEN, HD))
    column = pl.BlockSpec((GLEN, HD), lambda h: (0, h))
    return pl.pallas_call(
        attend_kernel,
        grid=(heads,),
        in_specs=[
            SMEM_SPEC, SMEM_SPEC, SMEM_SPEC,
            head_block((3, 1, GLEN, HD), 1), head_block((1, HD, HD)), head_block((1, 1, HD)),
        ],
        out_specs=[
            column, row_block, row_block, head_block((1, GLEN, 1)),
            head_block((1, HD, HD)), head_block((1, 1, HD)),
        ],
        out_shape=[
            jax.ShapeDtypeStruct((GLEN, heads * HD), jnp.bfloat16),
            jax.ShapeDtypeStruct((heads, GLEN, HD), f32),
            jax.ShapeDtypeStruct((heads, GLEN, HD), f32),
            jax.ShapeDtypeStruct((heads, GLEN, 1), f32),
            jax.ShapeDtypeStruct((heads, HD, HD), f32),
            jax.ShapeDtypeStruct((heads, 1, HD), f32),
        ],
        compiler_params=pltpu.CompilerParams(vmem_limit_bytes=BIG_VMEM),
        cost_estimate=pl.CostEstimate(
            flops=heads * 800_000_000, bytes_accessed=heads * 6_000_000, transcendentals=heads * 1_300_000
        ),
        name="attend",
    )(offsets, lengths, gate_value, heads_all, memory_one, norm_one[:, None, :])


def attend_back_kernel(
    offsets_ref, lengths_ref, gate_ref, qkv_ref, grad_ref, dot_ref, part_ref, logsum_ref,
    memory_ref, norm_ref, out_ref, gate_out_ref, key_sum, value_sum,
):
    head = pl.program_id(0)
    gate = gate_ref[head]
    keep = 1.0 - gate
    scale = HD ** (-0.5)
    q_ref, k_ref, v_ref = qkv_ref.at[0, 0], qkv_ref.at[1, 0], qkv_ref.at[2, 0]
    memory_one = memory_ref[0]
    norm_one = norm_ref[0]
    gate_row = jnp.zeros((1, HD), jnp.float32)
    key_sum[...] = jnp.zeros_like(key_sum)
    value_sum[...] = jnp.zeros_like(value_sum)
    for tile in range(TILES):
        rows = slice(tile * QT, (tile + 1) * QT)
        q = q_ref[rows]
        grad = grad_ref[0, rows, :]
        grad_float = grad.astype(jnp.float32)
        memory_part = part_ref[0, rows, :]
        dot_part = dot_ref[0, rows, :]
        against_dot = jnp.sum(grad_float * dot_part, axis=1, keepdims=True)
        gate_row += jnp.sum(grad_float * (memory_part - dot_part), axis=0, keepdims=True)
        logsum = logsum_ref[0, rows, :]
        ahead, own, seen = tile_scores(tile, q, k_ref, offsets_ref, lengths_ref)
        own = jnp.exp(own - logsum)
        value_sum[rows, :] += plain_dot(own.astype(jnp.bfloat16), grad, TN)
        own = (keep * own * (plain_dot(grad, v_ref[rows], NT) - against_dot)).astype(jnp.bfloat16)
        key_sum[rows, :] += plain_dot(own, q, TN)
        grad_q = plain_dot(own, k_ref[rows], NN)
        if ahead is not None:
            ahead = jnp.exp(ahead - logsum)
            value_sum[:seen, :] += plain_dot(ahead.astype(jnp.bfloat16), grad, TN)
            ahead = (keep * ahead * (plain_dot(grad, v_ref[:seen], NT) - against_dot)).astype(
                jnp.bfloat16
            )
            key_sum[:seen, :] += plain_dot(ahead, q, TN)
            grad_q += plain_dot(ahead, k_ref[:seen], NN)
        q_float = q.astype(jnp.float32)
        lifted = feature_map(q_float)
        inverse = gate / jnp.sum(lifted * norm_one, axis=1, keepdims=True)
        against_memory = jnp.sum(grad_float * memory_part, axis=1, keepdims=True)
        grad_lifted = inverse * (narrow_dot(grad, memory_one, NT) - against_memory * norm_one)
        out_ref[0, rows, :] = (grad_q * scale + grad_lifted * feature_slope(q_float)).astype(
            jnp.bfloat16
        )
    out_ref[1, :, :] = (key_sum[...] * scale).astype(jnp.bfloat16)
    out_ref[2, :, :] = (value_sum[...] * keep).astype(jnp.bfloat16)
    gate_out_ref[0] = gate_row


def attend_back(heads_all, grad_heads, dot_part, memory_part, logsum, memory_one, norm_one, offsets, lengths, gate_value):
    heads = heads_all.shape[1]
    f32 = jnp.float32
    row_block = head_block((1, GLEN, HD))
    return pl.pallas_call(
        attend_back_kernel,
        grid=(heads,),
        in_specs=[
            SMEM_SPEC, SMEM_SPEC, SMEM_SPEC,
            head_block((3, 1, GLEN, HD), 1), row_block, row_block, row_block,
            head_block((1, GLEN, 1)), head_block((1, HD, HD)), head_block((1, 1, HD)),
        ],
        out_specs=[
            pl.BlockSpec((3, GLEN, HD), lambda h: (0, 0, h)),
            head_block((1, 1, HD)),
        ],
        out_shape=[
            jax.ShapeDtypeStruct((3, GLEN, heads * HD), jnp.bfloat16),
            jax.ShapeDtypeStruct((heads, 1, HD), f32),
        ],
        scratch_shapes=[pltpu.VMEM((GLEN, HD), f32), pltpu.VMEM((GLEN, HD), f32)],
        compiler_params=pltpu.CompilerParams(vmem_limit_bytes=BIG_VMEM),
        cost_estimate=pl.CostEstimate(
            flops=heads * 2_000_000_000, bytes_accessed=heads * 6_000_000, transcendentals=heads * 1_300_000
        ),
        name="attend_back",
    )(
        offsets, lengths, gate_value, heads_all, grad_heads, dot_part, memory_part, logsum,
        memory_one, norm_one[:, None, :],
    )


ANY = pl.BlockSpec(memory_space=pl.ANY)
VMEM = pl.BlockSpec(memory_space=pltpu.VMEM)
MESH_ID = pl.DeviceIdType.MESH
HALF = D // 2
AG_CUTS = 4


def remote(source, target, send, receive, device):
    return pltpu.make_async_remote_copy(
        src_ref=source, dst_ref=target, send_sem=send, recv_sem=receive,
        device_id=device, device_id_type=MESH_ID,
    )


def greet(peers):
    barrier = pltpu.get_barrier_semaphore()
    for peer in peers:
        pl.semaphore_signal(barrier, inc=1, device_id=peer, device_id_type=MESH_ID)
    pl.semaphore_wait(barrier, len(peers))


def square(row):
    along_x = (row // 2) * 2 + (1 - lax.rem(row, 2))
    along_y = lax.rem(row + 2, 4)
    across = (along_y // 2) * 2 + (1 - lax.rem(along_y, 2))
    return along_x, along_y, across


class Gather:
    def __init__(self, size, source, land, send, receive, own):
        self.size, self.source, self.land = size, source, land
        self.send, self.receive, self.own = send, receive, own
        self.row, self.col = lax.axis_index("row"), lax.axis_index("col")
        self.piece = source.shape[0]

    @staticmethod
    def semaphores(size):
        return 3 * AG_CUTS if size == 4 else size - 1

    def at(self, cut):
        height = self.piece // AG_CUTS
        return pl.ds(cut * height, height)

    def start(self):
        row, col = self.row, self.col
        if self.size != 4:
            peers = [lax.rem(row + d, self.size) for d in range(1, self.size)]
            greet([(peer, col) for peer in peers])
            self.order = [lax.rem(row + self.size - d, self.size) for d in range(1, self.size)]
            self.copies = [
                remote(self.source, self.land.at[row], self.send.at[i], self.receive.at[i], (peer, col))
                for i, peer in enumerate(peers)
            ]
            for copy in self.copies:
                copy.start()
        else:
            rx, ry, rd = square(row)
            self.order = [rx, ry, rd]
            self.px, self.py = (rx, col), (ry, col)
            greet([self.px, self.py])
            self.to_x, self.to_y, self.onward = {}, {}, []
            for step in range(AG_CUTS):
                for table, peer, base, cut in (
                    (self.to_x, self.px, 0, step),
                    (self.to_y, self.py, AG_CUTS, (step + AG_CUTS // 2) % AG_CUTS),
                ):
                    table[cut] = remote(
                        self.source.at[self.at(cut)], self.land.at[row, self.at(cut)],
                        self.send.at[base + cut], self.receive.at[base + cut], peer,
                    )
                    table[cut].start()
        self.keep = pltpu.make_async_copy(self.source, self.land.at[row], self.own)
        self.keep.start()
        self.keep.wait()

    def forward(self):
        if self.size != 4:
            return
        rx, ry, _ = self.order
        for step in range(AG_CUTS // 2):
            for table, peer, owner, cut in (
                (self.to_x, self.py, rx, step),
                (self.to_y, self.px, ry, step + AG_CUTS // 2),
            ):
                table[cut].wait_recv()
                place = self.land.at[owner, self.at(cut)]
                copy = remote(
                    place, place, self.send.at[2 * AG_CUTS + cut], self.receive.at[2 * AG_CUTS + cut], peer
                )
                copy.start()
                self.onward.append(copy)

    def wait(self, step):
        if self.size != 4:
            self.copies[step].wait_recv()
        elif step == 0:
            for cut in range(AG_CUTS // 2, AG_CUTS):
                self.to_x[cut].wait_recv()
        elif step == 1:
            for cut in range(AG_CUTS // 2):
                self.to_y[cut].wait_recv()
        else:
            for copy in self.onward:
                copy.wait_recv()
        return self.order[step]

    def finish(self):
        if self.size != 4:
            for copy in self.copies:
                copy.wait_send()
            return
        for copy in [*self.to_x.values(), *self.to_y.values(), *self.onward]:
            copy.wait_send()


class Scatter:
    def __init__(self, size, stage, land, total, send, receive):
        self.size, self.stage, self.land, self.total = size, stage, land, total
        self.send, self.receive = send, receive
        self.row, self.col = lax.axis_index("row"), lax.axis_index("col")

    @staticmethod
    def semaphores(size):
        return 6 if size == 4 else size - 1

    @staticmethod
    def stage_shape(size, piece):
        return (3 if size == 4 else size - 1, 2, piece, HALF)

    @staticmethod
    def land_shape(size, piece):
        return (6, piece, HALF) if size == 4 else (size - 1, 2, piece, HALF)

    def copy(self, index, source, peer):
        return remote(source, self.land.at[index], self.send.at[index], self.receive.at[index], peer)

    def run(self, partial, between=None, late=None):
        row, col = self.row, self.col

        def into(slot):
            def store(half, columns, value):
                self.stage[slot, half, :, columns] = value.astype(jnp.bfloat16)

            return store

        def into_total(half, columns, value):
            self.total[half, :, columns] = value

        if self.size != 4:
            peers = [lax.rem(row + d, self.size) for d in range(1, self.size)]
            greet([(peer, col) for peer in peers])
            copies = []
            for slot, peer in enumerate(peers):
                partial(peer, into(slot))
                copies.append(self.copy(slot, self.stage.at[slot], (peer, col)))
                copies[-1].start()
            partial(row, into_total)
            if between is not None:
                between()
            if late is not None:
                late()
            for slot, copy in enumerate(copies):
                copy.wait_recv()
                self.add_total(0, self.land.at[slot, 0])
                self.add_total(1, self.land.at[slot, 1])
            for copy in copies:
                copy.wait_send()
            return
        rx, ry, rd = square(row)
        px, py = (rx, col), (ry, col)
        greet([px, py])
        partial(rd, into(0))
        first = [self.copy(0, self.stage.at[0, 0], px), self.copy(1, self.stage.at[0, 1], py)]
        for copy in first:
            copy.start()
        partial(rx, into(1))
        first.append(self.copy(2, self.stage.at[1, 0], px))
        first[2].start()
        partial(ry, into(2))
        first.append(self.copy(3, self.stage.at[2, 1], py))
        first[3].start()
        if between is not None:
            between()
        first[0].wait_recv()
        self.add_stage(2, 0, self.land.at[0])
        second = [self.copy(4, self.stage.at[2, 0], py)]
        second[0].start()
        first[1].wait_recv()
        self.add_stage(1, 1, self.land.at[1])
        second.append(self.copy(5, self.stage.at[1, 1], px))
        second[1].start()
        partial(row, into_total)
        if late is not None:
            late()
        first[2].wait_recv()
        self.add_total(0, self.land.at[2])
        first[3].wait_recv()
        self.add_total(1, self.land.at[3])
        second[0].wait_recv()
        self.add_total(0, self.land.at[4])
        second[1].wait_recv()
        self.add_total(1, self.land.at[5])
        for copy in first + second:
            copy.wait_send()

    def add_stage(self, slot, half, landed):
        @pl.loop(0, landed.shape[0] // STRIP)
        def _(i):
            rows = pl.ds(pl.multiple_of(i * STRIP, STRIP), STRIP)
            value = self.stage[slot, half, rows, :].astype(jnp.float32) + landed[rows, :].astype(jnp.float32)
            self.stage[slot, half, rows, :] = value.astype(jnp.bfloat16)

    def add_total(self, half, landed):
        @pl.loop(0, landed.shape[0] // STRIP)
        def _(i):
            rows = pl.ds(pl.multiple_of(i * STRIP, STRIP), STRIP)
            self.total[half, rows, :] += landed[rows, :].astype(jnp.float32)


STRIP = 32


def scatter_scratch(size, piece):
    count = Scatter.semaphores(size)
    return [
        pltpu.VMEM(Scatter.stage_shape(size, piece), jnp.bfloat16),
        pltpu.VMEM(Scatter.land_shape(size, piece), jnp.bfloat16),
        pltpu.VMEM((2, piece, HALF), jnp.float32),
        pltpu.SemaphoreType.DMA((count,)),
        pltpu.SemaphoreType.DMA((count,)),
    ]


def gather_scratch(size, piece):
    count = Gather.semaphores(size)
    return [
        pltpu.VMEM((size, piece, D), jnp.bfloat16),
        pltpu.SemaphoreType.DMA((count,)),
        pltpu.SemaphoreType.DMA((count,)),
        pltpu.SemaphoreType.DMA,
    ]


def fetches(pairs, semaphores):
    copies = [pltpu.make_async_copy(a, b, semaphores.at[i]) for i, (a, b) in enumerate(pairs)]
    for copy in copies:
        copy.start()
    return copies


def wait_all(copies):
    for copy in copies:
        copy.wait()


def tiles_of(width, tile):
    def run(body):
        @pl.loop(0, width // tile)
        def _(t):
            body(t, pl.ds(pl.multiple_of(t * tile, tile), tile))

    return run


def comm_params(identity):
    return pltpu.CompilerParams(
        collective_id=identity, has_side_effects=True, vmem_limit_bytes=BIG_VMEM
    )


def bf(*shape):
    return jax.ShapeDtypeStruct(shape, jnp.bfloat16)


def fl(*shape):
    return jax.ShapeDtypeStruct(shape, jnp.float32)


def project_heads(size, normed, w_all):
    piece = normed.shape[0]
    cols, _, depth, width = w_all.shape
    heads = width // HD

    def kernel(x_ref, w_ref, heads_ref, all_ref, land, send, receive, own, w, w_sem, all_sem):
        loads = fetches([(w_ref.at[c], w.at[:, pl.ds(c * depth, depth), :]) for c in range(cols)], w_sem)
        gather = Gather(size, x_ref, land, send, receive, own)
        gather.start()

        def compute(row, slot):
            store = pltpu.make_async_copy(land.at[row], all_ref.at[row], all_sem.at[slot])
            store.start()
            rows = pl.ds(pl.multiple_of(row * piece, piece), piece)

            @pl.loop(0, 3)
            def _(j):
                value = jnp.dot(land[row], w[j], preferred_element_type=jnp.float32).astype(jnp.bfloat16)
                for head in range(heads):
                    heads_ref[j, head, rows, :] = value[:, head * HD : (head + 1) * HD]

            return store

        wait_all(loads)
        stores = [compute(gather.row, 0)]
        gather.forward()
        for step in range(size - 1):
            stores.append(compute(gather.wait(step), step + 1))
        wait_all(stores)
        gather.finish()

    return pl.pallas_call(
        kernel,
        out_shape=[bf(3, heads, GLEN, HD), bf(size, piece, D)],
        in_specs=[ANY, ANY],
        out_specs=[VMEM, ANY],
        scratch_shapes=gather_scratch(size, piece)
        + [
            pltpu.VMEM((3, D, width), jnp.bfloat16),
            pltpu.SemaphoreType.DMA((cols,)),
            pltpu.SemaphoreType.DMA((size,)),
        ],
        compiler_params=comm_params(1),
        cost_estimate=pl.CostEstimate(flops=6 * GLEN * D * width, bytes_accessed=40_000_000, transcendentals=0),
        name="project_heads",
    )(normed, w_all)


def strip_loop(piece, body):
    @pl.loop(0, piece // STRIP)
    def _(i):
        body(pl.ds(pl.multiple_of(i * STRIP, STRIP), STRIP))


def row_mean(first, second):
    return (jnp.sum(first, axis=1, keepdims=True) + jnp.sum(second, axis=1, keepdims=True)) / D


def lanes(first, second):
    lane = lax.broadcasted_iota(jnp.int32, (STRIP, HD), 1)
    return jnp.where(lane == 0, first, jnp.where(lane == 1, second, 0.0))


LEFT, RIGHT = slice(0, HALF), slice(HALF, D)


def branch_out(size, attn, w_all, x, gain):
    piece = GLEN // size
    cols, width, depth = w_all.shape

    def kernel(attn_ref, w_ref, x_ref, gain_ref, middle_ref, normed_ref, stat_ref, stage, land, total, send, receive, w, w_sem):
        loads = fetches([(w_ref.at[c], w.at[:, pl.ds(c * depth, depth)]) for c in range(cols)], w_sem)
        scatter = Scatter(size, stage, land, total, send, receive)
        wait_all(loads)

        def partial(row, store):
            rows = pl.ds(pl.multiple_of(row * piece, piece), piece)
            left = attn_ref[rows, :]
            for half in range(2):
                for t in range(2):
                    columns = slice(half * HALF + t * HALF // 2, half * HALF + (t + 1) * HALF // 2)
                    store(
                        half, slice(t * HALF // 2, (t + 1) * HALF // 2),
                        jnp.dot(left, w[:, columns], preferred_element_type=jnp.float32),
                    )

        scatter.run(partial)

        def finish(rows):
            branch = (total[0, rows, :], total[1, rows, :])
            middle = (
                x_ref[rows, LEFT].astype(jnp.float32) + branch[0],
                x_ref[rows, RIGHT].astype(jnp.float32) + branch[1],
            )
            mean = row_mean(middle[0] * middle[0], middle[1] * middle[1])
            inverse = lax.rsqrt(mean + EPSILON)
            for part, columns in zip(middle, (LEFT, RIGHT)):
                middle_ref[rows, columns] = part
                normed_ref[rows, columns] = (part * inverse * gain_ref[:, columns]).astype(jnp.bfloat16)
            stat_ref[rows, :] = lanes(row_mean(branch[0] * branch[0], branch[1] * branch[1]), mean)

        strip_loop(piece, finish)

    return pl.pallas_call(
        kernel,
        out_shape=[fl(piece, D), bf(piece, D), fl(piece, HD)],
        in_specs=[VMEM, ANY, VMEM, VMEM],
        out_specs=[VMEM, VMEM, VMEM],
        scratch_shapes=scatter_scratch(size, piece)
        + [pltpu.VMEM((width, D), jnp.bfloat16), pltpu.SemaphoreType.DMA((cols,))],
        compiler_params=comm_params(2),
        cost_estimate=pl.CostEstimate(flops=2 * GLEN * D * width, bytes_accessed=40_000_000, transcendentals=0),
        name="branch_out",
    )(attn, w_all, x, gain)


def feed_forward(size, normed, w_gu, w_down, cot):
    piece = normed.shape[0]
    cols, _, depth, wide = w_gu.shape
    tile = min(wide, 512)

    def kernel(
        x_ref, gu_ref, down_ref, cot_ref, hidden_ref, grad_ref, all_ref,
        land, send, receive, own, gu, down, cot_all, back, stage, gu_sem, down_sem, cot_sem, out_sem, all_sem,
    ):
        down_loads = fetches(
            [(down_ref.at[c], down.at[:, pl.ds(c * depth, depth)]) for c in range(cols)], down_sem
        )
        cot_load = pltpu.make_async_copy(cot_ref, cot_all, cot_sem)
        cot_load.start()
        gu_loads = fetches([(gu_ref.at[c], gu.at[:, pl.ds(c * depth, depth), :]) for c in range(cols)], gu_sem)
        gather = Gather(size, x_ref, land, send, receive, own)
        gather.start()
        wait_all(down_loads)
        cot_load.wait()

        def backward(row):
            @tiles_of(wide, tile)
            def _(t, columns):
                back[row, :, columns] = plain_dot(cot_all[row], down[columns, :], NT).astype(jnp.bfloat16)

        def moves(row, slot, columns):
            rows = pl.ds(pl.multiple_of(row * piece, piece), piece)
            return [
                pltpu.make_async_copy(stage.at[slot, 0], hidden_ref.at[rows, columns], out_sem.at[slot, 0]),
                pltpu.make_async_copy(stage.at[slot, 1], grad_ref.at[0, rows, columns], out_sem.at[slot, 1]),
                pltpu.make_async_copy(stage.at[slot, 2], grad_ref.at[1, rows, columns], out_sem.at[slot, 2]),
            ]

        count = wide // tile

        def compute(row, first):
            pltpu.make_async_copy(land.at[row], all_ref.at[row], all_sem).start()

            @pl.loop(0, count)
            def _(t):
                columns = pl.ds(pl.multiple_of(t * tile, tile), tile)
                slot = lax.rem(t, 2)
                x = land[row]
                gate_pre = jnp.dot(x, gu[0, :, columns], preferred_element_type=jnp.float32)
                up_pre = jnp.dot(x, gu[1, :, columns], preferred_element_type=jnp.float32)
                sigmoid = jax.nn.sigmoid(gate_pre)
                silu = gate_pre * sigmoid
                grad_hidden = back[row, :, columns].astype(jnp.float32)

                @pl.when(t >= 2)
                def _():
                    wait_all(moves(row, slot, columns))

                stage[slot, 0] = (silu * up_pre).astype(jnp.bfloat16)
                stage[slot, 1] = (grad_hidden * up_pre * (sigmoid + silu * (1.0 - sigmoid))).astype(jnp.bfloat16)
                stage[slot, 2] = (grad_hidden * silu).astype(jnp.bfloat16)
                for move in moves(row, slot, columns):
                    move.start()

            for slot in range(min(2, count)):
                wait_all(moves(row, slot, pl.ds(slot * tile, tile)))
            pltpu.make_async_copy(land.at[row], all_ref.at[row], all_sem).wait()

        backward(gather.row)
        gather.forward()
        for step in range(size - 1):
            backward(gather.order[step])
        wait_all(gu_loads)
        compute(gather.row, True)
        for step in range(size - 1):
            compute(gather.wait(step), False)
        gather.finish()

    return pl.pallas_call(
        kernel,
        out_shape=[bf(GLEN, wide), bf(2, GLEN, wide), bf(size, piece, D)],
        in_specs=[ANY, ANY, ANY, ANY],
        out_specs=[ANY, ANY, ANY],
        scratch_shapes=gather_scratch(size, piece)
        + [
            pltpu.VMEM((2, D, wide), jnp.bfloat16),
            pltpu.VMEM((wide, D), jnp.bfloat16),
            pltpu.VMEM((size, piece, D), jnp.bfloat16),
            pltpu.VMEM((size, piece, wide), jnp.bfloat16),
            pltpu.VMEM((2, 3, piece, tile), jnp.bfloat16),
            pltpu.SemaphoreType.DMA((cols,)),
            pltpu.SemaphoreType.DMA((cols,)),
            pltpu.SemaphoreType.DMA,
            pltpu.SemaphoreType.DMA((2, 3)),
            pltpu.SemaphoreType.DMA,
        ],
        compiler_params=comm_params(3),
        cost_estimate=pl.CostEstimate(flops=6 * GLEN * D * wide, bytes_accessed=70_000_000, transcendentals=GLEN * wide),
        name="feed_forward",
    )(normed, w_gu, w_down, cot.reshape(size, piece, D))


def norm_back(rows, total, stream, inverse, gain_ref, base, store, gain_sum):
    u = [total[half, rows, :] * gain_ref[:, columns] for half, columns in enumerate((LEFT, RIGHT))]
    inner = row_mean(u[0] * stream[0], u[1] * stream[1]) * inverse * inverse * inverse
    for half, columns in enumerate((LEFT, RIGHT)):
        store(columns, base[half] + inverse * u[half] - stream[half] * inner)
        gain_sum[:, columns] += jnp.sum(total[half, rows, :] * stream[half] * inverse, axis=0, keepdims=True)


def middle_back(size, grads, w_gu, middle, cot, gain):
    piece = middle.shape[0]
    cols, _, depth, wide = w_gu.shape
    tile = 512

    def kernel(
        g_ref, gu_ref, middle_ref, cot_ref, gain_ref, grad_ref, low_ref, gain_sum,
        stage, land, total, send, receive, gu, g, gu_sem, g_sem,
    ):
        loads = fetches([(gu_ref.at[c], gu.at[:, pl.ds(c * depth, depth), :]) for c in range(cols)], gu_sem)
        scatter = Scatter(size, stage, land, total, send, receive)
        g_loads = fetches([(g_ref.at[j], g.at[j]) for j in range(2)], g_sem)
        wait_all(g_loads)
        wait_all(loads)
        gain_sum[...] = jnp.zeros_like(gain_sum)

        def partial(row, store):
            rows = pl.ds(pl.multiple_of(row * piece, piece), piece)
            for half in range(2):
                @pl.loop(0, HALF // tile)
                def _(t):
                    columns = pl.ds(pl.multiple_of(t * tile, tile), tile)
                    depth_rows = pl.ds(pl.multiple_of(half * HALF + t * tile, tile), tile)
                    value = plain_dot(g[0, rows, :], gu[0, depth_rows, :], NT)
                    value += plain_dot(g[1, rows, :], gu[1, depth_rows, :], NT)
                    store(half, columns, value)

        scatter.run(partial)

        def finish(rows):
            stream = [middle_ref[rows, columns] for columns in (LEFT, RIGHT)]
            base = [cot_ref[rows, columns].astype(jnp.float32) for columns in (LEFT, RIGHT)]
            inverse = lax.rsqrt(row_mean(stream[0] * stream[0], stream[1] * stream[1]) + EPSILON)

            def store(columns, value):
                grad_ref[rows, columns] = value
                low_ref[rows, columns] = value.astype(jnp.bfloat16)

            norm_back(rows, total, stream, inverse, gain_ref, base, store, gain_sum)

        strip_loop(piece, finish)

    return pl.pallas_call(
        kernel,
        out_shape=[fl(piece, D), bf(piece, D), fl(1, D)],
        in_specs=[ANY, ANY, VMEM, VMEM, VMEM],
        out_specs=[VMEM, VMEM, VMEM],
        scratch_shapes=scatter_scratch(size, piece)
        + [
            pltpu.VMEM((2, D, wide), jnp.bfloat16),
            pltpu.VMEM((2, GLEN, wide), jnp.bfloat16),
            pltpu.SemaphoreType.DMA((cols,)),
            pltpu.SemaphoreType.DMA((2,)),
        ],
        compiler_params=comm_params(4),
        cost_estimate=pl.CostEstimate(flops=4 * GLEN * D * wide, bytes_accessed=60_000_000, transcendentals=0),
        name="middle_back",
    )(grads, w_gu, middle, cot, gain)


def blocked_store(ref, rows, depth, columns, value):
    for i in range(value.shape[1] // depth):
        ref[columns.start // depth + i, rows, :] = value[:, i * depth : (i + 1) * depth]


def ffn_out(size, hidden, w_down, middle):
    piece = middle.shape[0]
    cols, wide, depth = w_down.shape
    tile = 512

    def kernel(h_ref, w_ref, middle_ref, out_ref, stat_ref, stage, land, total, send, receive, w, w_sem):
        loads = fetches([(w_ref.at[c], w.at[:, pl.ds(c * depth, depth)]) for c in range(cols)], w_sem)
        scatter = Scatter(size, stage, land, total, send, receive)
        wait_all(loads)

        def partial(row, store):
            rows = pl.ds(pl.multiple_of(row * piece, piece), piece)
            for half in range(2):
                @pl.loop(0, HALF // tile)
                def _(t):
                    columns = pl.ds(pl.multiple_of(t * tile, tile), tile)
                    whole = pl.ds(pl.multiple_of(half * HALF + t * tile, tile), tile)
                    store(half, columns, jnp.dot(h_ref[rows, :], w[:, whole], preferred_element_type=jnp.float32))

        scatter.run(partial)

        def finish(rows):
            ffn = [total[half, rows, :] for half in range(2)]
            result = [middle_ref[rows, columns] + ffn[half] for half, columns in enumerate((LEFT, RIGHT))]
            for half, columns in enumerate((LEFT, RIGHT)):
                blocked_store(out_ref, rows, depth, columns, result[half].astype(jnp.bfloat16))
            stat_ref[rows, :] = lanes(
                row_mean(ffn[0] * ffn[0], ffn[1] * ffn[1]),
                row_mean(result[0] * result[0], result[1] * result[1]),
            )

        strip_loop(piece, finish)

    return pl.pallas_call(
        kernel,
        out_shape=[bf(cols, piece, depth), fl(piece, HD)],
        in_specs=[VMEM, ANY, VMEM],
        out_specs=[VMEM, VMEM],
        scratch_shapes=scatter_scratch(size, piece)
        + [pltpu.VMEM((wide, D), jnp.bfloat16), pltpu.SemaphoreType.DMA((cols,))],
        compiler_params=comm_params(5),
        cost_estimate=pl.CostEstimate(flops=2 * GLEN * D * wide, bytes_accessed=50_000_000, transcendentals=0),
        name="ffn_out",
    )(hidden, w_down, middle)


def branch_back(size, low, w_all):
    piece = low.shape[0]
    cols, width, depth = w_all.shape
    heads = width // HD

    def kernel(x_ref, w_ref, heads_ref, all_ref, land, send, receive, own, w, w_sem, all_sem):
        loads = fetches([(w_ref.at[c], w.at[:, pl.ds(c * depth, depth)]) for c in range(cols)], w_sem)
        gather = Gather(size, x_ref, land, send, receive, own)
        gather.start()

        def compute(row, slot):
            store = pltpu.make_async_copy(land.at[row], all_ref.at[row], all_sem.at[slot])
            store.start()
            rows = pl.ds(pl.multiple_of(row * piece, piece), piece)
            value = plain_dot(land[row], w[...], NT).astype(jnp.bfloat16)
            for head in range(heads):
                heads_ref[head, rows, :] = value[:, head * HD : (head + 1) * HD]
            return store

        wait_all(loads)
        stores = [compute(gather.row, 0)]
        gather.forward()
        for step in range(size - 1):
            stores.append(compute(gather.wait(step), step + 1))
        wait_all(stores)
        gather.finish()

    return pl.pallas_call(
        kernel,
        out_shape=[bf(heads, GLEN, HD), bf(size, piece, D)],
        in_specs=[ANY, ANY],
        out_specs=[VMEM, ANY],
        scratch_shapes=gather_scratch(size, piece)
        + [
            pltpu.VMEM((width, D), jnp.bfloat16),
            pltpu.SemaphoreType.DMA((cols,)),
            pltpu.SemaphoreType.DMA((size,)),
        ],
        compiler_params=comm_params(6),
        cost_estimate=pl.CostEstimate(flops=2 * GLEN * D * width, bytes_accessed=40_000_000, transcendentals=0),
        name="branch_back",
    )(low, w_all)


def stream_back(size, grads, w_all, x, grad_middle, gain):
    piece = x.shape[0]
    cols, _, depth, width = w_all.shape
    tile = 512

    def kernel(
        g_ref, w_ref, x_ref, middle_ref, gain_ref, out_ref, gain_sum,
        stage, land, total, send, receive, w, w_sem,
    ):
        loads = fetches([(w_ref.at[c], w.at[:, pl.ds(c * depth, depth), :]) for c in range(cols)], w_sem)
        scatter = Scatter(size, stage, land, total, send, receive)
        wait_all(loads)
        gain_sum[...] = jnp.zeros_like(gain_sum)

        def partial(row, store):
            rows = pl.ds(pl.multiple_of(row * piece, piece), piece)
            for half in range(2):
                @pl.loop(0, HALF // tile)
                def _(t):
                    columns = pl.ds(pl.multiple_of(t * tile, tile), tile)
                    depth_rows = pl.ds(pl.multiple_of(half * HALF + t * tile, tile), tile)
                    value = plain_dot(g_ref[0, rows, :], w[0, depth_rows, :], NT)
                    for j in (1, 2):
                        value += plain_dot(g_ref[j, rows, :], w[j, depth_rows, :], NT)
                    store(half, columns, value)

        scatter.run(partial)

        def finish(rows):
            stream = [x_ref[rows, columns].astype(jnp.float32) for columns in (LEFT, RIGHT)]
            base = [middle_ref[rows, columns] for columns in (LEFT, RIGHT)]
            inverse = lax.rsqrt(row_mean(stream[0] * stream[0], stream[1] * stream[1]) + EPSILON)

            def store(columns, value):
                blocked_store(out_ref, rows, depth, columns, value.astype(jnp.bfloat16))

            norm_back(rows, total, stream, inverse, gain_ref, base, store, gain_sum)

        strip_loop(piece, finish)

    return pl.pallas_call(
        kernel,
        out_shape=[bf(cols, piece, depth), fl(1, D)],
        in_specs=[VMEM, ANY, VMEM, VMEM, VMEM],
        out_specs=[VMEM, VMEM],
        scratch_shapes=scatter_scratch(size, piece)
        + [pltpu.VMEM((3, D, width), jnp.bfloat16), pltpu.SemaphoreType.DMA((cols,))],
        compiler_params=comm_params(7),
        cost_estimate=pl.CostEstimate(flops=6 * GLEN * D * width, bytes_accessed=50_000_000, transcendentals=0),
        name="stream_back",
    )(grads, w_all, x, grad_middle, gain)


def unblock_kernel(x_ref, gain_ref, tokens_ref, normed_ref):
    cols, rows, depth = x_ref.shape
    total = jnp.zeros((rows, 1), jnp.float32)
    for c in range(cols):
        part = x_ref[c].astype(jnp.float32)
        tokens_ref[:, c * depth : (c + 1) * depth] = x_ref[c]
        total += jnp.sum(part * part, axis=1, keepdims=True)
    inverse = lax.rsqrt(total / D + EPSILON)
    for c in range(cols):
        columns = slice(c * depth, (c + 1) * depth)
        normed_ref[:, columns] = (
            x_ref[c].astype(jnp.float32) * inverse * gain_ref[:, columns]
        ).astype(jnp.bfloat16)


def enter(blocks, gain):
    cols, piece, depth = blocks.shape
    rows = piece // 4
    return pl.pallas_call(
        unblock_kernel,
        grid=(4,),
        in_specs=[
            pl.BlockSpec((cols, rows, depth), lambda i: (0, i, 0)),
            pl.BlockSpec((1, D), lambda i: (0, 0)),
        ],
        out_specs=[pl.BlockSpec((rows, D), lambda i: (i, 0))] * 2,
        out_shape=[bf(piece, D), bf(piece, D)],
        cost_estimate=pl.CostEstimate(flops=6 * piece * D, bytes_accessed=6 * piece * D, transcendentals=0),
        name="enter",
    )(blocks, gain)


def to_blocks(block):
    row_size = lax.axis_size("row")
    features = block.shape[1]
    groups = block.shape[0] // GLEN
    piece = GLEN // row_size
    split = block.reshape(groups, row_size, piece, features)
    split = lax.all_to_all(split, "row", split_axis=1, concat_axis=0, tiled=True)
    split = split.reshape(row_size * groups, piece, features)
    return lax.all_to_all(split, "col", split_axis=0, concat_axis=0, tiled=True)


def from_blocks(blocks):
    row_size = lax.axis_size("row")
    cols, piece, features = blocks.shape
    groups = cols // row_size
    split = lax.all_to_all(blocks, "col", split_axis=0, concat_axis=0, tiled=True)
    split = split.reshape(row_size, groups, piece, features)
    split = lax.all_to_all(split, "row", split_axis=0, concat_axis=2, tiled=True)
    return split.reshape(groups * GLEN, features)


def tokens_contract(left, right):
    return lax.dot_general(left, right, (TN, ((), ())), preferred_element_type=jnp.float32)


def over_col(partial, axis):
    return lax.psum_scatter(
        partial.astype(jnp.bfloat16), "col", scatter_dimension=axis, tiled=True
    ).astype(jnp.float32)


def local(
    stream_in,
    w_qkv,
    w_out,
    w_gate_up,
    w_down,
    gain_attn,
    gain_ffn,
    gate_logit,
    memory,
    memory_norm,
    offsets,
    lengths,
    cotangent,
):
    head_here = memory.shape[1]
    size = lax.axis_size("row")
    row_index = lax.axis_index("row")
    col_index = lax.axis_index("col")
    gains = lax.all_gather(jnp.stack([gain_attn, gain_ffn]), "col", axis=1, tiled=True)
    gain_in, gain_mid = gains[0:1], gains[1:2]
    all_qkv, all_out, all_gu, all_down = (
        lax.all_gather(w, "col", axis=0, tiled=False) for w in (w_qkv, w_out, w_gate_up, w_down)
    )
    gate_value = jax.nn.sigmoid(gate_logit)
    group = (memory[0], memory_norm[0], offsets[0], lengths[0], gate_value)
    stream, normed_in = enter(to_blocks(stream_in), gain_in)
    cot, _ = enter(to_blocks(cotangent), gain_in)
    all_cot = lax.all_gather(cot, "row", axis=0, tiled=True)
    heads_all, all_in = project_heads(size, normed_in, all_qkv)
    attn, dot_part, memory_part, logsum, memory_new, norm_new = attend(heads_all, *group)
    middle, normed_ffn, stat_branch = branch_out(size, attn, all_out, stream, gain_mid)
    hidden, grad_gu, all_ffn = feed_forward(size, normed_ffn, all_gu, all_down, all_cot)
    grad_middle, low_branch, part_gain_ffn = middle_back(size, grad_gu, all_gu, middle, cot, gain_mid)
    blocks_out, stat_ffn = ffn_out(size, hidden, all_down, middle)
    grad_heads, all_branch = branch_back(size, low_branch, all_out)
    grads_qkv, gate_sums = attend_back(
        heads_all, grad_heads, dot_part, memory_part, logsum, *group
    )
    blocks_grad, part_gain_attn = stream_back(size, grads_qkv, all_qkv, stream, grad_middle, gain_in)
    stream_out = from_blocks(blocks_out)
    stream_grad = from_blocks(blocks_grad).astype(jnp.float32)

    def flat(pieces):
        return pieces.reshape(GLEN, D)

    grad_down = over_col(tokens_contract(hidden, all_cot), 1)
    grad_gate_up = over_col(
        jnp.einsum("td,jto->jdo", flat(all_ffn), grad_gu, preferred_element_type=jnp.float32), 1
    )
    grad_out = over_col(tokens_contract(attn, flat(all_branch)), 1)
    grad_qkv = over_col(
        jnp.einsum("td,jto->jdo", flat(all_in), grads_qkv, preferred_element_type=jnp.float32), 1
    )
    logit_part = gate_value * (1.0 - gate_value) * jnp.sum(gate_sums, axis=(1, 2))
    logit_slots = lax.dynamic_update_slice(
        jnp.zeros((size * head_here,), jnp.float32), logit_part, (row_index * head_here,)
    )
    small = lax.psum(
        jnp.concatenate([part_gain_attn[0], part_gain_ffn[0], logit_slots]), ("row", "col")
    )
    features_here = gain_attn.shape[0]
    grad_gain_attn = lax.dynamic_slice(small, (col_index * features_here,), (features_here,))
    grad_gain_ffn = lax.dynamic_slice(small, (D + col_index * features_here,), (features_here,))
    grad_gate_logit = lax.dynamic_slice(small, (2 * D + row_index * head_here,), (head_here,))
    rms_here = jnp.sqrt(jnp.concatenate([stat_branch[:, :2], stat_ffn[:, :2]], axis=1).T)
    rms_all = lax.all_gather(rms_here, ("col", "row"), axis=1, tiled=True)
    rows_here = stream_in.shape[0]
    rms_table = lax.dynamic_slice(rms_all, (0, row_index * rows_here), (4, rows_here))
    return (
        stream_out,
        stream_grad,
        grad_qkv,
        grad_out,
        grad_gate_up,
        grad_down,
        grad_gain_attn,
        grad_gain_ffn,
        grad_gate_logit,
        memory_new[None],
        norm_new.reshape(1, head_here, HD),
        rms_table,
    )


def solution(mesh):
    return jax.shard_map(
        local,
        mesh=mesh,
        in_specs=(
            P("row", "col"),
            P(None, "col", "row"),
            P("row", "col"),
            P(None, "col", "row"),
            P("row", "col"),
            P("col"),
            P("col"),
            P("row"),
            P("col", "row", None, None),
            P("col", "row", None),
            P("col", None),
            P("col", None),
            P("row", "col"),
        ),
        out_specs=(
            P("row", "col"),
            P("row", "col"),
            P(None, "col", "row"),
            P("row", "col"),
            P(None, "col", "row"),
            P("row", "col"),
            P("col"),
            P("col"),
            P("row"),
            P("col", "row", None, None),
            P("col", "row", None),
            P(None, "row"),
        ),
        check_vma=False,
    )
```

time: 1670 us -> 1150 us (0.69)
  waiting for transfers between devices: 721 us -> 171 us
  Pallas kernels: 0 us -> 518 us
  matrix products: 349 us -> 75.6 us
  other arithmetic: 131 us -> 6.91 us
  local copies, waits for them, and re-layouts: 90.1 us -> 17.7 us
  blocking collectives: 319 us -> 295 us
    pallas_call x0 -> x11, Pallas kernels: none -> 518 us  [the longest x1 76.4 us: project_heads(): pl.pallas_call(kernel, out_shape=[bf(3, heads, GLEN, HD), bf(size, piece,...]
    all_gather x8 -> x5, waiting for transfers between devices: 399 us -> 117 us  [the longest x4 116 us: local(): lax.all_gather(w, 'col', axis=0, tiled=False)]
    dot_general x34 -> x4, matrix products: 349 us -> 75.6 us  [the longest x1 33.3 us: local(): jnp.einsum('td,jto->jdo', flat(all_ffn), grad_gu, preferred_element_type=...]
    reduce_scatter x8 -> x4, waiting for transfers between devices: 270 us -> 0.01 us  [over_col(): lax.psum_scatter(partial.astype(jnp.bfloat16), 'col', scatter_dimension=a...]
    unnamed x5 -> x0, other arithmetic: 69.1 us -> none
    unnamed x194 -> x24, local copies, waits for them, and re-layouts: 39.5 us -> 9 us
    convert_element_type x10 -> x3, other arithmetic: 32.7 us -> 4.76 us  [the longest x2 4.48 us: over_col(): return lax.psum_scatter(partial.astype(jnp.bfloat16), 'col', scatter_dime...]
    reduce_sum x9 -> x1, other arithmetic: 20.2 us -> 0.14 us  [local(): jnp.sum(gate_sums, axis=(1, 2))]
  transfers between devices with their start and end apart: 21 -> 14, of which waited for: 14 -> 3; matrix products, arithmetic and copies ran while one was open for 22% -> 8% of each run, Pallas kernels for 0% -> 28%
where the time goes in v2:
time: 1150 us; the launch traced here: 1130 us
  Pallas kernels  518 us (45%)
  blocking collectives  295 us (26%)
  waiting for transfers between devices  171 us (15%)
  matrix products  75.6 us (7%)
  starting transfers between devices  33.6 us (3%)
  local copies, waits for them, and re-layouts  17.7 us (2%)
  between operations  14.3 us (1%)
    all_gather x4, waiting for transfers between devices, local(): lax.all_gather(w, 'col', axis=0, tiled=False)  116 us
    pallas_call x1, Pallas kernels, project_heads(): pl.pallas_call(kernel, out_shape=[bf(3, heads, GLEN, HD), bf(size, piece,...  76.4 us
    pallas_call x1, Pallas kernels, middle_back(): pl.pallas_call(kernel, out_shape=[fl(piece, D), bf(piece, D), fl(1, D)],...  75.5 us
    pallas_call x1, Pallas kernels, feed_forward(): pl.pallas_call(kernel, out_shape=[bf(GLEN, wide), bf(2, GLEN, wide), bf(s...  71.5 us
    all_gather x1, blocking collectives, local(): lax.all_gather(jnp.stack([gain_attn, gain_ffn]), 'col', axis=1, tiled=True)  70.8 us
    pallas_call x1, Pallas kernels, stream_back(): pl.pallas_call(kernel, out_shape=[bf(cols, piece, depth), fl(1, D)], in_s...  66.3 us
    all_to_all x1, blocking collectives, from_blocks(): lax.all_to_all(blocks, 'col', split_axis=0, concat_axis=0, tiled=True)  65.1 us
    pallas_call x1, Pallas kernels, ffn_out(): pl.pallas_call(kernel, out_shape=[bf(cols, piece, depth), fl(piece, HD)],...  64.2 us
  transfers between devices with their start and end apart: 14, of which 3 were waited for; matrix products, arithmetic and copies ran while one was open for 8% of the time, Pallas kernels for 28%

profile of v2, /device:TPU:27, one launch (start us, length us, event | category | flops | bytes accessed | tf_op | source)
XLA Modules:
  0.0 1132.3 jit_solution(12026913758033616611)
XLA Ops:
  7.2 0.7 all-gather.12.cloned.1.call-update
  7.9 2.7 copy.35
  10.6 4.5 all-to-all-start.2
  15.1 0.7 all-gather.14.cloned.1.call-update
  15.9 17.7 %all-to-all-done.2 = bf16[2,4,384,256]{3,2,0,1:T(8,128)(2,1)} async-done(((bf16[2,4,384,256]{3,2,0,1:T(8,128)(2,1)}), bf16[2,4,384,256]{3,2,0,1:T(8,128)(2,1)}, u32[]{:S(2)}, u32[]{:S(2)}) %all-to-all-start.2) | async-done | bytes 1572896 | tf_op jit(solution)/shard_map/all_to_all | solution.py:993
  33.6 6.4 all-to-all-start.3
  40.0 70.8 %all_gather.33 = f32[2,2048]{1,0:T(2,128)S(1)} all-gather(f32[2,256]{1,0:T(2,128)S(1)} %pad_maximum_fusion.1), channel_id=1, replica_groups=mesh['row'=4,'col'=8] {'col'}, dimensions={1}, use_global_device_ids=true | all-gather | bytes 18432 | tf_op jit(solution)/shard_map/all_gather | solution.py:1037
  110.8 0.6 fusion.4
  111.4 1.1 copy-done
  112.6 4.1 enter.3
  117.3 0.5 all-gather.16.cloned.1.call-update
  118.0 22.1 %all_to_all.74 = bf16[2,4,384,256]{3,2,0,1:T(8,128)(2,1)} all-to-all(bf16[2,4,384,256]{3,2,0,1:T(8,128)(2,1)S(1)} %copy.34), channel_id=1, replica_groups=mesh['row'=4,'col'=8] {'row'}, dimensions={1} | all-to-all | bytes 3145728 | tf_op jit(solution)/shard_map/all_to_all | solution.py:993
  140.1 7.6 all-to-all-start.1
  147.6 0.5 add_divide_fusion.gate_ref
  148.2 34.6 %all-to-all-done.1.x_ref = bf16[8,384,256]{2,1,0:T(8,128)(2,1)S(1)} async-done(((bf16[8,384,256]{2,1,0:T(8,128)(2,1)}), bf16[8,384,256]{2,1,0:T(8,128)(2,1)S(1)}, u32[]{:S(2)}, u32[]{:S(2)}) %all-to-all-start.1) | async-done | bytes 1572896 | tf_op jit(solution)/shard_map/all_to_all | solution.py:995
  182.8 1.1 copy-done.1
  183.9 4.1 enter.2
  188.0 76.4 %project_heads.1 = (bf16[3,4,1536,128]{3,2,1,0:T(8,128)(2,1)}, bf16[4,384,2048]{2,1,0:T(8,128)(2,1)}) custom-call(bf16[384,2048]{1,0:T(8,128)(2,1)} %get-tuple-element.40.x_ref, bf16[8,3,256,512]{3,2,1,0:T(8,128)(2,1)} %bitcast.78), custom_call_target="tpu_custom_call" | custom-call | flops 9663676416 | bytes 40000000 | tf_op jit(solution)/shard_map/project_heads/pallas_call | solution.py:557
  264.4 16.6 %attend.1 = (bf16[1536,512]{1,0:T(8,128)(2,1)}, f32[4,1536,128]{2,1,0:T(8,128)}, f32[4,1536,128]{2,1,0:T(8,128)}, f32[4,1536,1]{2,1,0:T(8,128)}, f32[4,128,128]{2,1,0:T(8,128)}, /*index=5*/f32[4,1,128]{2,1,0:T(1,128)}) custom-call(s32[4]{0:T(128)} %bitcast.87, s32[4]{0:T(128)} %bitcast.89, f32[4]{0:T(128)} %add_divide_fusion.gate_ref, ...), custom_call_target="tpu_custom_call" | custom-call | flops 3200000000 | bytes 24000000 | tf_op jit(solution)/shard_map/attend/pallas_call | solution.py:138
  281.1 61.1 %branch_out.1 = (f32[384,2048]{1,0:T(8,128)}, bf16[384,2048]{1,0:T(8,128)(2,1)}, f32[384,128]{1,0:T(8,128)}) custom-call(bf16[1536,512]{1,0:T(8,128)(2,1)} %get-tuple-element.42.attn_ref, bf16[8,512,256]{2,1,0:T(8,128)(2,1)} %bitcast.81, bf16[384,2048]{1,0:T(8,128)(2,1)} %get-tuple-element.43.x_ref, f32[1,2048]{1,0:T(1,128)} %get-tuple-element.94.gain_ref), custom_call_target="tpu_custom_call" | custom-call | flops 3221225472 | bytes 40000000 | tf_op jit(solution)/shard_map/branch_out/pallas_call | solution.py:629
  342.3 116.4 %all-gather.16.cloned.1.call-done = bf16[16,256,2048]{2,1,0:T(8,128)(2,1)} async-done(((bf16[2,256,2048]{2,1,0:T(8,128)(2,1)}), bf16[16,256,2048]{2,1,0:T(8,128)(2,1)}) %all-gather.16.cloned.1.call-update) | async-done | bytes 16777232 | tf_op jit(solution)/shard_map/all_gather | solution.py:1040
  458.7 71.5 %feed_forward.1 = (bf16[1536,2048]{1,0:T(8,128)(2,1)}, bf16[2,1536,2048]{2,1,0:T(8,128)(2,1)}, bf16[4,384,2048]{2,1,0:T(8,128)(2,1)}) custom-call(bf16[384,2048]{1,0:T(8,128)(2,1)} %get-tuple-element.44.x_ref, bf16[8,2,256,2048]{3,2,1,0:T(8,128)(2,1)} %bitcast.74, bf16[8,2048,256]{2,1,0:T(8,128)(2,1)} %bitcast.76, bf16[4,384,2048]{2,1,0:T(8,128)(2,1)} %bitcast.80), custom_call_target="tpu_custom_call" | custom-call | flops 38654705664 | bytes 70000000 | tf_op jit(solution)/shard_map/feed_forward/pallas_call | solution.py:715
  530.3 75.5 %middle_back.1 = (f32[384,2048]{1,0:T(8,128)}, bf16[384,2048]{1,0:T(8,128)(2,1)}, f32[1,2048]{1,0:T(1,128)}) custom-call(bf16[2,1536,2048]{2,1,0:T(8,128)(2,1)} %get-tuple-element.49.g_ref, bf16[8,2,256,2048]{3,2,1,0:T(8,128)(2,1)} %bitcast.75, f32[384,2048]{1,0:T(8,128)} %get-tuple-element.47.middle_ref, bf16[384,2048]{1,0:T(8,128)(2,1)} %get-tuple-element.45.cot_ref, ...), custom_call_target="tpu_custom_call" | custom-call | flops 25769803776 | bytes 60000000 | tf_op jit(solution)/shard_map/middle_back/pallas_call | solution.py:789
  605.7 53.5 %branch_back.1 = (bf16[4,1536,128]{2,1,0:T(8,128)(2,1)}, bf16[4,384,2048]{2,1,0:T(8,128)(2,1)}) custom-call(bf16[384,2048]{1,0:T(8,128)(2,1)} %get-tuple-element.50.x_ref, bf16[8,512,256]{2,1,0:T(8,128)(2,1)} %bitcast.82), custom_call_target="tpu_custom_call" | custom-call | flops 3221225472 | bytes 40000000 | tf_op jit(solution)/shard_map/branch_back/pallas_call | solution.py:885
  659.3 7.6 convolution_convert_fusion.1
  666.9 24.7 %attend_back.1 = (bf16[3,1536,512]{2,1,0:T(8,128)(2,1)}, f32[4,1,128]{2,1,0:T(1,128)}) custom-call(s32[4]{0:T(128)} %bitcast.88, s32[4]{0:T(128)} %bitcast.90, f32[4]{0:T(128)} %add_divide_fusion.gate_ref, bf16[3,4,1536,128]{3,2,1,0:T(8,128)(2,1)} %get-tuple-element.41.qkv_ref, bf16[4,1536,128]{2,1,0:T(8,128)(2,1)} %get-tuple-element.51.grad_ref, ...), custom_call_target="tpu_custom_call" | custom-call | flops 8000000000 | bytes 24000000 | tf_op jit(solution)/shard_map/attend_back/pallas_call | solution.py:220
  691.7 15.3 %convert_bitcast_fusion.1 = bf16[3,2048,512]{1,2,0:T(8,128)(2,1)} fusion(bf16[3,1536,512]{2,1,0:T(8,128)(2,1)} %get-tuple-element.55.g_ref, bf16[1536,2048,1]{1,0,2:T(8,128)(2,1)} %bitcast.91), kind=kOutput, calls=%fused_computation.2 | convolution fusion | flops 9666822144 | bytes 17301504 | tf_op jit(solution)/shard_map/td,jto->jdo/dot_general | solution.py:1070
  707.1 19.4 %convolution_convert_fusion = bf16[2048,2048]{1,0:T(8,128)(2,1)} fusion(bf16[1536,2048]{1,0:T(8,128)(2,1)} %get-tuple-element.46.h_ref, bf16[1536,2048]{1,0:T(8,128)(2,1)} %all-gather.10.cloned.1.call-done), kind=kOutput, calls=%fused_computation.1 | convolution fusion | flops 12889096192 | bytes 20971520 | tf_op jit(solution)/shard_map/dot_general | solution.py:1009
  726.5 33.3 %convert_bitcast_fusion = bf16[2,2048,2048]{1,2,0:T(8,128)(2,1)} fusion(bf16[2,1536,2048]{2,1,0:T(8,128)(2,1)} %get-tuple-element.49.g_ref, bf16[1536,2048,1]{1,0,2:T(8,128)(2,1)} %bitcast.92), kind=kOutput, calls=%fused_computation | convolution fusion | flops 25778192384 | bytes 35651584 | tf_op jit(solution)/shard_map/td,jto->jdo/dot_general | solution.py:1066
  759.9 64.2 %ffn_out.1 = (bf16[8,384,256]{2,1,0:T(8,128)(2,1)}, f32[384,128]{1,0:T(8,128)}) custom-call(bf16[1536,2048]{1,0:T(8,128)(2,1)} %get-tuple-element.46.h_ref, bf16[8,2048,256]{2,1,0:T(8,128)(2,1)} %bitcast.77, f32[384,2048]{1,0:T(8,128)} %get-tuple-element.47.middle_ref), custom_call_target="tpu_custom_call" | custom-call | flops 12884901888 | bytes 50000000 | tf_op jit(solution)/shard_map/ffn_out/pallas_call | solution.py:845
  824.1 10.6 all-to-all-start.4
  834.7 66.3 %stream_back.1 = (bf16[8,384,256]{2,1,0:T(8,128)(2,1)}, f32[1,2048]{1,0:T(1,128)}) custom-call(bf16[3,1536,512]{2,1,0:T(8,128)(2,1)} %get-tuple-element.55.g_ref, bf16[8,3,256,512]{3,2,1,0:T(8,128)(2,1)} %bitcast.79, bf16[384,2048]{1,0:T(8,128)(2,1)} %get-tuple-element.43.x_ref, f32[384,2048]{1,0:T(8,128)} %get-tuple-element.56.middle_ref, ...), custom_call_target="tpu_custom_call" | custom-call | flops 9663676416 | bytes 50000000 | tf_op jit(solution)/shard_map/stream_back/pallas_call | solution.py:942
  901.0 65.1 %all_to_all.75 = bf16[8,384,256]{2,1,0:T(8,128)(2,1)} all-to-all(bf16[8,384,256]{2,1,0:T(8,128)(2,1)} %get-tuple-element.57), channel_id=1, replica_groups=mesh['row'=4,'col'=8] {'col'}, dimensions={0} | all-to-all | bytes 3145728 | tf_op jit(solution)/shard_map/all_to_all | solution.py:1002
  966.1 22.3 %all_to_all.76 = bf16[4,2,384,256]{3,2,1,0:T(8,128)(2,1)S(1)} all-to-all(bf16[4,2,384,256]{3,2,1,0:T(8,128)(2,1)S(1)} %bitcast.63), channel_id=1, replica_groups=mesh['row'=4,'col'=8] {'row'}, dimensions={0} | all-to-all | bytes 3145728 | tf_op jit(solution)/shard_map/all_to_all | solution.py:1004
  988.4 4.2 all-to-all-start.7
  993.0 0.8 fusion.2
  993.7 0.7 pad_maximum_fusion
  994.4 50.8 %psum.7 = f32[4112]{0:T(1024)S(1)} all-reduce(f32[4112]{0:T(1024)S(1)} %pad_maximum_fusion), channel_id=1, replica_groups=mesh['row'=4,'col'=8] {'row','col'}, use_global_device_ids=true, to_apply=%region_5.0 | all-reduce | flops 4112 | bytes 32896 | tf_op jit(solution)/shard_map/psum | solution.py:1076
  1045.2 0.6 dynamic_slice.14
  1045.9 63.7 %all_gather.43 = f32[4,12288]{1,0:T(4,128)S(1)} all-gather(f32[4,384]{1,0:T(4,128)S(1)} %fusion), channel_id=1, replica_groups=mesh['row'=4,'col'=8] {'col','row'}, dimensions={1}, use_global_device_ids=true | all-gather | bytes 202752 | tf_op jit(solution)/shard_map/all_gather | solution.py:1084
  1109.6 0.6 fusion.3
  1110.2 0.6 constant_dynamic-slice_fusion
  1110.8 1.2 copy.36
  1112.4 2.0 copy.37
  1114.4 1.8 convert_element_type.50
  1116.2 2.6 copy.42
  1118.7 2.7 convert_element_type.55
  1121.4 4.1 copy.43
  (54 shorter events, 1.7 us)
Async XLA Ops:
  7.2 180.8 %all-gather.12.cloned.1.call-start = ((), (), s32[]{:S(2)}) async-start(), calls=%async_computation.17 | async-start | bytes 7077888 | tf_op jit(solution)/shard_map/all_gather | solution.py:1040
  7.9 32.1 %copy-start.7 = (f32[256]{0:T(256)S(1)}, f32[256]{0:T(256)}, u32[]{:S(2)}) copy-start(f32[256]{0:T(256)} %param.19) | copy-start | bytes 3076
  7.9 32.1 %copy-start.8 = (f32[256]{0:T(256)S(1)}, f32[256]{0:T(256)}, u32[]{:S(2)}) copy-start(f32[256]{0:T(256)} %param.18) | copy-start | bytes 3076
  10.6 23.0 %all-to-all-start.2 = ((bf16[2,4,384,256]{3,2,0,1:T(8,128)(2,1)}), bf16[2,4,384,256]{3,2,0,1:T(8,128)(2,1)}, u32[]{:S(2)}, u32[]{:S(2)}) async-start(bf16[2,4,384,256]{3,2,0,1:T(8,128)(2,1)} %copy.35), calls=%async_computation.2 | async-start | bytes 3145728 | tf_op jit(solution)/shard_map/all_to_all | solution.py:993
  15.1 265.9 %all-gather.14.cloned.1.call-start = ((), (), s32[]{:S(2)}) async-start(), calls=%async_computation.18 | async-start | bytes 2359296 | tf_op jit(solution)/shard_map/all_gather | solution.py:1040
  33.6 84.3 %copy-start.2 = (bf16[3072,256]{1,0:T(8,128)(2,1)S(1)}, bf16[3072,256]{1,0:T(8,128)(2,1)}, u32[]{:S(2)}) copy-start(bf16[3072,256]{1,0:T(8,128)(2,1)} %param.13) | copy-start | bytes 4718596
  33.6 77.8 %all-to-all-start.3 = ((bf16[8,384,256]{2,1,0:T(8,128)(2,1)}), bf16[8,384,256]{2,1,0:T(8,128)(2,1)S(1)}, u32[]{:S(2)}, u32[]{:S(2)}) async-start(bf16[8,384,256]{2,1,0:T(8,128)(2,1)} %bitcast.17), calls=%async_computation.3 | async-start | bytes 3145728 | tf_op jit(solution)/shard_map/all_to_all | solution.py:995
  40.0 302.2 %all-gather.10.cloned.1.call-start = ((), (), s32[]{:S(2)}) async-start(), calls=%async_computation.12 | async-start | bytes 7864320 | tf_op jit(solution)/shard_map/all_gather | solution.py:1046
  111.4 1.1 copy-start
  116.7 225.6 %all-gather.18.cloned.1.call-start = ((), (), s32[]{:S(2)}) async-start(), calls=%async_computation.20 | async-start | bytes 9437184 | tf_op jit(solution)/shard_map/all_gather | solution.py:1040
  117.3 341.4 %all-gather.16.cloned.1.call-start = ((), (), s32[]{:S(2)}) async-start(), calls=%async_computation.19 | async-start | bytes 18874368 | tf_op jit(solution)/shard_map/all_gather | solution.py:1040
  117.9 29.7 %copy-start.9 = (f32[4]{0:T(128)S(1)}, f32[4]{0:T(128)}, u32[]{:S(2)}) copy-start(f32[4]{0:T(128)} %param.20) | copy-start | bytes 52
  140.1 42.7 %all-to-all-start.1 = ((bf16[8,384,256]{2,1,0:T(8,128)(2,1)}), bf16[8,384,256]{2,1,0:T(8,128)(2,1)S(1)}, u32[]{:S(2)}, u32[]{:S(2)}) async-start(bf16[8,384,256]{2,1,0:T(8,128)(2,1)} %bitcast.5), calls=%async_computation.1 | async-start | bytes 3145728 | tf_op jit(solution)/shard_map/all_to_all | solution.py:995
  147.6 966.8 %reduce-scatter.7.cloned.1.call-start = ((), (), s32[]{:S(2)}) async-start(), calls=%async_computation.14 | async-start | bytes 2359296 | tf_op jit(solution)/shard_map/reduce_scatter | solution.py:1013
  182.8 1.1 copy-start.1
  605.7 53.5 %copy-start.10 = (bf16[1536,512]{1,0:T(8,128)(2,1)S(1)}, bf16[1536,512]{1,0:T(8,128)(2,1)}, u32[]{:S(2)}) copy-start(bf16[1536,512]{1,0:T(8,128)(2,1)} %get-tuple-element.42.attn_ref) | copy-start | bytes 4718596
  666.9 449.3 %reduce-scatter.5.cloned.1.call-start = ((), (), s32[]{:S(2)}) async-start(), calls=%async_computation.13 | async-start | bytes 7077888 | tf_op jit(solution)/shard_map/reduce_scatter | solution.py:1013
  707.1 411.7 %reduce-scatter.11.cloned.1.call-start = ((), (), s32[]{:S(2)}) async-start(), calls=%async_computation.16 | async-start | bytes 9437184 | tf_op jit(solution)/shard_map/reduce_scatter | solution.py:1013
  726.5 395.0 %reduce-scatter.9.cloned.1.call-start = ((), (), s32[]{:S(2)}) async-start(), calls=%async_computation.15 | async-start | bytes 18874368 | tf_op jit(solution)/shard_map/reduce_scatter | solution.py:1013
  824.1 76.9 %all-to-all-start.4 = ((bf16[8,384,256]{2,1,0:T(8,128)(2,1)}), bf16[8,384,256]{2,1,0:T(8,128)(2,1)S(1)}, u32[]{:S(2)}, u32[]{:S(2)}) async-start(bf16[8,384,256]{2,1,0:T(8,128)(2,1)} %get-tuple-element.48), calls=%async_computation.4 | async-start | bytes 3145728 | tf_op jit(solution)/shard_map/all_to_all | solution.py:1002
  901.0 91.6 %copy-start.3 = (f32[384,128]{1,0:T(8,128)S(1)}, f32[384,128]{1,0:T(8,128)}, u32[]{:S(2)}) copy-start(f32[384,128]{1,0:T(8,128)} %get-tuple-element.66) | copy-start | bytes 589828
  901.0 91.7 %copy-start.4 = (f32[384,128]{1,0:T(8,128)S(1)}, f32[384,128]{1,0:T(8,128)}, u32[]{:S(2)}) copy-start(f32[384,128]{1,0:T(8,128)} %get-tuple-element.67) | copy-start | bytes 589828
  901.0 91.8 %copy-start.6 = (f32[4,1,128]{2,1,0:T(1,128)S(1)}, f32[4,1,128]{2,1,0:T(1,128)}, u32[]{:S(2)}) copy-start(f32[4,1,128]{2,1,0:T(1,128)} %get-tuple-element.63) | copy-start | bytes 6148
  901.0 92.7 %copy-start.5 = (f32[1,2048]{1,0:T(1,128)S(1)}, f32[1,2048]{1,0:T(1,128)}, u32[]{:S(2)}) copy-start(f32[1,2048]{1,0:T(1,128)} %get-tuple-element.62) | copy-start | bytes 24580
  988.4 123.7 %all-to-all-start.7 = ((bf16[4,2,384,256]{3,2,1,0:T(8,128)(2,1)}), bf16[4,2,384,256]{3,2,1,0:T(8,128)(2,1)S(1)}, u32[]{:S(2)}, u32[]{:S(2)}) async-start(bf16[4,2,384,256]{3,2,1,0:T(8,128)(2,1)} %bitcast.23), calls=%async_computation.7 | async-start | bytes 3145728 | tf_op jit(solution)/shard_map/all_to_all | solution.py:1004
Sparse Core Ops, SparseCore 0:
  9.7 95.3 all-gather.11
  106.6 29.4 all-gather.13
  138.0 87.8 all-gather.9
  227.4 80.4 all-gather.17
  309.3 149.3 all-gather.15
  667.0 37.4 reduce-scatter.6
  707.2 70.6 reduce-scatter.4
  780.2 113.2 reduce-scatter.10
  895.8 197.4 reduce-scatter.8

commit v3 on v2

--- a/solution.py
+++ b/solution.py
@@ -288,11 +288,12 @@
         height = self.piece // AG_CUTS
         return pl.ds(cut * height, height)
 
-    def start(self):
+    def start(self, greeted=False):
         row, col = self.row, self.col
         if self.size != 4:
             peers = [lax.rem(row + d, self.size) for d in range(1, self.size)]
-            greet([(peer, col) for peer in peers])
+            if not greeted:
+                greet([(peer, col) for peer in peers])
             self.order = [lax.rem(row + self.size - d, self.size) for d in range(1, self.size)]
             self.copies = [
                 remote(self.source, self.land.at[row], self.send.at[i], self.receive.at[i], (peer, col))
@@ -304,7 +305,8 @@
             rx, ry, rd = square(row)
             self.order = [rx, ry, rd]
             self.px, self.py = (rx, col), (ry, col)
-            greet([self.px, self.py])
+            if not greeted:
+                greet([self.px, self.py])
             self.to_x, self.to_y, self.onward = {}, {}, []
             for step in range(AG_CUTS):
                 for table, peer, base, cut in (
@@ -952,57 +954,349 @@
     )(grads, w_all, x, grad_middle, gain)
 
 
-def unblock_kernel(x_ref, gain_ref, tokens_ref, normed_ref):
-    cols, rows, depth = x_ref.shape
-    total = jnp.zeros((rows, 1), jnp.float32)
-    for c in range(cols):
-        part = x_ref[c].astype(jnp.float32)
-        tokens_ref[:, c * depth : (c + 1) * depth] = x_ref[c]
-        total += jnp.sum(part * part, axis=1, keepdims=True)
-    inverse = lax.rsqrt(total / D + EPSILON)
-    for c in range(cols):
-        columns = slice(c * depth, (c + 1) * depth)
-        normed_ref[:, columns] = (
-            x_ref[c].astype(jnp.float32) * inverse * gain_ref[:, columns]
-        ).astype(jnp.bfloat16)
-
-
-def enter(blocks, gain):
-    cols, piece, depth = blocks.shape
-    rows = piece // 4
+def here():
+    return lax.axis_index("row"), lax.axis_index("col")
+
+
+def row_and_col_peers(size, cols):
+    row, col = here()
+    return [(lax.rem(row + d, size), col) for d in range(1, size)] + [
+        (row, lax.rem(col + e, cols)) for e in range(1, cols)
+    ]
+
+
+def dma(*shape):
+    return pltpu.SemaphoreType.DMA(shape)
+
+
+class Inward:
+    def __init__(self, size, cols, source, middle, land, first_send, first_receive, send, receive, own):
+        self.size, self.cols, self.groups = size, cols, cols // size
+        self.source, self.middle, self.land = source, middle, land
+        self.first_send, self.first_receive = first_send, first_receive
+        self.send, self.receive, self.own = send, receive, own
+        self.row, self.col = here()
+
+    @staticmethod
+    def scratch(size, cols, piece, depth):
+        return [
+            pltpu.VMEM((size, cols // size, piece, depth), jnp.bfloat16),
+            pltpu.VMEM((cols, piece, depth), jnp.bfloat16),
+            dma(size - 1), dma(size - 1), dma(cols), dma(cols), dma(2),
+        ]
+
+    def start(self):
+        row, col = self.row, self.col
+        self.first = []
+        for d in range(1, self.size):
+            peer = lax.rem(row + d, self.size)
+            self.first.append(
+                remote(
+                    self.source.at[:, peer], self.middle.at[row],
+                    self.first_send.at[d - 1], self.first_receive.at[d - 1], (peer, col),
+                )
+            )
+            self.first[-1].start()
+        self.keep = pltpu.make_async_copy(self.source.at[:, row], self.middle.at[row], self.own.at[0])
+        self.keep.start()
+
+    def forward(self):
+        row, col = self.row, self.col
+        for d in range(self.size):
+            origin = lax.rem(row + self.size - d, self.size)
+            if d == 0:
+                self.keep.wait()
+            else:
+                self.first[d - 1].wait_recv()
+            for i in range(self.groups):
+                group = origin * self.groups + i
+
+                @pl.when(group != col)
+                def _():
+                    remote(
+                        self.middle.at[origin, i], self.land.at[col],
+                        self.send.at[group], self.receive.at[col], (row, group),
+                    ).start()
+
+                @pl.when(group == col)
+                def _():
+                    pltpu.make_async_copy(self.middle.at[origin, i], self.land.at[col], self.own.at[1]).start()
+
+    def finish(self):
+        row, col = self.row, self.col
+        pltpu.make_async_copy(self.middle.at[0, 0], self.land.at[col], self.own.at[1]).wait()
+        for e in range(1, self.cols):
+            peer = lax.rem(col + e, self.cols)
+            remote(
+                self.middle.at[0, 0], self.land.at[peer], self.send.at[peer], self.receive.at[peer], (row, peer)
+            ).wait()
+        for copy in self.first:
+            copy.wait_send()
+
+
+class Outward:
+    def __init__(self, size, cols, source, middle, target, first_send, first_receive, send, receive, own):
+        self.size, self.cols, self.groups = size, cols, cols // size
+        self.source, self.middle, self.target = source, middle, target
+        self.first_send, self.first_receive = first_send, first_receive
+        self.send, self.receive, self.own = send, receive, own
+        self.row, self.col = here()
+
+    @staticmethod
+    def scratch(size, cols, piece, depth):
+        return [
+            pltpu.VMEM((cols, piece, depth), jnp.bfloat16),
+            dma(cols - 1), dma(cols - 1), dma(cols), dma(cols), dma(cols // size),
+        ]
+
+    def start(self):
+        row, col = self.row, self.col
+        self.first = []
+        for e in range(1, self.cols):
+            peer = lax.rem(col + e, self.cols)
+            self.first.append(
+                remote(
+                    self.source.at[peer], self.middle.at[col],
+                    self.first_send.at[e - 1], self.first_receive.at[e - 1], (row, peer),
+                )
+            )
+            self.first[-1].start()
+
+    def forward(self):
+        row, col = self.row, self.col
+        for e in range(self.cols):
+            group = lax.rem(col + self.cols - e, self.cols)
+            if e:
+                self.first[e - 1].wait_recv()
+            block = self.middle.at[group] if e else self.source.at[col]
+            home, i = group // self.groups, lax.rem(group, self.groups)
+
+            @pl.when(home != row)
+            def _():
+                remote(
+                    block, self.target.at[i, row],
+                    self.send.at[group], self.receive.at[i * self.size + row], (home, col),
+                ).start()
+
+            @pl.when(home == row)
+            def _():
+                pltpu.make_async_copy(block, self.target.at[i, row], self.own.at[i]).start()
+
+    def finish(self):
+        row, col = self.row, self.col
+        for i in range(self.groups):
+            pltpu.make_async_copy(self.middle.at[0], self.target.at[i, row], self.own.at[i]).wait()
+            for d in range(1, self.size):
+                peer = lax.rem(row + d, self.size)
+                remote(
+                    self.middle.at[0], self.target.at[i, peer],
+                    self.send.at[peer * self.groups + i], self.receive.at[i * self.size + peer], (peer, col),
+                ).wait()
+        for copy in self.first:
+            copy.wait_send()
+
+
+def by_pieces(block, size):
+    return block.reshape(block.shape[0] // GLEN, size, GLEN // size, block.shape[1])
+
+
+def enter(size, cols, stream_in, gains):
+    pieces = by_pieces(stream_in, size)
+    piece, depth = pieces.shape[2:]
+
+    def kernel(x_ref, gains_ref, tokens_ref, normed_ref, gain_in_ref, gain_mid_ref, gains_land, gains_send, gains_receive, *rest):
+        greet(row_and_col_peers(size, cols))
+        exchange = Inward(size, cols, x_ref, *rest)
+        exchange.start()
+        row, col = here()
+        copies = []
+        for e in range(1, cols):
+            peer = lax.rem(col + e, cols)
+            copies.append(
+                remote(gains_ref, gains_land.at[col], gains_send.at[e - 1], gains_receive.at[e - 1], (row, peer))
+            )
+            copies[-1].start()
+        gains_land[col] = gains_ref[...]
+        exchange.forward()
+        for copy in copies:
+            copy.wait()
+        for c in range(cols):
+            gain_in_ref[:, c * depth : (c + 1) * depth] = gains_land[c, 0:1, :]
+            gain_mid_ref[:, c * depth : (c + 1) * depth] = gains_land[c, 1:2, :]
+        exchange.finish()
+        land = exchange.land
+
+        def norm(rows):
+            total = jnp.zeros((STRIP, 1), jnp.float32)
+            for c in range(cols):
+                part = land[c, rows, :]
+                tokens_ref[rows, c * depth : (c + 1) * depth] = part
+                part = part.astype(jnp.float32)
+                total += jnp.sum(part * part, axis=1, keepdims=True)
+            inverse = lax.rsqrt(total / D + EPSILON)
+            for c in range(cols):
+                columns = slice(c * depth, (c + 1) * depth)
+                normed_ref[rows, columns] = (
+                    land[c, rows, :].astype(jnp.float32) * inverse * gain_in_ref[:, columns]
+                ).astype(jnp.bfloat16)
+
+        strip_loop(piece, norm)
+
     return pl.pallas_call(
-        unblock_kernel,
-        grid=(4,),
-        in_specs=[
-            pl.BlockSpec((cols, rows, depth), lambda i: (0, i, 0)),
-            pl.BlockSpec((1, D), lambda i: (0, 0)),
+        kernel,
+        out_shape=[bf(piece, D), bf(piece, D), fl(1, D), fl(1, D)],
+        in_specs=[ANY, VMEM],
+        out_specs=[VMEM] * 4,
+        scratch_shapes=[pltpu.VMEM((cols, 8, depth), jnp.float32), dma(cols - 1), dma(cols - 1)]
+        + Inward.scratch(size, cols, piece, depth),
+        compiler_params=comm_params(8),
+        cost_estimate=pl.CostEstimate(flops=8 * piece * D, bytes_accessed=40_000_000, transcendentals=0),
+        name="enter",
+    )(pieces, jnp.pad(gains, ((0, 6), (0, 0))))
+
+
+def spread(size, cols, cotangent):
+    pieces = by_pieces(cotangent, size)
+    piece, depth = pieces.shape[2:]
+    count = Gather.semaphores(size)
+
+    def kernel(x_ref, tokens_ref, all_ref, send, receive, own, *rest):
+        greet(row_and_col_peers(size, cols))
+        exchange = Inward(size, cols, x_ref, *rest)
+        exchange.start()
+        exchange.forward()
+        exchange.finish()
+        land = exchange.land
+
+        def assemble(rows):
+            for c in range(cols):
+                tokens_ref[rows, c * depth : (c + 1) * depth] = land[c, rows, :]
+
+        strip_loop(piece, assemble)
+        gather = Gather(size, tokens_ref, all_ref, send, receive, own)
+        gather.start(greeted=True)
+        gather.forward()
+        for step in range(size - 1):
+            gather.wait(step)
+        gather.finish()
+
+    return pl.pallas_call(
+        kernel,
+        out_shape=[bf(piece, D), bf(size, piece, D)],
+        in_specs=[ANY],
+        out_specs=[VMEM, ANY],
+        scratch_shapes=[dma(count), dma(count), pltpu.SemaphoreType.DMA]
+        + Inward.scratch(size, cols, piece, depth),
+        compiler_params=comm_params(9),
+        cost_estimate=pl.CostEstimate(flops=piece * D, bytes_accessed=60_000_000, transcendentals=0),
+        name="spread",
+    )(pieces)
+
+
+def leave(size, cols, blocks_out, blocks_grad, stats, sums):
+    _, piece, depth = blocks_out.shape
+    groups = cols // size
+    half = len(Outward.scratch(size, cols, piece, depth))
+
+    def kernel(
+        out_ref, grad_ref, stats_ref, sums_ref, out_target, grad_target, stats_target, sums_target,
+        stats_row, stats_all, sums_col, sums_part, sums_row,
+        a_send, a_receive, b_send, b_receive, c_send, c_receive, d_send, d_receive, *rest,
+    ):
+        row, col = here()
+        greet(row_and_col_peers(size, cols))
+        grad = Outward(size, cols, grad_ref, rest[0], grad_target, *rest[1:half])
+        out = Outward(size, cols, out_ref, rest[half], out_target, *rest[half + 1 :])
+        home, slot = col // groups, lax.rem(col, groups)
+        col_peers = [lax.rem(col + e, cols) for e in range(1, cols)]
+        row_peers = [lax.rem(row + d, size) for d in range(1, size)]
+
+        def sums_first(peer):
+            return remote(sums_ref.at[peer], sums_col.at[col], c_send.at[peer], c_receive.at[col], (row, peer))
+
+        for peer in col_peers:
+            sums_first(peer).start()
+        sums_col[col] = sums_ref[col]
+
+        @pl.when(home != row)
+        def _():
+            remote(stats_ref, stats_row.at[row], a_send, a_receive.at[row], (home, col)).start()
+
+        @pl.when(home == row)
+        def _():
+            stats_row[row] = stats_ref[...]
+
+        grad.start()
+        out.start()
+        for peer in col_peers:
+            remote(sums_ref.at[peer], sums_col.at[peer], c_send.at[peer], c_receive.at[peer], (row, peer)).wait()
+        total = sums_col[0]
+        for c in range(1, cols):
+            total += sums_col[c]
+        sums_part[...] = total
+        sums_row[row] = total
+        for peer in row_peers:
+            remote(sums_part, sums_row.at[row], d_send.at[peer], d_receive.at[row], (peer, col)).start()
+
+        @pl.when(home == row)
+        def _():
+            for peer in row_peers:
+                remote(stats_ref, stats_row.at[peer], a_send, a_receive.at[peer], (peer, col)).wait_recv()
+            for e, peer in enumerate(col_peers):
+                remote(stats_row, stats_all.at[slot], b_send.at[e], b_receive.at[slot], (row, peer)).start()
+            stats_all[slot] = stats_row[...]
+
+        grad.forward()
+        out.forward()
+        for peer in row_peers:
+            remote(sums_part, sums_row.at[peer], d_send.at[peer], d_receive.at[peer], (peer, col)).wait()
+        whole = sums_row[0]
+        for r in range(1, size):
+            whole += sums_row[r]
+        line = lax.broadcasted_iota(jnp.int32, (8, depth), 0)
+        sums_target[...] = jnp.where(line < 2, whole, total)
+
+        @pl.when(home == row)
+        def _():
+            for e, peer in enumerate(col_peers):
+                remote(stats_row, stats_all.at[slot], b_send.at[e], b_receive.at[slot], (row, peer)).wait_send()
+
+        @pl.when(home != row)
+        def _():
+            remote(stats_ref, stats_row.at[row], a_send, a_receive.at[row], (home, col)).wait_send()
+
+        for i in range(groups):
+            group = row * groups + i
+
+            @pl.when(group != col)
+            def _():
+                remote(stats_row, stats_all.at[i], b_send.at[0], b_receive.at[i], (row, group)).wait_recv()
+
+        stats_target[...] = stats_all[...]
+        grad.finish()
+        out.finish()
+
+    return pl.pallas_call(
+        kernel,
+        out_shape=[
+            bf(groups, size, piece, depth), bf(groups, size, piece, depth),
+            fl(groups, size, 8, piece), fl(8, depth),
         ],
-        out_specs=[pl.BlockSpec((rows, D), lambda i: (i, 0))] * 2,
-        out_shape=[bf(piece, D), bf(piece, D)],
-        cost_estimate=pl.CostEstimate(flops=6 * piece * D, bytes_accessed=6 * piece * D, transcendentals=0),
-        name="enter",
-    )(blocks, gain)
-
-
-def to_blocks(block):
-    row_size = lax.axis_size("row")
-    features = block.shape[1]
-    groups = block.shape[0] // GLEN
-    piece = GLEN // row_size
-    split = block.reshape(groups, row_size, piece, features)
-    split = lax.all_to_all(split, "row", split_axis=1, concat_axis=0, tiled=True)
-    split = split.reshape(row_size * groups, piece, features)
-    return lax.all_to_all(split, "col", split_axis=0, concat_axis=0, tiled=True)
-
-
-def from_blocks(blocks):
-    row_size = lax.axis_size("row")
-    cols, piece, features = blocks.shape
-    groups = cols // row_size
-    split = lax.all_to_all(blocks, "col", split_axis=0, concat_axis=0, tiled=True)
-    split = split.reshape(row_size, groups, piece, features)
-    split = lax.all_to_all(split, "row", split_axis=0, concat_axis=2, tiled=True)
-    return split.reshape(groups * GLEN, features)
+        in_specs=[VMEM] * 4,
+        out_specs=[ANY, ANY, VMEM, VMEM],
+        scratch_shapes=[
+            pltpu.VMEM((size, 8, piece), jnp.float32),
+            pltpu.VMEM((groups, size, 8, piece), jnp.float32),
+            pltpu.VMEM((cols, 8, depth), jnp.float32),
+            pltpu.VMEM((8, depth), jnp.float32),
+            pltpu.VMEM((size, 8, depth), jnp.float32),
+            pltpu.SemaphoreType.DMA, dma(size), dma(cols - 1), dma(groups), dma(cols), dma(cols), dma(size), dma(size),
+        ]
+        + Outward.scratch(size, cols, piece, depth) * 2,
+        compiler_params=comm_params(10),
+        cost_estimate=pl.CostEstimate(flops=piece * D, bytes_accessed=60_000_000, transcendentals=0),
+        name="leave",
+    )(blocks_out, blocks_grad, stats, sums)
 
 
 def tokens_contract(left, right):
@@ -1013,6 +1307,10 @@
     return lax.psum_scatter(
         partial.astype(jnp.bfloat16), "col", scatter_dimension=axis, tiled=True
     ).astype(jnp.float32)
+
+
+def flat(pieces):
+    return pieces.reshape(GLEN, D)
 
 
 def local(
@@ -1032,58 +1330,64 @@
 ):
     head_here = memory.shape[1]
     size = lax.axis_size("row")
-    row_index = lax.axis_index("row")
-    col_index = lax.axis_index("col")
-    gains = lax.all_gather(jnp.stack([gain_attn, gain_ffn]), "col", axis=1, tiled=True)
-    gain_in, gain_mid = gains[0:1], gains[1:2]
+    cols = lax.axis_size("col")
     all_qkv, all_out, all_gu, all_down = (
         lax.all_gather(w, "col", axis=0, tiled=False) for w in (w_qkv, w_out, w_gate_up, w_down)
     )
     gate_value = jax.nn.sigmoid(gate_logit)
     group = (memory[0], memory_norm[0], offsets[0], lengths[0], gate_value)
-    stream, normed_in = enter(to_blocks(stream_in), gain_in)
-    cot, _ = enter(to_blocks(cotangent), gain_in)
-    all_cot = lax.all_gather(cot, "row", axis=0, tiled=True)
+    stream, normed_in, gain_in, gain_mid = enter(
+        size, cols, stream_in, jnp.stack([gain_attn, gain_ffn])
+    )
     heads_all, all_in = project_heads(size, normed_in, all_qkv)
     attn, dot_part, memory_part, logsum, memory_new, norm_new = attend(heads_all, *group)
+    cotangent, attn = lax.optimization_barrier((cotangent, attn))
+    cot, all_cot = spread(size, cols, cotangent)
+    all_cot, attn = lax.optimization_barrier((all_cot, attn))
+    all_cot = all_cot.reshape(GLEN, D)
     middle, normed_ffn, stat_branch = branch_out(size, attn, all_out, stream, gain_mid)
     hidden, grad_gu, all_ffn = feed_forward(size, normed_ffn, all_gu, all_down, all_cot)
+    part_gu = jnp.einsum(
+        "td,jto->jdo", flat(all_ffn), grad_gu, preferred_element_type=jnp.float32
+    ).astype(jnp.bfloat16)
+    part_down = tokens_contract(hidden, all_cot).astype(jnp.bfloat16)
+    grad_gu, part_gu, part_down = lax.optimization_barrier((grad_gu, part_gu, part_down))
+    grad_gate_up = over_col(part_gu, 1)
+    grad_down = over_col(part_down, 1)
     grad_middle, low_branch, part_gain_ffn = middle_back(size, grad_gu, all_gu, middle, cot, gain_mid)
-    blocks_out, stat_ffn = ffn_out(size, hidden, all_down, middle)
     grad_heads, all_branch = branch_back(size, low_branch, all_out)
     grads_qkv, gate_sums = attend_back(
         heads_all, grad_heads, dot_part, memory_part, logsum, *group
     )
+    hidden, grads_qkv = lax.optimization_barrier((hidden, grads_qkv))
+    blocks_out, stat_ffn = ffn_out(size, hidden, all_down, middle)
+    blocks_out, grads_qkv, grad_gate_up = lax.optimization_barrier((blocks_out, grads_qkv, grad_gate_up))
     blocks_grad, part_gain_attn = stream_back(size, grads_qkv, all_qkv, stream, grad_middle, gain_in)
-    stream_out = from_blocks(blocks_out)
-    stream_grad = from_blocks(blocks_grad).astype(jnp.float32)
-
-    def flat(pieces):
-        return pieces.reshape(GLEN, D)
-
-    grad_down = over_col(tokens_contract(hidden, all_cot), 1)
-    grad_gate_up = over_col(
-        jnp.einsum("td,jto->jdo", flat(all_ffn), grad_gu, preferred_element_type=jnp.float32), 1
-    )
+    blocks_grad, grad_down = lax.optimization_barrier((blocks_grad, grad_down))
     grad_out = over_col(tokens_contract(attn, flat(all_branch)), 1)
     grad_qkv = over_col(
         jnp.einsum("td,jto->jdo", flat(all_in), grads_qkv, preferred_element_type=jnp.float32), 1
     )
     logit_part = gate_value * (1.0 - gate_value) * jnp.sum(gate_sums, axis=(1, 2))
-    logit_slots = lax.dynamic_update_slice(
-        jnp.zeros((size * head_here,), jnp.float32), logit_part, (row_index * head_here,)
+    features_here = gain_attn.shape[0]
+    sums = jnp.concatenate(
+        [
+            part_gain_attn.reshape(cols, 1, features_here),
+            part_gain_ffn.reshape(cols, 1, features_here),
+            jnp.broadcast_to(
+                jnp.pad(logit_part, (0, features_here - head_here))[None, None], (cols, 6, features_here)
+            ),
+        ],
+        axis=1,
     )
-    small = lax.psum(
-        jnp.concatenate([part_gain_attn[0], part_gain_ffn[0], logit_slots]), ("row", "col")
+    stats = jnp.sqrt(jnp.concatenate([stat_branch[:, :2], stat_ffn[:, :2]], axis=1).T)
+    stream_out, stream_grad, stats_all, sums = leave(
+        size, cols, blocks_out, blocks_grad, jnp.pad(stats, ((0, 4), (0, 0))), sums
     )
-    features_here = gain_attn.shape[0]
-    grad_gain_attn = lax.dynamic_slice(small, (col_index * features_here,), (features_here,))
-    grad_gain_ffn = lax.dynamic_slice(small, (D + col_index * features_here,), (features_here,))
-    grad_gate_logit = lax.dynamic_slice(small, (2 * D + row_index * head_here,), (head_here,))
-    rms_here = jnp.sqrt(jnp.concatenate([stat_branch[:, :2], stat_ffn[:, :2]], axis=1).T)
-    rms_all = lax.all_gather(rms_here, ("col", "row"), axis=1, tiled=True)
-    rows_here = stream_in.shape[0]
-    rms_table = lax.dynamic_slice(rms_all, (0, row_index * rows_here), (4, rows_here))
+    stream_out = stream_out.reshape(stream_in.shape)
+    stream_grad = stream_grad.reshape(stream_in.shape).astype(jnp.float32)
+    rms_table = stats_all[:, :, :4].transpose(2, 0, 1, 3).reshape(4, stream_in.shape[0])
+    grad_gain_attn, grad_gain_ffn, grad_gate_logit = sums[0], sums[1], sums[2, :head_here]
     return (
         stream_out,
         stream_grad,

time: 1150 us -> 1010 us (0.88); the launches traced: 1130 us -> 1000 us
  blocking collectives: 295 us -> 0 us
  Pallas kernels: 518 us -> 769 us
  waiting for transfers between devices: 171 us -> 117 us
  starting transfers between devices: 33.6 us -> 0.31 us
    pallas_call x2 -> x3, Pallas kernels: 8.18 us -> 274 us  [the longest x1 112 us: spread(): pl.pallas_call(kernel, out_shape=[bf(piece, D), bf(size, piece, D)], in_s...]
    all_gather x2 -> x0, blocking collectives: 134 us -> none  [the longest x1 70.8 us: local(): lax.all_gather(jnp.stack([gain_attn, gain_ffn]), 'col', axis=1, tiled=True)]
    all_to_all x3 -> x0, blocking collectives: 109 us -> none  [the longest x1 65.1 us: from_blocks(): lax.all_to_all(blocks, 'col', split_axis=0, concat_axis=0, tiled=True)]
    all_to_all x5 -> x0, waiting for transfers between devices: 52.3 us -> none  [the longest x2 34.6 us: to_blocks(): return lax.all_to_all(split, 'col', split_axis=0, concat_axis=0, tiled=True)]
    psum x1 -> x0, blocking collectives: 50.8 us -> none  [local(): lax.psum(jnp.concatenate([part_gain_attn[0], part_gain_ffn[0], logit_slot...]
    all_gather x4, waiting for transfers between devices: 116 us -> 68 us  [local(): lax.all_gather(w, 'col', axis=0, tiled=False)]
    reduce_scatter x4, waiting for transfers between devices: 0.01 us -> 46.2 us  [over_col(): lax.psum_scatter(partial.astype(jnp.bfloat16), 'col', scatter_dimension=a...]
    all_to_all x5 -> x0, starting transfers between devices: 33.3 us -> none  [the longest x2 14 us: to_blocks(): return lax.all_to_all(split, 'col', split_axis=0, concat_axis=0, tiled=True)]
  transfers between devices with their start and end apart: 14 -> 8, of which waited for: 3 -> 3; matrix products, arithmetic and copies ran while one was open for 8% -> 5% of each run, Pallas kernels for 28% -> 69%
where the time goes in v3:
time: 1010 us; the launch traced here: 1000 us
  Pallas kernels  769 us (76%)
  waiting for transfers between devices  117 us (12%)
  matrix products  74 us (7%)
  local copies, waits for them, and re-layouts  15.1 us (1%)
  between operations  14.6 us (1%)
  other arithmetic  13.9 us (1%)
    pallas_call x1, Pallas kernels, spread(): pl.pallas_call(kernel, out_shape=[bf(piece, D), bf(size, piece, D)], in_s...  112 us
    pallas_call x1, Pallas kernels, leave(): pl.pallas_call(kernel, out_shape=[bf(groups, size, piece, depth), bf(grou...  92.6 us
    pallas_call x1, Pallas kernels, middle_back(): pl.pallas_call(kernel, out_shape=[fl(piece, D), bf(piece, D), fl(1, D)],...  76.4 us
    pallas_call x1, Pallas kernels, feed_forward(): pl.pallas_call(kernel, out_shape=[bf(GLEN, wide), bf(2, GLEN, wide), bf(s...  71.5 us
    pallas_call x1, Pallas kernels, enter(): pl.pallas_call(kernel, out_shape=[bf(piece, D), bf(piece, D), fl(1, D), f...  69.2 us
    all_gather x4, waiting for transfers between devices, local(): lax.all_gather(w, 'col', axis=0, tiled=False)  68 us
    pallas_call x1, Pallas kernels, stream_back(): pl.pallas_call(kernel, out_shape=[bf(cols, piece, depth), fl(1, D)], in_s...  65.8 us
    pallas_call x1, Pallas kernels, branch_out(): pl.pallas_call(kernel, out_shape=[fl(piece, D), bf(piece, D), fl(piece, H...  64.2 us
  transfers between devices with their start and end apart: 8, of which 3 were waited for; matrix products, arithmetic and copies ran while one was open for 5% of the time, Pallas kernels for 69%

profile of v3, /device:TPU:27, one launch (start us, length us, event | category | flops | bytes accessed | tf_op | source)
XLA Modules:
  0.0 1004.7 jit_solution(2714938548628798252)
XLA Ops:
  7.2 0.7 all-gather.9.cloned.1.call-update
  7.9 0.0 all-gather.11.cloned.1.call-start
  8.0 0.7 all-gather.11.cloned.1.call-update
  8.7 0.0 all-gather.15.cloned.1.call-start
  8.7 0.7 all-gather.15.cloned.1.call-update
  9.5 0.5 all-gather.13.cloned.1.call-update
  10.0 0.0 reduce-scatter.5.cloned.1.call-start
  10.0 1.3 select_maximum_fusion.gains_ref
  11.3 69.2 %enter.1 = (bf16[384,2048]{1,0:T(8,128)(2,1)}, bf16[384,2048]{1,0:T(8,128)(2,1)}, f32[1,2048]{1,0:T(1,128)}, f32[1,2048]{1,0:T(1,128)}) custom-call(bf16[2,4,384,256]{3,2,1,0:T(8,128)(2,1)} %bitcast.49, f32[8,256]{1,0:T(8,128)} %select_maximum_fusion.gains_ref), custom_call_target="tpu_custom_call" | custom-call | flops 6291456 | bytes 40000000 | tf_op jit(solution)/shard_map/enter/pallas_call | solution.py:1145
  80.6 0.5 add_divide_fusion.gate_ref
  81.1 26.0 %all-gather.9.cloned.1.call-done = bf16[24,256,512]{2,1,0:T(8,128)(2,1)} async-done(((bf16[3,256,512]{2,1,0:T(8,128)(2,1)}), bf16[24,256,512]{2,1,0:T(8,128)(2,1)}) %all-gather.9.cloned.1.call-update) | async-done | bytes 6291472 | tf_op jit(solution)/shard_map/all_gather | solution.py:1335
  107.1 58.3 %project_heads.1 = (bf16[3,4,1536,128]{3,2,1,0:T(8,128)(2,1)}, bf16[4,384,2048]{2,1,0:T(8,128)(2,1)}) custom-call(bf16[384,2048]{1,0:T(8,128)(2,1)} %get-tuple-element.61.x_ref, bf16[8,3,256,512]{3,2,1,0:T(8,128)(2,1)} %bitcast.63), custom_call_target="tpu_custom_call" | custom-call | flops 9663676416 | bytes 40000000 | tf_op jit(solution)/shard_map/project_heads/pallas_call | solution.py:559
  165.4 16.6 %attend.1 = (bf16[1536,512]{1,0:T(8,128)(2,1)}, f32[4,1536,128]{2,1,0:T(8,128)}, f32[4,1536,128]{2,1,0:T(8,128)}, f32[4,1536,1]{2,1,0:T(8,128)}, f32[4,128,128]{2,1,0:T(8,128)}, /*index=5*/f32[4,1,128]{2,1,0:T(1,128)}) custom-call(s32[4]{0:T(128)} %bitcast.72, s32[4]{0:T(128)} %bitcast.74, f32[4]{0:T(128)} %add_divide_fusion.gate_ref, ...), custom_call_target="tpu_custom_call" | custom-call | flops 3200000000 | bytes 24000000 | tf_op jit(solution)/shard_map/attend/pallas_call | solution.py:138
  182.0 112.4 %spread.1 = (bf16[384,2048]{1,0:T(8,128)(2,1)}, bf16[4,384,2048]{2,1,0:T(8,128)(2,1)}) custom-call(bf16[2,4,384,256]{3,2,1,0:T(8,128)(2,1)} %bitcast.50), custom_call_target="tpu_custom_call" | custom-call | flops 786432 | bytes 60000000 | tf_op jit(solution)/shard_map/spread/pallas_call | solution.py:1183
  294.5 64.2 %branch_out.1 = (f32[384,2048]{1,0:T(8,128)}, bf16[384,2048]{1,0:T(8,128)(2,1)}, f32[384,128]{1,0:T(8,128)}) custom-call(bf16[1536,512]{1,0:T(8,128)(2,1)} %get-tuple-element.67.attn_ref, bf16[8,512,256]{2,1,0:T(8,128)(2,1)} %bitcast.66, bf16[384,2048]{1,0:T(8,128)(2,1)} %get-tuple-element.68.x_ref, f32[1,2048]{1,0:T(1,128)} %get-tuple-element.69.gain_ref), custom_call_target="tpu_custom_call" | custom-call | flops 3221225472 | bytes 40000000 | tf_op jit(solution)/shard_map/branch_out/pallas_call | solution.py:631
  358.8 42.0 %all-gather.13.cloned.1.call-done = bf16[16,256,2048]{2,1,0:T(8,128)(2,1)} async-done(((bf16[2,256,2048]{2,1,0:T(8,128)(2,1)}), bf16[16,256,2048]{2,1,0:T(8,128)(2,1)}) %all-gather.13.cloned.1.call-update) | async-done | bytes 16777232 | tf_op jit(solution)/shard_map/all_gather | solution.py:1335
  400.8 71.5 %feed_forward.1 = (bf16[1536,2048]{1,0:T(8,128)(2,1)}, bf16[2,1536,2048]{2,1,0:T(8,128)(2,1)}, bf16[4,384,2048]{2,1,0:T(8,128)(2,1)}) custom-call(bf16[384,2048]{1,0:T(8,128)(2,1)} %get-tuple-element.70.x_ref, bf16[8,2,256,2048]{3,2,1,0:T(8,128)(2,1)} %bitcast.59, bf16[8,2048,256]{2,1,0:T(8,128)(2,1)} %bitcast.61, ...), custom_call_target="tpu_custom_call" | custom-call | flops 38654705664 | bytes 70000000 | tf_op jit(solution)/shard_map/feed_forward/pallas_call | solution.py:717
  472.3 19.4 %convolution_convert_fusion = bf16[2048,2048]{1,0:T(8,128)(2,1)} fusion(bf16[1536,2048]{1,0:T(8,128)(2,1)} %get-tuple-element.84.h_ref, bf16[1536,2048]{1,0:T(8,128)(2,1)} %bitcast.65), kind=kOutput, calls=%fused_computation.1 | convolution fusion | flops 12889096192 | bytes 20971520 | tf_op jit(solution)/shard_map/dot_general | solution.py:1303
  491.6 32.8 %convert_bitcast_fusion = bf16[2,2048,2048]{1,2,0:T(8,128)(2,1)} fusion(bf16[2,1536,2048]{2,1,0:T(8,128)(2,1)} %get-tuple-element.75.g_ref, bf16[1536,2048,1]{1,0,2:T(8,128)(2,1)} %bitcast.77), kind=kOutput, calls=%fused_computation | convolution fusion | flops 25778192384 | bytes 35651584 | tf_op jit(solution)/shard_map/td,jto->jdo/dot_general | solution.py:1350
  524.4 0.0 reduce-scatter.11.cloned.1.call-start
  524.5 76.4 %middle_back.1 = (f32[384,2048]{1,0:T(8,128)}, bf16[384,2048]{1,0:T(8,128)(2,1)}, f32[1,2048]{1,0:T(1,128)}) custom-call(bf16[2,1536,2048]{2,1,0:T(8,128)(2,1)} %get-tuple-element.75.g_ref, bf16[8,2,256,2048]{3,2,1,0:T(8,128)(2,1)} %bitcast.60, f32[384,2048]{1,0:T(8,128)} %get-tuple-element.76.middle_ref, bf16[384,2048]{1,0:T(8,128)(2,1)} %get-tuple-element.77.cot_ref, ...), custom_call_target="tpu_custom_call" | custom-call | flops 25769803776 | bytes 60000000 | tf_op jit(solution)/shard_map/middle_back/pallas_call | solution.py:791
  600.9 53.3 %branch_back.1 = (bf16[4,1536,128]{2,1,0:T(8,128)(2,1)}, bf16[4,384,2048]{2,1,0:T(8,128)(2,1)}) custom-call(bf16[384,2048]{1,0:T(8,128)(2,1)} %get-tuple-element.78.x_ref, bf16[8,512,256]{2,1,0:T(8,128)(2,1)} %bitcast.67), custom_call_target="tpu_custom_call" | custom-call | flops 3221225472 | bytes 40000000 | tf_op jit(solution)/shard_map/branch_back/pallas_call | solution.py:887
  654.2 7.5 convolution_convert_fusion.1
  661.7 0.0 reduce-scatter.7.cloned.1.call-start
  661.7 0.7 reduce-scatter.7.cloned.1.call-update
  662.4 0.0 reduce-scatter.9.cloned.1.call-start
  662.5 24.7 %attend_back.1 = (bf16[3,1536,512]{2,1,0:T(8,128)(2,1)}, f32[4,1,128]{2,1,0:T(1,128)}) custom-call(s32[4]{0:T(128)} %bitcast.73, s32[4]{0:T(128)} %bitcast.75, f32[4]{0:T(128)} %add_divide_fusion.gate_ref, bf16[3,4,1536,128]{3,2,1,0:T(8,128)(2,1)} %get-tuple-element.62.qkv_ref, bf16[4,1536,128]{2,1,0:T(8,128)(2,1)} %get-tuple-element.79.grad_ref, ...), custom_call_target="tpu_custom_call" | custom-call | flops 8000000000 | bytes 24000000 | tf_op jit(solution)/shard_map/attend_back/pallas_call | solution.py:220
  687.2 64.1 %ffn_out.1 = (bf16[8,384,256]{2,1,0:T(8,128)(2,1)}, f32[384,128]{1,0:T(8,128)}) custom-call(bf16[1536,2048]{1,0:T(8,128)(2,1)} %get-tuple-element.84.h_ref, bf16[8,2048,256]{2,1,0:T(8,128)(2,1)} %bitcast.62, f32[384,2048]{1,0:T(8,128)} %get-tuple-element.76.middle_ref), custom_call_target="tpu_custom_call" | custom-call | flops 12884901888 | bytes 50000000 | tf_op jit(solution)/shard_map/ffn_out/pallas_call | solution.py:847
  751.3 4.1 convert_element_type.45
  755.4 14.5 %convert_bitcast_fusion.1 = bf16[3,2048,512]{1,2,0:T(8,128)(2,1)} fusion(bf16[3,1536,512]{2,1,0:T(8,128)(2,1)S(1)} %copy-done.9, bf16[1536,2048,1]{1,0,2:T(8,128)(2,1)} %bitcast.76), kind=kOutput, calls=%fused_computation.2 | convolution fusion | flops 9666822144 | bytes 17301504 | tf_op jit(solution)/shard_map/td,jto->jdo/dot_general | solution.py:1369
  769.9 0.9 copy-done.2
  770.8 0.1 copy.32
  770.9 0.1 reduce_sum.9
  771.1 0.1 copy.33
  771.3 0.6 pad.13.stats_ref
  771.9 1.8 convert_element_type.53
  773.6 46.1 %reduce-scatter.7.cloned.1.call-done = bf16[2048,256]{1,0:T(8,128)(2,1)} async-done(((bf16[2048,2048]{1,0:T(8,128)(2,1)}), bf16[2048,256]{1,0:T(8,128)(2,1)}) %reduce-scatter.7.cloned.1.call-update) | async-done | bytes 1048592 | tf_op jit(solution)/shard_map/reduce_scatter | solution.py:1307
  819.8 2.7 convert_element_type.46
  822.5 65.8 %stream_back.1 = (bf16[8,384,256]{2,1,0:T(8,128)(2,1)}, f32[1,2048]{1,0:T(1,128)}) custom-call(bf16[3,1536,512]{2,1,0:T(8,128)(2,1)} %get-tuple-element.89.g_ref, bf16[8,3,256,512]{3,2,1,0:T(8,128)(2,1)} %bitcast.64, bf16[384,2048]{1,0:T(8,128)(2,1)} %get-tuple-element.68.x_ref, f32[384,2048]{1,0:T(8,128)} %get-tuple-element.90.middle_ref, ...), custom_call_target="tpu_custom_call" | custom-call | flops 9663676416 | bytes 50000000 | tf_op jit(solution)/shard_map/stream_back/pallas_call | solution.py:944
  888.3 1.4 pad_maximum_fusion.sums_ref
  889.7 92.6 %leave.1 = (bf16[2,4,384,256]{3,2,1,0:T(8,128)(2,1)}, bf16[2,4,384,256]{3,2,1,0:T(8,128)(2,1)}, f32[2,4,8,384]{3,2,1,0:T(8,128)}, f32[8,256]{1,0:T(8,128)}) custom-call(bf16[8,384,256]{2,1,0:T(8,128)(2,1)} %get-tuple-element.88.out_ref, bf16[8,384,256]{2,1,0:T(8,128)(2,1)} %get-tuple-element.94.grad_ref, f32[8,384]{1,0:T(8,128)} %pad.13.stats_ref, ...), custom_call_target="tpu_custom_call" | custom-call | flops 786432 | bytes 60000000 | tf_op jit(solution)/shard_map/leave/pallas_call | solution.py:1279
  982.3 1.6 slice.23
  984.0 5.3 copy.36
  989.3 1.3 slice_bitcast_fusion
  990.6 1.3 fusion.2
  991.9 2.0 bitcast_convert_fusion
  994.0 2.6 copy.35
  996.5 1.1 copy.40
  (35 shorter events, 0.3 us)
Async XLA Ops:
  7.2 73.4 %copy-start.6 = (f32[4]{0:T(128)S(1)}, f32[4]{0:T(128)}, u32[]{:S(2)}) copy-start(f32[4]{0:T(128)} %param.20) | copy-start | bytes 52
  7.2 99.9 %all-gather.9.cloned.1.call-start = ((), (), s32[]{:S(2)}) async-start(), calls=%async_computation.8 | async-start | bytes 7077888 | tf_op jit(solution)/shard_map/all_gather | solution.py:1335
  7.9 286.5 %all-gather.11.cloned.1.call-start = ((), (), s32[]{:S(2)}) async-start(), calls=%async_computation.9 | async-start | bytes 2359296 | tf_op jit(solution)/shard_map/all_gather | solution.py:1335
  8.7 350.1 %all-gather.15.cloned.1.call-start = ((), (), s32[]{:S(2)}) async-start(), calls=%async_computation.11 | async-start | bytes 9437184 | tf_op jit(solution)/shard_map/all_gather | solution.py:1335
  9.4 391.4 %all-gather.13.cloned.1.call-start = ((), (), s32[]{:S(2)}) async-start(), calls=%async_computation.10 | async-start | bytes 18874368 | tf_op jit(solution)/shard_map/all_gather | solution.py:1335
  10.0 741.3 %reduce-scatter.5.cloned.1.call-start = ((), (), s32[]{:S(2)}) async-start(), calls=%async_computation.4 | async-start | bytes 18874368 | tf_op jit(solution)/shard_map/reduce_scatter | solution.py:1307
  524.4 247.4 %reduce-scatter.11.cloned.1.call-start = ((), (), s32[]{:S(2)}) async-start(), calls=%async_computation.7 | async-start | bytes 2359296 | tf_op jit(solution)/shard_map/reduce_scatter | solution.py:1307
  600.9 53.3 %copy-start.8 = (bf16[1536,512]{1,0:T(8,128)(2,1)S(1)}, bf16[1536,512]{1,0:T(8,128)(2,1)}, u32[]{:S(2)}) copy-start(bf16[1536,512]{1,0:T(8,128)(2,1)} %get-tuple-element.67.attn_ref) | copy-start | bytes 4718596
  661.7 158.1 %reduce-scatter.7.cloned.1.call-start = ((), (), s32[]{:S(2)}) async-start(), calls=%async_computation.5 | async-start | bytes 9437184 | tf_op jit(solution)/shard_map/reduce_scatter | solution.py:1307
  662.4 331.5 %reduce-scatter.9.cloned.1.call-start = ((), (), s32[]{:S(2)}) async-start(), calls=%async_computation.6 | async-start | bytes 7077888 | tf_op jit(solution)/shard_map/reduce_scatter | solution.py:1307
  751.3 4.1 copy-start.9
  769.9 0.9 copy-start.2
  769.9 1.1 copy-start.5
  769.9 1.2 copy-start.7
  769.9 1.2 copy-start.3
  822.5 65.8 %copy-start.4 = (f32[1,2048]{1,0:T(1,128)S(1)}, f32[1,2048]{1,0:T(1,128)}, u32[]{:S(2)}) copy-start(f32[1,2048]{1,0:T(1,128)} %get-tuple-element.98) | copy-start | bytes 24580
  982.3 9.6 copy-start.1
  989.3 7.2 copy-start
Sparse Core Ops, SparseCore 0:
  9.7 97.3 all-gather.8
  108.7 27.7 all-gather.10
  138.1 104.6 all-gather.14
  244.3 156.4 all-gather.12
  524.5 167.6 reduce-scatter.4
  695.0 34.9 reduce-scatter.10
  732.3 87.4 reduce-scatter.6
  822.1 68.1 reduce-scatter.8

commit v4 on v3

--- a/solution.py
+++ b/solution.py
@@ -1,3 +1,5 @@
+import functools
+
 import jax
 import jax.numpy as jnp
 from jax import lax
@@ -16,6 +18,7 @@
 EPSILON = 1e-06
 MASKED_LOGIT = -1e30
 BIG_VMEM = 60 * 1024 * 1024
+SHORT = pl.CostEstimate(flops=1000, bytes_accessed=1000, transcendentals=0)
 
 
 def feature_map(values):
@@ -84,10 +87,17 @@
 
 
 def attend_kernel(
-    offsets_ref, lengths_ref, gate_ref, qkv_ref, memory_ref, norm_ref,
-    attn_ref, dot_ref, part_ref, logsum_ref, memory_new_ref, norm_new_ref,
+    size, offsets_ref, lengths_ref, gate_ref, qkv_ref, memory_ref, norm_ref, cot_ref,
+    attn_ref, dot_ref, part_ref, logsum_ref, memory_new_ref, norm_new_ref, all_cot_ref,
+    send, receive, own,
 ):
     head = pl.program_id(0)
+    gather = Gather(size, cot_ref, all_cot_ref, send, receive, own)
+
+    @pl.when(head == 0)
+    def _():
+        gather.start(hold=False)
+
     gate = gate_ref[head]
     q_ref, k_ref, v_ref = qkv_ref.at[0, 0], qkv_ref.at[1, 0], qkv_ref.at[2, 0]
     memory_one = memory_ref[0]
@@ -121,6 +131,14 @@
     memory_new_ref[0] = memory_one + (plain_dot(high, v, TN) + plain_dot(low, v, TN)) / PROMPT
     norm_new_ref[0] = norm_one + jnp.mean(lifted_keys, axis=0, keepdims=True)
 
+    @pl.when(head == pl.num_programs(0) - 1)
+    def _():
+        gather.forward()
+        for step in range(size - 1):
+            gather.wait(step)
+        gather.keep.wait()
+        gather.finish()
+
 
 def head_block(shape, lead=0):
     zeros = (0,) * (len(shape) - 1 - lead)
@@ -130,21 +148,22 @@
 SMEM_SPEC = pl.BlockSpec(memory_space=pltpu.SMEM)
 
 
-def attend(heads_all, memory_one, norm_one, offsets, lengths, gate_value):
+def attend(size, cot, heads_all, memory_one, norm_one, offsets, lengths, gate_value):
     heads = heads_all.shape[1]
     f32 = jnp.float32
     row_block = head_block((1, GLEN, HD))
     column = pl.BlockSpec((GLEN, HD), lambda h: (0, h))
     return pl.pallas_call(
-        attend_kernel,
+        functools.partial(attend_kernel, size),
         grid=(heads,),
         in_specs=[
             SMEM_SPEC, SMEM_SPEC, SMEM_SPEC,
             head_block((3, 1, GLEN, HD), 1), head_block((1, HD, HD)), head_block((1, 1, HD)),
+            ANY,
         ],
         out_specs=[
             column, row_block, row_block, head_block((1, GLEN, 1)),
-            head_block((1, HD, HD)), head_block((1, 1, HD)),
+            head_block((1, HD, HD)), head_block((1, 1, HD)), ANY,
         ],
         out_shape=[
             jax.ShapeDtypeStruct((GLEN, heads * HD), jnp.bfloat16),
@@ -153,13 +172,13 @@
             jax.ShapeDtypeStruct((heads, GLEN, 1), f32),
             jax.ShapeDtypeStruct((heads, HD, HD), f32),
             jax.ShapeDtypeStruct((heads, 1, HD), f32),
+            bf(size, GLEN // size, D),
         ],
-        compiler_params=pltpu.CompilerParams(vmem_limit_bytes=BIG_VMEM),
-        cost_estimate=pl.CostEstimate(
-            flops=heads * 800_000_000, bytes_accessed=heads * 6_000_000, transcendentals=heads * 1_300_000
-        ),
+        scratch_shapes=[dma(Gather.semaphores(size)), dma(Gather.semaphores(size)), pltpu.SemaphoreType.DMA],
+        compiler_params=comm_params(9),
+        cost_estimate=SHORT,
         name="attend",
-    )(offsets, lengths, gate_value, heads_all, memory_one, norm_one[:, None, :])
+    )(offsets, lengths, gate_value, heads_all, memory_one, norm_one[:, None, :], cot)
 
 
 def attend_back_kernel(
@@ -235,9 +254,7 @@
         ],
         scratch_shapes=[pltpu.VMEM((GLEN, HD), f32), pltpu.VMEM((GLEN, HD), f32)],
         compiler_params=pltpu.CompilerParams(vmem_limit_bytes=BIG_VMEM),
-        cost_estimate=pl.CostEstimate(
-            flops=heads * 2_000_000_000, bytes_accessed=heads * 6_000_000, transcendentals=heads * 1_300_000
-        ),
+        cost_estimate=SHORT,
         name="attend_back",
     )(
         offsets, lengths, gate_value, heads_all, grad_heads, dot_part, memory_part, logsum,
@@ -259,6 +276,10 @@
     )
 
 
+def here():
+    return lax.axis_index("row"), lax.axis_index("col")
+
+
 def greet(peers):
     barrier = pltpu.get_barrier_semaphore()
     for peer in peers:
@@ -275,90 +296,78 @@
 
 class Gather:
     def __init__(self, size, source, land, send, receive, own):
-        self.size, self.source, self.land = size, source, land
-        self.send, self.receive, self.own = send, receive, own
-        self.row, self.col = lax.axis_index("row"), lax.axis_index("col")
-        self.piece = source.shape[0]
+        self.size = size
+        row, col = self.row, self.col = here()
+        piece = source.shape[0]
+        self.keep = pltpu.make_async_copy(source, land.at[row], own)
+        if size != 4:
+            self.peers = [(lax.rem(row + d, size), col) for d in range(1, size)]
+            self.order = [lax.rem(row + size - d, size) for d in range(1, size)]
+            self.copies = [
+                remote(source, land.at[row], send.at[i], receive.at[i], peer) for i, peer in enumerate(self.peers)
+            ]
+            return
+        self.order = rx, ry, rd = square(row)
+        px, py = self.peers = [(rx, col), (ry, col)]
+        height = piece // AG_CUTS
+        cuts = [pl.ds(cut * height, height) for cut in range(AG_CUTS)]
+
+        def out(cut, base, peer):
+            return remote(
+                source.at[cuts[cut]], land.at[row, cuts[cut]], send.at[base + cut], receive.at[base + cut], peer
+            )
+
+        def onward(cut, owner, peer):
+            place = land.at[owner, cuts[cut]]
+            return remote(place, place, send.at[2 * AG_CUTS + cut], receive.at[2 * AG_CUTS + cut], peer)
+
+        middle = AG_CUTS // 2
+        self.to_x = [out(cut, 0, px) for cut in range(AG_CUTS)]
+        self.to_y = [out(cut, AG_CUTS, py) for cut in range(AG_CUTS)]
+        self.onward = [onward(cut, rx, py) for cut in range(middle)] + [
+            onward(cut, ry, px) for cut in range(middle, AG_CUTS)
+        ]
 
     @staticmethod
     def semaphores(size):
         return 3 * AG_CUTS if size == 4 else size - 1
 
-    def at(self, cut):
-        height = self.piece // AG_CUTS
-        return pl.ds(cut * height, height)
-
-    def start(self, greeted=False):
-        row, col = self.row, self.col
+    def start(self, greeted=False, hold=True):
+        if not greeted:
+            greet(self.peers)
         if self.size != 4:
-            peers = [lax.rem(row + d, self.size) for d in range(1, self.size)]
-            if not greeted:
-                greet([(peer, col) for peer in peers])
-            self.order = [lax.rem(row + self.size - d, self.size) for d in range(1, self.size)]
-            self.copies = [
-                remote(self.source, self.land.at[row], self.send.at[i], self.receive.at[i], (peer, col))
-                for i, peer in enumerate(peers)
-            ]
             for copy in self.copies:
                 copy.start()
         else:
-            rx, ry, rd = square(row)
-            self.order = [rx, ry, rd]
-            self.px, self.py = (rx, col), (ry, col)
-            if not greeted:
-                greet([self.px, self.py])
-            self.to_x, self.to_y, self.onward = {}, {}, []
             for step in range(AG_CUTS):
-                for table, peer, base, cut in (
-                    (self.to_x, self.px, 0, step),
-                    (self.to_y, self.py, AG_CUTS, (step + AG_CUTS // 2) % AG_CUTS),
-                ):
-                    table[cut] = remote(
-                        self.source.at[self.at(cut)], self.land.at[row, self.at(cut)],
-                        self.send.at[base + cut], self.receive.at[base + cut], peer,
-                    )
-                    table[cut].start()
-        self.keep = pltpu.make_async_copy(self.source, self.land.at[row], self.own)
+                self.to_x[step].start()
+                self.to_y[(step + AG_CUTS // 2) % AG_CUTS].start()
         self.keep.start()
-        self.keep.wait()
+        if hold:
+            self.keep.wait()
 
     def forward(self):
         if self.size != 4:
             return
-        rx, ry, _ = self.order
         for step in range(AG_CUTS // 2):
-            for table, peer, owner, cut in (
-                (self.to_x, self.py, rx, step),
-                (self.to_y, self.px, ry, step + AG_CUTS // 2),
-            ):
-                table[cut].wait_recv()
-                place = self.land.at[owner, self.at(cut)]
-                copy = remote(
-                    place, place, self.send.at[2 * AG_CUTS + cut], self.receive.at[2 * AG_CUTS + cut], peer
-                )
-                copy.start()
-                self.onward.append(copy)
+            later = step + AG_CUTS // 2
+            self.to_x[step].wait_recv()
+            self.onward[step].start()
+            self.to_y[later].wait_recv()
+            self.onward[later].start()
 
     def wait(self, step):
+        middle = AG_CUTS // 2
         if self.size != 4:
-            self.copies[step].wait_recv()
-        elif step == 0:
-            for cut in range(AG_CUTS // 2, AG_CUTS):
-                self.to_x[cut].wait_recv()
-        elif step == 1:
-            for cut in range(AG_CUTS // 2):
-                self.to_y[cut].wait_recv()
+            waits = [self.copies[step]]
         else:
-            for copy in self.onward:
-                copy.wait_recv()
+            waits = (self.to_x[middle:], self.to_y[:middle], self.onward)[step]
+        for copy in waits:
+            copy.wait_recv()
         return self.order[step]
 
     def finish(self):
-        if self.size != 4:
-            for copy in self.copies:
-                copy.wait_send()
-            return
-        for copy in [*self.to_x.values(), *self.to_y.values(), *self.onward]:
+        for copy in self.copies if self.size != 4 else [*self.to_x, *self.to_y, *self.onward]:
             copy.wait_send()
 
 
@@ -530,7 +539,10 @@
     cols, _, depth, width = w_all.shape
     heads = width // HD
 
-    def kernel(x_ref, w_ref, heads_ref, all_ref, land, send, receive, own, w, w_sem, all_sem):
+    def kernel(
+        x_ref, w_ref, heads_ref, all_ref,
+        land, send, receive, own, w, w_sem, all_sem,
+    ):
         loads = fetches([(w_ref.at[c], w.at[:, pl.ds(c * depth, depth), :]) for c in range(cols)], w_sem)
         gather = Gather(size, x_ref, land, send, receive, own)
         gather.start()
@@ -568,7 +580,7 @@
             pltpu.SemaphoreType.DMA((size,)),
         ],
         compiler_params=comm_params(1),
-        cost_estimate=pl.CostEstimate(flops=6 * GLEN * D * width, bytes_accessed=40_000_000, transcendentals=0),
+        cost_estimate=SHORT,
         name="project_heads",
     )(normed, w_all)
 
@@ -636,35 +648,43 @@
         scratch_shapes=scatter_scratch(size, piece)
         + [pltpu.VMEM((width, D), jnp.bfloat16), pltpu.SemaphoreType.DMA((cols,))],
         compiler_params=comm_params(2),
-        cost_estimate=pl.CostEstimate(flops=2 * GLEN * D * width, bytes_accessed=40_000_000, transcendentals=0),
+        cost_estimate=SHORT,
         name="branch_out",
     )(attn, w_all, x, gain)
 
 
-def feed_forward(size, normed, w_gu, w_down, cot):
-    piece = normed.shape[0]
-    cols, _, depth, wide = w_gu.shape
+def feed_forward(size, tokens, pack, cot, first):
+    piece = GLEN // size
+    cols, _, depth, wide = pack.shape
     tile = min(wide, 512)
-
-    def kernel(
-        x_ref, gu_ref, down_ref, cot_ref, hidden_ref, grad_ref, all_ref,
-        land, send, receive, own, gu, down, cot_all, back, stage, gu_sem, down_sem, cot_sem, out_sem, all_sem,
-    ):
-        down_loads = fetches(
-            [(down_ref.at[c], down.at[:, pl.ds(c * depth, depth)]) for c in range(cols)], down_sem
+    count = wide // tile
+
+    def kernel(x_ref, pack_ref, cot_ref, hidden_ref, grad_ref, *rest):
+        if first:
+            all_ref, land, send, receive, own, all_sem, *rest = rest
+        else:
+            land, own, *rest = rest
+        w, cot_all, back, stage, w_sem, cot_sem, out_sem = rest
+        if first:
+            gather = Gather(size, x_ref, land, send, receive, own)
+            gather.start()
+            order = [gather.row, *gather.order]
+        else:
+            order = list(range(size))
+        w_loads = fetches(
+            [(pack_ref.at[c, j], w.at[j, pl.ds(c * depth, depth), :]) for j in (2, 0, 1) for c in range(cols)], w_sem
         )
-        cot_load = pltpu.make_async_copy(cot_ref, cot_all, cot_sem)
-        cot_load.start()
-        gu_loads = fetches([(gu_ref.at[c], gu.at[:, pl.ds(c * depth, depth), :]) for c in range(cols)], gu_sem)
-        gather = Gather(size, x_ref, land, send, receive, own)
-        gather.start()
-        wait_all(down_loads)
-        cot_load.wait()
-
-        def backward(row):
+        cot_loads = fetches([(cot_ref.at[row], cot_all.at[row]) for row in order], cot_sem)
+        if not first:
+            x_loads = fetches([(x_ref.at[row], land.at[row]) for row in order], own)
+
+        def backward(step):
+            row = order[step]
+            cot_loads[step].wait()
+
             @tiles_of(wide, tile)
             def _(t, columns):
-                back[row, :, columns] = plain_dot(cot_all[row], down[columns, :], NT).astype(jnp.bfloat16)
+                back[row, :, columns] = plain_dot(cot_all[row], w[2, :, columns], NN).astype(jnp.bfloat16)
 
         def moves(row, slot, columns):
             rows = pl.ds(pl.multiple_of(row * piece, piece), piece)
@@ -674,18 +694,19 @@
                 pltpu.make_async_copy(stage.at[slot, 2], grad_ref.at[1, rows, columns], out_sem.at[slot, 2]),
             ]
 
-        count = wide // tile
-
-        def compute(row, first):
-            pltpu.make_async_copy(land.at[row], all_ref.at[row], all_sem).start()
+        def compute(step):
+            row = order[step]
+            if first:
+                store = pltpu.make_async_copy(land.at[row], all_ref.at[row], all_sem)
+                store.start()
 
             @pl.loop(0, count)
             def _(t):
                 columns = pl.ds(pl.multiple_of(t * tile, tile), tile)
                 slot = lax.rem(t, 2)
                 x = land[row]
-                gate_pre = jnp.dot(x, gu[0, :, columns], preferred_element_type=jnp.float32)
-                up_pre = jnp.dot(x, gu[1, :, columns], preferred_element_type=jnp.float32)
+                gate_pre = jnp.dot(x, w[0, :, columns], preferred_element_type=jnp.float32)
+                up_pre = jnp.dot(x, w[1, :, columns], preferred_element_type=jnp.float32)
                 sigmoid = jax.nn.sigmoid(gate_pre)
                 silu = gate_pre * sigmoid
                 grad_hidden = back[row, :, columns].astype(jnp.float32)
@@ -702,40 +723,74 @@
 
             for slot in range(min(2, count)):
                 wait_all(moves(row, slot, pl.ds(slot * tile, tile)))
-            pltpu.make_async_copy(land.at[row], all_ref.at[row], all_sem).wait()
-
-        backward(gather.row)
-        gather.forward()
-        for step in range(size - 1):
-            backward(gather.order[step])
-        wait_all(gu_loads)
-        compute(gather.row, True)
-        for step in range(size - 1):
-            compute(gather.wait(step), False)
-        gather.finish()
-
+            if first:
+                store.wait()
+
+        wait_all(w_loads[:cols])
+        backward(0)
+        if first:
+            gather.forward()
+        for step in range(1, size):
+            backward(step)
+        wait_all(w_loads[cols:])
+        for step in range(size):
+            if not first:
+                x_loads[step].wait()
+            elif step:
+                gather.wait(step - 1)
+            compute(step)
+        if first:
+            gather.finish()
+
+    out_shape = [bf(GLEN, wide), bf(2, GLEN, wide)]
+    if first:
+        out_shape.append(bf(size, piece, D))
+        scratch = gather_scratch(size, piece) + [pltpu.SemaphoreType.DMA]
+    else:
+        scratch = [pltpu.VMEM((size, piece, D), jnp.bfloat16), dma(size)]
     return pl.pallas_call(
         kernel,
-        out_shape=[bf(GLEN, wide), bf(2, GLEN, wide), bf(size, piece, D)],
-        in_specs=[ANY, ANY, ANY, ANY],
-        out_specs=[ANY, ANY, ANY],
-        scratch_shapes=gather_scratch(size, piece)
+        out_shape=out_shape,
+        in_specs=[ANY] * 3,
+        out_specs=[ANY] * len(out_shape),
+        scratch_shapes=scratch
         + [
-            pltpu.VMEM((2, D, wide), jnp.bfloat16),
-            pltpu.VMEM((wide, D), jnp.bfloat16),
+            pltpu.VMEM((3, D, wide), jnp.bfloat16),
             pltpu.VMEM((size, piece, D), jnp.bfloat16),
             pltpu.VMEM((size, piece, wide), jnp.bfloat16),
             pltpu.VMEM((2, 3, piece, tile), jnp.bfloat16),
-            pltpu.SemaphoreType.DMA((cols,)),
-            pltpu.SemaphoreType.DMA((cols,)),
-            pltpu.SemaphoreType.DMA,
-            pltpu.SemaphoreType.DMA((2, 3)),
-            pltpu.SemaphoreType.DMA,
+            dma(3 * cols), dma(size), dma(2, 3),
         ],
-        compiler_params=comm_params(3),
-        cost_estimate=pl.CostEstimate(flops=6 * GLEN * D * wide, bytes_accessed=70_000_000, transcendentals=GLEN * wide),
-        name="feed_forward",
-    )(normed, w_gu, w_down, cot.reshape(size, piece, D))
+        compiler_params=comm_params(3) if first else pltpu.CompilerParams(vmem_limit_bytes=BIG_VMEM),
+        cost_estimate=SHORT,
+        name="feed_first" if first else "feed_second",
+    )(tokens, pack, cot)
+
+
+def weight_grads_kernel(x_ref, y_ref, g_ref, h_ref, out_ref):
+    for j in range(2):
+        out_ref[j] = plain_dot(x_ref[...], g_ref[j], TN).astype(jnp.bfloat16)
+    out_ref[2] = plain_dot(y_ref[...], h_ref[...], TN).astype(jnp.bfloat16)
+
+
+def weight_grads(x, grads, y, hidden):
+    wide = hidden.shape[1]
+    tile = 256
+    block = pl.BlockSpec((GLEN, tile), lambda i: (0, i))
+    return pl.pallas_call(
+        weight_grads_kernel,
+        grid=(D // tile,),
+        in_specs=[
+            block, block,
+            pl.BlockSpec((2, GLEN, wide), lambda i: (0, 0, 0), pipeline_mode=pl.Buffered(1)),
+            pl.BlockSpec((GLEN, wide), lambda i: (0, 0), pipeline_mode=pl.Buffered(1)),
+        ],
+        out_specs=pl.BlockSpec((3, tile, wide), lambda i: (0, i, 0)),
+        out_shape=bf(3, D, wide),
+        compiler_params=pltpu.CompilerParams(vmem_limit_bytes=BIG_VMEM),
+        cost_estimate=SHORT,
+        name="weight_grads",
+    )(x, y, grads, hidden)
 
 
 def norm_back(rows, total, stream, inverse, gain_ref, base, store, gain_sum):
@@ -746,32 +801,74 @@
         gain_sum[:, columns] += jnp.sum(total[half, rows, :] * stream[half] * inverse, axis=0, keepdims=True)
 
 
-def middle_back(size, grads, w_gu, middle, cot, gain):
+def middle_back(size, grads, packs, middle, cot, gain):
     piece = middle.shape[0]
-    cols, _, depth, wide = w_gu.shape
+    cols, _, depth, wide = packs[0].shape
     tile = 512
+    halves = len(packs)
 
     def kernel(
-        g_ref, gu_ref, middle_ref, cot_ref, gain_ref, grad_ref, low_ref, gain_sum,
-        stage, land, total, send, receive, gu, g, gu_sem, g_sem,
+        *refs,
     ):
-        loads = fetches([(gu_ref.at[c], gu.at[:, pl.ds(c * depth, depth), :]) for c in range(cols)], gu_sem)
+        g_refs, pack_refs, refs = refs[:halves], refs[halves : 2 * halves], refs[2 * halves :]
+        (middle_ref, cot_ref, gain_ref, grad_ref, low_ref, gain_sum,
+         stage, land, total, send, receive, w, g, w_sem, g_sem) = refs
+        row, _ = here()
+        rows_order = [*reversed(square(row)), row] if size == 4 else [lax.rem(row + d, size) for d in range(size)]
+        if size == 4:
+            rows_order = [rows_order[0], rows_order[2], rows_order[1], row]
+
+        def piece_rows(at):
+            return pl.ds(pl.multiple_of(at * piece, piece), piece)
+
+        def g_load(h, at):
+            return pltpu.make_async_copy(
+                g_refs[h].at[:, piece_rows(at)], g.at[h, :, piece_rows(at)], g_sem.at[h, at]
+            )
+
+        def w_load(h, c):
+            return pltpu.make_async_copy(
+                pack_refs[h].at[c, pl.ds(0, 2)], w.at[h, :, pl.ds(c * depth, depth), :], w_sem.at[h, c]
+            )
+
+        for h in range(halves):
+            g_load(h, rows_order[0]).start()
+        for c in range(cols):
+            for h in range(halves):
+                w_load(h, c).start()
+        for at in rows_order[1:]:
+            for h in range(halves):
+                g_load(h, at).start()
         scatter = Scatter(size, stage, land, total, send, receive)
-        g_loads = fetches([(g_ref.at[j], g.at[j]) for j in range(2)], g_sem)
-        wait_all(g_loads)
-        wait_all(loads)
         gain_sum[...] = jnp.zeros_like(gain_sum)
-
-        def partial(row, store):
-            rows = pl.ds(pl.multiple_of(row * piece, piece), piece)
+        calls = []
+
+        def one(rows, depth_rows, store, half, columns):
+            value = 0.0
+            for h in range(halves):
+                for j in range(2):
+                    value += plain_dot(g[h, j, rows, :], w[h, j, depth_rows, :], NT)
+            store(half, columns, value)
+
+        def partial(at, store):
+            fresh = not calls
+            calls.append(at)
+            for h in range(halves):
+                g_load(h, at).wait()
+            rows = piece_rows(at)
+            if fresh:
+                for t in range(D // tile):
+                    for c in range(t * tile // depth, (t + 1) * tile // depth):
+                        for h in range(halves):
+                            w_load(h, c).wait()
+                    half, inside = divmod(t * tile, HALF)
+                    one(rows, slice(t * tile, (t + 1) * tile), store, half, slice(inside, inside + tile))
+                return
             for half in range(2):
                 @pl.loop(0, HALF // tile)
                 def _(t):
                     columns = pl.ds(pl.multiple_of(t * tile, tile), tile)
-                    depth_rows = pl.ds(pl.multiple_of(half * HALF + t * tile, tile), tile)
-                    value = plain_dot(g[0, rows, :], gu[0, depth_rows, :], NT)
-                    value += plain_dot(g[1, rows, :], gu[1, depth_rows, :], NT)
-                    store(half, columns, value)
+                    one(rows, pl.ds(pl.multiple_of(half * HALF + t * tile, tile), tile), store, half, columns)
 
         scatter.run(partial)
 
@@ -791,19 +888,18 @@
     return pl.pallas_call(
         kernel,
         out_shape=[fl(piece, D), bf(piece, D), fl(1, D)],
-        in_specs=[ANY, ANY, VMEM, VMEM, VMEM],
+        in_specs=[ANY] * (2 * halves) + [VMEM] * 3,
         out_specs=[VMEM, VMEM, VMEM],
         scratch_shapes=scatter_scratch(size, piece)
         + [
-            pltpu.VMEM((2, D, wide), jnp.bfloat16),
-            pltpu.VMEM((2, GLEN, wide), jnp.bfloat16),
-            pltpu.SemaphoreType.DMA((cols,)),
-            pltpu.SemaphoreType.DMA((2,)),
+            pltpu.VMEM((halves, 2, D, wide), jnp.bfloat16),
+            pltpu.VMEM((halves, 2, GLEN, wide), jnp.bfloat16),
+            dma(halves, cols), dma(halves, size),
         ],
         compiler_params=comm_params(4),
-        cost_estimate=pl.CostEstimate(flops=4 * GLEN * D * wide, bytes_accessed=60_000_000, transcendentals=0),
+        cost_estimate=SHORT,
         name="middle_back",
-    )(grads, w_gu, middle, cot, gain)
+    )(*grads, *packs, middle, cot, gain)
 
 
 def blocked_store(ref, rows, depth, columns, value):
@@ -811,24 +907,46 @@
         ref[columns.start // depth + i, rows, :] = value[:, i * depth : (i + 1) * depth]
 
 
-def ffn_out(size, hidden, w_down, middle):
+def ffn_out(size, hiddens, packs, middle):
     piece = middle.shape[0]
-    cols, wide, depth = w_down.shape
+    cols, _, depth, wide = packs[0].shape
     tile = 512
-
-    def kernel(h_ref, w_ref, middle_ref, out_ref, stat_ref, stage, land, total, send, receive, w, w_sem):
-        loads = fetches([(w_ref.at[c], w.at[:, pl.ds(c * depth, depth)]) for c in range(cols)], w_sem)
+    halves = len(packs)
+
+    def kernel(*refs):
+        h_refs, pack_refs, refs = refs[:halves], refs[halves : 2 * halves], refs[2 * halves :]
+        middle_ref, out_ref, stat_ref, stage, land, total, send, receive, w, w_sem = refs
+
+        def w_load(h, c):
+            return pltpu.make_async_copy(
+                pack_refs[h].at[c, 2], w.at[h, pl.ds(c * depth, depth), :], w_sem.at[h, c]
+            )
+
+        for c in range(cols):
+            for h in range(halves):
+                w_load(h, c).start()
         scatter = Scatter(size, stage, land, total, send, receive)
-        wait_all(loads)
-
-        def partial(row, store):
-            rows = pl.ds(pl.multiple_of(row * piece, piece), piece)
+        calls = []
+
+        def one(rows, depth_rows, store, half, columns):
+            value = 0.0
+            for h in range(halves):
+                value += plain_dot(h_refs[h][rows, :], w[h, depth_rows, :], NT)
+            store(half, columns, value)
+
+        def partial(at, store):
+            fresh = not calls
+            calls.append(at)
+            rows = pl.ds(pl.multiple_of(at * piece, piece), piece)
+            if fresh:
+                for c in range(cols):
+                    for h in range(halves):
+                        w_load(h, c).wait()
             for half in range(2):
                 @pl.loop(0, HALF // tile)
                 def _(t):
                     columns = pl.ds(pl.multiple_of(t * tile, tile), tile)
-                    whole = pl.ds(pl.multiple_of(half * HALF + t * tile, tile), tile)
-                    store(half, columns, jnp.dot(h_ref[rows, :], w[:, whole], preferred_element_type=jnp.float32))
+                    one(rows, pl.ds(pl.multiple_of(half * HALF + t * tile, tile), tile), store, half, columns)
 
         scatter.run(partial)
 
@@ -847,14 +965,14 @@
     return pl.pallas_call(
         kernel,
         out_shape=[bf(cols, piece, depth), fl(piece, HD)],
-        in_specs=[VMEM, ANY, VMEM],
+        in_specs=[VMEM] * halves + [ANY] * halves + [VMEM],
         out_specs=[VMEM, VMEM],
         scratch_shapes=scatter_scratch(size, piece)
-        + [pltpu.VMEM((wide, D), jnp.bfloat16), pltpu.SemaphoreType.DMA((cols,))],
+        + [pltpu.VMEM((halves, D, wide), jnp.bfloat16), dma(halves, cols)],
         compiler_params=comm_params(5),
-        cost_estimate=pl.CostEstimate(flops=2 * GLEN * D * wide, bytes_accessed=50_000_000, transcendentals=0),
+        cost_estimate=SHORT,
         name="ffn_out",
-    )(hidden, w_down, middle)
+    )(*hiddens, *packs, middle)
 
 
 def branch_back(size, low, w_all):
@@ -896,7 +1014,7 @@
             pltpu.SemaphoreType.DMA((size,)),
         ],
         compiler_params=comm_params(6),
-        cost_estimate=pl.CostEstimate(flops=2 * GLEN * D * width, bytes_accessed=40_000_000, transcendentals=0),
+        cost_estimate=SHORT,
         name="branch_back",
     )(low, w_all)
 
@@ -949,13 +1067,9 @@
         scratch_shapes=scatter_scratch(size, piece)
         + [pltpu.VMEM((3, D, width), jnp.bfloat16), pltpu.SemaphoreType.DMA((cols,))],
         compiler_params=comm_params(7),
-        cost_estimate=pl.CostEstimate(flops=6 * GLEN * D * width, bytes_accessed=50_000_000, transcendentals=0),
+        cost_estimate=SHORT,
         name="stream_back",
     )(grads, w_all, x, grad_middle, gain)
-
-
-def here():
-    return lax.axis_index("row"), lax.axis_index("col")
 
 
 def row_and_col_peers(size, cols):
@@ -1100,13 +1214,18 @@
     return block.reshape(block.shape[0] // GLEN, size, GLEN // size, block.shape[1])
 
 
-def enter(size, cols, stream_in, gains):
+def enter(size, cols, stream_in, cotangent, gains):
     pieces = by_pieces(stream_in, size)
     piece, depth = pieces.shape[2:]
-
-    def kernel(x_ref, gains_ref, tokens_ref, normed_ref, gain_in_ref, gain_mid_ref, gains_land, gains_send, gains_receive, *rest):
+    scratch = Inward.scratch(size, cols, piece, depth)
+
+    def kernel(
+        x_ref, cot_ref, gains_ref, tokens_ref, normed_ref, gain_in_ref, gain_mid_ref, cot_tokens_ref,
+        gains_land, gains_send, gains_receive, *rest,
+    ):
         greet(row_and_col_peers(size, cols))
-        exchange = Inward(size, cols, x_ref, *rest)
+        exchange = Inward(size, cols, x_ref, *rest[: len(scratch)])
+        second = Inward(size, cols, cot_ref, *rest[len(scratch) :])
         exchange.start()
         row, col = here()
         copies = []
@@ -1117,7 +1236,9 @@
             )
             copies[-1].start()
         gains_land[col] = gains_ref[...]
+        second.start()
         exchange.forward()
+        second.forward()
         for copy in copies:
             copy.wait()
         for c in range(cols):
@@ -1141,56 +1262,25 @@
                 ).astype(jnp.bfloat16)
 
         strip_loop(piece, norm)
+        second.finish()
+
+        def assemble(rows):
+            for c in range(cols):
+                cot_tokens_ref[rows, c * depth : (c + 1) * depth] = second.land[c, rows, :]
+
+        strip_loop(piece, assemble)
 
     return pl.pallas_call(
         kernel,
-        out_shape=[bf(piece, D), bf(piece, D), fl(1, D), fl(1, D)],
-        in_specs=[ANY, VMEM],
-        out_specs=[VMEM] * 4,
+        out_shape=[bf(piece, D), bf(piece, D), fl(1, D), fl(1, D), bf(piece, D)],
+        in_specs=[ANY, ANY, VMEM],
+        out_specs=[VMEM] * 5,
         scratch_shapes=[pltpu.VMEM((cols, 8, depth), jnp.float32), dma(cols - 1), dma(cols - 1)]
-        + Inward.scratch(size, cols, piece, depth),
+        + scratch * 2,
         compiler_params=comm_params(8),
-        cost_estimate=pl.CostEstimate(flops=8 * piece * D, bytes_accessed=40_000_000, transcendentals=0),
+        cost_estimate=SHORT,
         name="enter",
-    )(pieces, jnp.pad(gains, ((0, 6), (0, 0))))
-
-
-def spread(size, cols, cotangent):
-    pieces = by_pieces(cotangent, size)
-    piece, depth = pieces.shape[2:]
-    count = Gather.semaphores(size)
-
-    def kernel(x_ref, tokens_ref, all_ref, send, receive, own, *rest):
-        greet(row_and_col_peers(size, cols))
-        exchange = Inward(size, cols, x_ref, *rest)
-        exchange.start()
-        exchange.forward()
-        exchange.finish()
-        land = exchange.land
-
-        def assemble(rows):
-            for c in range(cols):
-                tokens_ref[rows, c * depth : (c + 1) * depth] = land[c, rows, :]
-
-        strip_loop(piece, assemble)
-        gather = Gather(size, tokens_ref, all_ref, send, receive, own)
-        gather.start(greeted=True)
-        gather.forward()
-        for step in range(size - 1):
-            gather.wait(step)
-        gather.finish()
-
-    return pl.pallas_call(
-        kernel,
-        out_shape=[bf(piece, D), bf(size, piece, D)],
-        in_specs=[ANY],
-        out_specs=[VMEM, ANY],
-        scratch_shapes=[dma(count), dma(count), pltpu.SemaphoreType.DMA]
-        + Inward.scratch(size, cols, piece, depth),
-        compiler_params=comm_params(9),
-        cost_estimate=pl.CostEstimate(flops=piece * D, bytes_accessed=60_000_000, transcendentals=0),
-        name="spread",
-    )(pieces)
+    )(pieces, by_pieces(cotangent, size), jnp.pad(gains, ((0, 6), (0, 0))))
 
 
 def leave(size, cols, blocks_out, blocks_grad, stats, sums):
@@ -1294,7 +1384,7 @@
         ]
         + Outward.scratch(size, cols, piece, depth) * 2,
         compiler_params=comm_params(10),
-        cost_estimate=pl.CostEstimate(flops=piece * D, bytes_accessed=60_000_000, transcendentals=0),
+        cost_estimate=SHORT,
         name="leave",
     )(blocks_out, blocks_grad, stats, sums)
 
@@ -1304,9 +1394,7 @@
 
 
 def over_col(partial, axis):
-    return lax.psum_scatter(
-        partial.astype(jnp.bfloat16), "col", scatter_dimension=axis, tiled=True
-    ).astype(jnp.float32)
+    return lax.psum_scatter(partial.astype(jnp.bfloat16), "col", scatter_dimension=axis, tiled=True)
 
 
 def flat(pieces):
@@ -1331,43 +1419,53 @@
     head_here = memory.shape[1]
     size = lax.axis_size("row")
     cols = lax.axis_size("col")
-    all_qkv, all_out, all_gu, all_down = (
-        lax.all_gather(w, "col", axis=0, tiled=False) for w in (w_qkv, w_out, w_gate_up, w_down)
-    )
+    all_qkv, all_out = (lax.all_gather(w, "col", axis=0, tiled=False) for w in (w_qkv, w_out))
     gate_value = jax.nn.sigmoid(gate_logit)
     group = (memory[0], memory_norm[0], offsets[0], lengths[0], gate_value)
-    stream, normed_in, gain_in, gain_mid = enter(
-        size, cols, stream_in, jnp.stack([gain_attn, gain_ffn])
+    stream, normed_in, gain_in, gain_mid, cot = enter(
+        size, cols, stream_in, cotangent, jnp.stack([gain_attn, gain_ffn])
     )
+    normed_in, w_gate_up, w_down = lax.optimization_barrier((normed_in, w_gate_up, w_down))
+    units = w_down.shape[0] // 2
+    packs = [
+        jnp.concatenate([w_gate_up[:, :, part], w_down[part].T[None]], axis=0)
+        for part in (slice(0, units), slice(units, None))
+    ]
+    all_packs = [lax.all_gather(pack, "col", axis=0, tiled=False) for pack in packs]
     heads_all, all_in = project_heads(size, normed_in, all_qkv)
-    attn, dot_part, memory_part, logsum, memory_new, norm_new = attend(heads_all, *group)
-    cotangent, attn = lax.optimization_barrier((cotangent, attn))
-    cot, all_cot = spread(size, cols, cotangent)
-    all_cot, attn = lax.optimization_barrier((all_cot, attn))
-    all_cot = all_cot.reshape(GLEN, D)
+    attn, dot_part, memory_part, logsum, memory_new, norm_new, all_cot = attend(size, cot, heads_all, *group)
     middle, normed_ffn, stat_branch = branch_out(size, attn, all_out, stream, gain_mid)
-    hidden, grad_gu, all_ffn = feed_forward(size, normed_ffn, all_gu, all_down, all_cot)
-    part_gu = jnp.einsum(
-        "td,jto->jdo", flat(all_ffn), grad_gu, preferred_element_type=jnp.float32
-    ).astype(jnp.bfloat16)
-    part_down = tokens_contract(hidden, all_cot).astype(jnp.bfloat16)
-    grad_gu, part_gu, part_down = lax.optimization_barrier((grad_gu, part_gu, part_down))
-    grad_gate_up = over_col(part_gu, 1)
-    grad_down = over_col(part_down, 1)
-    grad_middle, low_branch, part_gain_ffn = middle_back(size, grad_gu, all_gu, middle, cot, gain_mid)
+    hidden_first, grads_first, all_ffn = feed_forward(size, normed_ffn, all_packs[0], all_cot, True)
+    part_first = weight_grads(flat(all_ffn), grads_first, flat(all_cot), hidden_first)
+    part_first, all_ffn = lax.optimization_barrier((part_first, all_ffn))
+    scattered_first = over_col(part_first, 1)
+    hidden_second, grads_second = feed_forward(size, all_ffn, all_packs[1], all_cot, False)
+    part_second = weight_grads(flat(all_ffn), grads_second, flat(all_cot), hidden_second)
+    part_second, grads_second = lax.optimization_barrier((part_second, grads_second))
+    scattered_second = over_col(part_second, 1)
+    grad_middle, low_branch, part_gain_ffn = middle_back(
+        size, (grads_first, grads_second), all_packs, middle, cot, gain_mid
+    )
     grad_heads, all_branch = branch_back(size, low_branch, all_out)
     grads_qkv, gate_sums = attend_back(
         heads_all, grad_heads, dot_part, memory_part, logsum, *group
     )
-    hidden, grads_qkv = lax.optimization_barrier((hidden, grads_qkv))
-    blocks_out, stat_ffn = ffn_out(size, hidden, all_down, middle)
-    blocks_out, grads_qkv, grad_gate_up = lax.optimization_barrier((blocks_out, grads_qkv, grad_gate_up))
+    part_qkv = jnp.einsum(
+        "td,jto->jdo", flat(all_in), grads_qkv, preferred_element_type=jnp.float32
+    ).astype(jnp.bfloat16)
+    part_out = tokens_contract(attn, flat(all_branch)).astype(jnp.bfloat16)
+    hidden_first, grads_qkv, part_qkv, part_out, scattered_first = lax.optimization_barrier(
+        (hidden_first, grads_qkv, part_qkv, part_out, scattered_first)
+    )
+    blocks_out, stat_ffn = ffn_out(size, (hidden_first, hidden_second), all_packs, middle)
+    scattered_out, scattered_qkv = over_col(part_out, 1), over_col(part_qkv, 1)
+    blocks_out, grads_qkv, scattered_second = lax.optimization_barrier(
+        (blocks_out, grads_qkv, scattered_second)
+    )
     blocks_grad, part_gain_attn = stream_back(size, grads_qkv, all_qkv, stream, grad_middle, gain_in)
-    blocks_grad, grad_down = lax.optimization_barrier((blocks_grad, grad_down))
-    grad_out = over_col(tokens_contract(attn, flat(all_branch)), 1)
-    grad_qkv = over_col(
-        jnp.einsum("td,jto->jdo", flat(all_in), grads_qkv, preferred_element_type=jnp.float32), 1
-    )
+    grad_out, grad_qkv = scattered_out.astype(jnp.float32), scattered_qkv.astype(jnp.float32)
+    grad_gate_up = jnp.concatenate([scattered_first[:2], scattered_second[:2]], axis=2).astype(jnp.float32)
+    grad_down = jnp.concatenate([scattered_first[2], scattered_second[2]], axis=1).T.astype(jnp.float32)
     logit_part = gate_value * (1.0 - gate_value) * jnp.sum(gate_sums, axis=(1, 2))
     features_here = gain_attn.shape[0]
     sums = jnp.concatenate(

time: 1010 us -> 921 us (0.912)
  waiting for transfers between devices: 117 us -> 2.24 us
  Pallas kernels: 769 us -> 839 us
  matrix products: 74 us -> 23 us
    all_gather x4 -> x2, waiting for transfers between devices: 68 us -> 0.02 us  [local(): lax.all_gather(w, 'col', axis=0, tiled=False)]
    pallas_call x1, Pallas kernels: 69.2 us -> 125 us  [enter(): pl.pallas_call(kernel, out_shape=[bf(piece, D), bf(piece, D), fl(1, D), f...]
    reduce_scatter x4, waiting for transfers between devices: 46.2 us -> 0.03 us  [over_col(): lax.psum_scatter(partial.astype(jnp.bfloat16), 'col', scatter_dimension=a...]
    dot_general x1 -> x0, matrix products: 32.8 us -> none  [local(): jnp.einsum('td,jto->jdo', flat(all_ffn), grad_gu, preferred_element_type=...]
    dot_general x2 -> x1, matrix products: 26.8 us -> 7.65 us  [tokens_contract(): lax.dot_general(left, right, (TN, ((), ())), preferred_element_type=jnp.f...]
    pallas_call x3 -> x5, Pallas kernels: 201 us -> 213 us  [the longest x2 105 us: feed_forward(): pl.pallas_call(kernel, out_shape=out_shape, in_specs=[ANY] * 3, out_specs...]
  transfers between devices with their start and end apart: 8 -> 8, of which waited for: 3 -> 0; matrix products, arithmetic and copies ran while one was open for 5% -> 5% of each run, Pallas kernels for 69% -> 92%
where the time goes in v4:
time: 921 us; the launch traced here: 910 us
  Pallas kernels  839 us (91%)
  matrix products  23 us (2%)
  local copies, waits for them, and re-layouts  16.5 us (2%)
  between operations  14.9 us (2%)
  other arithmetic  13.9 us (2%)
    pallas_call x1, Pallas kernels, enter(): pl.pallas_call(kernel, out_shape=[bf(piece, D), bf(piece, D), fl(1, D), f...  125 us
    pallas_call x2, Pallas kernels, feed_forward(): pl.pallas_call(kernel, out_shape=out_shape, in_specs=[ANY] * 3, out_specs...  105 us
    pallas_call x1, Pallas kernels, leave(): pl.pallas_call(kernel, out_shape=[bf(groups, size, piece, depth), bf(grou...  97.6 us
    pallas_call x1, Pallas kernels, middle_back(): pl.pallas_call(kernel, out_shape=[fl(piece, D), bf(piece, D), fl(1, D)],...  71.1 us
    pallas_call x1, Pallas kernels, ffn_out(): pl.pallas_call(kernel, out_shape=[bf(cols, piece, depth), fl(piece, HD)],...  66.3 us
    pallas_call x1, Pallas kernels, stream_back(): pl.pallas_call(kernel, out_shape=[bf(cols, piece, depth), fl(1, D)], in_s...  65.3 us
    pallas_call x1, Pallas kernels, branch_out(): pl.pallas_call(kernel, out_shape=[fl(piece, D), bf(piece, D), fl(piece, H...  60.8 us
    pallas_call x1, Pallas kernels, project_heads(): pl.pallas_call(kernel, out_shape=[bf(3, heads, GLEN, HD), bf(size, piece,...  58.4 us
  transfers between devices with their start and end apart: 8, of which 0 were waited for; matrix products, arithmetic and copies ran while one was open for 5% of the time, Pallas kernels for 92%

profile of v4, /device:TPU:27, one launch (start us, length us, event | category | flops | bytes accessed | tf_op | source)
XLA Modules:
  0.0 909.8 jit_solution(5327242558969002279)
XLA Ops:
  7.2 0.7 all-gather.9.cloned.1.call-update
  8.0 0.7 all-gather.11.cloned.1.call-update
  8.7 1.3 select_maximum_fusion.gains_ref
  10.0 124.9 %enter.1 = (bf16[384,2048]{1,0:T(8,128)(2,1)}, bf16[384,2048]{1,0:T(8,128)(2,1)}, f32[1,2048]{1,0:T(1,128)}, f32[1,2048]{1,0:T(1,128)}, bf16[384,2048]{1,0:T(8,128)(2,1)}) custom-call(bf16[2,4,384,256]{3,2,1,0:T(8,128)(2,1)} %bitcast.70, bf16[2,4,384,256]{3,2,1,0:T(8,128)(2,1)} %bitcast.71, f32[8,256]{1,0:T(8,128)} %select_maximum_fusion.gains_ref), custom_call_target="tpu_custom_call" | custom-call | flops 1000 | bytes 1000 | tf_op jit(solution)/shard_map/enter/pallas_call | solution.py:1273
  134.9 1.6 copy.32
  136.5 0.9 slice_bitcast_fusion
  137.4 0.2 fusion.2
  137.6 1.3 pad_maximum_fusion
  138.9 0.0 all-gather.15.cloned.1.call-start
  139.0 1.3 pad_maximum_fusion.1
  140.3 0.0 reduce-scatter.5.cloned.1.call-start
  140.3 0.5 add_divide_fusion.gate_ref
  140.9 58.4 %project_heads.1 = (bf16[3,4,1536,128]{3,2,1,0:T(8,128)(2,1)}, bf16[4,384,2048]{2,1,0:T(8,128)(2,1)}) custom-call(bf16[384,2048]{1,0:T(8,128)(2,1)} %get-tuple-element.65.x_ref, bf16[8,3,256,512]{3,2,1,0:T(8,128)(2,1)} %bitcast.66), custom_call_target="tpu_custom_call" | custom-call | flops 1000 | bytes 1000 | tf_op jit(solution)/shard_map/project_heads/pallas_call | solution.py:571
  199.3 54.6 %attend.1 = (bf16[1536,512]{1,0:T(8,128)(2,1)}, f32[4,1536,128]{2,1,0:T(8,128)}, f32[4,1536,128]{2,1,0:T(8,128)}, f32[4,1536,1]{2,1,0:T(8,128)}, f32[4,128,128]{...) custom-call(s32[4]{0:T(128)} %bitcast.81, s32[4]{0:T(128)} %bitcast.83, f32[4]{0:T(128)} %add_divide_fusion.gate_ref, ...), custom_call_target="tpu_custom_call" | custom-call | flops 1000 | bytes 1000 | tf_op jit(solution)/shard_map/attend/pallas_call | solution.py:156
  253.9 60.8 %branch_out.1 = (f32[384,2048]{1,0:T(8,128)}, bf16[384,2048]{1,0:T(8,128)(2,1)}, f32[384,128]{1,0:T(8,128)}) custom-call(bf16[1536,512]{1,0:T(8,128)(2,1)} %get-tuple-element.68.attn_ref, bf16[8,512,256]{2,1,0:T(8,128)(2,1)} %bitcast.68, bf16[384,2048]{1,0:T(8,128)(2,1)} %get-tuple-element.69.x_ref, f32[1,2048]{1,0:T(1,128)} %get-tuple-element.70.gain_ref.refs_6_), custom_call_target="tpu_custom_call" | custom-call | flops 1000 | bytes 1000 | tf_op jit(solution)/shard_map/branch_out/pallas_call | solution.py:643
  314.7 58.9 %feed_first.1 = (bf16[1536,1024]{1,0:T(8,128)(2,1)}, bf16[2,1536,1024]{2,1,0:T(8,128)(2,1)}, bf16[4,384,2048]{2,1,0:T(8,128)(2,1)}) custom-call(bf16[384,2048]{1,0:T(8,128)(2,1)} %get-tuple-element.71.x_ref, bf16[8,3,256,1024]{3,2,1,0:T(8,128)(2,1)} %bitcast.56, bf16[4,384,2048]{2,1,0:T(8,128)(2,1)} %get-tuple-element.74.cot_ref), custom_call_target="tpu_custom_call" | custom-call | flops 1000 | bytes 1000 | tf_op jit(solution)/shard_map/feed_first/pallas_call | solution.py:751
  373.6 26.8 %weight_grads.2 = bf16[3,2048,1024]{2,1,0:T(8,128)(2,1)} custom-call(bf16[1536,2048]{1,0:T(8,128)(2,1)} %bitcast.64, bf16[1536,2048]{1,0:T(8,128)(2,1)} %bitcast.62, bf16[2,1536,1024]{2,1,0:T(8,128)(2,1)} %get-tuple-element.76.g_ref.refs_0_, bf16[1536,1024]{1,0:T(8,128)(2,1)} %get-tuple-element.92.h_ref.refs_0_), custom_call_target="tpu_custom_call" | custom-call | flops 1000 | bytes 1000 | tf_op jit(solution)/shard_map/weight_grads/pallas_call | solution.py:780
  400.5 46.1 %feed_second.1 = (bf16[1536,1024]{1,0:T(8,128)(2,1)}, bf16[2,1536,1024]{2,1,0:T(8,128)(2,1)}) custom-call(bf16[4,384,2048]{2,1,0:T(8,128)(2,1)} %get-tuple-element.78.x_ref, bf16[8,3,256,1024]{3,2,1,0:T(8,128)(2,1)} %bitcast.59, bf16[4,384,2048]{2,1,0:T(8,128)(2,1)} %get-tuple-element.74.cot_ref), custom_call_target="tpu_custom_call" | custom-call | flops 1000 | bytes 1000 | tf_op jit(solution)/shard_map/feed_second/pallas_call | solution.py:751
  446.6 26.7 %weight_grads.3 = bf16[3,2048,1024]{2,1,0:T(8,128)(2,1)} custom-call(bf16[1536,2048]{1,0:T(8,128)(2,1)} %bitcast.65, bf16[1536,2048]{1,0:T(8,128)(2,1)} %bitcast.63, bf16[2,1536,1024]{2,1,0:T(8,128)(2,1)} %get-tuple-element.81.g_ref.refs_1_, bf16[1536,1024]{1,0:T(8,128)(2,1)} %get-tuple-element.80.h_ref.refs_1_), custom_call_target="tpu_custom_call" | custom-call | flops 1000 | bytes 1000 | tf_op jit(solution)/shard_map/weight_grads/pallas_call | solution.py:780
  473.4 71.1 %middle_back.1 = (f32[384,2048]{1,0:T(8,128)}, bf16[384,2048]{1,0:T(8,128)(2,1)}, f32[1,2048]{1,0:T(1,128)}) custom-call(bf16[2,1536,1024]{2,1,0:T(8,128)(2,1)} %get-tuple-element.76.g_ref.refs_0_, bf16[2,1536,1024]{2,1,0:T(8,128)(2,1)} %get-tuple-element.81.g_ref.refs_1_, bf16[8,3,256,1024]{3,2,1,0:T(8,128)(2,1)} %bitcast.57, ...), custom_call_target="tpu_custom_call" | custom-call | flops 1000 | bytes 1000 | tf_op jit(solution)/shard_map/middle_back/pallas_call | solution.py:888
  544.5 56.5 %branch_back.1 = (bf16[4,1536,128]{2,1,0:T(8,128)(2,1)}, bf16[4,384,2048]{2,1,0:T(8,128)(2,1)}) custom-call(bf16[384,2048]{1,0:T(8,128)(2,1)} %get-tuple-element.83.x_ref, bf16[8,512,256]{2,1,0:T(8,128)(2,1)} %bitcast.69), custom_call_target="tpu_custom_call" | custom-call | flops 1000 | bytes 1000 | tf_op jit(solution)/shard_map/branch_back/pallas_call | solution.py:1005
  601.0 25.1 %attend_back.1 = (bf16[3,1536,512]{2,1,0:T(8,128)(2,1)}, f32[4,1,128]{2,1,0:T(1,128)}) custom-call(s32[4]{0:T(128)} %bitcast.82, s32[4]{0:T(128)} %bitcast.84, f32[4]{0:T(128)} %add_divide_fusion.gate_ref, bf16[3,4,1536,128]{3,2,1,0:T(8,128)(2,1)} %get-tuple-element.66.qkv_ref, bf16[4,1536,128]{2,1,0:T(8,128)(2,1)} %get-tuple-element.84.grad_ref, ...), custom_call_target="tpu_custom_call" | custom-call | flops 1000 | bytes 1000 | tf_op jit(solution)/shard_map/attend_back/pallas_call | solution.py:239
  626.1 7.6 convolution_convert_fusion
  633.8 15.4 %convert_bitcast_fusion = bf16[3,2048,512]{1,2,0:T(8,128)(2,1)} fusion(bf16[3,1536,512]{2,1,0:T(8,128)(2,1)} %get-tuple-element.97.g_ref, bf16[1536,2048,1]{1,0,2:T(8,128)(2,1)} %bitcast.90), kind=kOutput, calls=%fused_computation | convolution fusion | flops 9666822144 | bytes 17301504 | tf_op jit(solution)/shard_map/td,jto->jdo/dot_general | solution.py:1453
  649.2 0.7 reduce-scatter.9.cloned.1.call-update
  649.9 0.2 copy-done.9
  650.1 0.1 copy.35
  650.2 0.1 reduce_sum.9
  650.4 66.3 %ffn_out.1 = (bf16[8,384,256]{2,1,0:T(8,128)(2,1)}, f32[384,128]{1,0:T(8,128)}) custom-call(bf16[1536,1024]{1,0:T(8,128)(2,1)} %get-tuple-element.92.h_ref.refs_0_, bf16[1536,1024]{1,0:T(8,128)(2,1)} %get-tuple-element.80.h_ref.refs_1_, bf16[8,3,256,1024]{3,2,1,0:T(8,128)(2,1)} %bitcast.58, bf16[8,3,256,1024]{3,2,1,0:T(8,128)(2,1)} %bitcast.61, ...), custom_call_target="tpu_custom_call" | custom-call | flops 1000 | bytes 1000 | tf_op jit(solution)/shard_map/ffn_out/pallas_call | solution.py:965
  716.7 65.3 %stream_back.1 = (bf16[8,384,256]{2,1,0:T(8,128)(2,1)}, f32[1,2048]{1,0:T(1,128)}) custom-call(bf16[3,1536,512]{2,1,0:T(8,128)(2,1)} %get-tuple-element.97.g_ref, bf16[8,3,256,512]{3,2,1,0:T(8,128)(2,1)} %bitcast.67, bf16[384,2048]{1,0:T(8,128)(2,1)} %get-tuple-element.69.x_ref, f32[384,2048]{1,0:T(8,128)} %get-tuple-element.98.middle_ref, ...), custom_call_target="tpu_custom_call" | custom-call | flops 1000 | bytes 1000 | tf_op jit(solution)/shard_map/stream_back/pallas_call | solution.py:1062
  782.0 0.1 copy.36
  782.2 0.6 pad.13.stats_ref
  782.8 1.4 pad_maximum_fusion.2.sums_ref
  784.1 97.6 %leave.1 = (bf16[2,4,384,256]{3,2,1,0:T(8,128)(2,1)}, bf16[2,4,384,256]{3,2,1,0:T(8,128)(2,1)}, f32[2,4,8,384]{3,2,1,0:T(8,128)}, f32[8,256]{1,0:T(8,128)}) custom-call(bf16[8,384,256]{2,1,0:T(8,128)(2,1)} %get-tuple-element.96.out_ref, bf16[8,384,256]{2,1,0:T(8,128)(2,1)} %get-tuple-element.100.grad_ref, f32[8,384]{1,0:T(8,128)} %pad.13.stats_ref, ...), custom_call_target="tpu_custom_call" | custom-call | flops 1000 | bytes 1000 | tf_op jit(solution)/shard_map/leave/pallas_call | solution.py:1369
  881.8 1.5 slice.55
  883.3 1.0 slice.48
  884.3 0.7 copy-done
  885.1 0.2 convert_bitcast_fusion.1
  885.4 1.8 copy.38
  887.2 1.2 slice_bitcast_fusion.4
  888.4 1.3 fusion.3
  889.7 3.9 maximum_convert_fusion
  893.6 2.0 bitcast_convert_fusion
  895.6 1.9 convert_element_type.42
  897.5 2.6 copy.37
  900.1 1.1 copy.43
  901.2 0.7 copy.44
  902.0 0.6 copy.45
  (58 shorter events, 0.6 us)
Async XLA Ops:
  7.2 133.7 %all-gather.9.cloned.1.call-start = ((), (), s32[]{:S(2)}) async-start(), calls=%async_computation.8 | async-start | bytes 7077888 | tf_op jit(solution)/shard_map/all_gather | solution.py:1422
  7.9 246.0 %all-gather.11.cloned.1.call-start = ((), (), s32[]{:S(2)}) async-start(), calls=%async_computation.9 | async-start | bytes 2359296 | tf_op jit(solution)/shard_map/all_gather | solution.py:1422
  8.7 306.0 %all-gather.13.cloned.1.call-start = ((), (), s32[]{:S(2)}) async-start(), calls=%async_computation.10 | async-start | bytes 14155776 | tf_op jit(solution)/shard_map/all_gather | solution.py:1434
  134.9 2.5 copy-start.1
  137.6 1.4 copy-start.2
  138.9 261.6 %all-gather.15.cloned.1.call-start = ((), (), s32[]{:S(2)}) async-start(), calls=%async_computation.11 | async-start | bytes 14155776 | tf_op jit(solution)/shard_map/all_gather | solution.py:1434
  139.0 1.4 copy-start.14
  140.3 508.9 %reduce-scatter.5.cloned.1.call-start = ((), (), s32[]{:S(2)}) async-start(), calls=%async_computation.4 | async-start | bytes 14155776 | tf_op jit(solution)/shard_map/reduce_scatter | solution.py:1397
  400.5 316.2 %reduce-scatter.7.cloned.1.call-start = ((), (), s32[]{:S(2)}) async-start(), calls=%async_computation.5 | async-start | bytes 14155776 | tf_op jit(solution)/shard_map/reduce_scatter | solution.py:1397
  473.4 422.3 %reduce-scatter.11.cloned.1.call-start = ((), (), s32[]{:S(2)}) async-start(), calls=%async_computation.7 | async-start | bytes 2359296 | tf_op jit(solution)/shard_map/reduce_scatter | solution.py:1397
  601.0 25.1 %copy-start.5 = (bf16[1536,512]{1,0:T(8,128)(2,1)S(1)}, bf16[1536,512]{1,0:T(8,128)(2,1)}, u32[]{:S(2)}) copy-start(bf16[1536,512]{1,0:T(8,128)(2,1)} %get-tuple-element.68.attn_ref) | copy-start | bytes 4718596
  649.2 0.9 copy-start.9
  649.2 1.1 copy-start.12
  649.2 248.3 %reduce-scatter.9.cloned.1.call-start = ((), (), s32[]{:S(2)}) async-start(), calls=%async_computation.6 | async-start | bytes 7077888 | tf_op jit(solution)/shard_map/reduce_scatter | solution.py:1397
  650.2 66.4 %copy-start.8 = (f32[384,128]{0,1:T(8,128)}, f32[384,128]{0,1:T(8,128)S(1)}, u32[]{:S(2)}) copy-start(f32[384,128]{0,1:T(8,128)S(1)} %copy.35) | copy-start | bytes 589828
  716.7 65.3 %copy-start.10 = (f32[384,128]{1,0:T(8,128)S(1)}, f32[384,128]{1,0:T(8,128)}, u32[]{:S(2)}) copy-start(f32[384,128]{1,0:T(8,128)} %get-tuple-element.102) | copy-start | bytes 589828
  716.7 65.4 %slice-start.1 = ((f32[384,128]{0,1:T(8,128)}), f32[384,2]{0,1:T(2,128)S(1)}, s32[]{:S(2)}) async-start(f32[384,128]{0,1:T(8,128)} %copy-done.8), calls=%async_computation.13 | async-start | bytes 6144 | tf_op jit(solution)/shard_map/slice | solution.py:1481
  716.7 66.1 %copy-start.11 = (f32[1,2048]{1,0:T(1,128)S(1)}, f32[1,2048]{1,0:T(1,128)}, u32[]{:S(2)}) copy-start(f32[1,2048]{1,0:T(1,128)} %get-tuple-element.104) | copy-start | bytes 24580
  784.1 99.1 %copy-start.4 = (bf16[3,256,1024]{2,1,0:T(8,128)(2,1)S(1)}, bf16[3,256,1024]{2,1,0:T(8,128)(2,1)}, u32[]{:S(2)}) copy-start(bf16[3,256,1024]{2,1,0:T(8,128)(2,1)} %reduce-scatter.5.cloned.1.call-done) | copy-start | bytes 4718596
  883.3 1.8 copy-start
  885.4 4.4 slice-start
  889.7 3.9 copy-start.6
  895.6 4.5 copy-start.3
  900.1 1.2 copy-start.7
  900.1 1.9 copy-start.13
Sparse Core Ops, SparseCore 0:
  9.7 118.0 all-gather.8
  129.4 29.4 all-gather.10
  161.1 114.8 all-gather.12
  278.1 114.9 all-gather.14
  400.6 136.2 reduce-scatter.4
  539.1 127.5 reduce-scatter.6
  669.0 34.9 reduce-scatter.10
  706.3 67.6 reduce-scatter.8

commit v5 on v4

--- a/solution.py
+++ b/solution.py
@@ -87,17 +87,10 @@
 
 
 def attend_kernel(
-    size, offsets_ref, lengths_ref, gate_ref, qkv_ref, memory_ref, norm_ref, cot_ref,
-    attn_ref, dot_ref, part_ref, logsum_ref, memory_new_ref, norm_new_ref, all_cot_ref,
-    send, receive, own,
+    offsets_ref, lengths_ref, gate_ref, qkv_ref, memory_ref, norm_ref,
+    attn_ref, dot_ref, part_ref, logsum_ref, memory_new_ref, norm_new_ref,
 ):
     head = pl.program_id(0)
-    gather = Gather(size, cot_ref, all_cot_ref, send, receive, own)
-
-    @pl.when(head == 0)
-    def _():
-        gather.start(hold=False)
-
     gate = gate_ref[head]
     q_ref, k_ref, v_ref = qkv_ref.at[0, 0], qkv_ref.at[1, 0], qkv_ref.at[2, 0]
     memory_one = memory_ref[0]
@@ -131,14 +124,6 @@
     memory_new_ref[0] = memory_one + (plain_dot(high, v, TN) + plain_dot(low, v, TN)) / PROMPT
     norm_new_ref[0] = norm_one + jnp.mean(lifted_keys, axis=0, keepdims=True)
 
-    @pl.when(head == pl.num_programs(0) - 1)
-    def _():
-        gather.forward()
-        for step in range(size - 1):
-            gather.wait(step)
-        gather.keep.wait()
-        gather.finish()
-
 
 def head_block(shape, lead=0):
     zeros = (0,) * (len(shape) - 1 - lead)
@@ -148,22 +133,21 @@
 SMEM_SPEC = pl.BlockSpec(memory_space=pltpu.SMEM)
 
 
-def attend(size, cot, heads_all, memory_one, norm_one, offsets, lengths, gate_value):
+def attend(heads_all, memory_one, norm_one, offsets, lengths, gate_value):
     heads = heads_all.shape[1]
     f32 = jnp.float32
     row_block = head_block((1, GLEN, HD))
     column = pl.BlockSpec((GLEN, HD), lambda h: (0, h))
     return pl.pallas_call(
-        functools.partial(attend_kernel, size),
+        attend_kernel,
         grid=(heads,),
         in_specs=[
             SMEM_SPEC, SMEM_SPEC, SMEM_SPEC,
             head_block((3, 1, GLEN, HD), 1), head_block((1, HD, HD)), head_block((1, 1, HD)),
-            ANY,
         ],
         out_specs=[
             column, row_block, row_block, head_block((1, GLEN, 1)),
-            head_block((1, HD, HD)), head_block((1, 1, HD)), ANY,
+            head_block((1, HD, HD)), head_block((1, 1, HD)),
         ],
         out_shape=[
             jax.ShapeDtypeStruct((GLEN, heads * HD), jnp.bfloat16),
@@ -172,20 +156,75 @@
             jax.ShapeDtypeStruct((heads, GLEN, 1), f32),
             jax.ShapeDtypeStruct((heads, HD, HD), f32),
             jax.ShapeDtypeStruct((heads, 1, HD), f32),
-            bf(size, GLEN // size, D),
         ],
-        scratch_shapes=[dma(Gather.semaphores(size)), dma(Gather.semaphores(size)), pltpu.SemaphoreType.DMA],
-        compiler_params=comm_params(9),
+        compiler_params=pltpu.CompilerParams(vmem_limit_bytes=BIG_VMEM),
         cost_estimate=SHORT,
         name="attend",
-    )(offsets, lengths, gate_value, heads_all, memory_one, norm_one[:, None, :], cot)
+    )(offsets, lengths, gate_value, heads_all, memory_one, norm_one[:, None, :])
 
 
 def attend_back_kernel(
+    size, cols, depth, wide,
     offsets_ref, lengths_ref, gate_ref, qkv_ref, grad_ref, dot_ref, part_ref, logsum_ref,
-    memory_ref, norm_ref, out_ref, gate_out_ref, key_sum, value_sum,
+    memory_ref, norm_ref, middle_ref, hidden_a, hidden_b, pack_a, pack_b,
+    out_ref, gate_out_ref, blocks_ref, stat_ref,
+    key_sum, value_sum, stage, land, total, send, receive, h, w, h_sem, w_sem,
 ):
     head = pl.program_id(0)
+    piece = GLEN // size
+    span = 512
+    scatter = Scatter(size, stage, land, total, send, receive)
+
+    def h_load(i, step):
+        rows = pl.ds(pl.multiple_of(scatter.order[step] * piece, piece), piece)
+        return pltpu.make_async_copy((hidden_a, hidden_b)[i].at[rows], h.at[i, rows], h_sem.at[i, step])
+
+    def w_load(i, c):
+        return pltpu.make_async_copy(
+            (pack_a, pack_b)[i].at[c, 2], w.at[i, pl.ds(c * depth, depth), :], w_sem.at[i, c]
+        )
+
+    def partial(step, at, store):
+        for i in range(2):
+            h_load(i, step).wait()
+
+        def one(depth_rows, half, columns):
+            rows = pl.ds(pl.multiple_of(at * piece, piece), piece)
+            store(
+                half, columns,
+                plain_dot(h[0, rows, :], w[0, depth_rows, :], NT) + plain_dot(h[1, rows, :], w[1, depth_rows, :], NT),
+            )
+
+        if step == 0:
+            for t in range(D // span):
+                for c in range(t * span // depth, (t + 1) * span // depth):
+                    for i in range(2):
+                        w_load(i, c).wait()
+                half, inside = divmod(t * span, HALF)
+                one(slice(t * span, (t + 1) * span), half, slice(inside, inside + span))
+            return
+        for half in range(2):
+            @pl.loop(0, HALF // span)
+            def _(t):
+                columns = pl.ds(pl.multiple_of(t * span, span), span)
+                one(pl.ds(pl.multiple_of(half * HALF + t * span, span), span), half, columns)
+
+    @pl.when(head == 0)
+    def _():
+        for i in range(2):
+            h_load(i, 0).start()
+        for c in range(cols):
+            for i in range(2):
+                w_load(i, c).start()
+        for step in range(1, size):
+            for i in range(2):
+                h_load(i, step).start()
+        scatter.begin(partial)
+
+    @pl.when(head == pl.num_programs(0) // 2)
+    def _():
+        scatter.middle()
+
     gate = gate_ref[head]
     keep = 1.0 - gate
     scale = HD ** (-0.5)
@@ -231,34 +270,63 @@
     out_ref[2, :, :] = (value_sum[...] * keep).astype(jnp.bfloat16)
     gate_out_ref[0] = gate_row
 
-
-def attend_back(heads_all, grad_heads, dot_part, memory_part, logsum, memory_one, norm_one, offsets, lengths, gate_value):
+    def finish(rows):
+        ffn = [total[half, rows, :] for half in range(2)]
+        result = [middle_ref[rows, columns] + ffn[half] for half, columns in enumerate((LEFT, RIGHT))]
+        for half, columns in enumerate((LEFT, RIGHT)):
+            blocked_store(blocks_ref, rows, depth, columns, result[half].astype(jnp.bfloat16))
+        stat_ref[rows, :] = lanes(
+            row_mean(ffn[0] * ffn[0], ffn[1] * ffn[1]),
+            row_mean(result[0] * result[0], result[1] * result[1]),
+        )
+
+    @pl.when(head == pl.num_programs(0) - 1)
+    def _():
+        scatter.own(partial)
+        scatter.end()
+        strip_loop(piece, finish)
+
+
+def whole_block(shape):
+    return pl.BlockSpec(shape, lambda h: (0,) * len(shape), pipeline_mode=pl.Buffered(1))
+
+
+def attend_back(
+    size, heads_all, grad_heads, dot_part, memory_part, logsum, memory_one, norm_one, offsets, lengths, gate_value,
+    hiddens, packs, middle,
+):
     heads = heads_all.shape[1]
-    f32 = jnp.float32
+    piece = middle.shape[0]
+    cols, _, depth, wide = packs[0].shape
     row_block = head_block((1, GLEN, HD))
     return pl.pallas_call(
-        attend_back_kernel,
+        functools.partial(attend_back_kernel, size, cols, depth, wide),
         grid=(heads,),
         in_specs=[
             SMEM_SPEC, SMEM_SPEC, SMEM_SPEC,
             head_block((3, 1, GLEN, HD), 1), row_block, row_block, row_block,
             head_block((1, GLEN, 1)), head_block((1, HD, HD)), head_block((1, 1, HD)),
+            whole_block((piece, D)), ANY, ANY, ANY, ANY,
         ],
         out_specs=[
             pl.BlockSpec((3, GLEN, HD), lambda h: (0, 0, h)),
             head_block((1, 1, HD)),
+            whole_block((cols, piece, depth)), whole_block((piece, HD)),
         ],
-        out_shape=[
-            jax.ShapeDtypeStruct((3, GLEN, heads * HD), jnp.bfloat16),
-            jax.ShapeDtypeStruct((heads, 1, HD), f32),
+        out_shape=[bf(3, GLEN, heads * HD), fl(heads, 1, HD), bf(cols, piece, depth), fl(piece, HD)],
+        scratch_shapes=[pltpu.VMEM((GLEN, HD), jnp.float32), pltpu.VMEM((GLEN, HD), jnp.float32)]
+        + scatter_scratch(size, piece)
+        + [
+            pltpu.VMEM((2, GLEN, wide), jnp.bfloat16),
+            pltpu.VMEM((2, D, wide), jnp.bfloat16),
+            dma(2, size), dma(2, cols),
         ],
-        scratch_shapes=[pltpu.VMEM((GLEN, HD), f32), pltpu.VMEM((GLEN, HD), f32)],
-        compiler_params=pltpu.CompilerParams(vmem_limit_bytes=BIG_VMEM),
+        compiler_params=comm_params(5),
         cost_estimate=SHORT,
         name="attend_back",
     )(
         offsets, lengths, gate_value, heads_all, grad_heads, dot_part, memory_part, logsum,
-        memory_one, norm_one[:, None, :],
+        memory_one, norm_one[:, None, :], middle, *hiddens, *packs,
     )
 
 
@@ -375,7 +443,8 @@
     def __init__(self, size, stage, land, total, send, receive):
         self.size, self.stage, self.land, self.total = size, stage, land, total
         self.send, self.receive = send, receive
-        self.row, self.col = lax.axis_index("row"), lax.axis_index("col")
+        self.row, self.col = here()
+        self.plan()
 
     @staticmethod
     def semaphores(size):
@@ -389,77 +458,76 @@
     def land_shape(size, piece):
         return (6, piece, HALF) if size == 4 else (size - 1, 2, piece, HALF)
 
-    def copy(self, index, source, peer):
-        return remote(source, self.land.at[index], self.send.at[index], self.receive.at[index], peer)
-
-    def run(self, partial, between=None, late=None):
-        row, col = self.row, self.col
-
-        def into(slot):
+    def plan(self):
+        row, col, stage = self.row, self.col, self.stage
+
+        def copy(index, source, peer):
+            return remote(source, self.land.at[index], self.send.at[index], self.receive.at[index], peer)
+
+        if self.size != 4:
+            others = [lax.rem(row + d, self.size) for d in range(1, self.size)]
+            self.peers = [(peer, col) for peer in others]
+            self.order = [*others, row]
+            self.copies = [copy(slot, stage.at[slot], peer) for slot, peer in enumerate(self.peers)]
+            self.after = [[slot] for slot in range(self.size - 1)]
+            return
+        rx, ry, rd = square(row)
+        px, py = self.peers = [(rx, col), (ry, col)]
+        self.order = [rd, rx, ry, row]
+        self.copies = [
+            copy(0, stage.at[0, 0], px), copy(1, stage.at[0, 1], py), copy(2, stage.at[1, 0], px),
+            copy(3, stage.at[2, 1], py), copy(4, stage.at[2, 0], py), copy(5, stage.at[1, 1], px),
+        ]
+        self.after = [[0, 1], [2], [3]]
+
+    def begin(self, partial, greeted=False):
+        if not greeted:
+            greet(self.peers)
+        for step, row in enumerate(self.order[:-1]):
+
             def store(half, columns, value):
-                self.stage[slot, half, :, columns] = value.astype(jnp.bfloat16)
-
-            return store
-
-        def into_total(half, columns, value):
+                self.stage[step, half, :, columns] = value.astype(jnp.bfloat16)
+
+            partial(step, row, store)
+            for index in self.after[step]:
+                self.copies[index].start()
+
+    def middle(self):
+        if self.size != 4:
+            return
+        self.copies[0].wait_recv()
+        self.add_stage(2, 0, self.land.at[0])
+        self.copies[4].start()
+        self.copies[1].wait_recv()
+        self.add_stage(1, 1, self.land.at[1])
+        self.copies[5].start()
+
+    def own(self, partial):
+        def store(half, columns, value):
             self.total[half, :, columns] = value
 
+        partial(self.size - 1, self.order[-1], store)
+
+    def end(self):
         if self.size != 4:
-            peers = [lax.rem(row + d, self.size) for d in range(1, self.size)]
-            greet([(peer, col) for peer in peers])
-            copies = []
-            for slot, peer in enumerate(peers):
-                partial(peer, into(slot))
-                copies.append(self.copy(slot, self.stage.at[slot], (peer, col)))
-                copies[-1].start()
-            partial(row, into_total)
-            if between is not None:
-                between()
-            if late is not None:
-                late()
-            for slot, copy in enumerate(copies):
+            for slot, copy in enumerate(self.copies):
                 copy.wait_recv()
                 self.add_total(0, self.land.at[slot, 0])
                 self.add_total(1, self.land.at[slot, 1])
-            for copy in copies:
-                copy.wait_send()
-            return
-        rx, ry, rd = square(row)
-        px, py = (rx, col), (ry, col)
-        greet([px, py])
-        partial(rd, into(0))
-        first = [self.copy(0, self.stage.at[0, 0], px), self.copy(1, self.stage.at[0, 1], py)]
-        for copy in first:
-            copy.start()
-        partial(rx, into(1))
-        first.append(self.copy(2, self.stage.at[1, 0], px))
-        first[2].start()
-        partial(ry, into(2))
-        first.append(self.copy(3, self.stage.at[2, 1], py))
-        first[3].start()
-        if between is not None:
-            between()
-        first[0].wait_recv()
-        self.add_stage(2, 0, self.land.at[0])
-        second = [self.copy(4, self.stage.at[2, 0], py)]
-        second[0].start()
-        first[1].wait_recv()
-        self.add_stage(1, 1, self.land.at[1])
-        second.append(self.copy(5, self.stage.at[1, 1], px))
-        second[1].start()
-        partial(row, into_total)
+        else:
+            for index, half in ((2, 0), (3, 1), (4, 0), (5, 1)):
+                self.copies[index].wait_recv()
+                self.add_total(half, self.land.at[index])
+        for copy in self.copies:
+            copy.wait_send()
+
+    def run(self, partial, late=None, greeted=False):
+        self.begin(partial, greeted)
+        self.middle()
+        self.own(partial)
         if late is not None:
             late()
-        first[2].wait_recv()
-        self.add_total(0, self.land.at[2])
-        first[3].wait_recv()
-        self.add_total(1, self.land.at[3])
-        second[0].wait_recv()
-        self.add_total(0, self.land.at[4])
-        second[1].wait_recv()
-        self.add_total(1, self.land.at[5])
-        for copy in first + second:
-            copy.wait_send()
+        self.end()
 
     def add_stage(self, slot, half, landed):
         @pl.loop(0, landed.shape[0] // STRIP)
@@ -612,7 +680,7 @@
         scatter = Scatter(size, stage, land, total, send, receive)
         wait_all(loads)
 
-        def partial(row, store):
+        def partial(step, row, store):
             rows = pl.ds(pl.multiple_of(row * piece, piece), piece)
             left = attn_ref[rows, :]
             for half in range(2):
@@ -801,76 +869,120 @@
         gain_sum[:, columns] += jnp.sum(total[half, rows, :] * stream[half] * inverse, axis=0, keepdims=True)
 
 
-def middle_back(size, grads, packs, middle, cot, gain):
+def middle_back(size, grads, packs, middle, cot, gain, tokens, all_cot, hidden):
     piece = middle.shape[0]
     cols, _, depth, wide = packs[0].shape
     tile = 512
-    halves = len(packs)
+    block = 256
 
     def kernel(
-        *refs,
+        first_ref, second_ref, pack_a, pack_b, middle_ref, cot_ref, gain_ref, x_ref, y_ref, hidden_ref,
+        grad_ref, low_ref, gain_sum, part_ref,
+        stage, land, total, send, receive, w, g_first, g_second, h, x, part,
+        w_sem, first_sem, second_sem, h_sem, x_sem, part_sem,
     ):
-        g_refs, pack_refs, refs = refs[:halves], refs[halves : 2 * halves], refs[2 * halves :]
-        (middle_ref, cot_ref, gain_ref, grad_ref, low_ref, gain_sum,
-         stage, land, total, send, receive, w, g, w_sem, g_sem) = refs
-        row, _ = here()
-        rows_order = [*reversed(square(row)), row] if size == 4 else [lax.rem(row + d, size) for d in range(size)]
-        if size == 4:
-            rows_order = [rows_order[0], rows_order[2], rows_order[1], row]
+        pack_refs = (pack_a, pack_b)
+        scatter = Scatter(size, stage, land, total, send, receive)
 
         def piece_rows(at):
             return pl.ds(pl.multiple_of(at * piece, piece), piece)
 
-        def g_load(h, at):
+        def first_load(step):
             return pltpu.make_async_copy(
-                g_refs[h].at[:, piece_rows(at)], g.at[h, :, piece_rows(at)], g_sem.at[h, at]
+                first_ref.at[:, piece_rows(scatter.order[step])], g_first.at[step % 2], first_sem.at[step % 2]
             )
 
-        def w_load(h, c):
+        def second_load(step):
+            rows = piece_rows(scatter.order[step])
+            return pltpu.make_async_copy(second_ref.at[:, rows], g_second.at[:, rows], second_sem.at[step])
+
+        def w_load(i, c):
             return pltpu.make_async_copy(
-                pack_refs[h].at[c, pl.ds(0, 2)], w.at[h, :, pl.ds(c * depth, depth), :], w_sem.at[h, c]
+                pack_refs[i].at[c, pl.ds(0, 2)], w.at[i, :, pl.ds(c * depth, depth), :], w_sem.at[i, c]
             )
 
-        for h in range(halves):
-            g_load(h, rows_order[0]).start()
+        first_load(0).start()
+        second_load(0).start()
         for c in range(cols):
-            for h in range(halves):
-                w_load(h, c).start()
-        for at in rows_order[1:]:
-            for h in range(halves):
-                g_load(h, at).start()
-        scatter = Scatter(size, stage, land, total, send, receive)
+            for i in range(2):
+                w_load(i, c).start()
+        first_load(1).start()
+        for step in range(1, size):
+            second_load(step).start()
+        h_load = pltpu.make_async_copy(hidden_ref, h, h_sem)
+        h_load.start()
         gain_sum[...] = jnp.zeros_like(gain_sum)
-        calls = []
-
-        def one(rows, depth_rows, store, half, columns):
+
+        def one(step, rows, depth_rows, store, half, columns):
             value = 0.0
-            for h in range(halves):
-                for j in range(2):
-                    value += plain_dot(g[h, j, rows, :], w[h, j, depth_rows, :], NT)
+            for j in range(2):
+                value += plain_dot(g_first[step % 2, j], w[0, j, depth_rows, :], NT)
+                value += plain_dot(g_second[j, rows, :], w[1, j, depth_rows, :], NT)
             store(half, columns, value)
 
-        def partial(at, store):
-            fresh = not calls
-            calls.append(at)
-            for h in range(halves):
-                g_load(h, at).wait()
+        def partial(step, at, store):
+            first_load(step).wait()
+            second_load(step).wait()
             rows = piece_rows(at)
-            if fresh:
+            if step == 0:
                 for t in range(D // tile):
                     for c in range(t * tile // depth, (t + 1) * tile // depth):
-                        for h in range(halves):
-                            w_load(h, c).wait()
+                        for i in range(2):
+                            w_load(i, c).wait()
                     half, inside = divmod(t * tile, HALF)
-                    one(rows, slice(t * tile, (t + 1) * tile), store, half, slice(inside, inside + tile))
-                return
-            for half in range(2):
-                @pl.loop(0, HALF // tile)
-                def _(t):
-                    columns = pl.ds(pl.multiple_of(t * tile, tile), tile)
-                    one(rows, pl.ds(pl.multiple_of(half * HALF + t * tile, tile), tile), store, half, columns)
-
-        scatter.run(partial)
+                    one(step, rows, slice(t * tile, (t + 1) * tile), store, half, slice(inside, inside + tile))
+            else:
+                for half in range(2):
+                    @pl.loop(0, HALF // tile)
+                    def _(t):
+                        columns = pl.ds(pl.multiple_of(t * tile, tile), tile)
+                        depth_rows = pl.ds(pl.multiple_of(half * HALF + t * tile, tile), tile)
+                        one(step, rows, depth_rows, store, half, columns)
+            if step + 2 < size:
+                first_load(step + 2).start()
+
+        def x_loads(i, slot):
+            columns = pl.ds(pl.multiple_of(i * block, block), block)
+            return [
+                pltpu.make_async_copy(source.at[:, :, columns], x.at[slot, k], x_sem.at[slot, k])
+                for k, source in enumerate((x_ref, y_ref))
+            ]
+
+        def part_move(i, slot):
+            columns = pl.ds(pl.multiple_of(i * block, block), block)
+            return pltpu.make_async_copy(part.at[slot], part_ref.at[:, columns, :], part_sem.at[slot])
+
+        def weights():
+            count = D // block
+            for load in x_loads(0, 0):
+                load.start()
+            h_load.wait()
+
+            @pl.loop(0, count)
+            def _(i):
+                slot = lax.rem(i, 2)
+
+                @pl.when(i + 1 < count)
+                def _():
+                    for load in x_loads(i + 1, 1 - slot):
+                        load.start()
+
+                wait_all(x_loads(i, slot))
+
+                @pl.when(i >= 2)
+                def _():
+                    part_move(i, slot).wait()
+
+                left = x[slot, 0].reshape(GLEN, block)
+                for j in range(2):
+                    part[slot, j] = plain_dot(left, g_second[j], TN).astype(jnp.bfloat16)
+                part[slot, 2] = plain_dot(x[slot, 1].reshape(GLEN, block), h[...], TN).astype(jnp.bfloat16)
+                part_move(i, slot).start()
+
+            for slot in range(2):
+                part_move(slot, slot).wait()
+
+        scatter.run(partial, weights)
 
         def finish(rows):
             stream = [middle_ref[rows, columns] for columns in (LEFT, RIGHT)]
@@ -887,92 +999,28 @@
 
     return pl.pallas_call(
         kernel,
-        out_shape=[fl(piece, D), bf(piece, D), fl(1, D)],
-        in_specs=[ANY] * (2 * halves) + [VMEM] * 3,
-        out_specs=[VMEM, VMEM, VMEM],
+        out_shape=[fl(piece, D), bf(piece, D), fl(1, D), bf(3, D, wide)],
+        in_specs=[ANY] * 4 + [VMEM] * 3 + [ANY] * 3,
+        out_specs=[VMEM, VMEM, VMEM, ANY],
         scratch_shapes=scatter_scratch(size, piece)
         + [
-            pltpu.VMEM((halves, 2, D, wide), jnp.bfloat16),
-            pltpu.VMEM((halves, 2, GLEN, wide), jnp.bfloat16),
-            dma(halves, cols), dma(halves, size),
+            pltpu.VMEM((2, 2, D, wide), jnp.bfloat16),
+            pltpu.VMEM((2, 2, piece, wide), jnp.bfloat16),
+            pltpu.VMEM((2, GLEN, wide), jnp.bfloat16),
+            pltpu.VMEM((GLEN, wide), jnp.bfloat16),
+            pltpu.VMEM((2, 2, size, piece, block), jnp.bfloat16),
+            pltpu.VMEM((2, 3, block, wide), jnp.bfloat16),
+            dma(2, cols), dma(2), dma(size), pltpu.SemaphoreType.DMA, dma(2, 2), dma(2),
         ],
         compiler_params=comm_params(4),
         cost_estimate=SHORT,
         name="middle_back",
-    )(*grads, *packs, middle, cot, gain)
+    )(*grads, *packs, middle, cot, gain, tokens, all_cot, hidden)
 
 
 def blocked_store(ref, rows, depth, columns, value):
     for i in range(value.shape[1] // depth):
         ref[columns.start // depth + i, rows, :] = value[:, i * depth : (i + 1) * depth]
-
-
-def ffn_out(size, hiddens, packs, middle):
-    piece = middle.shape[0]
-    cols, _, depth, wide = packs[0].shape
-    tile = 512
-    halves = len(packs)
-
-    def kernel(*refs):
-        h_refs, pack_refs, refs = refs[:halves], refs[halves : 2 * halves], refs[2 * halves :]
-        middle_ref, out_ref, stat_ref, stage, land, total, send, receive, w, w_sem = refs
-
-        def w_load(h, c):
-            return pltpu.make_async_copy(
-                pack_refs[h].at[c, 2], w.at[h, pl.ds(c * depth, depth), :], w_sem.at[h, c]
-            )
-
-        for c in range(cols):
-            for h in range(halves):
-                w_load(h, c).start()
-        scatter = Scatter(size, stage, land, total, send, receive)
-        calls = []
-
-        def one(rows, depth_rows, store, half, columns):
-            value = 0.0
-            for h in range(halves):
-                value += plain_dot(h_refs[h][rows, :], w[h, depth_rows, :], NT)
-            store(half, columns, value)
-
-        def partial(at, store):
-            fresh = not calls
-            calls.append(at)
-            rows = pl.ds(pl.multiple_of(at * piece, piece), piece)
-            if fresh:
-                for c in range(cols):
-                    for h in range(halves):
-                        w_load(h, c).wait()
-            for half in range(2):
-                @pl.loop(0, HALF // tile)
-                def _(t):
-                    columns = pl.ds(pl.multiple_of(t * tile, tile), tile)
-                    one(rows, pl.ds(pl.multiple_of(half * HALF + t * tile, tile), tile), store, half, columns)
-
-        scatter.run(partial)
-
-        def finish(rows):
-            ffn = [total[half, rows, :] for half in range(2)]
-            result = [middle_ref[rows, columns] + ffn[half] for half, columns in enumerate((LEFT, RIGHT))]
-            for half, columns in enumerate((LEFT, RIGHT)):
-                blocked_store(out_ref, rows, depth, columns, result[half].astype(jnp.bfloat16))
-            stat_ref[rows, :] = lanes(
-                row_mean(ffn[0] * ffn[0], ffn[1] * ffn[1]),
-                row_mean(result[0] * result[0], result[1] * result[1]),
-            )
-
-        strip_loop(piece, finish)
-
-    return pl.pallas_call(
-        kernel,
-        out_shape=[bf(cols, piece, depth), fl(piece, HD)],
-        in_specs=[VMEM] * halves + [ANY] * halves + [VMEM],
-        out_specs=[VMEM, VMEM],
-        scratch_shapes=scatter_scratch(size, piece)
-        + [pltpu.VMEM((halves, D, wide), jnp.bfloat16), dma(halves, cols)],
-        compiler_params=comm_params(5),
-        cost_estimate=SHORT,
-        name="ffn_out",
-    )(*hiddens, *packs, middle)
 
 
 def branch_back(size, low, w_all):
@@ -1019,21 +1067,24 @@
     )(low, w_all)
 
 
-def stream_back(size, grads, w_all, x, grad_middle, gain):
+def stream_back(size, grads, w_all, x, grad_middle, gain, blocks_out):
     piece = x.shape[0]
     cols, _, depth, width = w_all.shape
     tile = 512
 
     def kernel(
-        g_ref, w_ref, x_ref, middle_ref, gain_ref, out_ref, gain_sum,
-        stage, land, total, send, receive, w, w_sem,
+        g_ref, w_ref, x_ref, middle_ref, gain_ref, blocks_ref, out_ref, gain_sum, target_ref,
+        stage, land, total, send, receive, w, w_sem, *rest,
     ):
+        greet(row_and_col_peers(size, cols))
+        outward = Outward(size, cols, blocks_ref, rest[0], target_ref, *rest[1:])
+        outward.start()
         loads = fetches([(w_ref.at[c], w.at[:, pl.ds(c * depth, depth), :]) for c in range(cols)], w_sem)
         scatter = Scatter(size, stage, land, total, send, receive)
         wait_all(loads)
         gain_sum[...] = jnp.zeros_like(gain_sum)
 
-        def partial(row, store):
+        def partial(step, row, store):
             rows = pl.ds(pl.multiple_of(row * piece, piece), piece)
             for half in range(2):
                 @pl.loop(0, HALF // tile)
@@ -1045,7 +1096,7 @@
                         value += plain_dot(g_ref[j, rows, :], w[j, depth_rows, :], NT)
                     store(half, columns, value)
 
-        scatter.run(partial)
+        scatter.run(partial, outward.forward, greeted=True)
 
         def finish(rows):
             stream = [x_ref[rows, columns].astype(jnp.float32) for columns in (LEFT, RIGHT)]
@@ -1058,18 +1109,20 @@
             norm_back(rows, total, stream, inverse, gain_ref, base, store, gain_sum)
 
         strip_loop(piece, finish)
+        outward.finish()
 
     return pl.pallas_call(
         kernel,
-        out_shape=[bf(cols, piece, depth), fl(1, D)],
-        in_specs=[VMEM, ANY, VMEM, VMEM, VMEM],
-        out_specs=[VMEM, VMEM],
+        out_shape=[bf(cols, piece, depth), fl(1, D), bf(cols // size, size, piece, depth)],
+        in_specs=[VMEM, ANY, VMEM, VMEM, VMEM, VMEM],
+        out_specs=[VMEM, VMEM, ANY],
         scratch_shapes=scatter_scratch(size, piece)
-        + [pltpu.VMEM((3, D, width), jnp.bfloat16), pltpu.SemaphoreType.DMA((cols,))],
+        + [pltpu.VMEM((3, D, width), jnp.bfloat16), pltpu.SemaphoreType.DMA((cols,))]
+        + Outward.scratch(size, cols, piece, depth),
         compiler_params=comm_params(7),
         cost_estimate=SHORT,
         name="stream_back",
-    )(grads, w_all, x, grad_middle, gain)
+    )(grads, w_all, x, grad_middle, gain, blocks_out)
 
 
 def row_and_col_peers(size, cols):
@@ -1220,12 +1273,14 @@
     scratch = Inward.scratch(size, cols, piece, depth)
 
     def kernel(
-        x_ref, cot_ref, gains_ref, tokens_ref, normed_ref, gain_in_ref, gain_mid_ref, cot_tokens_ref,
-        gains_land, gains_send, gains_receive, *rest,
+        x_ref, cot_ref, gains_ref, tokens_ref, normed_ref, gain_in_ref, gain_mid_ref, cot_tokens_ref, all_cot_ref,
+        gains_land, gains_send, gains_receive, gather_send, gather_receive, gather_own, *rest,
     ):
         greet(row_and_col_peers(size, cols))
         exchange = Inward(size, cols, x_ref, *rest[: len(scratch)])
         second = Inward(size, cols, cot_ref, *rest[len(scratch) :])
+        gather = Gather(size, cot_tokens_ref, all_cot_ref, gather_send, gather_receive, gather_own)
+        second.start()
         exchange.start()
         row, col = here()
         copies = []
@@ -1236,9 +1291,17 @@
             )
             copies[-1].start()
         gains_land[col] = gains_ref[...]
-        second.start()
+        second.forward()
         exchange.forward()
-        second.forward()
+        second.finish()
+
+        def assemble(rows):
+            for c in range(cols):
+                cot_tokens_ref[rows, c * depth : (c + 1) * depth] = second.land[c, rows, :]
+
+        strip_loop(piece, assemble)
+        gather.start(greeted=True, hold=False)
+        gather.forward()
         for copy in copies:
             copy.wait()
         for c in range(cols):
@@ -1262,20 +1325,18 @@
                 ).astype(jnp.bfloat16)
 
         strip_loop(piece, norm)
-        second.finish()
-
-        def assemble(rows):
-            for c in range(cols):
-                cot_tokens_ref[rows, c * depth : (c + 1) * depth] = second.land[c, rows, :]
-
-        strip_loop(piece, assemble)
+        for step in range(size - 1):
+            gather.wait(step)
+        gather.keep.wait()
+        gather.finish()
 
     return pl.pallas_call(
         kernel,
-        out_shape=[bf(piece, D), bf(piece, D), fl(1, D), fl(1, D), bf(piece, D)],
+        out_shape=[bf(piece, D), bf(piece, D), fl(1, D), fl(1, D), bf(piece, D), bf(size, piece, D)],
         in_specs=[ANY, ANY, VMEM],
-        out_specs=[VMEM] * 5,
+        out_specs=[VMEM] * 5 + [ANY],
         scratch_shapes=[pltpu.VMEM((cols, 8, depth), jnp.float32), dma(cols - 1), dma(cols - 1)]
+        + [dma(Gather.semaphores(size)), dma(Gather.semaphores(size)), pltpu.SemaphoreType.DMA]
         + scratch * 2,
         compiler_params=comm_params(8),
         cost_estimate=SHORT,
@@ -1283,20 +1344,18 @@
     )(pieces, by_pieces(cotangent, size), jnp.pad(gains, ((0, 6), (0, 0))))
 
 
-def leave(size, cols, blocks_out, blocks_grad, stats, sums):
-    _, piece, depth = blocks_out.shape
+def leave(size, cols, blocks_grad, stats, sums):
+    _, piece, depth = blocks_grad.shape
     groups = cols // size
-    half = len(Outward.scratch(size, cols, piece, depth))
 
     def kernel(
-        out_ref, grad_ref, stats_ref, sums_ref, out_target, grad_target, stats_target, sums_target,
+        grad_ref, stats_ref, sums_ref, grad_target, stats_target, sums_target,
         stats_row, stats_all, sums_col, sums_part, sums_row,
         a_send, a_receive, b_send, b_receive, c_send, c_receive, d_send, d_receive, *rest,
     ):
         row, col = here()
         greet(row_and_col_peers(size, cols))
-        grad = Outward(size, cols, grad_ref, rest[0], grad_target, *rest[1:half])
-        out = Outward(size, cols, out_ref, rest[half], out_target, *rest[half + 1 :])
+        grad = Outward(size, cols, grad_ref, rest[0], grad_target, *rest[1:])
         home, slot = col // groups, lax.rem(col, groups)
         col_peers = [lax.rem(col + e, cols) for e in range(1, cols)]
         row_peers = [lax.rem(row + d, size) for d in range(1, size)]
@@ -1317,7 +1376,6 @@
             stats_row[row] = stats_ref[...]
 
         grad.start()
-        out.start()
         for peer in col_peers:
             remote(sums_ref.at[peer], sums_col.at[peer], c_send.at[peer], c_receive.at[peer], (row, peer)).wait()
         total = sums_col[0]
@@ -1337,7 +1395,6 @@
             stats_all[slot] = stats_row[...]
 
         grad.forward()
-        out.forward()
         for peer in row_peers:
             remote(sums_part, sums_row.at[peer], d_send.at[peer], d_receive.at[peer], (peer, col)).wait()
         whole = sums_row[0]
@@ -1364,16 +1421,15 @@
 
         stats_target[...] = stats_all[...]
         grad.finish()
-        out.finish()
 
     return pl.pallas_call(
         kernel,
         out_shape=[
-            bf(groups, size, piece, depth), bf(groups, size, piece, depth),
+            bf(groups, size, piece, depth),
             fl(groups, size, 8, piece), fl(8, depth),
         ],
-        in_specs=[VMEM] * 4,
-        out_specs=[ANY, ANY, VMEM, VMEM],
+        in_specs=[VMEM] * 3,
+        out_specs=[ANY, VMEM, VMEM],
         scratch_shapes=[
             pltpu.VMEM((size, 8, piece), jnp.float32),
             pltpu.VMEM((groups, size, 8, piece), jnp.float32),
@@ -1382,11 +1438,11 @@
             pltpu.VMEM((size, 8, depth), jnp.float32),
             pltpu.SemaphoreType.DMA, dma(size), dma(cols - 1), dma(groups), dma(cols), dma(cols), dma(size), dma(size),
         ]
-        + Outward.scratch(size, cols, piece, depth) * 2,
+        + Outward.scratch(size, cols, piece, depth),
         compiler_params=comm_params(10),
         cost_estimate=SHORT,
         name="leave",
-    )(blocks_out, blocks_grad, stats, sums)
+    )(blocks_grad, stats, sums)
 
 
 def tokens_contract(left, right):
@@ -1422,7 +1478,7 @@
     all_qkv, all_out = (lax.all_gather(w, "col", axis=0, tiled=False) for w in (w_qkv, w_out))
     gate_value = jax.nn.sigmoid(gate_logit)
     group = (memory[0], memory_norm[0], offsets[0], lengths[0], gate_value)
-    stream, normed_in, gain_in, gain_mid, cot = enter(
+    stream, normed_in, gain_in, gain_mid, cot, all_cot = enter(
         size, cols, stream_in, cotangent, jnp.stack([gain_attn, gain_ffn])
     )
     normed_in, w_gate_up, w_down = lax.optimization_barrier((normed_in, w_gate_up, w_down))
@@ -1433,36 +1489,35 @@
     ]
     all_packs = [lax.all_gather(pack, "col", axis=0, tiled=False) for pack in packs]
     heads_all, all_in = project_heads(size, normed_in, all_qkv)
-    attn, dot_part, memory_part, logsum, memory_new, norm_new, all_cot = attend(size, cot, heads_all, *group)
+    attn, dot_part, memory_part, logsum, memory_new, norm_new = attend(heads_all, *group)
     middle, normed_ffn, stat_branch = branch_out(size, attn, all_out, stream, gain_mid)
     hidden_first, grads_first, all_ffn = feed_forward(size, normed_ffn, all_packs[0], all_cot, True)
     part_first = weight_grads(flat(all_ffn), grads_first, flat(all_cot), hidden_first)
     part_first, all_ffn = lax.optimization_barrier((part_first, all_ffn))
     scattered_first = over_col(part_first, 1)
     hidden_second, grads_second = feed_forward(size, all_ffn, all_packs[1], all_cot, False)
-    part_second = weight_grads(flat(all_ffn), grads_second, flat(all_cot), hidden_second)
-    part_second, grads_second = lax.optimization_barrier((part_second, grads_second))
+    grad_middle, low_branch, part_gain_ffn, part_second = middle_back(
+        size, (grads_first, grads_second), all_packs, middle, cot, gain_mid, all_ffn, all_cot, hidden_second
+    )
     scattered_second = over_col(part_second, 1)
-    grad_middle, low_branch, part_gain_ffn = middle_back(
-        size, (grads_first, grads_second), all_packs, middle, cot, gain_mid
-    )
     grad_heads, all_branch = branch_back(size, low_branch, all_out)
-    grads_qkv, gate_sums = attend_back(
-        heads_all, grad_heads, dot_part, memory_part, logsum, *group
+    part_out = tokens_contract(attn, flat(all_branch)).astype(jnp.bfloat16)
+    part_out, grad_heads = lax.optimization_barrier((part_out, grad_heads))
+    grads_qkv, gate_sums, blocks_out, stat_ffn = attend_back(
+        size, heads_all, grad_heads, dot_part, memory_part, logsum, *group,
+        (hidden_first, hidden_second), all_packs, middle,
     )
     part_qkv = jnp.einsum(
         "td,jto->jdo", flat(all_in), grads_qkv, preferred_element_type=jnp.float32
     ).astype(jnp.bfloat16)
-    part_out = tokens_contract(attn, flat(all_branch)).astype(jnp.bfloat16)
-    hidden_first, grads_qkv, part_qkv, part_out, scattered_first = lax.optimization_barrier(
-        (hidden_first, grads_qkv, part_qkv, part_out, scattered_first)
+    grads_qkv, part_qkv, part_out, scattered_first = lax.optimization_barrier(
+        (grads_qkv, part_qkv, part_out, scattered_first)
     )
-    blocks_out, stat_ffn = ffn_out(size, (hidden_first, hidden_second), all_packs, middle)
     scattered_out, scattered_qkv = over_col(part_out, 1), over_col(part_qkv, 1)
-    blocks_out, grads_qkv, scattered_second = lax.optimization_barrier(
-        (blocks_out, grads_qkv, scattered_second)
+    blocks_grad, part_gain_attn, stream_out = stream_back(
+        size, grads_qkv, all_qkv, stream, grad_middle, gain_in, blocks_out
     )
-    blocks_grad, part_gain_attn = stream_back(size, grads_qkv, all_qkv, stream, grad_middle, gain_in)
+    blocks_grad, scattered_second = lax.optimization_barrier((blocks_grad, scattered_second))
     grad_out, grad_qkv = scattered_out.astype(jnp.float32), scattered_qkv.astype(jnp.float32)
     grad_gate_up = jnp.concatenate([scattered_first[:2], scattered_second[:2]], axis=2).astype(jnp.float32)
     grad_down = jnp.concatenate([scattered_first[2], scattered_second[2]], axis=1).T.astype(jnp.float32)
@@ -1479,8 +1534,8 @@
         axis=1,
     )
     stats = jnp.sqrt(jnp.concatenate([stat_branch[:, :2], stat_ffn[:, :2]], axis=1).T)
-    stream_out, stream_grad, stats_all, sums = leave(
-        size, cols, blocks_out, blocks_grad, jnp.pad(stats, ((0, 4), (0, 0))), sums
+    stream_grad, stats_all, sums = leave(
+        size, cols, blocks_grad, jnp.pad(stats, ((0, 4), (0, 0))), sums
     )
     stream_out = stream_out.reshape(stream_in.shape)
     stream_grad = stream_grad.reshape(stream_in.shape).astype(jnp.float32)

time: 921 us -> 862 us (0.936)
  Pallas kernels: 839 us -> 744 us
  waiting for transfers between devices: 2.24 us -> 41.7 us
    pallas_call x6 -> x5, Pallas kernels: 380 us -> 323 us  [the longest x1 86.7 us: stream_back(): pl.pallas_call(kernel, out_shape=[bf(cols, piece, depth), fl(1, D), bf(co...]
    all_gather x2, waiting for transfers between devices: 0.04 us -> 39.5 us  [local(): lax.all_gather(pack, 'col', axis=0, tiled=False)]
    pallas_call x2 -> x1, Pallas kernels: 53.5 us -> 26.8 us  [weight_grads(): pl.pallas_call(weight_grads_kernel, grid=(D // tile,), in_specs=[block, b...]
    pallas_call x2, Pallas kernels: 105 us -> 94 us  [feed_forward(): pl.pallas_call(kernel, out_shape=out_shape, in_specs=[ANY] * 3, out_specs...]
  transfers between devices with their start and end apart: 8 -> 8, of which waited for: 0 -> 2; matrix products, arithmetic and copies ran while one was open for 5% -> 6% of each run, Pallas kernels for 92% -> 87%
where the time goes in v5:
time: 862 us; the launch traced here: 853 us
  Pallas kernels  744 us (86%)
  waiting for transfers between devices  41.7 us (5%)
  matrix products  22.8 us (3%)
  local copies, waits for them, and re-layouts  15.2 us (2%)
  between operations  14.6 us (2%)
  other arithmetic  14 us (2%)
    pallas_call x1, Pallas kernels, enter(): pl.pallas_call(kernel, out_shape=[bf(piece, D), bf(piece, D), fl(1, D), f...  127 us
    pallas_call x2, Pallas kernels, feed_forward(): pl.pallas_call(kernel, out_shape=out_shape, in_specs=[ANY] * 3, out_specs...  94 us
    pallas_call x1, Pallas kernels, stream_back(): pl.pallas_call(kernel, out_shape=[bf(cols, piece, depth), fl(1, D), bf(co...  86.7 us
    pallas_call x1, Pallas kernels, leave(): pl.pallas_call(kernel, out_shape=[bf(groups, size, piece, depth), fl(grou...  80.6 us
    pallas_call x1, Pallas kernels, middle_back(): pl.pallas_call(kernel, out_shape=[fl(piece, D), bf(piece, D), fl(1, D), b...  73.8 us
    pallas_call x1, Pallas kernels, attend_back(): pl.pallas_call(functools.partial(attend_back_kernel, size, cols, depth, w...  65.5 us
    pallas_call x1, Pallas kernels, branch_out(): pl.pallas_call(kernel, out_shape=[fl(piece, D), bf(piece, D), fl(piece, H...  59.7 us
    pallas_call x1, Pallas kernels, project_heads(): pl.pallas_call(kernel, out_shape=[bf(3, heads, GLEN, HD), bf(size, piece,...  58.4 us
  transfers between devices with their start and end apart: 8, of which 2 were waited for; matrix products, arithmetic and copies ran while one was open for 6% of the time, Pallas kernels for 87%

profile of v5, /device:TPU:27, one launch (start us, length us, event | category | flops | bytes accessed | tf_op | source)
XLA Modules:
  0.0 852.7 jit_solution(2229530479424818431)
XLA Ops:
  7.2 0.7 all-gather.9.cloned.1.call-update
  8.0 0.7 all-gather.11.cloned.1.call-update
  8.7 1.3 select_maximum_fusion.gains_ref
  10.0 126.8 %enter.1 = (bf16[384,2048]{1,0:T(8,128)(2,1)}, bf16[384,2048]{1,0:T(8,128)(2,1)}, f32[1,2048]{1,0:T(1,128)}, f32[1,2048]{1,0:T(1,128)}, bf16[384,2048]{1,0:T(8,128)(2,1)}, /*index=5*/bf16[4,384,2048]{2,1,0:T(8,128)(2,1)}) custom-call(bf16[2,4,384,256]{3,2,1,0:T(8,128)(2,1)} %bitcast.67, bf16[2,4,384,256]{3,2,1,0:T(8,128)(2,1)} %bitcast.68, ...), custom_call_target="tpu_custom_call" | custom-call | flops 1000 | bytes 1000 | tf_op jit(solution)/shard_map/enter/pallas_call | solution.py:1333
  136.8 1.7 copy.32
  138.5 0.9 slice_bitcast_fusion
  139.4 0.2 fusion.2
  139.5 1.3 pad_maximum_fusion
  140.8 0.0 all-gather.15.cloned.1.call-start
  140.9 1.3 pad_maximum_fusion.1
  142.2 0.0 reduce-scatter.5.cloned.1.call-start
  142.3 0.5 add_divide_fusion.gate_ref
  142.8 58.4 %project_heads.1 = (bf16[3,4,1536,128]{3,2,1,0:T(8,128)(2,1)}, bf16[4,384,2048]{2,1,0:T(8,128)(2,1)}) custom-call(bf16[384,2048]{1,0:T(8,128)(2,1)} %get-tuple-element.64.x_ref, bf16[8,3,256,512]{3,2,1,0:T(8,128)(2,1)} %bitcast.63), custom_call_target="tpu_custom_call" | custom-call | flops 1000 | bytes 1000 | tf_op jit(solution)/shard_map/project_heads/pallas_call | solution.py:639
  201.2 16.6 %attend.1 = (bf16[1536,512]{1,0:T(8,128)(2,1)}, f32[4,1536,128]{2,1,0:T(8,128)}, f32[4,1536,128]{2,1,0:T(8,128)}, f32[4,1536,1]{2,1,0:T(8,128)}, f32[4,128,128]{2,1,0:T(8,128)}, /*index=5*/f32[4,1,128]{2,1,0:T(1,128)}) custom-call(s32[4]{0:T(128)} %bitcast.77, s32[4]{0:T(128)} %bitcast.79, f32[4]{0:T(128)} %add_divide_fusion.gate_ref, ...), custom_call_target="tpu_custom_call" | custom-call | flops 1000 | bytes 1000 | tf_op jit(solution)/shard_map/attend/pallas_call | solution.py:141
  217.8 59.7 %branch_out.1 = (f32[384,2048]{1,0:T(8,128)}, bf16[384,2048]{1,0:T(8,128)(2,1)}, f32[384,128]{1,0:T(8,128)}) custom-call(bf16[1536,512]{1,0:T(8,128)(2,1)} %get-tuple-element.66.attn_ref, bf16[8,512,256]{2,1,0:T(8,128)(2,1)} %bitcast.65, bf16[384,2048]{1,0:T(8,128)(2,1)} %get-tuple-element.67.x_ref, f32[1,2048]{1,0:T(1,128)} %get-tuple-element.68.gain_ref), custom_call_target="tpu_custom_call" | custom-call | flops 1000 | bytes 1000 | tf_op jit(solution)/shard_map/branch_out/pallas_call | solution.py:711
  277.5 8.3 all-gather.13.cloned.1.call-done
  285.8 58.9 %feed_first.1 = (bf16[1536,1024]{1,0:T(8,128)(2,1)}, bf16[2,1536,1024]{2,1,0:T(8,128)(2,1)}, bf16[4,384,2048]{2,1,0:T(8,128)(2,1)}) custom-call(bf16[384,2048]{1,0:T(8,128)(2,1)} %get-tuple-element.69.x_ref, bf16[8,3,256,1024]{3,2,1,0:T(8,128)(2,1)} %bitcast.55, bf16[4,384,2048]{2,1,0:T(8,128)(2,1)} %get-tuple-element.72.cot_ref.y_ref), custom_call_target="tpu_custom_call" | custom-call | flops 1000 | bytes 1000 | tf_op jit(solution)/shard_map/feed_first/pallas_call | solution.py:819
  344.7 26.8 %weight_grads.1 = bf16[3,2048,1024]{2,1,0:T(8,128)(2,1)} custom-call(bf16[1536,2048]{1,0:T(8,128)(2,1)} %bitcast.62, bf16[1536,2048]{1,0:T(8,128)(2,1)} %bitcast.61, bf16[2,1536,1024]{2,1,0:T(8,128)(2,1)} %get-tuple-element.73.g_ref.first_ref, bf16[1536,1024]{1,0:T(8,128)(2,1)} %get-tuple-element.75.h_ref.hidden_a), custom_call_target="tpu_custom_call" | custom-call | flops 1000 | bytes 1000 | tf_op jit(solution)/shard_map/weight_grads/pallas_call | solution.py:848
  371.6 0.0 reduce-scatter.7.cloned.1.call-start
  371.7 31.2 %all-gather.15.cloned.1.call-done = bf16[24,256,1024]{2,1,0:T(8,128)(2,1)} async-done(((bf16[3,256,1024]{2,1,0:T(8,128)(2,1)}), bf16[24,256,1024]{2,1,0:T(8,128)(2,1)}) %all-gather.15.cloned.1.call-update) | async-done | bytes 12582928 | tf_op jit(solution)/shard_map/all_gather | solution.py:1490
  402.9 35.1 %feed_second.1 = (bf16[1536,1024]{1,0:T(8,128)(2,1)}, bf16[2,1536,1024]{2,1,0:T(8,128)(2,1)}) custom-call(bf16[4,384,2048]{2,1,0:T(8,128)(2,1)} %get-tuple-element.76.x_ref, bf16[8,3,256,1024]{3,2,1,0:T(8,128)(2,1)} %bitcast.58, bf16[4,384,2048]{2,1,0:T(8,128)(2,1)} %get-tuple-element.72.cot_ref.y_ref), custom_call_target="tpu_custom_call" | custom-call | flops 1000 | bytes 1000 | tf_op jit(solution)/shard_map/feed_second/pallas_call | solution.py:819
  437.9 73.8 %middle_back.1 = (f32[384,2048]{1,0:T(8,128)}, bf16[384,2048]{1,0:T(8,128)(2,1)}, f32[1,2048]{1,0:T(1,128)}, bf16[3,2048,1024]{2,1,0:T(8,128)(2,1)}) custom-call(bf16[2,1536,1024]{2,1,0:T(8,128)(2,1)} %get-tuple-element.73.g_ref.first_ref, bf16[2,1536,1024]{2,1,0:T(8,128)(2,1)} %get-tuple-element.77.second_ref, bf16[8,3,256,1024]{3,2,1,0:T(8,128)(2,1)} %bitcast.56, ...), custom_call_target="tpu_custom_call" | custom-call | flops 1000 | bytes 1000 | tf_op jit(solution)/shard_map/middle_back/pallas_call | solution.py:1000
  511.8 0.0 reduce-scatter.11.cloned.1.call-start
  511.9 55.1 %branch_back.1 = (bf16[4,1536,128]{2,1,0:T(8,128)(2,1)}, bf16[4,384,2048]{2,1,0:T(8,128)(2,1)}) custom-call(bf16[384,2048]{1,0:T(8,128)(2,1)} %get-tuple-element.81.x_ref, bf16[8,512,256]{2,1,0:T(8,128)(2,1)} %bitcast.66), custom_call_target="tpu_custom_call" | custom-call | flops 1000 | bytes 1000 | tf_op jit(solution)/shard_map/branch_back/pallas_call | solution.py:1053
  567.0 7.5 convolution_convert_fusion
  574.6 65.5 %attend_back.1 = (bf16[3,1536,512]{2,1,0:T(8,128)(2,1)}, f32[4,1,128]{2,1,0:T(1,128)}, bf16[8,384,256]{2,1,0:T(8,128)(2,1)}, f32[384,128]{1,0:T(8,128)}) custom-call(s32[4]{0:T(128)} %bitcast.78, s32[4]{0:T(128)} %bitcast.80, f32[4]{0:T(128)} %add_divide_fusion.gate_ref, bf16[3,4,1536,128]{3,2,1,0:T(8,128)(2,1)} %get-tuple-element.65.qkv_ref, ...), custom_call_target="tpu_custom_call" | custom-call | flops 1000 | bytes 1000 | tf_op jit(solution)/shard_map/attend_back/pallas_call | solution.py:302
  640.1 15.2 %convert_bitcast_fusion = bf16[3,2048,512]{1,2,0:T(8,128)(2,1)} fusion(bf16[3,1536,512]{2,1,0:T(8,128)(2,1)} %get-tuple-element.92.g_ref, bf16[1536,2048,1]{1,0,2:T(8,128)(2,1)} %bitcast.85), kind=kOutput, calls=%fused_computation | convolution fusion | flops 9666822144 | bytes 17301504 | tf_op jit(solution)/shard_map/td,jto->jdo/dot_general | solution.py:1510
  655.4 0.7 reduce-scatter.9.cloned.1.call-update
  656.1 0.1 copy-done.7
  656.3 0.1 copy.35
  656.4 0.1 reduce_sum.9
  656.5 0.1 copy.36
  656.7 0.6 pad.13.stats_ref
  657.3 86.7 %stream_back.1 = (bf16[8,384,256]{2,1,0:T(8,128)(2,1)}, f32[1,2048]{1,0:T(1,128)}, bf16[2,4,384,256]{3,2,1,0:T(8,128)(2,1)}) custom-call(bf16[3,1536,512]{2,1,0:T(8,128)(2,1)} %get-tuple-element.92.g_ref, bf16[8,3,256,512]{3,2,1,0:T(8,128)(2,1)} %bitcast.64, bf16[384,2048]{1,0:T(8,128)(2,1)} %get-tuple-element.67.x_ref, ...), custom_call_target="tpu_custom_call" | custom-call | flops 1000 | bytes 1000 | tf_op jit(solution)/shard_map/stream_back/pallas_call | solution.py:1114
  744.1 1.5 pad_maximum_fusion.2.sums_ref
  745.6 80.6 %leave.1 = (bf16[2,4,384,256]{3,2,1,0:T(8,128)(2,1)}, f32[2,4,8,384]{3,2,1,0:T(8,128)}, f32[8,256]{1,0:T(8,128)}) custom-call(bf16[8,384,256]{2,1,0:T(8,128)(2,1)} %get-tuple-element.99.grad_ref, f32[8,384]{1,0:T(8,128)} %pad.13.stats_ref, f32[8,8,256]{2,1,0:T(8,128)} %pad_maximum_fusion.2.sums_ref), custom_call_target="tpu_custom_call" | custom-call | flops 1000 | bytes 1000 | tf_op jit(solution)/shard_map/leave/pallas_call | solution.py:1425
  826.1 1.5 slice.55
  827.7 1.0 slice.48
  828.7 0.7 copy-done
  829.5 0.2 convert_bitcast_fusion.1
  829.8 1.8 copy.38
  831.6 1.2 slice_bitcast_fusion.4
  832.8 1.3 fusion.3
  834.1 3.9 maximum_convert_fusion
  838.0 2.0 bitcast_convert_fusion
  840.0 1.9 convert_element_type.42
  841.9 2.6 copy.37
  844.5 1.1 copy.41
  (47 shorter events, 0.5 us)
Async XLA Ops:
  7.2 135.6 %all-gather.9.cloned.1.call-start = ((), (), s32[]{:S(2)}) async-start(), calls=%async_computation.8 | async-start | bytes 7077888 | tf_op jit(solution)/shard_map/all_gather | solution.py:1478
  7.9 209.9 %all-gather.11.cloned.1.call-start = ((), (), s32[]{:S(2)}) async-start(), calls=%async_computation.9 | async-start | bytes 2359296 | tf_op jit(solution)/shard_map/all_gather | solution.py:1478
  8.7 277.1 %all-gather.13.cloned.1.call-start = ((), (), s32[]{:S(2)}) async-start(), calls=%async_computation.10 | async-start | bytes 14155776 | tf_op jit(solution)/shard_map/all_gather | solution.py:1490
  136.8 2.5 copy-start.1
  139.5 1.4 copy-start.2
  140.8 262.0 %all-gather.15.cloned.1.call-start = ((), (), s32[]{:S(2)}) async-start(), calls=%async_computation.11 | async-start | bytes 14155776 | tf_op jit(solution)/shard_map/all_gather | solution.py:1490
  140.9 1.4 copy-start.11
  142.2 513.1 %reduce-scatter.5.cloned.1.call-start = ((), (), s32[]{:S(2)}) async-start(), calls=%async_computation.4 | async-start | bytes 14155776 | tf_op jit(solution)/shard_map/reduce_scatter | solution.py:1453
  371.6 372.5 %reduce-scatter.7.cloned.1.call-start = ((), (), s32[]{:S(2)}) async-start(), calls=%async_computation.5 | async-start | bytes 14155776 | tf_op jit(solution)/shard_map/reduce_scatter | solution.py:1453
  511.8 55.2 %copy-start.5 = (bf16[1536,512]{1,0:T(8,128)(2,1)S(1)}, bf16[1536,512]{1,0:T(8,128)(2,1)}, u32[]{:S(2)}) copy-start(bf16[1536,512]{1,0:T(8,128)(2,1)} %get-tuple-element.66.attn_ref) | copy-start | bytes 4718596
  511.8 328.2 %reduce-scatter.11.cloned.1.call-start = ((), (), s32[]{:S(2)}) async-start(), calls=%async_computation.7 | async-start | bytes 2359296 | tf_op jit(solution)/shard_map/reduce_scatter | solution.py:1453
  655.3 0.9 copy-start.7
  655.3 1.1 copy-start.10
  655.3 1.2 copy-start.8
  655.4 186.6 %reduce-scatter.9.cloned.1.call-start = ((), (), s32[]{:S(2)}) async-start(), calls=%async_computation.6 | async-start | bytes 7077888 | tf_op jit(solution)/shard_map/reduce_scatter | solution.py:1453
  657.3 86.8 %copy-start.9 = (f32[1,2048]{1,0:T(1,128)S(1)}, f32[1,2048]{1,0:T(1,128)}, u32[]{:S(2)}) copy-start(f32[1,2048]{1,0:T(1,128)} %get-tuple-element.103) | copy-start | bytes 24580
  744.0 83.6 %copy-start.4 = (bf16[3,256,1024]{2,1,0:T(8,128)(2,1)S(1)}, bf16[3,256,1024]{2,1,0:T(8,128)(2,1)}, u32[]{:S(2)}) copy-start(bf16[3,256,1024]{2,1,0:T(8,128)(2,1)} %reduce-scatter.5.cloned.1.call-done) | copy-start | bytes 4718596
  827.7 1.8 copy-start
  829.8 4.4 slice-start
  834.1 3.9 copy-start.6
  840.0 4.5 copy-start.3
Sparse Core Ops, SparseCore 0:
  9.7 118.0 all-gather.8
  129.4 29.4 all-gather.10
  161.1 124.6 all-gather.12
  287.9 114.9 all-gather.14
  405.0 127.2 reduce-scatter.4
  534.4 127.5 reduce-scatter.6
  664.3 57.6 reduce-scatter.10
  724.3 97.7 reduce-scatter.8

commit v6 on v5

--- a/solution.py
+++ b/solution.py
@@ -172,7 +172,6 @@
 ):
     head = pl.program_id(0)
     piece = GLEN // size
-    span = 512
     scatter = Scatter(size, stage, land, total, send, receive)
 
     def h_load(i, step):
@@ -181,33 +180,24 @@
 
     def w_load(i, c):
         return pltpu.make_async_copy(
-            (pack_a, pack_b)[i].at[c, 2], w.at[i, pl.ds(c * depth, depth), :], w_sem.at[i, c]
+            (pack_a, pack_b)[i].at[c, 2], w.at[i, pl.ds(pl.multiple_of(c * depth, depth), depth), :], w_sem.at[i, c]
         )
 
     def partial(step, at, store):
         for i in range(2):
             h_load(i, step).wait()
 
-        def one(depth_rows, half, columns):
+        @span_loop
+        def _(t, half, columns, depth_rows):
+            if step == 0:
+                for k in range(SPAN // depth):
+                    for i in range(2):
+                        w_load(i, t * (SPAN // depth) + k).wait()
             rows = pl.ds(pl.multiple_of(at * piece, piece), piece)
             store(
                 half, columns,
                 plain_dot(h[0, rows, :], w[0, depth_rows, :], NT) + plain_dot(h[1, rows, :], w[1, depth_rows, :], NT),
             )
-
-        if step == 0:
-            for t in range(D // span):
-                for c in range(t * span // depth, (t + 1) * span // depth):
-                    for i in range(2):
-                        w_load(i, c).wait()
-                half, inside = divmod(t * span, HALF)
-                one(slice(t * span, (t + 1) * span), half, slice(inside, inside + span))
-            return
-        for half in range(2):
-            @pl.loop(0, HALF // span)
-            def _(t):
-                columns = pl.ds(pl.multiple_of(t * span, span), span)
-                one(pl.ds(pl.multiple_of(half * HALF + t * span, span), span), half, columns)
 
     @pl.when(head == 0)
     def _():
@@ -344,6 +334,10 @@
     )
 
 
+def dma(*shape):
+    return pltpu.SemaphoreType.DMA(shape)
+
+
 def here():
     return lax.axis_index("row"), lax.axis_index("col")
 
@@ -439,6 +433,44 @@
             copy.wait_send()
 
 
+class CoreGather:
+    def __init__(self, cols, source, target, far_send, far_receive, near_send, near_receive, own):
+        row, col = here()
+        pair = (col // 2) * 2 + 1 - lax.rem(col, 2)
+        chips = cols // 2
+        self.greets = [(row, lax.rem(col + 2 * e, cols)) for e in range(1, chips)] + [(row, pair)]
+        self.far = [
+            remote(source, target.at[col], far_send.at[e], far_receive.at[e], peer)
+            for e, peer in enumerate(self.greets[:-1])
+        ]
+        self.near = [remote(source, target.at[col], near_send.at[0], near_receive.at[0], (row, pair))]
+        for e in range(1, chips):
+            place = target.at[lax.rem(col + cols - 2 * e, cols)]
+            self.near.append(remote(place, place, near_send.at[e], near_receive.at[e], (row, pair)))
+        self.keep = pltpu.make_async_copy(source, target.at[col], own)
+
+    @staticmethod
+    def scratch(cols):
+        far, near = cols // 2 - 1, cols // 2
+        return [dma(far), dma(far), dma(near), dma(near), pltpu.SemaphoreType.DMA]
+
+    def start(self):
+        for copy in [*self.far, self.near[0], self.keep]:
+            copy.start()
+
+    def forward(self):
+        for e, copy in enumerate(self.far):
+            copy.wait_recv()
+            self.near[e + 1].start()
+
+    def finish(self):
+        for copy in self.near:
+            copy.wait()
+        for copy in self.far:
+            copy.wait_send()
+        self.keep.wait()
+
+
 class Scatter:
     def __init__(self, size, stage, land, total, send, receive):
         self.size, self.stage, self.land, self.total = size, stage, land, total
@@ -588,6 +620,21 @@
     return run
 
 
+SPAN = 512
+
+
+def span_loop(body):
+    inside = HALF // SPAN
+
+    @pl.loop(0, D // SPAN)
+    def _(t):
+        body(
+            t, t // inside,
+            pl.ds(pl.multiple_of(lax.rem(t, inside) * SPAN, SPAN), SPAN),
+            pl.ds(pl.multiple_of(t * SPAN, SPAN), SPAN),
+        )
+
+
 def comm_params(identity):
     return pltpu.CompilerParams(
         collective_id=identity, has_side_effects=True, vmem_limit_bytes=BIG_VMEM
@@ -602,18 +649,21 @@
     return jax.ShapeDtypeStruct(shape, jnp.float32)
 
 
-def project_heads(size, normed, w_all):
+def project_heads(size, normed, w_all, w_out):
     piece = normed.shape[0]
     cols, _, depth, width = w_all.shape
     heads = width // HD
 
     def kernel(
-        x_ref, w_ref, heads_ref, all_ref,
-        land, send, receive, own, w, w_sem, all_sem,
+        x_ref, w_ref, out_ref, heads_ref, all_ref, all_out_ref,
+        land, send, receive, own, w, w_sem, all_sem, *rest,
     ):
         loads = fetches([(w_ref.at[c], w.at[:, pl.ds(c * depth, depth), :]) for c in range(cols)], w_sem)
         gather = Gather(size, x_ref, land, send, receive, own)
-        gather.start()
+        beside = CoreGather(cols, out_ref, all_out_ref, *rest)
+        greet([*gather.peers, *beside.greets])
+        gather.start(greeted=True)
+        beside.start()
 
         def compute(row, slot):
             store = pltpu.make_async_copy(land.at[row], all_ref.at[row], all_sem.at[slot])
@@ -631,26 +681,29 @@
         wait_all(loads)
         stores = [compute(gather.row, 0)]
         gather.forward()
+        beside.forward()
         for step in range(size - 1):
             stores.append(compute(gather.wait(step), step + 1))
+        beside.finish()
         wait_all(stores)
         gather.finish()
 
     return pl.pallas_call(
         kernel,
-        out_shape=[bf(3, heads, GLEN, HD), bf(size, piece, D)],
-        in_specs=[ANY, ANY],
-        out_specs=[VMEM, ANY],
+        out_shape=[bf(3, heads, GLEN, HD), bf(size, piece, D), bf(cols, *w_out.shape)],
+        in_specs=[ANY, ANY, ANY],
+        out_specs=[VMEM, ANY, ANY],
         scratch_shapes=gather_scratch(size, piece)
         + [
             pltpu.VMEM((3, D, width), jnp.bfloat16),
             pltpu.SemaphoreType.DMA((cols,)),
             pltpu.SemaphoreType.DMA((size,)),
-        ],
+        ]
+        + CoreGather.scratch(cols),
         compiler_params=comm_params(1),
         cost_estimate=SHORT,
         name="project_heads",
-    )(normed, w_all)
+    )(normed, w_all, w_out)
 
 
 def strip_loop(piece, body):
@@ -683,13 +736,10 @@
         def partial(step, row, store):
             rows = pl.ds(pl.multiple_of(row * piece, piece), piece)
             left = attn_ref[rows, :]
-            for half in range(2):
-                for t in range(2):
-                    columns = slice(half * HALF + t * HALF // 2, half * HALF + (t + 1) * HALF // 2)
-                    store(
-                        half, slice(t * HALF // 2, (t + 1) * HALF // 2),
-                        jnp.dot(left, w[:, columns], preferred_element_type=jnp.float32),
-                    )
+
+            @span_loop
+            def _(t, half, columns, depth_rows):
+                store(half, columns, plain_dot(left, w[:, depth_rows], NN))
 
         scatter.run(partial)
 
@@ -746,10 +796,7 @@
         if not first:
             x_loads = fetches([(x_ref.at[row], land.at[row]) for row in order], own)
 
-        def backward(step):
-            row = order[step]
-            cot_loads[step].wait()
-
+        def backward(row):
             @tiles_of(wide, tile)
             def _(t, columns):
                 back[row, :, columns] = plain_dot(cot_all[row], w[2, :, columns], NN).astype(jnp.bfloat16)
@@ -762,8 +809,7 @@
                 pltpu.make_async_copy(stage.at[slot, 2], grad_ref.at[1, rows, columns], out_sem.at[slot, 2]),
             ]
 
-        def compute(step):
-            row = order[step]
+        def compute(row):
             if first:
                 store = pltpu.make_async_copy(land.at[row], all_ref.at[row], all_sem)
                 store.start()
@@ -795,20 +841,35 @@
                 store.wait()
 
         wait_all(w_loads[:cols])
-        backward(0)
         if first:
+            cot_loads[0].wait()
+            backward(order[0])
             gather.forward()
-        for step in range(1, size):
-            backward(step)
+            wait_all(cot_loads[1:])
+
+            @pl.loop(1, size)
+            def _(d):
+                backward(lax.rem(gather.row + d, size))
+
+            wait_all(w_loads[cols:])
+            for step in range(size):
+                if step:
+                    gather.wait(step - 1)
+                compute(order[step])
+            gather.finish()
+            return
+
+        @pl.loop(0, size)
+        def _(row):
+            pltpu.make_async_copy(cot_ref.at[row], cot_all.at[row], cot_sem.at[row]).wait()
+            backward(row)
+
         wait_all(w_loads[cols:])
-        for step in range(size):
-            if not first:
-                x_loads[step].wait()
-            elif step:
-                gather.wait(step - 1)
-            compute(step)
-        if first:
-            gather.finish()
+
+        @pl.loop(0, size)
+        def _(row):
+            pltpu.make_async_copy(x_ref.at[row], land.at[row], own.at[row]).wait()
+            compute(row)
 
     out_shape = [bf(GLEN, wide), bf(2, GLEN, wide)]
     if first:
@@ -836,13 +897,14 @@
 
 
 def weight_grads_kernel(x_ref, y_ref, g_ref, h_ref, out_ref):
-    for j in range(2):
+    count = g_ref.shape[0]
+    for j in range(count):
         out_ref[j] = plain_dot(x_ref[...], g_ref[j], TN).astype(jnp.bfloat16)
-    out_ref[2] = plain_dot(y_ref[...], h_ref[...], TN).astype(jnp.bfloat16)
+    out_ref[count] = plain_dot(y_ref[...], h_ref[...], TN).astype(jnp.bfloat16)
 
 
 def weight_grads(x, grads, y, hidden):
-    wide = hidden.shape[1]
+    count, _, wide = grads.shape
     tile = 256
     block = pl.BlockSpec((GLEN, tile), lambda i: (0, i))
     return pl.pallas_call(
@@ -850,11 +912,11 @@
         grid=(D // tile,),
         in_specs=[
             block, block,
-            pl.BlockSpec((2, GLEN, wide), lambda i: (0, 0, 0), pipeline_mode=pl.Buffered(1)),
+            pl.BlockSpec((count, GLEN, wide), lambda i: (0, 0, 0), pipeline_mode=pl.Buffered(1)),
             pl.BlockSpec((GLEN, wide), lambda i: (0, 0), pipeline_mode=pl.Buffered(1)),
         ],
-        out_specs=pl.BlockSpec((3, tile, wide), lambda i: (0, i, 0)),
-        out_shape=bf(3, D, wide),
+        out_specs=pl.BlockSpec((count + 1, tile, wide), lambda i: (0, i, 0)),
+        out_shape=bf(count + 1, D, wide),
         compiler_params=pltpu.CompilerParams(vmem_limit_bytes=BIG_VMEM),
         cost_estimate=SHORT,
         name="weight_grads",
@@ -872,7 +934,6 @@
 def middle_back(size, grads, packs, middle, cot, gain, tokens, all_cot, hidden):
     piece = middle.shape[0]
     cols, _, depth, wide = packs[0].shape
-    tile = 512
     block = 256
 
     def kernel(
@@ -898,7 +959,7 @@
 
         def w_load(i, c):
             return pltpu.make_async_copy(
-                pack_refs[i].at[c, pl.ds(0, 2)], w.at[i, :, pl.ds(c * depth, depth), :], w_sem.at[i, c]
+                pack_refs[i].at[c, pl.ds(0, 2)], w.at[i, :, pl.ds(pl.multiple_of(c * depth, depth), depth), :], w_sem.at[i, c]
             )
 
         first_load(0).start()
@@ -913,31 +974,23 @@
         h_load.start()
         gain_sum[...] = jnp.zeros_like(gain_sum)
 
-        def one(step, rows, depth_rows, store, half, columns):
-            value = 0.0
-            for j in range(2):
-                value += plain_dot(g_first[step % 2, j], w[0, j, depth_rows, :], NT)
-                value += plain_dot(g_second[j, rows, :], w[1, j, depth_rows, :], NT)
-            store(half, columns, value)
-
         def partial(step, at, store):
             first_load(step).wait()
             second_load(step).wait()
-            rows = piece_rows(at)
-            if step == 0:
-                for t in range(D // tile):
-                    for c in range(t * tile // depth, (t + 1) * tile // depth):
+
+            @span_loop
+            def _(t, half, columns, depth_rows):
+                if step == 0:
+                    for k in range(SPAN // depth):
                         for i in range(2):
-                            w_load(i, c).wait()
-                    half, inside = divmod(t * tile, HALF)
-                    one(step, rows, slice(t * tile, (t + 1) * tile), store, half, slice(inside, inside + tile))
-            else:
-                for half in range(2):
-                    @pl.loop(0, HALF // tile)
-                    def _(t):
-                        columns = pl.ds(pl.multiple_of(t * tile, tile), tile)
-                        depth_rows = pl.ds(pl.multiple_of(half * HALF + t * tile, tile), tile)
-                        one(step, rows, depth_rows, store, half, columns)
+                            w_load(i, t * (SPAN // depth) + k).wait()
+                rows = piece_rows(at)
+                value = 0.0
+                for j in range(2):
+                    value += plain_dot(g_first[step % 2, j], w[0, j, depth_rows, :], NT)
+                    value += plain_dot(g_second[j, rows, :], w[1, j, depth_rows, :], NT)
+                store(half, columns, value)
+
             if step + 2 < size:
                 first_load(step + 2).start()
 
@@ -1070,7 +1123,6 @@
 def stream_back(size, grads, w_all, x, grad_middle, gain, blocks_out):
     piece = x.shape[0]
     cols, _, depth, width = w_all.shape
-    tile = 512
 
     def kernel(
         g_ref, w_ref, x_ref, middle_ref, gain_ref, blocks_ref, out_ref, gain_sum, target_ref,
@@ -1085,16 +1137,13 @@
         gain_sum[...] = jnp.zeros_like(gain_sum)
 
         def partial(step, row, store):
-            rows = pl.ds(pl.multiple_of(row * piece, piece), piece)
-            for half in range(2):
-                @pl.loop(0, HALF // tile)
-                def _(t):
-                    columns = pl.ds(pl.multiple_of(t * tile, tile), tile)
-                    depth_rows = pl.ds(pl.multiple_of(half * HALF + t * tile, tile), tile)
-                    value = plain_dot(g_ref[0, rows, :], w[0, depth_rows, :], NT)
-                    for j in (1, 2):
-                        value += plain_dot(g_ref[j, rows, :], w[j, depth_rows, :], NT)
-                    store(half, columns, value)
+            @span_loop
+            def _(t, half, columns, depth_rows):
+                rows = pl.ds(pl.multiple_of(row * piece, piece), piece)
+                value = plain_dot(g_ref[0, rows, :], w[0, depth_rows, :], NT)
+                for j in (1, 2):
+                    value += plain_dot(g_ref[j, rows, :], w[j, depth_rows, :], NT)
+                store(half, columns, value)
 
         scatter.run(partial, outward.forward, greeted=True)
 
@@ -1130,10 +1179,6 @@
     return [(lax.rem(row + d, size), col) for d in range(1, size)] + [
         (row, lax.rem(col + e, cols)) for e in range(1, cols)
     ]
-
-
-def dma(*shape):
-    return pltpu.SemaphoreType.DMA(shape)
 
 
 class Inward:
@@ -1445,10 +1490,6 @@
     )(blocks_grad, stats, sums)
 
 
-def tokens_contract(left, right):
-    return lax.dot_general(left, right, (TN, ((), ())), preferred_element_type=jnp.float32)
-
-
 def over_col(partial, axis):
     return lax.psum_scatter(partial.astype(jnp.bfloat16), "col", scatter_dimension=axis, tiled=True)
 
@@ -1475,20 +1516,19 @@
     head_here = memory.shape[1]
     size = lax.axis_size("row")
     cols = lax.axis_size("col")
-    all_qkv, all_out = (lax.all_gather(w, "col", axis=0, tiled=False) for w in (w_qkv, w_out))
-    gate_value = jax.nn.sigmoid(gate_logit)
-    group = (memory[0], memory_norm[0], offsets[0], lengths[0], gate_value)
-    stream, normed_in, gain_in, gain_mid, cot, all_cot = enter(
-        size, cols, stream_in, cotangent, jnp.stack([gain_attn, gain_ffn])
-    )
-    normed_in, w_gate_up, w_down = lax.optimization_barrier((normed_in, w_gate_up, w_down))
+    all_qkv = lax.all_gather(w_qkv, "col", axis=0, tiled=False)
     units = w_down.shape[0] // 2
     packs = [
         jnp.concatenate([w_gate_up[:, :, part], w_down[part].T[None]], axis=0)
         for part in (slice(0, units), slice(units, None))
     ]
     all_packs = [lax.all_gather(pack, "col", axis=0, tiled=False) for pack in packs]
-    heads_all, all_in = project_heads(size, normed_in, all_qkv)
+    gate_value = jax.nn.sigmoid(gate_logit)
+    group = (memory[0], memory_norm[0], offsets[0], lengths[0], gate_value)
+    stream, normed_in, gain_in, gain_mid, cot, all_cot = enter(
+        size, cols, stream_in, cotangent, jnp.stack([gain_attn, gain_ffn])
+    )
+    heads_all, all_in, all_out = project_heads(size, normed_in, all_qkv, w_out)
     attn, dot_part, memory_part, logsum, memory_new, norm_new = attend(heads_all, *group)
     middle, normed_ffn, stat_branch = branch_out(size, attn, all_out, stream, gain_mid)
     hidden_first, grads_first, all_ffn = feed_forward(size, normed_ffn, all_packs[0], all_cot, True)
@@ -1501,26 +1541,20 @@
     )
     scattered_second = over_col(part_second, 1)
     grad_heads, all_branch = branch_back(size, low_branch, all_out)
-    part_out = tokens_contract(attn, flat(all_branch)).astype(jnp.bfloat16)
-    part_out, grad_heads = lax.optimization_barrier((part_out, grad_heads))
     grads_qkv, gate_sums, blocks_out, stat_ffn = attend_back(
         size, heads_all, grad_heads, dot_part, memory_part, logsum, *group,
         (hidden_first, hidden_second), all_packs, middle,
     )
-    part_qkv = jnp.einsum(
-        "td,jto->jdo", flat(all_in), grads_qkv, preferred_element_type=jnp.float32
-    ).astype(jnp.bfloat16)
-    grads_qkv, part_qkv, part_out, scattered_first = lax.optimization_barrier(
-        (grads_qkv, part_qkv, part_out, scattered_first)
-    )
-    scattered_out, scattered_qkv = over_col(part_out, 1), over_col(part_qkv, 1)
+    part_attn = weight_grads(flat(all_in), grads_qkv, flat(all_branch), attn)
+    grads_qkv, part_attn, scattered_first = lax.optimization_barrier((grads_qkv, part_attn, scattered_first))
+    scattered_attn = over_col(part_attn, 1)
     blocks_grad, part_gain_attn, stream_out = stream_back(
         size, grads_qkv, all_qkv, stream, grad_middle, gain_in, blocks_out
     )
-    blocks_grad, scattered_second = lax.optimization_barrier((blocks_grad, scattered_second))
-    grad_out, grad_qkv = scattered_out.astype(jnp.float32), scattered_qkv.astype(jnp.float32)
     grad_gate_up = jnp.concatenate([scattered_first[:2], scattered_second[:2]], axis=2).astype(jnp.float32)
     grad_down = jnp.concatenate([scattered_first[2], scattered_second[2]], axis=1).T.astype(jnp.float32)
+    blocks_grad, grad_gate_up, grad_down = lax.optimization_barrier((blocks_grad, grad_gate_up, grad_down))
+    grad_qkv, grad_out = scattered_attn[:3].astype(jnp.float32), scattered_attn[3].T.astype(jnp.float32)
     logit_part = gate_value * (1.0 - gate_value) * jnp.sum(gate_sums, axis=(1, 2))
     features_here = gain_attn.shape[0]
     sums = jnp.concatenate(

time: 862 us -> 841 us (0.976)
  waiting for transfers between devices: 41.7 us -> 4.48 us
  Pallas kernels: 744 us -> 780 us
  matrix products: 22.8 us -> 0 us
    pallas_call x1, Pallas kernels: 58.4 us -> 95.5 us  [project_heads(): pl.pallas_call(kernel, out_shape=[bf(3, heads, GLEN, HD), bf(size, piece,...]
    all_gather x2, waiting for transfers between devices: 39.5 us -> 3.67 us  [local(): lax.all_gather(pack, 'col', axis=0, tiled=False)]
    dot_general x2 -> x0, matrix products: 22.8 us -> none  [the longest x1 15.2 us: local(): jnp.einsum('td,jto->jdo', flat(all_in), grads_qkv, preferred_element_type...]
    pallas_call x1, Pallas kernels: 86.7 us -> 108 us  [stream_back(): pl.pallas_call(kernel, out_shape=[bf(cols, piece, depth), fl(1, D), bf(co...]
    pallas_call x1 -> x2, Pallas kernels: 26.8 us -> 45.9 us  [weight_grads(): pl.pallas_call(weight_grads_kernel, grid=(D // tile,), in_specs=[block, b...]
  transfers between devices with their start and end apart: 8 -> 6, of which waited for: 2 -> 1; matrix products, arithmetic and copies ran while one was open for 6% -> 3% of each run, Pallas kernels for 87% -> 94%
where the time goes in v6:
time: 841 us; the launch traced here: 831 us
  Pallas kernels  780 us (93%)
  local copies, waits for them, and re-layouts  17.3 us (2%)
  between operations  14.6 us (2%)
  other arithmetic  14.2 us (2%)
    pallas_call x1, Pallas kernels, enter(): pl.pallas_call(kernel, out_shape=[bf(piece, D), bf(piece, D), fl(1, D), f...  123 us
    pallas_call x1, Pallas kernels, stream_back(): pl.pallas_call(kernel, out_shape=[bf(cols, piece, depth), fl(1, D), bf(co...  108 us
    pallas_call x1, Pallas kernels, project_heads(): pl.pallas_call(kernel, out_shape=[bf(3, heads, GLEN, HD), bf(size, piece,...  95.5 us
    pallas_call x2, Pallas kernels, feed_forward(): pl.pallas_call(kernel, out_shape=out_shape, in_specs=[ANY] * 3, out_specs...  86.8 us
    pallas_call x1, Pallas kernels, leave(): pl.pallas_call(kernel, out_shape=[bf(groups, size, piece, depth), fl(grou...  73.5 us
    pallas_call x1, Pallas kernels, middle_back(): pl.pallas_call(kernel, out_shape=[fl(piece, D), bf(piece, D), fl(1, D), b...  70.1 us
    pallas_call x1, Pallas kernels, attend_back(): pl.pallas_call(functools.partial(attend_back_kernel, size, cols, depth, w...  58 us
    pallas_call x1, Pallas kernels, branch_out(): pl.pallas_call(kernel, out_shape=[fl(piece, D), bf(piece, D), fl(piece, H...  55.8 us
  transfers between devices with their start and end apart: 6, of which 1 were waited for; matrix products, arithmetic and copies ran while one was open for 3% of the time, Pallas kernels for 94%

profile of v6, /device:TPU:27, one launch (start us, length us, event | category | flops | bytes accessed | tf_op | source)
XLA Modules:
  0.0 831.3 jit_solution(7833793157943010451)
XLA Ops:
  7.2 0.7 all-gather.7.cloned.1.call-update
  8.0 2.1 fusion.3
  10.0 1.0 copy.37
  11.0 0.2 fusion.2
  11.2 0.9 copy-done.4
  12.1 1.3 pad_maximum_fusion
  13.4 0.0 all-gather.11.cloned.1.call-start
  13.4 0.2 copy.38
  13.7 1.3 pad_maximum_fusion.1
  15.0 0.0 reduce-scatter.4.cloned.1.call-start
  15.1 0.6 select_maximum_fusion.gains_ref
  15.7 122.6 %enter.1 = (bf16[384,2048]{1,0:T(8,128)(2,1)}, bf16[384,2048]{1,0:T(8,128)(2,1)}, f32[1,2048]{1,0:T(1,128)}, f32[1,2048]{1,0:T(1,128)}, bf16[384,2048]{1,0:T(8,128)(2,1)}, /*index=5*/bf16[4,384,2048]{2,1,0:T(8,128)(2,1)}) custom-call(bf16[2,4,384,256]{3,2,1,0:T(8,128)(2,1)} %bitcast.65, bf16[2,4,384,256]{3,2,1,0:T(8,128)(2,1)} %bitcast.66, ...), custom_call_target="tpu_custom_call" | custom-call | flops 1000 | bytes 1000 | tf_op jit(solution)/shard_map/enter/pallas_call | solution.py:1378
  138.2 0.5 add_divide_fusion.gate_ref
  138.8 95.5 %project_heads.1 = (bf16[3,4,1536,128]{3,2,1,0:T(8,128)(2,1)}, bf16[4,384,2048]{2,1,0:T(8,128)(2,1)}, bf16[8,512,256]{2,1,0:T(8,128)(2,1)}) custom-call(bf16[384,2048]{1,0:T(8,128)(2,1)} %get-tuple-element.59.x_ref, bf16[8,3,256,512]{3,2,1,0:T(8,128)(2,1)} %bitcast.59, bf16[512,256]{1,0:T(8,128)(2,1)} %out_ref.1), custom_call_target="tpu_custom_call" | custom-call | flops 1000 | bytes 1000 | tf_op jit(solution)/shard_map/project_heads/pallas_call | solution.py:691
  234.3 16.6 %attend.1 = (bf16[1536,512]{1,0:T(8,128)(2,1)}, f32[4,1536,128]{2,1,0:T(8,128)}, f32[4,1536,128]{2,1,0:T(8,128)}, f32[4,1536,1]{2,1,0:T(8,128)}, f32[4,128,128]{2,1,0:T(8,128)}, /*index=5*/f32[4,1,128]{2,1,0:T(1,128)}) custom-call(s32[4]{0:T(128)} %bitcast.75, s32[4]{0:T(128)} %bitcast.77, f32[4]{0:T(128)} %add_divide_fusion.gate_ref, ...), custom_call_target="tpu_custom_call" | custom-call | flops 1000 | bytes 1000 | tf_op jit(solution)/shard_map/attend/pallas_call | solution.py:141
  250.9 55.8 %branch_out.1 = (f32[384,2048]{1,0:T(8,128)}, bf16[384,2048]{1,0:T(8,128)(2,1)}, f32[384,128]{1,0:T(8,128)}) custom-call(bf16[1536,512]{1,0:T(8,128)(2,1)} %get-tuple-element.61.attn_ref.h_ref, bf16[8,512,256]{2,1,0:T(8,128)(2,1)} %get-tuple-element.62.w_ref, bf16[384,2048]{1,0:T(8,128)(2,1)} %get-tuple-element.63.x_ref, f32[1,2048]{1,0:T(1,128)} %get-tuple-element.64.gain_ref), custom_call_target="tpu_custom_call" | custom-call | flops 1000 | bytes 1000 | tf_op jit(solution)/shard_map/branch_out/pallas_call | solution.py:761
  306.7 52.1 %feed_first.1 = (bf16[1536,1024]{1,0:T(8,128)(2,1)}, bf16[2,1536,1024]{2,1,0:T(8,128)(2,1)}, bf16[4,384,2048]{2,1,0:T(8,128)(2,1)}) custom-call(bf16[384,2048]{1,0:T(8,128)(2,1)} %get-tuple-element.65.x_ref, bf16[8,3,256,1024]{3,2,1,0:T(8,128)(2,1)} %bitcast.51, bf16[4,384,2048]{2,1,0:T(8,128)(2,1)} %get-tuple-element.66.cot_ref.y_ref), custom_call_target="tpu_custom_call" | custom-call | flops 1000 | bytes 1000 | tf_op jit(solution)/shard_map/feed_first/pallas_call | solution.py:880
  358.8 26.7 %weight_grads.2 = bf16[3,2048,1024]{2,1,0:T(8,128)(2,1)} custom-call(bf16[1536,2048]{1,0:T(8,128)(2,1)} %bitcast.58, bf16[1536,2048]{1,0:T(8,128)(2,1)} %bitcast.57, bf16[2,1536,1024]{2,1,0:T(8,128)(2,1)} %get-tuple-element.67.g_ref.first_ref, bf16[1536,1024]{1,0:T(8,128)(2,1)} %get-tuple-element.69.h_ref.hidden_a), custom_call_target="tpu_custom_call" | custom-call | flops 1000 | bytes 1000 | tf_op jit(solution)/shard_map/weight_grads/pallas_call | solution.py:910
  385.5 0.0 reduce-scatter.6.cloned.1.call-start
  385.6 3.6 all-gather.11.cloned.1.call-done
  389.2 34.7 %feed_second.1 = (bf16[1536,1024]{1,0:T(8,128)(2,1)}, bf16[2,1536,1024]{2,1,0:T(8,128)(2,1)}) custom-call(bf16[4,384,2048]{2,1,0:T(8,128)(2,1)} %get-tuple-element.70.x_ref, bf16[8,3,256,1024]{3,2,1,0:T(8,128)(2,1)} %bitcast.54, bf16[4,384,2048]{2,1,0:T(8,128)(2,1)} %get-tuple-element.66.cot_ref.y_ref), custom_call_target="tpu_custom_call" | custom-call | flops 1000 | bytes 1000 | tf_op jit(solution)/shard_map/feed_second/pallas_call | solution.py:880
  423.9 70.1 %middle_back.1 = (f32[384,2048]{1,0:T(8,128)}, bf16[384,2048]{1,0:T(8,128)(2,1)}, f32[1,2048]{1,0:T(1,128)}, bf16[3,2048,1024]{2,1,0:T(8,128)(2,1)}) custom-call(bf16[2,1536,1024]{2,1,0:T(8,128)(2,1)} %get-tuple-element.67.g_ref.first_ref, bf16[2,1536,1024]{2,1,0:T(8,128)(2,1)} %get-tuple-element.71.second_ref, bf16[8,3,256,1024]{3,2,1,0:T(8,128)(2,1)} %bitcast.52, ...), custom_call_target="tpu_custom_call" | custom-call | flops 1000 | bytes 1000 | tf_op jit(solution)/shard_map/middle_back/pallas_call | solution.py:1053
  494.2 48.1 %branch_back.1 = (bf16[4,1536,128]{2,1,0:T(8,128)(2,1)}, bf16[4,384,2048]{2,1,0:T(8,128)(2,1)}) custom-call(bf16[384,2048]{1,0:T(8,128)(2,1)} %get-tuple-element.75.x_ref, bf16[8,512,256]{2,1,0:T(8,128)(2,1)} %get-tuple-element.62.w_ref), custom_call_target="tpu_custom_call" | custom-call | flops 1000 | bytes 1000 | tf_op jit(solution)/shard_map/branch_back/pallas_call | solution.py:1106
  542.2 58.0 %attend_back.1 = (bf16[3,1536,512]{2,1,0:T(8,128)(2,1)}, f32[4,1,128]{2,1,0:T(1,128)}, bf16[8,384,256]{2,1,0:T(8,128)(2,1)}, f32[384,128]{1,0:T(8,128)}) custom-call(s32[4]{0:T(128)} %bitcast.76, s32[4]{0:T(128)} %bitcast.78, f32[4]{0:T(128)} %add_divide_fusion.gate_ref, bf16[3,4,1536,128]{3,2,1,0:T(8,128)(2,1)} %get-tuple-element.60.qkv_ref, ...), custom_call_target="tpu_custom_call" | custom-call | flops 1000 | bytes 1000 | tf_op jit(solution)/shard_map/attend_back/pallas_call | solution.py:292
  600.2 19.2 %weight_grads.3 = bf16[4,2048,512]{2,1,0:T(8,128)(2,1)} custom-call(bf16[1536,2048]{1,0:T(8,128)(2,1)} %bitcast.61, bf16[1536,2048]{1,0:T(8,128)(2,1)} %bitcast.62, bf16[3,1536,512]{2,1,0:T(8,128)(2,1)} %get-tuple-element.84.g_ref, bf16[1536,512]{1,0:T(8,128)(2,1)} %get-tuple-element.61.attn_ref.h_ref), custom_call_target="tpu_custom_call" | custom-call | flops 1000 | bytes 1000 | tf_op jit(solution)/shard_map/weight_grads/pallas_call | solution.py:910
  619.4 0.9 copy-done.6
  620.3 0.1 copy.33
  620.5 0.1 reduce_sum.9
  620.6 0.1 copy.34
  620.8 0.6 pad.13.stats_ref
  621.4 107.6 %stream_back.1 = (bf16[8,384,256]{2,1,0:T(8,128)(2,1)}, f32[1,2048]{1,0:T(1,128)}, bf16[2,4,384,256]{3,2,1,0:T(8,128)(2,1)}) custom-call(bf16[3,1536,512]{2,1,0:T(8,128)(2,1)} %get-tuple-element.84.g_ref, bf16[8,3,256,512]{3,2,1,0:T(8,128)(2,1)} %bitcast.60, bf16[384,2048]{1,0:T(8,128)(2,1)} %get-tuple-element.63.x_ref, ...), custom_call_target="tpu_custom_call" | custom-call | flops 1000 | bytes 1000 | tf_op jit(solution)/shard_map/stream_back/pallas_call | solution.py:1163
  729.1 1.4 copy-done
  730.5 0.4 copy-done.1
  731.0 0.2 convert_bitcast_fusion
  731.2 0.9 slice-done
  732.2 0.3 slice-done.1
  732.5 2.5 maximum_convert_fusion
  735.1 0.7 pad_maximum_fusion.2.sums_ref
  735.7 73.5 %leave.1 = (bf16[2,4,384,256]{3,2,1,0:T(8,128)(2,1)}, f32[2,4,8,384]{3,2,1,0:T(8,128)}, f32[8,256]{1,0:T(8,128)}) custom-call(bf16[8,384,256]{2,1,0:T(8,128)(2,1)} %get-tuple-element.92.grad_ref, f32[8,384]{1,0:T(8,128)} %pad.13.stats_ref, f32[8,8,256]{2,1,0:T(8,128)} %pad_maximum_fusion.2.sums_ref), custom_call_target="tpu_custom_call" | custom-call | flops 1000 | bytes 1000 | tf_op jit(solution)/shard_map/leave/pallas_call | solution.py:1470
  809.2 1.5 slice.63
  810.8 1.8 copy.36
  812.6 1.2 slice_bitcast_fusion.3
  813.8 1.3 fusion.4
  815.1 3.3 bitcast_convert_fusion
  818.4 1.1 convert_bitcast_fusion.1
  819.5 1.0 copy.35
  820.5 2.5 slice_convert_fusion
  823.0 1.1 copy.40
  (47 shorter events, 0.4 us)
Async XLA Ops:
  7.2 3.9 copy-start.2
  7.2 131.6 %all-gather.7.cloned.1.call-start = ((), (), s32[]{:S(2)}) async-start(), calls=%async_computation.6 | async-start | bytes 7077888 | tf_op jit(solution)/shard_map/all_gather | solution.py:1519
  7.9 298.7 %all-gather.9.cloned.1.call-start = ((), (), s32[]{:S(2)}) async-start(), calls=%async_computation.7 | async-start | bytes 14155776 | tf_op jit(solution)/shard_map/all_gather | solution.py:1525
  11.0 1.0 copy-start.4
  12.1 1.4 copy-start.3
  13.4 375.9 %all-gather.11.cloned.1.call-start = ((), (), s32[]{:S(2)}) async-start(), calls=%async_computation.8 | async-start | bytes 14155776 | tf_op jit(solution)/shard_map/all_gather | solution.py:1525
  13.7 1.4 copy-start.11
  13.7 1.4 copy-start.12
  15.0 123.3 %copy-start.13 = (f32[4]{0:T(128)S(1)}, f32[4]{0:T(128)}, u32[]{:S(2)}) copy-start(f32[4]{0:T(128)} %param.20) | copy-start | bytes 52
  15.0 604.4 %reduce-scatter.4.cloned.1.call-start = ((), (), s32[]{:S(2)}) async-start(), calls=%async_computation.3 | async-start | bytes 14155776 | tf_op jit(solution)/shard_map/reduce_scatter | solution.py:1494
  385.5 343.5 %reduce-scatter.6.cloned.1.call-start = ((), (), s32[]{:S(2)}) async-start(), calls=%async_computation.4 | async-start | bytes 14155776 | tf_op jit(solution)/shard_map/reduce_scatter | solution.py:1494
  494.1 324.3 %reduce-scatter.8.cloned.1.call-start = ((), (), s32[]{:S(2)}) async-start(), calls=%async_computation.5 | async-start | bytes 9437184 | tf_op jit(solution)/shard_map/reduce_scatter | solution.py:1494
  619.4 0.9 copy-start.6
  619.4 1.1 copy-start.10
  619.4 1.2 copy-start.7
  729.0 1.5 copy-start
  729.1 1.9 copy-start.1
  731.0 1.2 slice-start
  731.0 1.6 slice-start.1
  732.5 2.6 copy-start.8
  732.5 2.6 copy-start.9
  818.4 4.6 copy-start.5
Sparse Core Ops, SparseCore 0:
  9.7 115.5 all-gather.6
  127.5 144.5 all-gather.8
  274.3 114.8 all-gather.10
  391.4 134.3 reduce-scatter.3
  527.9 127.5 reduce-scatter.5
  657.7 121.9 reduce-scatter.7

commit v7 on v6

--- a/solution.py
+++ b/solution.py
@@ -65,13 +65,17 @@
 TILES = GLEN // QT
 
 
+def tile_rows(tile):
+    return pl.ds(pl.multiple_of(tile * QT, QT), QT) if not isinstance(tile, int) else slice(tile * QT, (tile + 1) * QT)
+
+
 def tile_scores(tile, q, k_ref, offsets_ref, lengths_ref):
     scale = HD ** (-0.5)
     row = lax.broadcasted_iota(jnp.int32, (QT, QT), 0)
     column = lax.broadcasted_iota(jnp.int32, (QT, QT), 1)
-    seen = min(tile * QT, PROMPT)
-    own = plain_dot(q, k_ref[tile * QT : (tile + 1) * QT], NT) * scale
-    if tile < PROMPT_TILES:
+    own = plain_dot(q, k_ref[tile_rows(tile)], NT) * scale
+    if isinstance(tile, int) and tile < PROMPT_TILES:
+        seen = tile * QT
         own = jnp.where(row >= column, own, MASKED_LOGIT)
         ahead = plain_dot(q, k_ref[:seen], NT) * scale if seen else None
         return ahead, own, seen
@@ -81,9 +85,15 @@
     live = jnp.where(upper, lengths_ref[first + 1] + CLEN, lengths_ref[first])
     same = (row >= CLEN) == (column >= CLEN)
     own = jnp.where((row >= column) & same & (column < live), own, MASKED_LOGIT)
-    ahead = plain_dot(q, k_ref[:seen], NT) * scale
+    ahead = plain_dot(q, k_ref[:PROMPT], NT) * scale
     position = lax.broadcasted_iota(jnp.int32, (QT, PROMPT), 1)
-    return jnp.where(position < limit, ahead, MASKED_LOGIT), own, seen
+    return jnp.where(position < limit, ahead, MASKED_LOGIT), own, PROMPT
+
+
+def each_tile(body):
+    for tile in range(PROMPT_TILES):
+        body(tile)
+    pl.loop(PROMPT_TILES, TILES)(body)
 
 
 def attend_kernel(
@@ -168,14 +178,14 @@
     offsets_ref, lengths_ref, gate_ref, qkv_ref, grad_ref, dot_ref, part_ref, logsum_ref,
     memory_ref, norm_ref, middle_ref, hidden_a, hidden_b, pack_a, pack_b,
     out_ref, gate_out_ref, blocks_ref, stat_ref,
-    key_sum, value_sum, stage, land, total, send, receive, h, w, h_sem, w_sem,
+    key_sum, value_sum, query_sum, stage, land, total, send, receive, h, w, h_sem, w_sem,
 ):
     head = pl.program_id(0)
     piece = GLEN // size
     scatter = Scatter(size, stage, land, total, send, receive)
 
     def h_load(i, step):
-        rows = pl.ds(pl.multiple_of(scatter.order[step] * piece, piece), piece)
+        rows = pl.ds(pl.multiple_of(scatter.row_at(step) * piece, piece), piece)
         return pltpu.make_async_copy((hidden_a, hidden_b)[i].at[rows], h.at[i, rows], h_sem.at[i, step])
 
     def w_load(i, c):
@@ -189,10 +199,12 @@
 
         @span_loop
         def _(t, half, columns, depth_rows):
-            if step == 0:
+            @pl.when(step == 0)
+            def _():
                 for k in range(SPAN // depth):
                     for i in range(2):
                         w_load(i, t * (SPAN // depth) + k).wait()
+
             rows = pl.ds(pl.multiple_of(at * piece, piece), piece)
             store(
                 half, columns,
@@ -221,18 +233,30 @@
     q_ref, k_ref, v_ref = qkv_ref.at[0, 0], qkv_ref.at[1, 0], qkv_ref.at[2, 0]
     memory_one = memory_ref[0]
     norm_one = norm_ref[0]
-    gate_row = jnp.zeros((1, HD), jnp.float32)
+    gate_out_ref[0] = jnp.zeros((1, HD), jnp.float32)
     key_sum[...] = jnp.zeros_like(key_sum)
     value_sum[...] = jnp.zeros_like(value_sum)
-    for tile in range(TILES):
-        rows = slice(tile * QT, (tile + 1) * QT)
+
+    @pl.loop(0, TILES)
+    def _(tile):
+        rows = tile_rows(tile)
+        grad = grad_ref[0, rows, :]
+        grad_float = grad.astype(jnp.float32)
+        memory_part = part_ref[0, rows, :]
+        gate_out_ref[0] += jnp.sum(grad_float * (memory_part - dot_ref[0, rows, :]), axis=0, keepdims=True)
+        q_float = q_ref[rows].astype(jnp.float32)
+        lifted = feature_map(q_float)
+        inverse = gate / jnp.sum(lifted * norm_one, axis=1, keepdims=True)
+        against_memory = jnp.sum(grad_float * memory_part, axis=1, keepdims=True)
+        grad_lifted = inverse * (narrow_dot(grad, memory_one, NT) - against_memory * norm_one)
+        query_sum[rows, :] = grad_lifted * feature_slope(q_float)
+
+    def one(tile):
+        rows = tile_rows(tile)
         q = q_ref[rows]
         grad = grad_ref[0, rows, :]
         grad_float = grad.astype(jnp.float32)
-        memory_part = part_ref[0, rows, :]
-        dot_part = dot_ref[0, rows, :]
-        against_dot = jnp.sum(grad_float * dot_part, axis=1, keepdims=True)
-        gate_row += jnp.sum(grad_float * (memory_part - dot_part), axis=0, keepdims=True)
+        against_dot = jnp.sum(grad_float * dot_ref[0, rows, :], axis=1, keepdims=True)
         logsum = logsum_ref[0, rows, :]
         ahead, own, seen = tile_scores(tile, q, k_ref, offsets_ref, lengths_ref)
         own = jnp.exp(own - logsum)
@@ -248,17 +272,11 @@
             )
             key_sum[:seen, :] += plain_dot(ahead, q, TN)
             grad_q += plain_dot(ahead, k_ref[:seen], NN)
-        q_float = q.astype(jnp.float32)
-        lifted = feature_map(q_float)
-        inverse = gate / jnp.sum(lifted * norm_one, axis=1, keepdims=True)
-        against_memory = jnp.sum(grad_float * memory_part, axis=1, keepdims=True)
-        grad_lifted = inverse * (narrow_dot(grad, memory_one, NT) - against_memory * norm_one)
-        out_ref[0, rows, :] = (grad_q * scale + grad_lifted * feature_slope(q_float)).astype(
-            jnp.bfloat16
-        )
+        out_ref[0, rows, :] = (grad_q * scale + query_sum[rows, :]).astype(jnp.bfloat16)
+
+    each_tile(one)
     out_ref[1, :, :] = (key_sum[...] * scale).astype(jnp.bfloat16)
     out_ref[2, :, :] = (value_sum[...] * keep).astype(jnp.bfloat16)
-    gate_out_ref[0] = gate_row
 
     def finish(rows):
         ffn = [total[half, rows, :] for half in range(2)]
@@ -304,7 +322,7 @@
             whole_block((cols, piece, depth)), whole_block((piece, HD)),
         ],
         out_shape=[bf(3, GLEN, heads * HD), fl(heads, 1, HD), bf(cols, piece, depth), fl(piece, HD)],
-        scratch_shapes=[pltpu.VMEM((GLEN, HD), jnp.float32), pltpu.VMEM((GLEN, HD), jnp.float32)]
+        scratch_shapes=[pltpu.VMEM((GLEN, HD), jnp.float32)] * 3
         + scatter_scratch(size, piece)
         + [
             pltpu.VMEM((2, GLEN, wide), jnp.bfloat16),
@@ -428,6 +446,25 @@
             copy.wait_recv()
         return self.order[step]
 
+    def row_at(self, step):
+        if self.size != 4:
+            return lax.rem(self.row + self.size - step, self.size)
+        along_x = lax.rem(lax.rem(self.row, 2) + lax.rem(step, 2), 2)
+        return 2 * lax.rem(self.row // 2 + step // 2, 2) + along_x
+
+    def each(self, body, between):
+        @pl.loop(0, self.size)
+        def _(step):
+            for k in range(1, self.size):
+
+                @pl.when(step == k)
+                def _():
+                    if k == 1:
+                        between()
+                    self.wait(k - 1)
+
+            body(step, self.row_at(step))
+
     def finish(self):
         for copy in self.copies if self.size != 4 else [*self.to_x, *self.to_y, *self.onward]:
             copy.wait_send()
@@ -515,14 +552,25 @@
     def begin(self, partial, greeted=False):
         if not greeted:
             greet(self.peers)
-        for step, row in enumerate(self.order[:-1]):
-
+
+        @pl.loop(0, self.size - 1)
+        def _(step):
             def store(half, columns, value):
                 self.stage[step, half, :, columns] = value.astype(jnp.bfloat16)
 
-            partial(step, row, store)
-            for index in self.after[step]:
-                self.copies[index].start()
+            partial(step, self.row_at(step), store)
+            for k, indices in enumerate(self.after):
+
+                @pl.when(step == k)
+                def _():
+                    for index in indices:
+                        self.copies[index].start()
+
+    def row_at(self, step):
+        if self.size != 4:
+            return lax.rem(self.row + 1 + step, self.size)
+        along_x = lax.rem(lax.rem(self.row, 2) + 3 - step // 2, 2)
+        return 2 * lax.rem(self.row // 2 + 3 - lax.rem(step, 2), 2) + along_x
 
     def middle(self):
         if self.size != 4:
@@ -561,6 +609,32 @@
             late()
         self.end()
 
+    def run_short(self, partial, late=None, greeted=False):
+        if not greeted:
+            greet(self.peers)
+
+        @pl.loop(0, self.size)
+        def _(step):
+            @pl.when(step == self.size - 1)
+            def _():
+                self.middle()
+
+            def store(half, columns, value):
+                self.total[half, :, columns] = value
+                self.stage[step, half, :, columns] = value.astype(jnp.bfloat16)
+
+            partial(step, self.row_at(step), store)
+            for k, indices in enumerate(self.after):
+
+                @pl.when(step == k)
+                def _():
+                    for index in indices:
+                        self.copies[index].start()
+
+        if late is not None:
+            late()
+        self.end()
+
     def add_stage(self, slot, half, landed):
         @pl.loop(0, landed.shape[0] // STRIP)
         def _(i):
@@ -578,10 +652,11 @@
 STRIP = 32
 
 
-def scatter_scratch(size, piece):
+def scatter_scratch(size, piece, spare=0):
     count = Scatter.semaphores(size)
+    slots, *shape = Scatter.stage_shape(size, piece)
     return [
-        pltpu.VMEM(Scatter.stage_shape(size, piece), jnp.bfloat16),
+        pltpu.VMEM((slots + spare, *shape), jnp.bfloat16),
         pltpu.VMEM(Scatter.land_shape(size, piece), jnp.bfloat16),
         pltpu.VMEM((2, piece, HALF), jnp.float32),
         pltpu.SemaphoreType.DMA((count,)),
@@ -665,9 +740,11 @@
         gather.start(greeted=True)
         beside.start()
 
-        def compute(row, slot):
-            store = pltpu.make_async_copy(land.at[row], all_ref.at[row], all_sem.at[slot])
-            store.start()
+        def keep(step, row):
+            return pltpu.make_async_copy(land.at[row], all_ref.at[row], all_sem.at[step])
+
+        def compute(step, row):
+            keep(step, row).start()
             rows = pl.ds(pl.multiple_of(row * piece, piece), piece)
 
             @pl.loop(0, 3)
@@ -676,16 +753,15 @@
                 for head in range(heads):
                     heads_ref[j, head, rows, :] = value[:, head * HD : (head + 1) * HD]
 
-            return store
+        def between():
+            gather.forward()
+            beside.forward()
 
         wait_all(loads)
-        stores = [compute(gather.row, 0)]
-        gather.forward()
-        beside.forward()
-        for step in range(size - 1):
-            stores.append(compute(gather.wait(step), step + 1))
+        gather.each(compute, between)
         beside.finish()
-        wait_all(stores)
+        for step in range(size):
+            keep(step, gather.row_at(step)).wait()
         gather.finish()
 
     return pl.pallas_call(
@@ -741,7 +817,7 @@
             def _(t, half, columns, depth_rows):
                 store(half, columns, plain_dot(left, w[:, depth_rows], NN))
 
-        scatter.run(partial)
+        scatter.run_short(partial)
 
         def finish(rows):
             branch = (total[0, rows, :], total[1, rows, :])
@@ -763,7 +839,7 @@
         out_shape=[fl(piece, D), bf(piece, D), fl(piece, HD)],
         in_specs=[VMEM, ANY, VMEM, VMEM],
         out_specs=[VMEM, VMEM, VMEM],
-        scratch_shapes=scatter_scratch(size, piece)
+        scratch_shapes=scatter_scratch(size, piece, 1)
         + [pltpu.VMEM((width, D), jnp.bfloat16), pltpu.SemaphoreType.DMA((cols,))],
         compiler_params=comm_params(2),
         cost_estimate=SHORT,
@@ -843,19 +919,18 @@
         wait_all(w_loads[:cols])
         if first:
             cot_loads[0].wait()
-            backward(order[0])
-            gather.forward()
-            wait_all(cot_loads[1:])
-
-            @pl.loop(1, size)
+
+            @pl.loop(0, size)
             def _(d):
+                @pl.when(d == 1)
+                def _():
+                    gather.forward()
+                    wait_all(cot_loads[1:])
+
                 backward(lax.rem(gather.row + d, size))
 
             wait_all(w_loads[cols:])
-            for step in range(size):
-                if step:
-                    gather.wait(step - 1)
-                compute(order[step])
+            gather.each(lambda step, row: compute(row), lambda: None)
             gather.finish()
             return
 
@@ -949,12 +1024,13 @@
             return pl.ds(pl.multiple_of(at * piece, piece), piece)
 
         def first_load(step):
+            slot = lax.rem(step, 2)
             return pltpu.make_async_copy(
-                first_ref.at[:, piece_rows(scatter.order[step])], g_first.at[step % 2], first_sem.at[step % 2]
+                first_ref.at[:, piece_rows(scatter.row_at(step))], g_first.at[slot], first_sem.at[slot]
             )
 
         def second_load(step):
-            rows = piece_rows(scatter.order[step])
+            rows = piece_rows(scatter.row_at(step))
             return pltpu.make_async_copy(second_ref.at[:, rows], g_second.at[:, rows], second_sem.at[step])
 
         def w_load(i, c):
@@ -980,18 +1056,21 @@
 
             @span_loop
             def _(t, half, columns, depth_rows):
-                if step == 0:
+                @pl.when(step == 0)
+                def _():
                     for k in range(SPAN // depth):
                         for i in range(2):
                             w_load(i, t * (SPAN // depth) + k).wait()
+
                 rows = piece_rows(at)
                 value = 0.0
                 for j in range(2):
-                    value += plain_dot(g_first[step % 2, j], w[0, j, depth_rows, :], NT)
+                    value += plain_dot(g_first[lax.rem(step, 2), j], w[0, j, depth_rows, :], NT)
                     value += plain_dot(g_second[j, rows, :], w[1, j, depth_rows, :], NT)
                 store(half, columns, value)
 
-            if step + 2 < size:
+            @pl.when(step + 2 < size)
+            def _():
                 first_load(step + 2).start()
 
         def x_loads(i, slot):
@@ -1026,16 +1105,18 @@
                 def _():
                     part_move(i, slot).wait()
 
-                left = x[slot, 0].reshape(GLEN, block)
-                for j in range(2):
-                    part[slot, j] = plain_dot(left, g_second[j], TN).astype(jnp.bfloat16)
+
+                @pl.loop(0, 2)
+                def _(j):
+                    part[slot, j] = plain_dot(x[slot, 0].reshape(GLEN, block), g_second[j], TN).astype(jnp.bfloat16)
+
                 part[slot, 2] = plain_dot(x[slot, 1].reshape(GLEN, block), h[...], TN).astype(jnp.bfloat16)
                 part_move(i, slot).start()
 
             for slot in range(2):
                 part_move(slot, slot).wait()
 
-        scatter.run(partial, weights)
+        scatter.run_short(partial, weights)
 
         def finish(rows):
             stream = [middle_ref[rows, columns] for columns in (LEFT, RIGHT)]
@@ -1055,7 +1136,7 @@
         out_shape=[fl(piece, D), bf(piece, D), fl(1, D), bf(3, D, wide)],
         in_specs=[ANY] * 4 + [VMEM] * 3 + [ANY] * 3,
         out_specs=[VMEM, VMEM, VMEM, ANY],
-        scratch_shapes=scatter_scratch(size, piece)
+        scratch_shapes=scatter_scratch(size, piece, 1)
         + [
             pltpu.VMEM((2, 2, D, wide), jnp.bfloat16),
             pltpu.VMEM((2, 2, piece, wide), jnp.bfloat16),
@@ -1086,21 +1167,20 @@
         gather = Gather(size, x_ref, land, send, receive, own)
         gather.start()
 
-        def compute(row, slot):
-            store = pltpu.make_async_copy(land.at[row], all_ref.at[row], all_sem.at[slot])
-            store.start()
+        def keep(step, row):
+            return pltpu.make_async_copy(land.at[row], all_ref.at[row], all_sem.at[step])
+
+        def compute(step, row):
+            keep(step, row).start()
             rows = pl.ds(pl.multiple_of(row * piece, piece), piece)
             value = plain_dot(land[row], w[...], NT).astype(jnp.bfloat16)
             for head in range(heads):
                 heads_ref[head, rows, :] = value[:, head * HD : (head + 1) * HD]
-            return store
 
         wait_all(loads)
-        stores = [compute(gather.row, 0)]
-        gather.forward()
-        for step in range(size - 1):
-            stores.append(compute(gather.wait(step), step + 1))
-        wait_all(stores)
+        gather.each(compute, gather.forward)
+        for step in range(size):
+            keep(step, gather.row_at(step)).wait()
         gather.finish()
 
     return pl.pallas_call(
@@ -1145,7 +1225,7 @@
                     value += plain_dot(g_ref[j, rows, :], w[j, depth_rows, :], NT)
                 store(half, columns, value)
 
-        scatter.run(partial, outward.forward, greeted=True)
+        scatter.run_short(partial, outward.forward, greeted=True)
 
         def finish(rows):
             stream = [x_ref[rows, columns].astype(jnp.float32) for columns in (LEFT, RIGHT)]
@@ -1165,7 +1245,7 @@
         out_shape=[bf(cols, piece, depth), fl(1, D), bf(cols // size, size, piece, depth)],
         in_specs=[VMEM, ANY, VMEM, VMEM, VMEM, VMEM],
         out_specs=[VMEM, VMEM, ANY],
-        scratch_shapes=scatter_scratch(size, piece)
+        scratch_shapes=scatter_scratch(size, piece, 1)
         + [pltpu.VMEM((3, D, width), jnp.bfloat16), pltpu.SemaphoreType.DMA((cols,))]
         + Outward.scratch(size, cols, piece, depth),
         compiler_params=comm_params(7),

time: 841 us -> 833 us (level); the launches traced: 831 us -> 832 us
  no operation moved by 1% of the time
where the time goes in v7:
time: 833 us; the launch traced here: 832 us
  Pallas kernels  781 us (94%)
  local copies, waits for them, and re-layouts  17.3 us (2%)
  between operations  14.4 us (2%)
  other arithmetic  14.2 us (2%)
    pallas_call x1, Pallas kernels, enter(): pl.pallas_call(kernel, out_shape=[bf(piece, D), bf(piece, D), fl(1, D), f...  123 us
    pallas_call x1, Pallas kernels, stream_back(): pl.pallas_call(kernel, out_shape=[bf(cols, piece, depth), fl(1, D), bf(co...  109 us
    pallas_call x1, Pallas kernels, project_heads(): pl.pallas_call(kernel, out_shape=[bf(3, heads, GLEN, HD), bf(size, piece,...  95.5 us
    pallas_call x2, Pallas kernels, feed_forward(): pl.pallas_call(kernel, out_shape=out_shape, in_specs=[ANY] * 3, out_specs...  86.8 us
    pallas_call x1, Pallas kernels, leave(): pl.pallas_call(kernel, out_shape=[bf(groups, size, piece, depth), fl(grou...  76.3 us
    pallas_call x1, Pallas kernels, middle_back(): pl.pallas_call(kernel, out_shape=[fl(piece, D), bf(piece, D), fl(1, D), b...  70.7 us
    pallas_call x1, Pallas kernels, attend_back(): pl.pallas_call(functools.partial(attend_back_kernel, size, cols, depth, w...  58.1 us
    pallas_call x1, Pallas kernels, branch_out(): pl.pallas_call(kernel, out_shape=[fl(piece, D), bf(piece, D), fl(piece, H...  55.8 us
  transfers between devices with their start and end apart: 6, of which 1 were waited for; matrix products, arithmetic and copies ran while one was open for 3% of the time, Pallas kernels for 94%

profile of v7, /device:TPU:27, one launch (start us, length us, event | category | flops | bytes accessed | tf_op | source)
XLA Modules:
  0.0 832.1 jit_solution(14242672915730234104)
XLA Ops:
  7.2 0.7 all-gather.7.cloned.1.call-update
  8.0 2.1 fusion.3
  10.0 1.0 copy.37
  11.0 0.2 fusion.2
  11.2 0.9 copy-done.4
  12.1 1.3 pad_maximum_fusion
  13.4 0.0 all-gather.11.cloned.1.call-start
  13.4 0.2 copy.38
  13.7 1.3 pad_maximum_fusion.1
  15.0 0.0 reduce-scatter.4.cloned.1.call-start
  15.1 0.6 select_maximum_fusion.gains_ref
  15.7 122.6 %enter.1 = (bf16[384,2048]{1,0:T(8,128)(2,1)}, bf16[384,2048]{1,0:T(8,128)(2,1)}, f32[1,2048]{1,0:T(1,128)}, f32[1,2048]{1,0:T(1,128)}, bf16[384,2048]{1,0:T(8,128)(2,1)}, /*index=5*/bf16[4,384,2048]{2,1,0:T(8,128)(2,1)}) custom-call(bf16[2,4,384,256]{3,2,1,0:T(8,128)(2,1)} %bitcast.65, bf16[2,4,384,256]{3,2,1,0:T(8,128)(2,1)} %bitcast.66, ...), custom_call_target="tpu_custom_call" | custom-call | flops 1000 | bytes 1000 | tf_op jit(solution)/shard_map/enter/pallas_call | solution.py:1458
  138.2 0.5 add_divide_fusion.gate_ref
  138.8 95.5 %project_heads.1 = (bf16[3,4,1536,128]{3,2,1,0:T(8,128)(2,1)}, bf16[4,384,2048]{2,1,0:T(8,128)(2,1)}, bf16[8,512,256]{2,1,0:T(8,128)(2,1)}) custom-call(bf16[384,2048]{1,0:T(8,128)(2,1)} %get-tuple-element.59.x_ref, bf16[8,3,256,512]{3,2,1,0:T(8,128)(2,1)} %bitcast.59, bf16[512,256]{1,0:T(8,128)(2,1)} %out_ref.1), custom_call_target="tpu_custom_call" | custom-call | flops 1000 | bytes 1000 | tf_op jit(solution)/shard_map/project_heads/pallas_call | solution.py:767
  234.3 16.6 %attend.1 = (bf16[1536,512]{1,0:T(8,128)(2,1)}, f32[4,1536,128]{2,1,0:T(8,128)}, f32[4,1536,128]{2,1,0:T(8,128)}, f32[4,1536,1]{2,1,0:T(8,128)}, f32[4,128,128]{2,1,0:T(8,128)}, /*index=5*/f32[4,1,128]{2,1,0:T(1,128)}) custom-call(s32[4]{0:T(128)} %bitcast.75, s32[4]{0:T(128)} %bitcast.77, f32[4]{0:T(128)} %add_divide_fusion.gate_ref, ...), custom_call_target="tpu_custom_call" | custom-call | flops 1000 | bytes 1000 | tf_op jit(solution)/shard_map/attend/pallas_call | solution.py:151
  250.9 55.8 %branch_out.1 = (f32[384,2048]{1,0:T(8,128)}, bf16[384,2048]{1,0:T(8,128)(2,1)}, f32[384,128]{1,0:T(8,128)}) custom-call(bf16[1536,512]{1,0:T(8,128)(2,1)} %get-tuple-element.61.attn_ref.h_ref, bf16[8,512,256]{2,1,0:T(8,128)(2,1)} %get-tuple-element.62.w_ref, bf16[384,2048]{1,0:T(8,128)(2,1)} %get-tuple-element.63.x_ref, f32[1,2048]{1,0:T(1,128)} %get-tuple-element.64.gain_ref), custom_call_target="tpu_custom_call" | custom-call | flops 1000 | bytes 1000 | tf_op jit(solution)/shard_map/branch_out/pallas_call | solution.py:837
  306.7 52.1 %feed_first.1 = (bf16[1536,1024]{1,0:T(8,128)(2,1)}, bf16[2,1536,1024]{2,1,0:T(8,128)(2,1)}, bf16[4,384,2048]{2,1,0:T(8,128)(2,1)}) custom-call(bf16[384,2048]{1,0:T(8,128)(2,1)} %get-tuple-element.65.x_ref, bf16[8,3,256,1024]{3,2,1,0:T(8,128)(2,1)} %bitcast.51, bf16[4,384,2048]{2,1,0:T(8,128)(2,1)} %get-tuple-element.66.cot_ref.y_ref), custom_call_target="tpu_custom_call" | custom-call | flops 1000 | bytes 1000 | tf_op jit(solution)/shard_map/feed_first/pallas_call | solution.py:955
  358.8 26.7 %weight_grads.2 = bf16[3,2048,1024]{2,1,0:T(8,128)(2,1)} custom-call(bf16[1536,2048]{1,0:T(8,128)(2,1)} %bitcast.58, bf16[1536,2048]{1,0:T(8,128)(2,1)} %bitcast.57, bf16[2,1536,1024]{2,1,0:T(8,128)(2,1)} %get-tuple-element.67.g_ref.first_ref, bf16[1536,1024]{1,0:T(8,128)(2,1)} %get-tuple-element.69.h_ref.hidden_a), custom_call_target="tpu_custom_call" | custom-call | flops 1000 | bytes 1000 | tf_op jit(solution)/shard_map/weight_grads/pallas_call | solution.py:985
  385.5 0.2 reduce-scatter.6.cloned.1.call-start
  385.8 3.5 all-gather.11.cloned.1.call-done
  389.2 34.7 %feed_second.1 = (bf16[1536,1024]{1,0:T(8,128)(2,1)}, bf16[2,1536,1024]{2,1,0:T(8,128)(2,1)}) custom-call(bf16[4,384,2048]{2,1,0:T(8,128)(2,1)} %get-tuple-element.70.x_ref, bf16[8,3,256,1024]{3,2,1,0:T(8,128)(2,1)} %bitcast.54, bf16[4,384,2048]{2,1,0:T(8,128)(2,1)} %get-tuple-element.66.cot_ref.y_ref), custom_call_target="tpu_custom_call" | custom-call | flops 1000 | bytes 1000 | tf_op jit(solution)/shard_map/feed_second/pallas_call | solution.py:955
  423.9 70.7 %middle_back.1 = (f32[384,2048]{1,0:T(8,128)}, bf16[384,2048]{1,0:T(8,128)(2,1)}, f32[1,2048]{1,0:T(1,128)}, bf16[3,2048,1024]{2,1,0:T(8,128)(2,1)}) custom-call(bf16[2,1536,1024]{2,1,0:T(8,128)(2,1)} %get-tuple-element.67.g_ref.first_ref, bf16[2,1536,1024]{2,1,0:T(8,128)(2,1)} %get-tuple-element.71.second_ref, bf16[8,3,256,1024]{3,2,1,0:T(8,128)(2,1)} %bitcast.52, ...), custom_call_target="tpu_custom_call" | custom-call | flops 1000 | bytes 1000 | tf_op jit(solution)/shard_map/middle_back/pallas_call | solution.py:1134
  494.7 44.1 %branch_back.1 = (bf16[4,1536,128]{2,1,0:T(8,128)(2,1)}, bf16[4,384,2048]{2,1,0:T(8,128)(2,1)}) custom-call(bf16[384,2048]{1,0:T(8,128)(2,1)} %get-tuple-element.75.x_ref, bf16[8,512,256]{2,1,0:T(8,128)(2,1)} %get-tuple-element.62.w_ref), custom_call_target="tpu_custom_call" | custom-call | flops 1000 | bytes 1000 | tf_op jit(solution)/shard_map/branch_back/pallas_call | solution.py:1186
  538.8 58.1 %attend_back.1 = (bf16[3,1536,512]{2,1,0:T(8,128)(2,1)}, f32[4,1,128]{2,1,0:T(1,128)}, bf16[8,384,256]{2,1,0:T(8,128)(2,1)}, f32[384,128]{1,0:T(8,128)}) custom-call(s32[4]{0:T(128)} %bitcast.76, s32[4]{0:T(128)} %bitcast.78, f32[4]{0:T(128)} %add_divide_fusion.gate_ref, bf16[3,4,1536,128]{3,2,1,0:T(8,128)(2,1)} %get-tuple-element.60.qkv_ref, ...), custom_call_target="tpu_custom_call" | custom-call | flops 1000 | bytes 1000 | tf_op jit(solution)/shard_map/attend_back/pallas_call | solution.py:310
  596.9 19.3 %weight_grads.3 = bf16[4,2048,512]{2,1,0:T(8,128)(2,1)} custom-call(bf16[1536,2048]{1,0:T(8,128)(2,1)} %bitcast.61, bf16[1536,2048]{1,0:T(8,128)(2,1)} %bitcast.62, bf16[3,1536,512]{2,1,0:T(8,128)(2,1)} %get-tuple-element.84.g_ref, bf16[1536,512]{1,0:T(8,128)(2,1)} %get-tuple-element.61.attn_ref.h_ref), custom_call_target="tpu_custom_call" | custom-call | flops 1000 | bytes 1000 | tf_op jit(solution)/shard_map/weight_grads/pallas_call | solution.py:985
  616.2 0.9 copy-done.6
  617.1 0.1 copy.33
  617.2 0.1 reduce_sum.9
  617.4 0.1 copy.34
  617.5 0.6 pad.13.stats_ref
  618.1 109.1 %stream_back.1 = (bf16[8,384,256]{2,1,0:T(8,128)(2,1)}, f32[1,2048]{1,0:T(1,128)}, bf16[2,4,384,256]{3,2,1,0:T(8,128)(2,1)}) custom-call(bf16[3,1536,512]{2,1,0:T(8,128)(2,1)} %get-tuple-element.84.g_ref, bf16[8,3,256,512]{3,2,1,0:T(8,128)(2,1)} %bitcast.60, bf16[384,2048]{1,0:T(8,128)(2,1)} %get-tuple-element.63.x_ref, ...), custom_call_target="tpu_custom_call" | custom-call | flops 1000 | bytes 1000 | tf_op jit(solution)/shard_map/stream_back/pallas_call | solution.py:1243
  727.3 1.4 copy-done
  728.8 0.4 copy-done.1
  729.2 0.2 convert_bitcast_fusion
  729.5 1.0 slice-done
  730.4 0.3 slice-done.1
  730.8 2.5 maximum_convert_fusion
  733.4 0.7 pad_maximum_fusion.2.sums_ref
  734.0 76.3 %leave.1 = (bf16[2,4,384,256]{3,2,1,0:T(8,128)(2,1)}, f32[2,4,8,384]{3,2,1,0:T(8,128)}, f32[8,256]{1,0:T(8,128)}) custom-call(bf16[8,384,256]{2,1,0:T(8,128)(2,1)} %get-tuple-element.92.grad_ref, f32[8,384]{1,0:T(8,128)} %pad.13.stats_ref, f32[8,8,256]{2,1,0:T(8,128)} %pad_maximum_fusion.2.sums_ref), custom_call_target="tpu_custom_call" | custom-call | flops 1000 | bytes 1000 | tf_op jit(solution)/shard_map/leave/pallas_call | solution.py:1550
  810.3 1.5 slice.63
  811.9 1.8 copy.36
  813.7 1.2 slice_bitcast_fusion.3
  814.9 1.3 fusion.4
  816.2 3.3 bitcast_convert_fusion
  819.5 1.1 convert_bitcast_fusion.1
  820.6 1.0 copy.35
  821.6 2.5 slice_convert_fusion
  824.1 1.1 copy.40
  (47 shorter events, 0.4 us)
Async XLA Ops:
  7.2 3.9 copy-start.2
  7.2 131.6 %all-gather.7.cloned.1.call-start = ((), (), s32[]{:S(2)}) async-start(), calls=%async_computation.6 | async-start | bytes 7077888 | tf_op jit(solution)/shard_map/all_gather | solution.py:1599
  7.9 298.8 %all-gather.9.cloned.1.call-start = ((), (), s32[]{:S(2)}) async-start(), calls=%async_computation.7 | async-start | bytes 14155776 | tf_op jit(solution)/shard_map/all_gather | solution.py:1605
  11.0 1.0 copy-start.4
  12.1 1.4 copy-start.3
  13.4 375.9 %all-gather.11.cloned.1.call-start = ((), (), s32[]{:S(2)}) async-start(), calls=%async_computation.8 | async-start | bytes 14155776 | tf_op jit(solution)/shard_map/all_gather | solution.py:1605
  13.7 1.4 copy-start.11
  13.7 1.4 copy-start.12
  15.0 123.3 %copy-start.13 = (f32[4]{0:T(128)S(1)}, f32[4]{0:T(128)}, u32[]{:S(2)}) copy-start(f32[4]{0:T(128)} %param.20) | copy-start | bytes 52
  15.0 601.2 %reduce-scatter.4.cloned.1.call-start = ((), (), s32[]{:S(2)}) async-start(), calls=%async_computation.3 | async-start | bytes 14155776 | tf_op jit(solution)/shard_map/reduce_scatter | solution.py:1574
  385.5 341.8 %reduce-scatter.6.cloned.1.call-start = ((), (), s32[]{:S(2)}) async-start(), calls=%async_computation.4 | async-start | bytes 14155776 | tf_op jit(solution)/shard_map/reduce_scatter | solution.py:1574
  494.7 324.9 %reduce-scatter.8.cloned.1.call-start = ((), (), s32[]{:S(2)}) async-start(), calls=%async_computation.5 | async-start | bytes 9437184 | tf_op jit(solution)/shard_map/reduce_scatter | solution.py:1574
  616.1 0.9 copy-start.6
  616.1 1.1 copy-start.10
  616.1 1.2 copy-start.7
  727.3 1.4 copy-start
  727.3 1.9 copy-start.1
  729.2 1.2 slice-start
  729.2 1.6 slice-start.1
  730.8 2.6 copy-start.8
  730.8 2.6 copy-start.9
  819.5 4.6 copy-start.5
Sparse Core Ops, SparseCore 0:
  9.7 115.5 all-gather.6
  127.5 144.5 all-gather.8
  274.3 114.8 all-gather.10
  391.4 134.3 reduce-scatter.3
  528.0 128.9 reduce-scatter.5
  659.1 129.9 reduce-scatter.7

commit v8 on v7

--- a/solution.py
+++ b/solution.py
@@ -176,9 +176,9 @@
 def attend_back_kernel(
     size, cols, depth, wide,
     offsets_ref, lengths_ref, gate_ref, qkv_ref, grad_ref, dot_ref, part_ref, logsum_ref,
-    memory_ref, norm_ref, middle_ref, hidden_a, hidden_b, pack_a, pack_b,
+    memory_ref, norm_ref, middle_hbm, hidden_a, hidden_b, pack_a, pack_b,
     out_ref, gate_out_ref, blocks_ref, stat_ref,
-    key_sum, value_sum, query_sum, stage, land, total, send, receive, h, w, h_sem, w_sem,
+    key_sum, value_sum, query_sum, stage, land, total, send, receive, h, w, h_sem, w_sem, middle_ref, middle_sem,
 ):
     head = pl.program_id(0)
     piece = GLEN // size
@@ -210,6 +210,8 @@
                 half, columns,
                 plain_dot(h[0, rows, :], w[0, depth_rows, :], NT) + plain_dot(h[1, rows, :], w[1, depth_rows, :], NT),
             )
+
+    middle_load = pltpu.make_async_copy(middle_hbm, middle_ref, middle_sem)
 
     @pl.when(head == 0)
     def _():
@@ -221,6 +223,7 @@
         for step in range(1, size):
             for i in range(2):
                 h_load(i, step).start()
+        middle_load.start()
         scatter.begin(partial)
 
     @pl.when(head == pl.num_programs(0) // 2)
@@ -292,6 +295,7 @@
     def _():
         scatter.own(partial)
         scatter.end()
+        middle_load.wait()
         strip_loop(piece, finish)
 
 
@@ -314,7 +318,7 @@
             SMEM_SPEC, SMEM_SPEC, SMEM_SPEC,
             head_block((3, 1, GLEN, HD), 1), row_block, row_block, row_block,
             head_block((1, GLEN, 1)), head_block((1, HD, HD)), head_block((1, 1, HD)),
-            whole_block((piece, D)), ANY, ANY, ANY, ANY,
+            ANY, ANY, ANY, ANY, ANY,
         ],
         out_specs=[
             pl.BlockSpec((3, GLEN, HD), lambda h: (0, 0, h)),
@@ -327,7 +331,7 @@
         + [
             pltpu.VMEM((2, GLEN, wide), jnp.bfloat16),
             pltpu.VMEM((2, D, wide), jnp.bfloat16),
-            dma(2, size), dma(2, cols),
+            dma(2, size), dma(2, cols), pltpu.VMEM((piece, D), jnp.float32), pltpu.SemaphoreType.DMA,
         ],
         compiler_params=comm_params(5),
         cost_estimate=SHORT,
@@ -753,12 +757,9 @@
                 for head in range(heads):
                     heads_ref[j, head, rows, :] = value[:, head * HD : (head + 1) * HD]
 
-        def between():
-            gather.forward()
-            beside.forward()
-
         wait_all(loads)
-        gather.each(compute, between)
+        gather.each(compute, gather.forward)
+        beside.forward()
         beside.finish()
         for step in range(size):
             keep(step, gather.row_at(step)).wait()
@@ -804,8 +805,12 @@
     piece = GLEN // size
     cols, width, depth = w_all.shape
 
-    def kernel(attn_ref, w_ref, x_ref, gain_ref, middle_ref, normed_ref, stat_ref, stage, land, total, send, receive, w, w_sem):
+    def kernel(
+        attn_ref, w_ref, x_hbm, gain_ref, middle_ref, normed_ref, stat_ref,
+        stage, land, total, send, receive, w, w_sem, x_ref, x_sem,
+    ):
         loads = fetches([(w_ref.at[c], w.at[:, pl.ds(c * depth, depth)]) for c in range(cols)], w_sem)
+        x_load = fetches([(x_hbm, x_ref)], x_sem)
         scatter = Scatter(size, stage, land, total, send, receive)
         wait_all(loads)
 
@@ -832,15 +837,16 @@
                 normed_ref[rows, columns] = (part * inverse * gain_ref[:, columns]).astype(jnp.bfloat16)
             stat_ref[rows, :] = lanes(row_mean(branch[0] * branch[0], branch[1] * branch[1]), mean)
 
+        wait_all(x_load)
         strip_loop(piece, finish)
 
     return pl.pallas_call(
         kernel,
         out_shape=[fl(piece, D), bf(piece, D), fl(piece, HD)],
-        in_specs=[VMEM, ANY, VMEM, VMEM],
+        in_specs=[VMEM, ANY, ANY, VMEM],
         out_specs=[VMEM, VMEM, VMEM],
         scratch_shapes=scatter_scratch(size, piece, 1)
-        + [pltpu.VMEM((width, D), jnp.bfloat16), pltpu.SemaphoreType.DMA((cols,))],
+        + [pltpu.VMEM((width, D), jnp.bfloat16), dma(cols), pltpu.VMEM((piece, D), jnp.bfloat16), dma(1)],
         compiler_params=comm_params(2),
         cost_estimate=SHORT,
         name="branch_out",
@@ -1012,10 +1018,10 @@
     block = 256
 
     def kernel(
-        first_ref, second_ref, pack_a, pack_b, middle_ref, cot_ref, gain_ref, x_ref, y_ref, hidden_ref,
+        first_ref, second_ref, pack_a, pack_b, middle_hbm, cot_hbm, gain_ref, x_ref, y_ref, hidden_ref,
         grad_ref, low_ref, gain_sum, part_ref,
         stage, land, total, send, receive, w, g_first, g_second, h, x, part,
-        w_sem, first_sem, second_sem, h_sem, x_sem, part_sem,
+        w_sem, first_sem, second_sem, h_sem, x_sem, part_sem, middle_ref, cot_ref, late_sem,
     ):
         pack_refs = (pack_a, pack_b)
         scatter = Scatter(size, stage, land, total, send, receive)
@@ -1048,6 +1054,7 @@
             second_load(step).start()
         h_load = pltpu.make_async_copy(hidden_ref, h, h_sem)
         h_load.start()
+        late = fetches([(middle_hbm, middle_ref), (cot_hbm, cot_ref)], late_sem)
         gain_sum[...] = jnp.zeros_like(gain_sum)
 
         def partial(step, at, store):
@@ -1129,12 +1136,13 @@
 
             norm_back(rows, total, stream, inverse, gain_ref, base, store, gain_sum)
 
+        wait_all(late)
         strip_loop(piece, finish)
 
     return pl.pallas_call(
         kernel,
         out_shape=[fl(piece, D), bf(piece, D), fl(1, D), bf(3, D, wide)],
-        in_specs=[ANY] * 4 + [VMEM] * 3 + [ANY] * 3,
+        in_specs=[ANY] * 6 + [VMEM] + [ANY] * 3,
         out_specs=[VMEM, VMEM, VMEM, ANY],
         scratch_shapes=scatter_scratch(size, piece, 1)
         + [
@@ -1145,6 +1153,7 @@
             pltpu.VMEM((2, 2, size, piece, block), jnp.bfloat16),
             pltpu.VMEM((2, 3, block, wide), jnp.bfloat16),
             dma(2, cols), dma(2), dma(size), pltpu.SemaphoreType.DMA, dma(2, 2), dma(2),
+            pltpu.VMEM((piece, D), jnp.float32), pltpu.VMEM((piece, D), jnp.bfloat16), dma(2),
         ],
         compiler_params=comm_params(4),
         cost_estimate=SHORT,
@@ -1205,18 +1214,28 @@
     cols, _, depth, width = w_all.shape
 
     def kernel(
-        g_ref, w_ref, x_ref, middle_ref, gain_ref, blocks_ref, out_ref, gain_sum, target_ref,
-        stage, land, total, send, receive, w, w_sem, *rest,
+        g_hbm, w_ref, x_hbm, middle_hbm, gain_ref, blocks_ref, out_ref, gain_sum, target_ref,
+        stage, land, total, send, receive, w, w_sem, g_ref, x_ref, middle_ref, g_sem, late_sem, *rest,
     ):
+        loads = fetches([(w_ref.at[c], w.at[:, pl.ds(c * depth, depth), :]) for c in range(cols)], w_sem)
         greet(row_and_col_peers(size, cols))
         outward = Outward(size, cols, blocks_ref, rest[0], target_ref, *rest[1:])
         outward.start()
-        loads = fetches([(w_ref.at[c], w.at[:, pl.ds(c * depth, depth), :]) for c in range(cols)], w_sem)
         scatter = Scatter(size, stage, land, total, send, receive)
+
+        def g_load(step):
+            rows = pl.ds(pl.multiple_of(scatter.row_at(step) * piece, piece), piece)
+            return pltpu.make_async_copy(g_hbm.at[:, rows], g_ref.at[:, rows], g_sem.at[step])
+
+        for step in range(size):
+            g_load(step).start()
+        late = fetches([(x_hbm, x_ref), (middle_hbm, middle_ref)], late_sem)
         wait_all(loads)
         gain_sum[...] = jnp.zeros_like(gain_sum)
 
         def partial(step, row, store):
+            g_load(step).wait()
+
             @span_loop
             def _(t, half, columns, depth_rows):
                 rows = pl.ds(pl.multiple_of(row * piece, piece), piece)
@@ -1237,16 +1256,21 @@
 
             norm_back(rows, total, stream, inverse, gain_ref, base, store, gain_sum)
 
+        wait_all(late)
         strip_loop(piece, finish)
         outward.finish()
 
     return pl.pallas_call(
         kernel,
         out_shape=[bf(cols, piece, depth), fl(1, D), bf(cols // size, size, piece, depth)],
-        in_specs=[VMEM, ANY, VMEM, VMEM, VMEM, VMEM],
+        in_specs=[ANY, ANY, ANY, ANY, VMEM, ANY],
         out_specs=[VMEM, VMEM, ANY],
         scratch_shapes=scatter_scratch(size, piece, 1)
-        + [pltpu.VMEM((3, D, width), jnp.bfloat16), pltpu.SemaphoreType.DMA((cols,))]
+        + [pltpu.VMEM((3, D, width), jnp.bfloat16), dma(cols)]
+        + [
+            pltpu.VMEM((3, GLEN, width), jnp.bfloat16), pltpu.VMEM((piece, D), jnp.bfloat16),
+            pltpu.VMEM((piece, D), jnp.float32), dma(size), dma(2),
+        ]
         + Outward.scratch(size, cols, piece, depth),
         compiler_params=comm_params(7),
         cost_estimate=SHORT,

time: 833 us -> 830 us (level)
    pallas_call x1, Pallas kernels: 109 us -> 83.4 us  [stream_back(): pl.pallas_call(kernel, out_shape=[bf(cols, piece, depth), fl(1, D), bf(co...]
  transfers between devices with their start and end apart: 6 -> 6, of which waited for: 1 -> 0; matrix products, arithmetic and copies ran while one was open for 3% -> 3% of each run, Pallas kernels for 94% -> 94%
where the time goes in v8:
time: 830 us; the launch traced here: 828 us
  Pallas kernels  780 us (94%)
  local copies, waits for them, and re-layouts  17.3 us (2%)
  between operations  14.4 us (2%)
  other arithmetic  14.2 us (2%)
    pallas_call x1, Pallas kernels, enter(): pl.pallas_call(kernel, out_shape=[bf(piece, D), bf(piece, D), fl(1, D), f...  123 us
    pallas_call x1, Pallas kernels, project_heads(): pl.pallas_call(kernel, out_shape=[bf(3, heads, GLEN, HD), bf(size, piece,...  94.8 us
    pallas_call x2, Pallas kernels, feed_forward(): pl.pallas_call(kernel, out_shape=out_shape, in_specs=[ANY] * 3, out_specs...  93 us
    pallas_call x1, Pallas kernels, stream_back(): pl.pallas_call(kernel, out_shape=[bf(cols, piece, depth), fl(1, D), bf(co...  83.4 us
    pallas_call x1, Pallas kernels, leave(): pl.pallas_call(kernel, out_shape=[bf(groups, size, piece, depth), fl(grou...  78.3 us
    pallas_call x1, Pallas kernels, middle_back(): pl.pallas_call(kernel, out_shape=[fl(piece, D), bf(piece, D), fl(1, D), b...  71.2 us
    pallas_call x1, Pallas kernels, branch_out(): pl.pallas_call(kernel, out_shape=[fl(piece, D), bf(piece, D), fl(piece, H...  61.7 us
    pallas_call x1, Pallas kernels, attend_back(): pl.pallas_call(functools.partial(attend_back_kernel, size, cols, depth, w...  61.1 us
  transfers between devices with their start and end apart: 6, of which 0 were waited for; matrix products, arithmetic and copies ran while one was open for 3% of the time, Pallas kernels for 94%

profile of v8, /device:TPU:27, one launch (start us, length us, event | category | flops | bytes accessed | tf_op | source)
XLA Modules:
  0.0 827.6 jit_solution(18324025887110700318)
XLA Ops:
  7.2 0.7 all-gather.7.cloned.1.call-update
  8.0 2.1 fusion.3
  10.0 1.0 copy.37
  11.0 0.2 fusion.2
  11.2 0.9 copy-done.4
  12.1 1.3 pad_maximum_fusion
  13.4 0.0 all-gather.11.cloned.1.call-start
  13.4 0.2 copy.38
  13.7 1.3 pad_maximum_fusion.1
  15.0 0.0 reduce-scatter.4.cloned.1.call-start
  15.1 0.6 select_maximum_fusion.gains_ref
  15.7 122.6 %enter.1 = (bf16[384,2048]{1,0:T(8,128)(2,1)}, bf16[384,2048]{1,0:T(8,128)(2,1)}, f32[1,2048]{1,0:T(1,128)}, f32[1,2048]{1,0:T(1,128)}, bf16[384,2048]{1,0:T(8,128)(2,1)}, /*index=5*/bf16[4,384,2048]{2,1,0:T(8,128)(2,1)}) custom-call(bf16[2,4,384,256]{3,2,1,0:T(8,128)(2,1)} %bitcast.65, bf16[2,4,384,256]{3,2,1,0:T(8,128)(2,1)} %bitcast.66, ...), custom_call_target="tpu_custom_call" | custom-call | flops 1000 | bytes 1000 | tf_op jit(solution)/shard_map/enter/pallas_call | solution.py:1482
  138.2 0.5 add_divide_fusion.gate_ref
  138.8 94.8 %project_heads.1 = (bf16[3,4,1536,128]{3,2,1,0:T(8,128)(2,1)}, bf16[4,384,2048]{2,1,0:T(8,128)(2,1)}, bf16[8,512,256]{2,1,0:T(8,128)(2,1)}) custom-call(bf16[384,2048]{1,0:T(8,128)(2,1)} %get-tuple-element.59.x_ref, bf16[8,3,256,512]{3,2,1,0:T(8,128)(2,1)} %bitcast.59, bf16[512,256]{1,0:T(8,128)(2,1)} %out_ref.1), custom_call_target="tpu_custom_call" | custom-call | flops 1000 | bytes 1000 | tf_op jit(solution)/shard_map/project_heads/pallas_call | solution.py:768
  233.6 16.6 %attend.1 = (bf16[1536,512]{1,0:T(8,128)(2,1)}, f32[4,1536,128]{2,1,0:T(8,128)}, f32[4,1536,128]{2,1,0:T(8,128)}, f32[4,1536,1]{2,1,0:T(8,128)}, f32[4,128,128]{2,1,0:T(8,128)}, /*index=5*/f32[4,1,128]{2,1,0:T(1,128)}) custom-call(s32[4]{0:T(128)} %bitcast.75, s32[4]{0:T(128)} %bitcast.77, f32[4]{0:T(128)} %add_divide_fusion.gate_ref, ...), custom_call_target="tpu_custom_call" | custom-call | flops 1000 | bytes 1000 | tf_op jit(solution)/shard_map/attend/pallas_call | solution.py:151
  250.2 61.7 %branch_out.1 = (f32[384,2048]{1,0:T(8,128)}, bf16[384,2048]{1,0:T(8,128)(2,1)}, f32[384,128]{1,0:T(8,128)}) custom-call(bf16[1536,512]{1,0:T(8,128)(2,1)} %get-tuple-element.61.attn_ref.h_ref, bf16[8,512,256]{2,1,0:T(8,128)(2,1)} %get-tuple-element.62.w_ref, bf16[384,2048]{1,0:T(8,128)(2,1)} %get-tuple-element.63.x_hbm, f32[1,2048]{1,0:T(1,128)} %get-tuple-element.64.gain_ref), custom_call_target="tpu_custom_call" | custom-call | flops 1000 | bytes 1000 | tf_op jit(solution)/shard_map/branch_out/pallas_call | solution.py:843
  312.0 58.3 %feed_first.1 = (bf16[1536,1024]{1,0:T(8,128)(2,1)}, bf16[2,1536,1024]{2,1,0:T(8,128)(2,1)}, bf16[4,384,2048]{2,1,0:T(8,128)(2,1)}) custom-call(bf16[384,2048]{1,0:T(8,128)(2,1)} %get-tuple-element.65.x_ref, bf16[8,3,256,1024]{3,2,1,0:T(8,128)(2,1)} %bitcast.51, bf16[4,384,2048]{2,1,0:T(8,128)(2,1)} %get-tuple-element.66.cot_ref.y_ref), custom_call_target="tpu_custom_call" | custom-call | flops 1000 | bytes 1000 | tf_op jit(solution)/shard_map/feed_first/pallas_call | solution.py:961
  370.3 26.8 %weight_grads.2 = bf16[3,2048,1024]{2,1,0:T(8,128)(2,1)} custom-call(bf16[1536,2048]{1,0:T(8,128)(2,1)} %bitcast.58, bf16[1536,2048]{1,0:T(8,128)(2,1)} %bitcast.57, bf16[2,1536,1024]{2,1,0:T(8,128)(2,1)} %get-tuple-element.67.g_ref.first_ref, bf16[1536,1024]{1,0:T(8,128)(2,1)} %get-tuple-element.69.h_ref.hidden_a), custom_call_target="tpu_custom_call" | custom-call | flops 1000 | bytes 1000 | tf_op jit(solution)/shard_map/weight_grads/pallas_call | solution.py:991
  397.1 0.2 reduce-scatter.6.cloned.1.call-start
  397.4 34.7 %feed_second.1 = (bf16[1536,1024]{1,0:T(8,128)(2,1)}, bf16[2,1536,1024]{2,1,0:T(8,128)(2,1)}) custom-call(bf16[4,384,2048]{2,1,0:T(8,128)(2,1)} %get-tuple-element.70.x_ref, bf16[8,3,256,1024]{3,2,1,0:T(8,128)(2,1)} %bitcast.54, bf16[4,384,2048]{2,1,0:T(8,128)(2,1)} %get-tuple-element.66.cot_ref.y_ref), custom_call_target="tpu_custom_call" | custom-call | flops 1000 | bytes 1000 | tf_op jit(solution)/shard_map/feed_second/pallas_call | solution.py:961
  432.1 71.2 %middle_back.1 = (f32[384,2048]{1,0:T(8,128)}, bf16[384,2048]{1,0:T(8,128)(2,1)}, f32[1,2048]{1,0:T(1,128)}, bf16[3,2048,1024]{2,1,0:T(8,128)(2,1)}) custom-call(bf16[2,1536,1024]{2,1,0:T(8,128)(2,1)} %get-tuple-element.67.g_ref.first_ref, bf16[2,1536,1024]{2,1,0:T(8,128)(2,1)} %get-tuple-element.71.second_ref, bf16[8,3,256,1024]{3,2,1,0:T(8,128)(2,1)} %bitcast.52, ...), custom_call_target="tpu_custom_call" | custom-call | flops 1000 | bytes 1000 | tf_op jit(solution)/shard_map/middle_back/pallas_call | solution.py:1142
  503.3 0.0 reduce-scatter.8.cloned.1.call-start
  503.3 51.9 %branch_back.1 = (bf16[4,1536,128]{2,1,0:T(8,128)(2,1)}, bf16[4,384,2048]{2,1,0:T(8,128)(2,1)}) custom-call(bf16[384,2048]{1,0:T(8,128)(2,1)} %get-tuple-element.75.x_ref, bf16[8,512,256]{2,1,0:T(8,128)(2,1)} %get-tuple-element.62.w_ref), custom_call_target="tpu_custom_call" | custom-call | flops 1000 | bytes 1000 | tf_op jit(solution)/shard_map/branch_back/pallas_call | solution.py:1195
  555.2 61.1 %attend_back.1 = (bf16[3,1536,512]{2,1,0:T(8,128)(2,1)}, f32[4,1,128]{2,1,0:T(1,128)}, bf16[8,384,256]{2,1,0:T(8,128)(2,1)}, f32[384,128]{1,0:T(8,128)}) custom-call(s32[4]{0:T(128)} %bitcast.76, s32[4]{0:T(128)} %bitcast.78, f32[4]{0:T(128)} %add_divide_fusion.gate_ref, bf16[3,4,1536,128]{3,2,1,0:T(8,128)(2,1)} %get-tuple-element.60.qkv_ref, ...), custom_call_target="tpu_custom_call" | custom-call | flops 1000 | bytes 1000 | tf_op jit(solution)/shard_map/attend_back/pallas_call | solution.py:314
  616.3 19.1 %weight_grads.3 = bf16[4,2048,512]{2,1,0:T(8,128)(2,1)} custom-call(bf16[1536,2048]{1,0:T(8,128)(2,1)} %bitcast.61, bf16[1536,2048]{1,0:T(8,128)(2,1)} %bitcast.62, bf16[3,1536,512]{2,1,0:T(8,128)(2,1)} %get-tuple-element.84.g_ref.g_hbm, bf16[1536,512]{1,0:T(8,128)(2,1)} %get-tuple-element.61.attn_ref.h_ref), custom_call_target="tpu_custom_call" | custom-call | flops 1000 | bytes 1000 | tf_op jit(solution)/shard_map/weight_grads/pallas_call | solution.py:991
  635.5 0.9 copy-done.6
  636.4 0.1 copy.33
  636.5 0.1 reduce_sum.9
  636.7 0.1 copy.34
  636.9 0.6 pad.13.stats_ref
  637.5 83.4 %stream_back.1 = (bf16[8,384,256]{2,1,0:T(8,128)(2,1)}, f32[1,2048]{1,0:T(1,128)}, bf16[2,4,384,256]{3,2,1,0:T(8,128)(2,1)}) custom-call(bf16[3,1536,512]{2,1,0:T(8,128)(2,1)} %get-tuple-element.84.g_ref.g_hbm, bf16[8,3,256,512]{3,2,1,0:T(8,128)(2,1)} %bitcast.60, bf16[384,2048]{1,0:T(8,128)(2,1)} %get-tuple-element.63.x_hbm, ...), custom_call_target="tpu_custom_call" | custom-call | flops 1000 | bytes 1000 | tf_op jit(solution)/shard_map/stream_back/pallas_call | solution.py:1263
  720.9 1.4 copy-done
  722.3 0.5 copy-done.1
  722.8 0.2 convert_bitcast_fusion
  723.1 0.9 slice-done
  724.0 0.3 slice-done.1
  724.3 2.5 maximum_convert_fusion
  726.9 0.7 pad_maximum_fusion.2.sums_ref
  727.6 78.3 %leave.1 = (bf16[2,4,384,256]{3,2,1,0:T(8,128)(2,1)}, f32[2,4,8,384]{3,2,1,0:T(8,128)}, f32[8,256]{1,0:T(8,128)}) custom-call(bf16[8,384,256]{2,1,0:T(8,128)(2,1)} %get-tuple-element.92.grad_ref, f32[8,384]{1,0:T(8,128)} %pad.13.stats_ref, f32[8,8,256]{2,1,0:T(8,128)} %pad_maximum_fusion.2.sums_ref), custom_call_target="tpu_custom_call" | custom-call | flops 1000 | bytes 1000 | tf_op jit(solution)/shard_map/leave/pallas_call | solution.py:1574
  805.8 1.5 slice.63
  807.4 1.8 copy.36
  809.2 1.2 slice_bitcast_fusion.3
  810.4 1.3 fusion.4
  811.7 3.3 bitcast_convert_fusion
  815.0 1.1 convert_bitcast_fusion.1
  816.1 1.0 copy.35
  817.1 2.5 slice_convert_fusion
  819.6 1.1 copy.40
  (47 shorter events, 0.4 us)
Async XLA Ops:
  7.2 3.9 copy-start.2
  7.2 131.6 %all-gather.7.cloned.1.call-start = ((), (), s32[]{:S(2)}) async-start(), calls=%async_computation.6 | async-start | bytes 7077888 | tf_op jit(solution)/shard_map/all_gather | solution.py:1623
  7.9 304.1 %all-gather.9.cloned.1.call-start = ((), (), s32[]{:S(2)}) async-start(), calls=%async_computation.7 | async-start | bytes 14155776 | tf_op jit(solution)/shard_map/all_gather | solution.py:1629
  11.0 1.0 copy-start.4
  12.1 1.4 copy-start.3
  13.4 384.0 %all-gather.11.cloned.1.call-start = ((), (), s32[]{:S(2)}) async-start(), calls=%async_computation.8 | async-start | bytes 14155776 | tf_op jit(solution)/shard_map/all_gather | solution.py:1629
  13.7 1.4 copy-start.11
  13.7 1.4 copy-start.12
  15.0 123.3 %copy-start.13 = (f32[4]{0:T(128)S(1)}, f32[4]{0:T(128)}, u32[]{:S(2)}) copy-start(f32[4]{0:T(128)} %param.20) | copy-start | bytes 52
  15.0 620.5 %reduce-scatter.4.cloned.1.call-start = ((), (), s32[]{:S(2)}) async-start(), calls=%async_computation.3 | async-start | bytes 14155776 | tf_op jit(solution)/shard_map/reduce_scatter | solution.py:1598
  397.1 323.7 %reduce-scatter.6.cloned.1.call-start = ((), (), s32[]{:S(2)}) async-start(), calls=%async_computation.4 | async-start | bytes 14155776 | tf_op jit(solution)/shard_map/reduce_scatter | solution.py:1598
  503.3 311.7 %reduce-scatter.8.cloned.1.call-start = ((), (), s32[]{:S(2)}) async-start(), calls=%async_computation.5 | async-start | bytes 9437184 | tf_op jit(solution)/shard_map/reduce_scatter | solution.py:1598
  635.5 0.9 copy-start.6
  635.5 1.1 copy-start.10
  635.5 1.2 copy-start.7
  720.9 1.4 copy-start
  720.9 1.9 copy-start.1
  722.8 1.2 slice-start
  722.8 1.5 slice-start.1
  724.3 2.6 copy-start.8
  724.3 2.6 copy-start.9
  815.0 4.6 copy-start.5
Sparse Core Ops, SparseCore 0:
  9.7 115.5 all-gather.6
  127.5 144.5 all-gather.8
  274.3 114.8 all-gather.10
  397.3 128.1 reduce-scatter.3
  527.6 133.0 reduce-scatter.5
  662.8 131.2 reduce-scatter.7

commit v9 on v8

--- a/solution.py
+++ b/solution.py
@@ -346,7 +346,7 @@
 VMEM = pl.BlockSpec(memory_space=pltpu.VMEM)
 MESH_ID = pl.DeviceIdType.MESH
 HALF = D // 2
-AG_CUTS = 4
+AG_CUTS = 8
 
 
 def remote(source, target, send, receive, device):

time: 830 us -> 830 us (level)
  no operation moved by 1% of the time
where the time goes in v9:
time: 830 us; the launch traced here: 828 us
  Pallas kernels  781 us (94%)
  local copies, waits for them, and re-layouts  17.3 us (2%)
  between operations  14.4 us (2%)
  other arithmetic  14.2 us (2%)
    pallas_call x1, Pallas kernels, enter(): pl.pallas_call(kernel, out_shape=[bf(piece, D), bf(piece, D), fl(1, D), f...  123 us
    pallas_call x1, Pallas kernels, project_heads(): pl.pallas_call(kernel, out_shape=[bf(3, heads, GLEN, HD), bf(size, piece,...  95.1 us
    pallas_call x2, Pallas kernels, feed_forward(): pl.pallas_call(kernel, out_shape=out_shape, in_specs=[ANY] * 3, out_specs...  93.2 us
    pallas_call x1, Pallas kernels, stream_back(): pl.pallas_call(kernel, out_shape=[bf(cols, piece, depth), fl(1, D), bf(co...  84.4 us
    pallas_call x1, Pallas kernels, leave(): pl.pallas_call(kernel, out_shape=[bf(groups, size, piece, depth), fl(grou...  77.6 us
    pallas_call x1, Pallas kernels, middle_back(): pl.pallas_call(kernel, out_shape=[fl(piece, D), bf(piece, D), fl(1, D), b...  71.1 us
    pallas_call x1, Pallas kernels, branch_out(): pl.pallas_call(kernel, out_shape=[fl(piece, D), bf(piece, D), fl(piece, H...  61.8 us
    pallas_call x1, Pallas kernels, attend_back(): pl.pallas_call(functools.partial(attend_back_kernel, size, cols, depth, w...  60.6 us
  transfers between devices with their start and end apart: 6, of which 0 were waited for; matrix products, arithmetic and copies ran while one was open for 3% of the time, Pallas kernels for 94%

profile of v9, /device:TPU:27, one launch (start us, length us, event | category | flops | bytes accessed | tf_op | source)
XLA Modules:
  0.0 828.2 jit_solution(2701460943694706906)
XLA Ops:
  7.2 0.7 all-gather.7.cloned.1.call-update
  8.0 2.1 fusion.3
  10.0 1.0 copy.37
  11.0 0.2 fusion.2
  11.2 0.9 copy-done.4
  12.1 1.3 pad_maximum_fusion
  13.4 0.0 all-gather.11.cloned.1.call-start
  13.4 0.2 copy.38
  13.7 1.3 pad_maximum_fusion.1
  15.0 0.0 reduce-scatter.4.cloned.1.call-start
  15.1 0.6 select_maximum_fusion.gains_ref
  15.7 122.8 %enter.1 = (bf16[384,2048]{1,0:T(8,128)(2,1)}, bf16[384,2048]{1,0:T(8,128)(2,1)}, f32[1,2048]{1,0:T(1,128)}, f32[1,2048]{1,0:T(1,128)}, bf16[384,2048]{1,0:T(8,128)(2,1)}, /*index=5*/bf16[4,384,2048]{2,1,0:T(8,128)(2,1)}) custom-call(bf16[2,4,384,256]{3,2,1,0:T(8,128)(2,1)} %bitcast.65, bf16[2,4,384,256]{3,2,1,0:T(8,128)(2,1)} %bitcast.66, ...), custom_call_target="tpu_custom_call" | custom-call | flops 1000 | bytes 1000 | tf_op jit(solution)/shard_map/enter/pallas_call | solution.py:1482
  138.5 0.5 add_divide_fusion.gate_ref
  139.0 95.1 %project_heads.1 = (bf16[3,4,1536,128]{3,2,1,0:T(8,128)(2,1)}, bf16[4,384,2048]{2,1,0:T(8,128)(2,1)}, bf16[8,512,256]{2,1,0:T(8,128)(2,1)}) custom-call(bf16[384,2048]{1,0:T(8,128)(2,1)} %get-tuple-element.59.x_ref, bf16[8,3,256,512]{3,2,1,0:T(8,128)(2,1)} %bitcast.59, bf16[512,256]{1,0:T(8,128)(2,1)} %out_ref.1), custom_call_target="tpu_custom_call" | custom-call | flops 1000 | bytes 1000 | tf_op jit(solution)/shard_map/project_heads/pallas_call | solution.py:768
  234.1 16.6 %attend.1 = (bf16[1536,512]{1,0:T(8,128)(2,1)}, f32[4,1536,128]{2,1,0:T(8,128)}, f32[4,1536,128]{2,1,0:T(8,128)}, f32[4,1536,1]{2,1,0:T(8,128)}, f32[4,128,128]{2,1,0:T(8,128)}, /*index=5*/f32[4,1,128]{2,1,0:T(1,128)}) custom-call(s32[4]{0:T(128)} %bitcast.75, s32[4]{0:T(128)} %bitcast.77, f32[4]{0:T(128)} %add_divide_fusion.gate_ref, ...), custom_call_target="tpu_custom_call" | custom-call | flops 1000 | bytes 1000 | tf_op jit(solution)/shard_map/attend/pallas_call | solution.py:151
  250.7 61.8 %branch_out.1 = (f32[384,2048]{1,0:T(8,128)}, bf16[384,2048]{1,0:T(8,128)(2,1)}, f32[384,128]{1,0:T(8,128)}) custom-call(bf16[1536,512]{1,0:T(8,128)(2,1)} %get-tuple-element.61.attn_ref.h_ref, bf16[8,512,256]{2,1,0:T(8,128)(2,1)} %get-tuple-element.62.w_ref, bf16[384,2048]{1,0:T(8,128)(2,1)} %get-tuple-element.63.x_hbm, f32[1,2048]{1,0:T(1,128)} %get-tuple-element.64.gain_ref), custom_call_target="tpu_custom_call" | custom-call | flops 1000 | bytes 1000 | tf_op jit(solution)/shard_map/branch_out/pallas_call | solution.py:843
  312.5 58.6 %feed_first.1 = (bf16[1536,1024]{1,0:T(8,128)(2,1)}, bf16[2,1536,1024]{2,1,0:T(8,128)(2,1)}, bf16[4,384,2048]{2,1,0:T(8,128)(2,1)}) custom-call(bf16[384,2048]{1,0:T(8,128)(2,1)} %get-tuple-element.65.x_ref, bf16[8,3,256,1024]{3,2,1,0:T(8,128)(2,1)} %bitcast.51, bf16[4,384,2048]{2,1,0:T(8,128)(2,1)} %get-tuple-element.66.cot_ref.y_ref), custom_call_target="tpu_custom_call" | custom-call | flops 1000 | bytes 1000 | tf_op jit(solution)/shard_map/feed_first/pallas_call | solution.py:961
  371.0 26.8 %weight_grads.2 = bf16[3,2048,1024]{2,1,0:T(8,128)(2,1)} custom-call(bf16[1536,2048]{1,0:T(8,128)(2,1)} %bitcast.58, bf16[1536,2048]{1,0:T(8,128)(2,1)} %bitcast.57, bf16[2,1536,1024]{2,1,0:T(8,128)(2,1)} %get-tuple-element.67.g_ref.first_ref, bf16[1536,1024]{1,0:T(8,128)(2,1)} %get-tuple-element.69.h_ref.hidden_a), custom_call_target="tpu_custom_call" | custom-call | flops 1000 | bytes 1000 | tf_op jit(solution)/shard_map/weight_grads/pallas_call | solution.py:991
  397.8 0.2 reduce-scatter.6.cloned.1.call-start
  398.1 34.7 %feed_second.1 = (bf16[1536,1024]{1,0:T(8,128)(2,1)}, bf16[2,1536,1024]{2,1,0:T(8,128)(2,1)}) custom-call(bf16[4,384,2048]{2,1,0:T(8,128)(2,1)} %get-tuple-element.70.x_ref, bf16[8,3,256,1024]{3,2,1,0:T(8,128)(2,1)} %bitcast.54, bf16[4,384,2048]{2,1,0:T(8,128)(2,1)} %get-tuple-element.66.cot_ref.y_ref), custom_call_target="tpu_custom_call" | custom-call | flops 1000 | bytes 1000 | tf_op jit(solution)/shard_map/feed_second/pallas_call | solution.py:961
  432.8 71.1 %middle_back.1 = (f32[384,2048]{1,0:T(8,128)}, bf16[384,2048]{1,0:T(8,128)(2,1)}, f32[1,2048]{1,0:T(1,128)}, bf16[3,2048,1024]{2,1,0:T(8,128)(2,1)}) custom-call(bf16[2,1536,1024]{2,1,0:T(8,128)(2,1)} %get-tuple-element.67.g_ref.first_ref, bf16[2,1536,1024]{2,1,0:T(8,128)(2,1)} %get-tuple-element.71.second_ref, bf16[8,3,256,1024]{3,2,1,0:T(8,128)(2,1)} %bitcast.52, ...), custom_call_target="tpu_custom_call" | custom-call | flops 1000 | bytes 1000 | tf_op jit(solution)/shard_map/middle_back/pallas_call | solution.py:1142
  503.9 0.0 reduce-scatter.8.cloned.1.call-start
  504.0 52.0 %branch_back.1 = (bf16[4,1536,128]{2,1,0:T(8,128)(2,1)}, bf16[4,384,2048]{2,1,0:T(8,128)(2,1)}) custom-call(bf16[384,2048]{1,0:T(8,128)(2,1)} %get-tuple-element.75.x_ref, bf16[8,512,256]{2,1,0:T(8,128)(2,1)} %get-tuple-element.62.w_ref), custom_call_target="tpu_custom_call" | custom-call | flops 1000 | bytes 1000 | tf_op jit(solution)/shard_map/branch_back/pallas_call | solution.py:1195
  556.0 60.6 %attend_back.1 = (bf16[3,1536,512]{2,1,0:T(8,128)(2,1)}, f32[4,1,128]{2,1,0:T(1,128)}, bf16[8,384,256]{2,1,0:T(8,128)(2,1)}, f32[384,128]{1,0:T(8,128)}) custom-call(s32[4]{0:T(128)} %bitcast.76, s32[4]{0:T(128)} %bitcast.78, f32[4]{0:T(128)} %add_divide_fusion.gate_ref, bf16[3,4,1536,128]{3,2,1,0:T(8,128)(2,1)} %get-tuple-element.60.qkv_ref, ...), custom_call_target="tpu_custom_call" | custom-call | flops 1000 | bytes 1000 | tf_op jit(solution)/shard_map/attend_back/pallas_call | solution.py:314
  616.6 19.1 %weight_grads.3 = bf16[4,2048,512]{2,1,0:T(8,128)(2,1)} custom-call(bf16[1536,2048]{1,0:T(8,128)(2,1)} %bitcast.61, bf16[1536,2048]{1,0:T(8,128)(2,1)} %bitcast.62, bf16[3,1536,512]{2,1,0:T(8,128)(2,1)} %get-tuple-element.84.g_ref.g_hbm, bf16[1536,512]{1,0:T(8,128)(2,1)} %get-tuple-element.61.attn_ref.h_ref), custom_call_target="tpu_custom_call" | custom-call | flops 1000 | bytes 1000 | tf_op jit(solution)/shard_map/weight_grads/pallas_call | solution.py:991
  635.8 0.9 copy-done.6
  636.7 0.1 copy.33
  636.8 0.1 reduce_sum.9
  637.0 0.1 copy.34
  637.1 0.6 pad.13.stats_ref
  637.7 84.4 %stream_back.1 = (bf16[8,384,256]{2,1,0:T(8,128)(2,1)}, f32[1,2048]{1,0:T(1,128)}, bf16[2,4,384,256]{3,2,1,0:T(8,128)(2,1)}) custom-call(bf16[3,1536,512]{2,1,0:T(8,128)(2,1)} %get-tuple-element.84.g_ref.g_hbm, bf16[8,3,256,512]{3,2,1,0:T(8,128)(2,1)} %bitcast.60, bf16[384,2048]{1,0:T(8,128)(2,1)} %get-tuple-element.63.x_hbm, ...), custom_call_target="tpu_custom_call" | custom-call | flops 1000 | bytes 1000 | tf_op jit(solution)/shard_map/stream_back/pallas_call | solution.py:1263
  722.2 1.4 copy-done
  723.6 0.4 copy-done.1
  724.1 0.2 convert_bitcast_fusion
  724.3 1.0 slice-done
  725.3 0.3 slice-done.1
  725.6 2.5 maximum_convert_fusion
  728.2 0.7 pad_maximum_fusion.2.sums_ref
  728.9 77.6 %leave.1 = (bf16[2,4,384,256]{3,2,1,0:T(8,128)(2,1)}, f32[2,4,8,384]{3,2,1,0:T(8,128)}, f32[8,256]{1,0:T(8,128)}) custom-call(bf16[8,384,256]{2,1,0:T(8,128)(2,1)} %get-tuple-element.92.grad_ref, f32[8,384]{1,0:T(8,128)} %pad.13.stats_ref, f32[8,8,256]{2,1,0:T(8,128)} %pad_maximum_fusion.2.sums_ref), custom_call_target="tpu_custom_call" | custom-call | flops 1000 | bytes 1000 | tf_op jit(solution)/shard_map/leave/pallas_call | solution.py:1574
  806.5 1.5 slice.63
  808.0 1.8 copy.36
  809.8 1.2 slice_bitcast_fusion.3
  811.0 1.3 fusion.4
  812.3 3.3 bitcast_convert_fusion
  815.6 1.1 convert_bitcast_fusion.1
  816.8 1.0 copy.35
  817.8 2.5 slice_convert_fusion
  820.3 1.1 copy.40
  (47 shorter events, 0.4 us)
Async XLA Ops:
  7.2 3.9 copy-start.2
  7.2 131.8 %all-gather.7.cloned.1.call-start = ((), (), s32[]{:S(2)}) async-start(), calls=%async_computation.6 | async-start | bytes 7077888 | tf_op jit(solution)/shard_map/all_gather | solution.py:1623
  7.9 304.5 %all-gather.9.cloned.1.call-start = ((), (), s32[]{:S(2)}) async-start(), calls=%async_computation.7 | async-start | bytes 14155776 | tf_op jit(solution)/shard_map/all_gather | solution.py:1629
  11.0 1.0 copy-start.4
  12.1 1.4 copy-start.3
  13.4 384.7 %all-gather.11.cloned.1.call-start = ((), (), s32[]{:S(2)}) async-start(), calls=%async_computation.8 | async-start | bytes 14155776 | tf_op jit(solution)/shard_map/all_gather | solution.py:1629
  13.7 1.4 copy-start.11
  13.7 1.4 copy-start.12
  15.0 123.5 %copy-start.13 = (f32[4]{0:T(128)S(1)}, f32[4]{0:T(128)}, u32[]{:S(2)}) copy-start(f32[4]{0:T(128)} %param.20) | copy-start | bytes 52
  15.0 620.8 %reduce-scatter.4.cloned.1.call-start = ((), (), s32[]{:S(2)}) async-start(), calls=%async_computation.3 | async-start | bytes 14155776 | tf_op jit(solution)/shard_map/reduce_scatter | solution.py:1598
  397.8 324.3 %reduce-scatter.6.cloned.1.call-start = ((), (), s32[]{:S(2)}) async-start(), calls=%async_computation.4 | async-start | bytes 14155776 | tf_op jit(solution)/shard_map/reduce_scatter | solution.py:1598
  503.9 311.7 %reduce-scatter.8.cloned.1.call-start = ((), (), s32[]{:S(2)}) async-start(), calls=%async_computation.5 | async-start | bytes 9437184 | tf_op jit(solution)/shard_map/reduce_scatter | solution.py:1598
  635.8 0.9 copy-start.6
  635.8 1.1 copy-start.10
  635.8 1.2 copy-start.7
  722.1 1.4 copy-start
  722.2 1.9 copy-start.1
  724.0 1.2 slice-start
  724.0 1.6 slice-start.1
  725.6 2.6 copy-start.8
  725.6 2.6 copy-start.9
  815.6 4.6 copy-start.5
Sparse Core Ops, SparseCore 0:
  9.7 115.5 all-gather.6
  127.5 144.5 all-gather.8
  274.3 114.8 all-gather.10
  397.9 127.9 reduce-scatter.3
  528.0 132.4 reduce-scatter.5
  662.7 131.3 reduce-scatter.7
